TPU v7x, 256 devices: a whole 4x4x8 slice. The times are simulated.
256 devices in a mesh: shot: 32 (over y_hi, z, core), rcv: 8 (over x, y_lo).
Axes of the slice: x: 4, y: 4 (y_hi: 2, y_lo: 2; y = y_hi * 2 + y_lo), z: 8, core: 2. Of those that a mesh axis runs over, the one named last changes fastest.
Arguments:
- record: bfloat16 [768, 262144], P('rcv', 'shot'), may hold values from -6 to 6
- shot_fire_samples: int32 [1024], P('shot'), may hold values from 0 to 262143, as said below
Outputs:
- psf_gram: float32 [2, 4, 768, 768], P(None, None, 'rcv', 'shot')
Inputs may be any that keep to these rules, and one draw needn't show every extreme that they name: `shot_fire_samples`: shot s fires at a sample from s * 256 to s * 256 + 255.
All inputs are finite; a program needn't handle non-finite values.
Results may differ from a plain program's by a relative error of at most 0.0025.
Values may be sent and summed in bfloat16 or wider, within the bound.
No kernel may reach another device: no remote copies, remote signals or barrier semaphores. Data moves between devices by JAX's collectives and lax.ppermute only.
A program may use at most 64 MiB of HBM per device.

v0:
```python
import math

import jax
import jax.numpy as jnp
from jax import lax
from jax.sharding import PartitionSpec as P

WIN = 2048
SPACING = 256


freq_bins = (24, 40, 56, 80)


def shifted(block, axis, distance):
    devices = range(lax.axis_size(axis))
    route = [(i - distance, i) for i in devices if i - distance in devices]
    return lax.ppermute(block, axis, route)


def dft_table(window_len):
    lag_index = jnp.arange(window_len, dtype=jnp.int32)
    bin_list = jnp.array(freq_bins, dtype=jnp.int32)
    turn_count = lag_index[:, None] * bin_list[None, :] % window_len
    phase_angle = 2.0 * math.pi / window_len * turn_count.astype(jnp.float32)
    dft_rows = jnp.concatenate([jnp.cos(phase_angle), -jnp.sin(phase_angle)], axis=1) / math.sqrt(
        window_len
    )
    return dft_rows.astype(jnp.bfloat16)


def shifted_tables(jitter, span):
    lag_index = jnp.arange(span, dtype=jnp.int32)[None, :] - jitter[:, None]
    inside = (lag_index >= 0) & (lag_index < WIN)
    clipped = jnp.clip(lag_index, 0, WIN - 1)
    bin_list = jnp.array(freq_bins, dtype=jnp.int32)
    turn_count = clipped[:, None, :] * bin_list[None, :, None] % WIN
    phase_angle = 2.0 * math.pi / WIN * turn_count.astype(jnp.float32)
    table = jnp.concatenate([jnp.cos(phase_angle), -jnp.sin(phase_angle)], axis=1) / math.sqrt(WIN)
    table = jnp.where(inside[:, None, :], table, 0.0)
    return table.astype(jnp.bfloat16)


def local_spectra(extended, sample_offsets, dft_rows):
    count_of_shots = sample_offsets.shape[0]
    reach_blocks = WIN // SPACING + 1
    jitter = sample_offsets - jnp.arange(count_of_shots, dtype=jnp.int32) * SPACING
    tables = shifted_tables(jitter, reach_blocks * SPACING)
    tables = tables.reshape(count_of_shots, dft_rows.shape[1], reach_blocks, SPACING)
    blocks = extended.reshape(extended.shape[0], extended.shape[1] // SPACING, SPACING)
    total = jnp.zeros((count_of_shots, dft_rows.shape[1], extended.shape[0]), jnp.float32)
    for offset in range(reach_blocks):
        record_part = blocks[:, offset : offset + count_of_shots, :]
        total = total + jnp.einsum(
            "rsu,scu->scr", record_part, tables[:, :, offset, :], preferred_element_type=jnp.float32
        )
    return total


def gram_terms(left, right):
    nfreq = len(freq_bins)
    left_re = left[:, :nfreq, :]
    left_im = left[:, nfreq:, :]
    right_re = right[:, :nfreq, :]
    right_im = right[:, nfreq:, :]
    gram_real = jnp.einsum("sfr,sfq->frq", left_re, right_re, preferred_element_type=jnp.float32)
    gram_real = gram_real + jnp.einsum(
        "sfr,sfq->frq", left_im, right_im, preferred_element_type=jnp.float32
    )
    gram_imag = jnp.einsum("sfr,sfq->frq", left_re, right_im, preferred_element_type=jnp.float32)
    gram_imag = gram_imag - jnp.einsum(
        "sfr,sfq->frq", left_im, right_re, preferred_element_type=jnp.float32
    )
    return jnp.stack([gram_real, gram_imag], axis=0)


def per_device(record, shot_fire_samples):
    trace_segment_length = record.shape[1]
    count_of_shots = shot_fire_samples.shape[0]
    dft_rows = dft_table(WIN)
    sample_offsets = shot_fire_samples - lax.axis_index("shot") * trace_segment_length
    head_rows = record[:, :WIN]
    rim_rows = shifted(head_rows, "shot", -1)
    extended = jnp.concatenate([record, rim_rows], axis=1)
    trace_spectra = local_spectra(extended, sample_offsets, dft_rows)
    trace_spectra = trace_spectra.astype(jnp.bfloat16)
    all_receivers = lax.all_gather(trace_spectra, "rcv", axis=2, tiled=True)
    total_shots = count_of_shots * lax.axis_size("shot")
    partial_gram = gram_terms(trace_spectra, all_receivers)
    result = lax.psum_scatter(partial_gram, "shot", scatter_dimension=3, tiled=True)
    return result / total_shots


def solution(mesh):
    return jax.shard_map(
        per_device,
        mesh=mesh,
        in_specs=(P("rcv", "shot"), P("shot")),
        out_specs=P(None, None, "rcv", "shot"),
        check_vma=False,
    )
```

profile of v0, /device:TPU:4, one launch (start us, length us, event | category | flops | bytes accessed | tf_op | source)
XLA Modules:
  0.0 362.5 jit_solution(5917377322379942619)
XLA Ops:
  6.5 0.0 all-reduce.3.cloned.1.call-start
  6.5 1.0 slice.70
  7.6 1.3 collective-permute-start
  8.9 0.7 multiply_subtract_fusion
  9.5 0.1 subtract_clamp_fusion
  9.7 10.4 %fusion.52 = (f32[32,4,9,256]{3,1,0,2:T(4,128)S(1)}, f32[32,4,9,256]{3,1,0,2:T(4,128)S(1)}) fusion(s32[4]{0:T(128)} %constant.43.clone, s32[32,9,256]{2,0,1:T(8,128)S(1)} %subtract_clamp_fusion), kind=kLoop, calls=%fused_computation.45 | loop fusion | flops 4423680 | bytes 2654224 | tf_op jit(solution)/shard_map/cos | solution.py:39
  20.1 0.1 fusion.53
  20.2 0.0 copy-start
  20.2 0.8 fusion.1
  21.1 0.0 collective-permute-done
  21.1 0.5 copy-done
  21.6 0.1 pad_maximum_fusion.1
  21.8 0.5 copy.78
  22.3 3.3 fusion.60
  25.6 0.9 fusion.16
  26.5 0.9 fusion.14
  27.5 0.9 fusion.12
  28.4 0.9 fusion.8
  29.4 0.9 fusion.6
  30.3 0.9 fusion.2
  31.2 1.0 fusion.31
  32.2 1.0 fusion.40
  33.2 1.0 fusion.49
  34.2 0.2 copy.58
  34.4 34.7 %all_gather.3 = bf16[32,8,768]{0,1,2:T(8,128)(2,1)S(1)} all-gather(bf16[32,8,96]{0,1,2:T(8,128)(2,1)S(1)} %copy.58), channel_id=1, replica_groups=mesh['shot'=32,'rcv'=8] {'rcv'}, dimensions={2}, use_global_device_ids=true | all-gather | bytes 442368 | tf_op jit(solution)/shard_map/all_gather | solution.py:87
  69.1 0.5 fusion.61
  69.6 0.5 copy.76
  70.1 0.5 copy.77
  70.6 0.4 fusion.58
  71.0 0.4 fusion.56
  71.3 0.4 fusion.21
  71.7 0.4 fusion.20
  72.1 0.2 pad_maximum_fusion
  72.2 2.8 copy.65
  75.1 0.0 copy-start.1
  75.1 0.0 all-reduce.3.cloned.1.call-update
  75.1 0.6 copy-done.1
  75.7 0.6 dynamic-slice
  77.0 277.1 %all-reduce.3.cloned.1.call-done = f32[2,4,96,768]{2,1,0,3:T(4,128)} async-done(((f32[2,4,96,768]{2,1,0,3:T(4,128)}), f32[2,4,96,768]{2,1,0,3:T(4,128)}) %all-reduce.3.cloned.1.call-update) | async-done | bytes 2359312
  354.1 0.9 constant_dynamic-slice_fusion
  355.0 0.7 copy_multiply_fusion
  (2 shorter events, 0.0 us)
Async XLA Ops:
  6.5 347.5 %all-reduce.3.cloned.1.call-start = ((), (), s32[]{:S(2)}) async-start(), calls=%async_computation | async-start | bytes 6291456
  7.6 13.5 %collective-permute-start = (bf16[96,2048]{1,0:T(8,128)(2,1)S(1)}, bf16[96,2048]{1,0:T(8,128)(2,1)S(1)}, u32[]{:S(2)}, u32[]{:S(2)}) collective-permute-start(bf16[96,2048]{1,0:T(8,128)(2,1)S(1)} %slice.70), channel_id=1, source_target_pairs={{8,0},{16,8},{24,16},{32,24},{40,32},{48,40},{56,48},{64,56},{72,6... | collective-permute-start | bytes 1179656 | tf_op jit(solution)/shard_map/ppermute | solution.py:18
  20.2 1.4 copy-start
  75.1 0.7 copy-start.1
Sparse Core Ops, SparseCore 0:
  75.2 278.8 all-reduce.2
where the time goes:
time: 364 us; the launch traced here: 362 us
  waiting for transfers between devices  277 us (76%)
  blocking collectives  34.7 us (10%)
  between operations  14.2 us (4%)
  other arithmetic  13.1 us (4%)
  local copies, waits for them, and re-layouts  12 us (3%)
  matrix products  9.99 us (3%)
    unnamed x2, waiting for transfers between devices  277 us
    all_gather x1, blocking collectives, per_device(): all_receivers = lax.all_gather(trace_spectra, 'rcv', axis=2, tiled=True)  34.7 us
    cos x1, other arithmetic, shifted_tables(): jnp.cos(phase_angle)  10.4 us
    dot_general x9, matrix products, local_spectra(): jnp.einsum('rsu,scu->scr', record_part, tables[:, :, offset, :], preferre...  8.57 us
  transfers between devices with their start and end apart: 2, of which 1 were waited for; matrix products, arithmetic and copies ran while one was open for 4% of the time, Pallas kernels for 0%

commit v1 on v0

v1 whole, which is shorter than its diff:
```python
import math

import jax
import jax.numpy as jnp
import numpy as np
from jax import lax
from jax.experimental import pallas as pl
from jax.experimental.pallas import tpu as pltpu
from jax.sharding import PartitionSpec as P

import ml_dtypes

WIN = 2048
SPACING = 256
PAIR = 2 * SPACING
SPAN = WIN + PAIR
FREQ_BINS = (24, 40, 56, 80)
NF = len(FREQ_BINS)
ROWS = 2 * NF

SHOT_DEVICES = 32
RCV_DEVICES = 8
QUARTERS = 4


def dft_master():
    turns = np.arange(WIN)[None, :] * np.array(FREQ_BINS)[:, None] % WIN
    angle = 2.0 * math.pi / WIN * turns
    rows = np.concatenate([np.cos(angle), -np.sin(angle)], axis=0) / math.sqrt(WIN)
    rows = rows.astype(np.float32).astype(ml_dtypes.bfloat16).astype(np.float32)
    return np.concatenate([rows, np.zeros((ROWS, SPAN - WIN), np.float32)], axis=1)


def send(block, to):
    route = []
    for shot in range(SHOT_DEVICES):
        for rcv in range(RCV_DEVICES):
            target = to(shot >> 3, (shot >> 2) & 1, shot & 3, rcv >> 1, rcv & 1)
            if target is not None:
                e, z1, k, x, yl = target
                route.append((shot * RCV_DEVICES + rcv, (e << 3 | z1 << 2 | k) * RCV_DEVICES + (x << 1 | yl)))
    return lax.ppermute(block, ("shot", "rcv"), route)


def shot_index():
    return lax.axis_index("shot")


def vmem(count):
    return [pl.BlockSpec(memory_space=pltpu.VMEM)] * count


def own_kernel(fire, table, record, total, tables, scratch):
    pairs = total.shape[0] // (2 * ROWS)
    reach = SPAN // PAIR
    master = table[...]
    for p in range(pairs):
        first = pltpu.roll(master, fire[2 * p] & (SPACING - 1), 1)
        second = pltpu.roll(master, (fire[2 * p + 1] & (SPACING - 1)) + SPACING, 1)
        scratch[p] = jnp.concatenate([first, second], axis=0).astype(jnp.bfloat16)
    total[...] = jnp.zeros_like(total)
    for u in range(pairs):
        low = max(0, u - reach + 1)
        left = jnp.concatenate(
            [scratch[p, :, PAIR * (u - p) : PAIR * (u - p + 1)] for p in range(low, u + 1)], axis=0
        )
        part = lax.dot_general(
            left, record[:, PAIR * u : PAIR * (u + 1)], (((1,), (1,)), ((), ())), preferred_element_type=jnp.float32
        )
        rows = slice(2 * ROWS * low, 2 * ROWS * (u + 1))
        total[rows, :] += part
    for p in range(reach - 1):
        tables[p] = scratch[pairs - reach + 1 + p]


def rim_kernel(total, tables, rim, out, scratch):
    pairs = total.shape[0] // (2 * ROWS)
    reach = SPAN // PAIR
    scratch[...] = total[...]
    for v in range(reach - 1):
        u = pairs + v
        low = u - reach + 1
        left = jnp.concatenate(
            [tables[p - (pairs - reach + 1), :, PAIR * (u - p) : PAIR * (u - p + 1)] for p in range(low, pairs)], axis=0
        )
        part = lax.dot_general(
            left, rim[:, PAIR * v : PAIR * (v + 1)], (((1,), (1,)), ((), ())), preferred_element_type=jnp.float32
        )
        scratch[2 * ROWS * low :, :] += part
    shots = 2 * pairs
    ordered = jnp.concatenate([scratch[pl.ds(c, shots, stride=ROWS), :] for c in range(ROWS)], axis=0)
    turned = ordered.T
    count = out.shape[1]
    for k in range(QUARTERS):
        out[k] = turned[count * k : count * (k + 1), :].astype(out.dtype)


def collect_kernel(y0, y1, y2, y3, gathered, quarter):
    k = shot_index() & 3
    for m, y in enumerate((y0, y1, y2, y3)):
        gathered[k ^ m] = y[...]
        quarter[k ^ m] = y[k]


def choose_kernel(own, ring, cross, out):
    straight = ((shot_index() >> 2) & 1) == (lax.axis_index("rcv") & 1)

    @pl.when(straight)
    def _():
        out[0] = own[...]

    @pl.when(jnp.logical_not(straight))
    def _():
        out[0] = cross[...]

    out[1] = ring[...]


def gram_kernel(scale, here, there, q0, q1, q2, q3, p0, p1, p2, p3, right, total):
    shot, rcv = shot_index(), lax.axis_index("rcv")
    e, x = shot >> 3, rcv >> 1
    swapped = ((shot >> 2) & 1) ^ (rcv & 1)
    count = q0.shape[2]
    lanes = q0.shape[3]
    half = lanes // 2
    span = QUARTERS * count
    for slot, block in ((swapped, here), (1 - swapped, there)):
        for k in range(QUARTERS):
            z = block[k].astype(jnp.float32).reshape(span, lanes)
            w = jnp.concatenate([-z[:, half:], z[:, :half]], axis=1)
            right[slot, k] = jnp.concatenate([z, w], axis=0).astype(jnp.bfloat16)
    per = half // NF
    lane = lax.broadcasted_iota(jnp.int32, (count, lanes), 1) % half // per
    for t, q in enumerate((q0, q1, q2, q3)):
        acc = jnp.zeros((NF * count, 2 * span), jnp.float32)
        for slot in range(2):
            for k in range(QUARTERS):
                rows = q[slot, k].astype(jnp.float32)
                left = jnp.concatenate([jnp.where(lane == f, rows, 0.0) for f in range(NF)], axis=0)
                acc = acc + lax.dot_general(
                    left.astype(jnp.bfloat16),
                    right[slot, k],
                    (((1,), (1,)), ((), ())),
                    preferred_element_type=jnp.float32,
                )
        m = (x + t - e) & 3
        total[m, : NF * count, :] = acc[:, :span] * scale
        total[m, NF * count :, :] = acc[:, span:] * scale
    for m, out in enumerate((p0, p1, p2, p3)):
        out[...] = total[m].astype(out.dtype)


def per_device(record, shot_fire_samples):
    receivers, samples = record.shape
    shots = shot_fire_samples.shape[0]
    pairs = shots // 2
    reach = SPAN // PAIR
    lanes = ROWS * shots
    count = receivers // QUARTERS
    bf16, f32 = jnp.bfloat16, jnp.float32
    shape = jax.ShapeDtypeStruct

    def before(e, z1, k, x, yl):
        shot = (e << 3 | z1 << 2 | k) - 1
        return None if shot < 0 else (shot >> 3, (shot >> 2) & 1, shot & 3, x, yl)

    rim = send(record[:, :WIN], before)
    total, tables = pl.pallas_call(
        own_kernel,
        out_shape=(shape((lanes, receivers), f32), shape((reach - 1, 2 * ROWS, SPAN), bf16)),
        in_specs=[pl.BlockSpec(memory_space=pltpu.SMEM)] + vmem(2),
        out_specs=tuple(vmem(2)),
        scratch_shapes=[pltpu.VMEM((pairs, 2 * ROWS, SPAN), bf16)],
        cost_estimate=pl.CostEstimate(
            flops=2 * lanes * receivers * SPAN, bytes_accessed=2 * receivers * samples, transcendentals=0
        ),
        name="own_spectra",
    )(shot_fire_samples, jnp.asarray(dft_master()), record)
    y0 = pl.pallas_call(
        rim_kernel,
        out_shape=shape((QUARTERS, count, lanes), bf16),
        in_specs=vmem(3),
        out_specs=vmem(1)[0],
        scratch_shapes=[pltpu.VMEM((lanes, receivers), f32)],
        name="rim_spectra",
    )(total, tables, rim)

    ys = [send(y0, lambda e, z1, k, x, yl, m=m: (e, z1, k ^ m, x, yl)) for m in (1, 2, 3)]
    here, own = pl.pallas_call(
        collect_kernel,
        out_shape=(shape((QUARTERS, QUARTERS, count, lanes), bf16), shape((QUARTERS, count, lanes), bf16)),
        in_specs=vmem(4),
        out_specs=tuple(vmem(2)),
        name="collect",
    )(y0, *ys)

    turn = {(1, 0): (0, 0), (0, 0): (0, 1), (0, 1): (1, 1), (1, 1): (1, 0)}
    ring = send(own, lambda e, z1, k, x, yl: (e, turn[z1, yl][0], k, x, turn[z1, yl][1]))
    cross = send(own, lambda e, z1, k, x, yl: (e, yl, k, x, z1) if z1 != yl else None)
    there = send(here, lambda e, z1, k, x, yl: (e, 1 - z1, k, x, yl))
    q0 = pl.pallas_call(
        choose_kernel,
        out_shape=shape((2, QUARTERS, count, lanes), bf16),
        in_specs=vmem(3),
        out_specs=vmem(1)[0],
        name="choose",
    )(own, ring, cross)
    qs = [send(q0, lambda e, z1, k, x, yl, t=t: (e, z1, k, (x - t) & 3, yl)) for t in (1, 3, 2)]
    q1, q3, q2 = qs

    total_shots = shots * lax.axis_size("shot")
    rows = 2 * NF * count
    p0, p1, p2, p3 = pl.pallas_call(
        lambda *refs: gram_kernel(1.0 / total_shots, *refs),
        out_shape=(shape((rows, receivers), f32),) + (shape((rows, receivers), bf16),) * 3,
        in_specs=vmem(6),
        out_specs=tuple(vmem(4)),
        scratch_shapes=[
            pltpu.VMEM((2, QUARTERS, 2 * receivers, lanes), bf16),
            pltpu.VMEM((QUARTERS, rows, receivers), f32),
        ],
        name="gram",
    )(here, there, q0, q1, q2, q3)
    sums = p0
    for m, p in ((1, p1), (2, p2), (3, p3)):
        sums = sums + send(p, lambda e, z1, k, x, yl, m=m: ((e + m) & 3, z1, k, x, yl)).astype(f32)
    return sums.reshape(2, NF, count, receivers).transpose(0, 1, 3, 2)


def solution(mesh):
    return jax.shard_map(
        per_device,
        mesh=mesh,
        in_specs=(P("rcv", "shot"), P("shot")),
        out_specs=P(None, None, "rcv", "shot"),
        check_vma=False,
    )
```

time: 364 us -> 71.9 us (0.20)
  waiting for transfers between devices: 277 us -> 19.7 us
  blocking collectives: 34.7 us -> 0 us
  starting transfers between devices: 1.29 us -> 33.2 us
  between operations: 14.2 us -> 0.05 us
  Pallas kernels: 0 us -> 11.8 us
  other arithmetic: 13.1 us -> 1.56 us
  matrix products: 9.99 us -> 0 us
  local copies, waits for them, and re-layouts: 12 us -> 4.9 us
    unnamed x2 -> x0, waiting for transfers between devices: 277 us -> none
    all_gather x1 -> x0, blocking collectives: 34.7 us -> none  [per_device(): all_receivers = lax.all_gather(trace_spectra, 'rcv', axis=2, tiled=True)]
    ppermute x1 -> x13, starting transfers between devices: 1.29 us -> 33.2 us  [send(): return lax.ppermute(block, ('shot', 'rcv'), route)]
    ppermute x1 -> x13, waiting for transfers between devices: 0.01 us -> 19.7 us  [send(): return lax.ppermute(block, ('shot', 'rcv'), route)]
    pallas_call x0 -> x5, Pallas kernels: none -> 11.8 us  [the longest x1 3.31 us: per_device(): pl.pallas_call(own_kernel, out_shape=(shape((lanes, receivers), f32), sha...]
    cos x1 -> x0, other arithmetic: 10.4 us -> none  [shifted_tables(): jnp.cos(phase_angle)]
    dot_general x13 -> x0, matrix products: 9.99 us -> none  [the longest x9 8.57 us: local_spectra(): jnp.einsum('rsu,scu->scr', record_part, tables[:, :, offset, :], preferre...]
    slice x4 -> x1, local copies, waits for them, and re-layouts: 4.89 us -> 1.02 us  [per_device(): rim = send(record[:, :WIN], before)]
  transfers between devices with their start and end apart: 2 -> 13, of which waited for: 1 -> 7; matrix products, arithmetic and copies ran while one was open for 4% -> 0% of each run, Pallas kernels for 0% -> 7%
where the time goes in v1:
time: 71.9 us; the launch traced here: 71.2 us
  starting transfers between devices  33.2 us (46%)
  waiting for transfers between devices  19.7 us (27%)
  Pallas kernels  11.8 us (16%)
  local copies, waits for them, and re-layouts  4.9 us (7%)
  other arithmetic  1.56 us (2%)
    ppermute x13, starting transfers between devices, send(): return lax.ppermute(block, ('shot', 'rcv'), route)  33.2 us
    ppermute x13, waiting for transfers between devices, send(): return lax.ppermute(block, ('shot', 'rcv'), route)  19.7 us
    unnamed x20, local copies, waits for them, and re-layouts  3.88 us
    pallas_call x1, Pallas kernels, per_device(): pl.pallas_call(own_kernel, out_shape=(shape((lanes, receivers), f32), sha...  3.31 us
    pallas_call x1, Pallas kernels, per_device(): pl.pallas_call(lambda *refs: gram_kernel(1.0 / total_shots, *refs), out_s...  3.29 us
    pallas_call x1, Pallas kernels, per_device(): pl.pallas_call(rim_kernel, out_shape=shape((QUARTERS, count, lanes), bf16...  2.11 us
    pallas_call x1, Pallas kernels, per_device(): pl.pallas_call(collect_kernel, out_shape=(shape((QUARTERS, QUARTERS, coun...  1.6 us
    add x1, other arithmetic, per_device(): sums + send(p, lambda e, z1, k, x, yl, m=m: (e + m & 3, z1, k, x, yl)).as...  1.56 us
  transfers between devices with their start and end apart: 13, of which 7 were waited for; matrix products, arithmetic and copies ran while one was open for 0% of the time, Pallas kernels for 7%

profile of v1, /device:TPU:4, one launch (start us, length us, event | category | flops | bytes accessed | tf_op | source)
XLA Modules:
  0.0 71.2 jit_solution(15093356540727033452)
XLA Ops:
  0.0 1.0 %slice.3 = bf16[96,2048]{1,0:T(8,128)(2,1)S(1)} slice(bf16[96,8192]{1,0:T(8,128)(2,1)} %record.1), slice={[0:96], [0:2048]} | slice | bytes 786432 | tf_op jit(solution)/shard_map/slice | solution.py:167
  1.0 1.3 %collective-permute-start = (bf16[96,2048]{1,0:T(8,128)(2,1)S(1)}, bf16[96,2048]{1,0:T(8,128)(2,1)S(1)}, u32[]{:S(2)}, u32[]{:S(2)}) collective-permute-start(bf16[96,2048]{1,0:T(8,128)(2,1)S(1)} %slice.3), channel_id=1, source_target_pairs={{8,0},{9,1},{10,2},{11,3},{12,4},{13,5},{14,6},{15,7},{16,8},{17,9... | collective-permute-start | bytes 1179656 | tf_op jit(solution)/shard_map/ppermute | solution.py:42
  2.3 3.3 %own_spectra.1 = (f32[256,96]{1,0:T(8,128)}, bf16[4,16,2560]{2,1,0:T(8,128)(2,1)}) custom-call(s32[32]{0:T(128)} %fire.1, f32[8,2560]{1,0:T(8,128)} %constant.2.clone.table, bf16[96,8192]{1,0:T(8,128)(2,1)} %record.1), custom_call_target="tpu_custom_call" | custom-call | flops 125829120 | bytes 1572864 | tf_op jit(solution)/shard_map/own_spectra/pallas_call | solution.py:168
  5.6 0.0 collective-permute-done.rim
  5.6 0.0 copy-start
  5.6 0.7 %copy-done = bf16[96,2048]{1,0:T(8,128)(2,1)} copy-done((bf16[96,2048]{1,0:T(8,128)(2,1)}, bf16[96,2048]{1,0:T(8,128)(2,1)S(1)}, u32[]{:S(2)}) %copy-start) | copy-done | bytes 393240
  6.4 2.1 %rim_spectra.1.y0 = bf16[4,24,256]{2,1,0:T(8,128)(2,1)} custom-call(f32[256,96]{1,0:T(8,128)} %get-tuple-element.13.total, bf16[4,16,2560]{2,1,0:T(8,128)(2,1)} %get-tuple-element.14.tables, bf16[96,2048]{1,0:T(8,128)(2,1)} %copy-done), custom_call_target="tpu_custom_call" | custom-call | tf_op jit(solution)/shard_map/rim_spectra/pallas_call | solution.py:179
  8.5 6.3 %collective-permute-start.3 = (bf16[4,24,256]{2,1,0:T(8,128)(2,1)}, bf16[4,24,256]{2,1,0:T(8,128)(2,1)S(1)}, u32[]{:S(2)}, u32[]{:S(2)}) collective-permute-start(bf16[4,24,256]{2,1,0:T(8,128)(2,1)} %rim_spectra.1.y0), channel_id=1, source_target_pairs={{0,24},{1,25},{2,26},{3,27},{4,28},{5,29},{6,30},{7,31},{8,16},{9,... | collective-permute-start | bytes 147464 | tf_op jit(solution)/shard_map/ppermute | solution.py:42
  14.8 0.1 collective-permute-start.2
  14.9 0.0 collective-permute-start.1
  14.9 2.0 %collective-permute-done.3.y3 = bf16[4,24,256]{2,1,0:T(8,128)(2,1)S(1)} collective-permute-done((bf16[4,24,256]{2,1,0:T(8,128)(2,1)}, bf16[4,24,256]{2,1,0:T(8,128)(2,1)S(1)}, u32[]{:S(2)}, u32[]{:S(2)}) %collective-permute-start.3) | collective-permute-done | bytes 49184 | tf_op jit(solution)/shard_map/ppermute | solution.py:42
  17.0 0.0 copy-start.5
  17.0 2.1 %collective-permute-done.2.y2 = bf16[4,24,256]{2,1,0:T(8,128)(2,1)S(1)} collective-permute-done((bf16[4,24,256]{2,1,0:T(8,128)(2,1)}, bf16[4,24,256]{2,1,0:T(8,128)(2,1)S(1)}, u32[]{:S(2)}, u32[]{:S(2)}) %collective-permute-start.2) | collective-permute-done | bytes 49184 | tf_op jit(solution)/shard_map/ppermute | solution.py:42
  19.1 0.0 copy-start.6
  19.1 0.0 collective-permute-done.1.y1
  19.1 0.0 copy-done.5
  19.1 0.6 copy-done.6
  19.7 0.0 copy-start.7
  19.7 0.6 copy-done.7
  20.3 1.6 %collect.1 = (bf16[4,4,24,256]{3,2,1,0:T(8,128)(2,1)}, bf16[4,24,256]{2,1,0:T(8,128)(2,1)}) custom-call(bf16[4,24,256]{2,1,0:T(8,128)(2,1)} %rim_spectra.1.y0, bf16[4,24,256]{2,1,0:T(8,128)(2,1)} %copy-done.7, bf16[4,24,256]{2,1,0:T(8,128)(2,1)} %copy-done.6, bf16[4,24,256]{2,1,0:T(8,128)(2,1)} %copy-done.5), custom_call_target="tpu_custom_call" | custom-call | tf_op jit(solution)/shard_map/collect/pallas_call | solution.py:189
  21.9 4.5 %collective-permute-start.4 = (bf16[4,4,24,256]{3,2,1,0:T(8,128)(2,1)}, bf16[4,4,24,256]{3,2,1,0:T(8,128)(2,1)S(1)}, u32[]{:S(2)}, u32[]{:S(2)}) collective-permute-start(bf16[4,4,24,256]{3,2,1,0:T(8,128)(2,1)} %get-tuple-element.15.refs_0_), channel_id=1, source_target_pairs={{0,32},{1,33},{2,34},{3,35},{4,36},{5,37},{6,38},{7,39},{8,40},{9,... | collective-permute-start | bytes 589832 | tf_op jit(solution)/shard_map/ppermute | solution.py:42
  26.4 0.7 collective-permute-start.6
  27.1 2.9 %collective-permute-start.5 = (bf16[4,24,256]{2,1,0:T(8,128)(2,1)}, bf16[4,24,256]{2,1,0:T(8,128)(2,1)S(1)}, u32[]{:S(2)}, u32[]{:S(2)}) collective-permute-start(bf16[4,24,256]{2,1,0:T(8,128)(2,1)} %get-tuple-element.16.own), channel_id=1, source_target_pairs={{0,1},{1,33},{2,3},{3,35},{4,5},{5,37},{6,7},{7,39},{8,9},{9,41},{... | collective-permute-start | bytes 147464 | tf_op jit(solution)/shard_map/ppermute | solution.py:42
  30.0 0.0 collective-permute-done.6.cross
  30.0 0.0 copy-start.8
  30.0 8.2 %collective-permute-done.5.ring = bf16[4,24,256]{2,1,0:T(8,128)(2,1)S(1)} collective-permute-done((bf16[4,24,256]{2,1,0:T(8,128)(2,1)}, bf16[4,24,256]{2,1,0:T(8,128)(2,1)S(1)}, u32[]{:S(2)}, u32[]{:S(2)}) %collective-permute-start.5) | collective-permute-done | bytes 49184 | tf_op jit(solution)/shard_map/ppermute | solution.py:42
  38.1 0.0 copy-done.8
  38.1 0.6 copy-done.9
  38.8 1.5 %choose.1.refs_2_ = bf16[2,4,24,256]{3,2,1,0:T(8,128)(2,1)} custom-call(bf16[4,24,256]{2,1,0:T(8,128)(2,1)} %get-tuple-element.16.own, bf16[4,24,256]{2,1,0:T(8,128)(2,1)} %copy-done.9, bf16[4,24,256]{2,1,0:T(8,128)(2,1)} %copy-done.8), custom_call_target="tpu_custom_call" | custom-call | tf_op jit(solution)/shard_map/choose/pallas_call | solution.py:201
  40.3 1.2 %collective-permute-start.9 = (bf16[2,4,24,256]{3,2,1,0:T(8,128)(2,1)}, bf16[2,4,24,256]{3,2,1,0:T(8,128)(2,1)S(1)}, u32[]{:S(2)}, u32[]{:S(2)}) collective-permute-start(bf16[2,4,24,256]{3,2,1,0:T(8,128)(2,1)} %choose.1.refs_2_), channel_id=1, source_target_pairs={{0,2},{1,3},{2,4},{3,5},{4,6},{5,7},{6,0},{7,1},{8,10},{9,11},{10,... | collective-permute-start | bytes 294920 | tf_op jit(solution)/shard_map/ppermute | solution.py:42
  41.4 0.8 %collective-permute-start.8 = (bf16[2,4,24,256]{3,2,1,0:T(8,128)(2,1)}, bf16[2,4,24,256]{3,2,1,0:T(8,128)(2,1)S(1)}, u32[]{:S(2)}, u32[]{:S(2)}) collective-permute-start(bf16[2,4,24,256]{3,2,1,0:T(8,128)(2,1)} %choose.1.refs_2_), channel_id=1, source_target_pairs={{0,4},{1,5},{2,6},{3,7},{4,0},{5,1},{6,2},{7,3},{8,12},{9,13},{10,... | collective-permute-start | bytes 294920 | tf_op jit(solution)/shard_map/ppermute | solution.py:42
  42.2 1.1 %collective-permute-start.7 = (bf16[2,4,24,256]{3,2,1,0:T(8,128)(2,1)}, bf16[2,4,24,256]{3,2,1,0:T(8,128)(2,1)S(1)}, u32[]{:S(2)}, u32[]{:S(2)}) collective-permute-start(bf16[2,4,24,256]{3,2,1,0:T(8,128)(2,1)} %choose.1.refs_2_), channel_id=1, source_target_pairs={{0,6},{1,7},{2,0},{3,1},{4,2},{5,3},{6,4},{7,5},{8,14},{9,15},{10,... | collective-permute-start | bytes 294920 | tf_op jit(solution)/shard_map/ppermute | solution.py:42
  43.4 2.6 %collective-permute-done.9.refs_5_ = bf16[2,4,24,256]{3,2,1,0:T(8,128)(2,1)S(1)} collective-permute-done((bf16[2,4,24,256]{3,2,1,0:T(8,128)(2,1)}, bf16[2,4,24,256]{3,2,1,0:T(8,128)(2,1)S(1)}, u32[]{:S(2)}, u32[]{:S(2)}) %collective-permute-start.9) | collective-permute-done | bytes 98336 | tf_op jit(solution)/shard_map/ppermute | solution.py:42
  46.0 1.8 %collective-permute-done.8.refs_4_ = bf16[2,4,24,256]{3,2,1,0:T(8,128)(2,1)S(1)} collective-permute-done((bf16[2,4,24,256]{3,2,1,0:T(8,128)(2,1)}, bf16[2,4,24,256]{3,2,1,0:T(8,128)(2,1)S(1)}, u32[]{:S(2)}, u32[]{:S(2)}) %collective-permute-start.8) | collective-permute-done | bytes 98336 | tf_op jit(solution)/shard_map/ppermute | solution.py:42
  47.8 0.5 collective-permute-done.7.refs_3_
  48.3 0.0 collective-permute-done.4.refs_1_
  48.3 0.0 copy-done.2
  48.3 0.2 copy-done.3
  48.4 0.5 copy-done.4
  48.9 0.7 copy-done.1
  49.5 3.3 %gram.1 = (f32[192,96]{1,0:T(8,128)}, bf16[192,96]{1,0:T(8,128)(2,1)}, bf16[192,96]{1,0:T(8,128)(2,1)}, bf16[192,96]{1,0:T(8,128)(2,1)}) custom-call(bf16[4,4,24,256]{3,2,1,0:T(8,128)(2,1)} %get-tuple-element.15.refs_0_, bf16[4,4,24,256]{3,2,1,0:T(8,128)(2,1)} %copy-done.1, bf16[2,4,24,256]{3,2,1,0:T(8,128)(2,1)} %choose.1.refs_2_, ...), custom_call_target="tpu_custom_call" | custom-call | tf_op jit(solution)/shard_map/gram/pallas_call | solution.py:213
  52.8 6.4 %collective-permute-start.10 = (bf16[192,96]{1,0:T(8,128)(2,1)}, bf16[192,96]{1,0:T(8,128)(2,1)S(1)}, u32[]{:S(2)}, u32[]{:S(2)}) collective-permute-start(bf16[192,96]{1,0:T(8,128)(2,1)} %get-tuple-element.18), channel_id=1, source_target_pairs={{0,64},{1,65},{2,66},{3,67},{4,68},{5,69},{6,70},{7,71},{8,72},{9,... | collective-permute-start | bytes 110600 | tf_op jit(solution)/shard_map/ppermute | solution.py:42
  59.3 1.6 %collective-permute-start.11 = (bf16[192,96]{1,0:T(8,128)(2,1)}, bf16[192,96]{1,0:T(8,128)(2,1)S(1)}, u32[]{:S(2)}, u32[]{:S(2)}) collective-permute-start(bf16[192,96]{1,0:T(8,128)(2,1)} %get-tuple-element.19), channel_id=1, source_target_pairs={{0,128},{1,129},{2,130},{3,131},{4,132},{5,133},{6,134},{7,135},{8... | collective-permute-start | bytes 110600 | tf_op jit(solution)/shard_map/ppermute | solution.py:42
  60.9 6.2 %collective-permute-start.12 = (bf16[192,96]{1,0:T(8,128)(2,1)}, bf16[192,96]{1,0:T(8,128)(2,1)S(1)}, u32[]{:S(2)}, u32[]{:S(2)}) collective-permute-start(bf16[192,96]{1,0:T(8,128)(2,1)} %get-tuple-element.20), channel_id=1, source_target_pairs={{0,192},{1,193},{2,194},{3,195},{4,196},{5,197},{6,198},{7,199},{8... | collective-permute-start | bytes 110600 | tf_op jit(solution)/shard_map/ppermute | solution.py:42
  67.1 0.0 collective-permute-done.10
  67.1 0.0 collective-permute-done.11
  67.2 2.5 %collective-permute-done.12 = bf16[192,96]{1,0:T(8,128)(2,1)S(1)} collective-permute-done((bf16[192,96]{1,0:T(8,128)(2,1)}, bf16[192,96]{1,0:T(8,128)(2,1)S(1)}, u32[]{:S(2)}, u32[]{:S(2)}) %collective-permute-start.12) | collective-permute-done | bytes 36896 | tf_op jit(solution)/shard_map/ppermute | solution.py:42
  69.6 1.6 %convert_add_fusion = f32[192,96]{1,0:T(8,128)} fusion(bf16[192,96]{1,0:T(8,128)(2,1)S(1)} %collective-permute-done.12, bf16[192,96]{1,0:T(8,128)(2,1)S(1)} %collective-permute-done.11, f32[192,96]{1,0:T(8,128)} %get-tuple-element.17, bf16[192,96]{1,0:T(8,128)(2,1)S(1)} %collective-permute-done.10), kind=kLoop, calls=%fused_computation | loop fusion | flops 110592 | bytes 258048 | tf_op jit(solution)/shard_map/add | solution.py:226
  (5 shorter events, 0.0 us)
Async XLA Ops:
  1.0 4.6 %collective-permute-start = (bf16[96,2048]{1,0:T(8,128)(2,1)S(1)}, bf16[96,2048]{1,0:T(8,128)(2,1)S(1)}, u32[]{:S(2)}, u32[]{:S(2)}) collective-permute-start(bf16[96,2048]{1,0:T(8,128)(2,1)S(1)} %slice.3), channel_id=1, source_target_pairs={{8,0},{9,1},{10,2},{11,3},{12,4},{13,5},{14,6},{15,7},{16,8},{17,9... | collective-permute-start | bytes 1179656 | tf_op jit(solution)/shard_map/ppermute | solution.py:42
  5.6 0.7 %copy-start = (bf16[96,2048]{1,0:T(8,128)(2,1)}, bf16[96,2048]{1,0:T(8,128)(2,1)S(1)}, u32[]{:S(2)}) copy-start(bf16[96,2048]{1,0:T(8,128)(2,1)S(1)} %collective-permute-done.rim) | copy-start | bytes 1179652
  8.5 8.5 %collective-permute-start.3 = (bf16[4,24,256]{2,1,0:T(8,128)(2,1)}, bf16[4,24,256]{2,1,0:T(8,128)(2,1)S(1)}, u32[]{:S(2)}, u32[]{:S(2)}) collective-permute-start(bf16[4,24,256]{2,1,0:T(8,128)(2,1)} %rim_spectra.1.y0), channel_id=1, source_target_pairs={{0,24},{1,25},{2,26},{3,27},{4,28},{5,29},{6,30},{7,31},{8,16},{9,... | collective-permute-start | bytes 147464 | tf_op jit(solution)/shard_map/ppermute | solution.py:42
  14.8 4.3 %collective-permute-start.2 = (bf16[4,24,256]{2,1,0:T(8,128)(2,1)}, bf16[4,24,256]{2,1,0:T(8,128)(2,1)S(1)}, u32[]{:S(2)}, u32[]{:S(2)}) collective-permute-start(bf16[4,24,256]{2,1,0:T(8,128)(2,1)} %rim_spectra.1.y0), channel_id=1, source_target_pairs={{0,16},{1,17},{2,18},{3,19},{4,20},{5,21},{6,22},{7,23},{8,24},{9,... | collective-permute-start | bytes 147464 | tf_op jit(solution)/shard_map/ppermute | solution.py:42
  14.9 4.2 %collective-permute-start.1 = (bf16[4,24,256]{2,1,0:T(8,128)(2,1)}, bf16[4,24,256]{2,1,0:T(8,128)(2,1)S(1)}, u32[]{:S(2)}, u32[]{:S(2)}) collective-permute-start(bf16[4,24,256]{2,1,0:T(8,128)(2,1)} %rim_spectra.1.y0), channel_id=1, source_target_pairs={{0,8},{1,9},{2,10},{3,11},{4,12},{5,13},{6,14},{7,15},{8,0},{9,1},... | collective-permute-start | bytes 147464 | tf_op jit(solution)/shard_map/ppermute | solution.py:42
  17.0 2.1 %copy-start.5 = (bf16[4,24,256]{2,1,0:T(8,128)(2,1)}, bf16[4,24,256]{2,1,0:T(8,128)(2,1)S(1)}, u32[]{:S(2)}) copy-start(bf16[4,24,256]{2,1,0:T(8,128)(2,1)S(1)} %collective-permute-done.3.y3) | copy-start | bytes 147460
  19.1 0.6 copy-start.6
  19.7 0.6 copy-start.7
  21.9 26.3 %collective-permute-start.4 = (bf16[4,4,24,256]{3,2,1,0:T(8,128)(2,1)}, bf16[4,4,24,256]{3,2,1,0:T(8,128)(2,1)S(1)}, u32[]{:S(2)}, u32[]{:S(2)}) collective-permute-start(bf16[4,4,24,256]{3,2,1,0:T(8,128)(2,1)} %get-tuple-element.15.refs_0_), channel_id=1, source_target_pairs={{0,32},{1,33},{2,34},{3,35},{4,36},{5,37},{6,38},{7,39},{8,40},{9,... | collective-permute-start | bytes 589832 | tf_op jit(solution)/shard_map/ppermute | solution.py:42
  26.4 3.6 %collective-permute-start.6 = (bf16[4,24,256]{2,1,0:T(8,128)(2,1)}, bf16[4,24,256]{2,1,0:T(8,128)(2,1)S(1)}, u32[]{:S(2)}, u32[]{:S(2)}) collective-permute-start(bf16[4,24,256]{2,1,0:T(8,128)(2,1)} %get-tuple-element.16.own), channel_id=1, source_target_pairs={{1,32},{3,34},{5,36},{7,38},{9,40},{11,42},{13,44},{15,46},{17,48}... | collective-permute-start | bytes 147464 | tf_op jit(solution)/shard_map/ppermute | solution.py:42
  27.1 11.1 %collective-permute-start.5 = (bf16[4,24,256]{2,1,0:T(8,128)(2,1)}, bf16[4,24,256]{2,1,0:T(8,128)(2,1)S(1)}, u32[]{:S(2)}, u32[]{:S(2)}) collective-permute-start(bf16[4,24,256]{2,1,0:T(8,128)(2,1)} %get-tuple-element.16.own), channel_id=1, source_target_pairs={{0,1},{1,33},{2,3},{3,35},{4,5},{5,37},{6,7},{7,39},{8,9},{9,41},{... | collective-permute-start | bytes 147464 | tf_op jit(solution)/shard_map/ppermute | solution.py:42
  30.0 8.2 %copy-start.8 = (bf16[4,24,256]{2,1,0:T(8,128)(2,1)}, bf16[4,24,256]{2,1,0:T(8,128)(2,1)S(1)}, u32[]{:S(2)}) copy-start(bf16[4,24,256]{2,1,0:T(8,128)(2,1)S(1)} %collective-permute-done.6.cross) | copy-start | bytes 147460
  38.1 0.6 copy-start.9
  40.3 5.7 %collective-permute-start.9 = (bf16[2,4,24,256]{3,2,1,0:T(8,128)(2,1)}, bf16[2,4,24,256]{3,2,1,0:T(8,128)(2,1)S(1)}, u32[]{:S(2)}, u32[]{:S(2)}) collective-permute-start(bf16[2,4,24,256]{3,2,1,0:T(8,128)(2,1)} %choose.1.refs_2_), channel_id=1, source_target_pairs={{0,2},{1,3},{2,4},{3,5},{4,6},{5,7},{6,0},{7,1},{8,10},{9,11},{10,... | collective-permute-start | bytes 294920 | tf_op jit(solution)/shard_map/ppermute | solution.py:42
  41.4 6.3 %collective-permute-start.8 = (bf16[2,4,24,256]{3,2,1,0:T(8,128)(2,1)}, bf16[2,4,24,256]{3,2,1,0:T(8,128)(2,1)S(1)}, u32[]{:S(2)}, u32[]{:S(2)}) collective-permute-start(bf16[2,4,24,256]{3,2,1,0:T(8,128)(2,1)} %choose.1.refs_2_), channel_id=1, source_target_pairs={{0,4},{1,5},{2,6},{3,7},{4,0},{5,1},{6,2},{7,3},{8,12},{9,13},{10,... | collective-permute-start | bytes 294920 | tf_op jit(solution)/shard_map/ppermute | solution.py:42
  42.2 6.0 %collective-permute-start.7 = (bf16[2,4,24,256]{3,2,1,0:T(8,128)(2,1)}, bf16[2,4,24,256]{3,2,1,0:T(8,128)(2,1)S(1)}, u32[]{:S(2)}, u32[]{:S(2)}) collective-permute-start(bf16[2,4,24,256]{3,2,1,0:T(8,128)(2,1)} %choose.1.refs_2_), channel_id=1, source_target_pairs={{0,6},{1,7},{2,0},{3,1},{4,2},{5,3},{6,4},{7,5},{8,14},{9,15},{10,... | collective-permute-start | bytes 294920 | tf_op jit(solution)/shard_map/ppermute | solution.py:42
  46.0 2.3 %copy-start.2 = (bf16[2,4,24,256]{3,2,1,0:T(8,128)(2,1)}, bf16[2,4,24,256]{3,2,1,0:T(8,128)(2,1)S(1)}, u32[]{:S(2)}) copy-start(bf16[2,4,24,256]{3,2,1,0:T(8,128)(2,1)S(1)} %collective-permute-done.9.refs_5_) | copy-start | bytes 294916
  47.8 0.6 copy-start.3
  48.2 0.6 copy-start.4
  48.9 0.7 copy-start.1
  52.8 14.3 %collective-permute-start.10 = (bf16[192,96]{1,0:T(8,128)(2,1)}, bf16[192,96]{1,0:T(8,128)(2,1)S(1)}, u32[]{:S(2)}, u32[]{:S(2)}) collective-permute-start(bf16[192,96]{1,0:T(8,128)(2,1)} %get-tuple-element.18), channel_id=1, source_target_pairs={{0,64},{1,65},{2,66},{3,67},{4,68},{5,69},{6,70},{7,71},{8,72},{9,... | collective-permute-start | bytes 110600 | tf_op jit(solution)/shard_map/ppermute | solution.py:42
  59.3 7.9 %collective-permute-start.11 = (bf16[192,96]{1,0:T(8,128)(2,1)}, bf16[192,96]{1,0:T(8,128)(2,1)S(1)}, u32[]{:S(2)}, u32[]{:S(2)}) collective-permute-start(bf16[192,96]{1,0:T(8,128)(2,1)} %get-tuple-element.19), channel_id=1, source_target_pairs={{0,128},{1,129},{2,130},{3,131},{4,132},{5,133},{6,134},{7,135},{8... | collective-permute-start | bytes 110600 | tf_op jit(solution)/shard_map/ppermute | solution.py:42
  60.9 8.7 %collective-permute-start.12 = (bf16[192,96]{1,0:T(8,128)(2,1)}, bf16[192,96]{1,0:T(8,128)(2,1)S(1)}, u32[]{:S(2)}, u32[]{:S(2)}) collective-permute-start(bf16[192,96]{1,0:T(8,128)(2,1)} %get-tuple-element.20), channel_id=1, source_target_pairs={{0,192},{1,193},{2,194},{3,195},{4,196},{5,197},{6,198},{7,199},{8... | collective-permute-start | bytes 110600 | tf_op jit(solution)/shard_map/ppermute | solution.py:42

commit v2 on v1

--- a/solution.py
+++ b/solution.py
@@ -50,45 +50,54 @@
     return [pl.BlockSpec(memory_space=pltpu.VMEM)] * count
 
 
-def own_kernel(fire, table, record, total, tables, scratch):
+def pair_tables(fire, table, p):
+    first = pltpu.roll(table, fire[2 * p] & (SPACING - 1), 1)
+    second = pltpu.roll(table, (fire[2 * p + 1] & (SPACING - 1)) + SPACING, 1)
+    return jnp.concatenate([first, second], axis=0).astype(jnp.bfloat16)
+
+
+def add_products(total, tables, record, blocks, pairs, first_row):
+    reach = SPAN // PAIR
+    for column, u in blocks:
+        low, high = max(0, u - reach + 1), min(u, pairs - 1)
+        left = jnp.concatenate(
+            [tables[p - first_row, :, PAIR * (u - p) : PAIR * (u - p + 1)] for p in range(low, high + 1)], axis=0
+        )
+        part = lax.dot_general(
+            left,
+            record[:, PAIR * column : PAIR * (column + 1)],
+            (((1,), (1,)), ((), ())),
+            preferred_element_type=jnp.float32,
+        )
+        total[2 * ROWS * (low - first_row) : 2 * ROWS * (high + 1 - first_row), :] += part
+
+
+def own_kernel(fire, table, record, total, tables):
     pairs = total.shape[0] // (2 * ROWS)
-    reach = SPAN // PAIR
     master = table[...]
     for p in range(pairs):
-        first = pltpu.roll(master, fire[2 * p] & (SPACING - 1), 1)
-        second = pltpu.roll(master, (fire[2 * p + 1] & (SPACING - 1)) + SPACING, 1)
-        scratch[p] = jnp.concatenate([first, second], axis=0).astype(jnp.bfloat16)
+        tables[p] = pair_tables(fire, master, p)
     total[...] = jnp.zeros_like(total)
-    for u in range(pairs):
-        low = max(0, u - reach + 1)
-        left = jnp.concatenate(
-            [scratch[p, :, PAIR * (u - p) : PAIR * (u - p + 1)] for p in range(low, u + 1)], axis=0
-        )
-        part = lax.dot_general(
-            left, record[:, PAIR * u : PAIR * (u + 1)], (((1,), (1,)), ((), ())), preferred_element_type=jnp.float32
-        )
-        rows = slice(2 * ROWS * low, 2 * ROWS * (u + 1))
-        total[rows, :] += part
-    for p in range(reach - 1):
-        tables[p] = scratch[pairs - reach + 1 + p]
-
-
-def rim_kernel(total, tables, rim, out, scratch):
-    pairs = total.shape[0] // (2 * ROWS)
+    add_products(total, tables, record, [(u, u) for u in range(pairs)], pairs, 0)
+
+
+def next_kernel(fire, table, record, total, tables):
+    pairs = fire.shape[0] // 2
     reach = SPAN // PAIR
-    scratch[...] = total[...]
-    for v in range(reach - 1):
-        u = pairs + v
-        low = u - reach + 1
-        left = jnp.concatenate(
-            [tables[p - (pairs - reach + 1), :, PAIR * (u - p) : PAIR * (u - p + 1)] for p in range(low, pairs)], axis=0
-        )
-        part = lax.dot_general(
-            left, rim[:, PAIR * v : PAIR * (v + 1)], (((1,), (1,)), ((), ())), preferred_element_type=jnp.float32
-        )
-        scratch[2 * ROWS * low :, :] += part
-    shots = 2 * pairs
-    ordered = jnp.concatenate([scratch[pl.ds(c, shots, stride=ROWS), :] for c in range(ROWS)], axis=0)
+    first_row = pairs - reach + 1
+    master = table[...]
+    for p in range(first_row, pairs):
+        tables[p - first_row] = pair_tables(fire, master, p)
+    total[...] = jnp.zeros_like(total)
+    add_products(total, tables, record, [(v, pairs + v) for v in range(reach - 1)], pairs, first_row)
+
+
+def finish_kernel(total, late, out, scratch):
+    lanes = total.shape[0]
+    split = lanes - late.shape[0]
+    scratch[:split, :] = total[:split, :]
+    scratch[split:, :] = total[split:, :] + late[...]
+    ordered = jnp.concatenate([scratch[pl.ds(c, lanes // ROWS, stride=ROWS), :] for c in range(ROWS)], axis=0)
     turned = ordered.T
     count = out.shape[1]
     for k in range(QUARTERS):
@@ -160,30 +169,52 @@
     bf16, f32 = jnp.bfloat16, jnp.float32
     shape = jax.ShapeDtypeStruct
 
-    def before(e, z1, k, x, yl):
-        shot = (e << 3 | z1 << 2 | k) - 1
-        return None if shot < 0 else (shot >> 3, (shot >> 2) & 1, shot & 3, x, yl)
-
-    rim = send(record[:, :WIN], before)
-    total, tables = pl.pallas_call(
+    def neighbour(step):
+        def to(e, z1, k, x, yl):
+            shot = (e << 3 | z1 << 2 | k) + step
+            return (shot >> 3, (shot >> 2) & 1, shot & 3, x, yl) if 0 <= shot < SHOT_DEVICES else None
+
+        return to
+
+    table = jnp.asarray(dft_master())
+    smem = pl.BlockSpec(memory_space=pltpu.SMEM)
+    fire_before = send(shot_fire_samples, neighbour(1))
+    total = pl.pallas_call(
         own_kernel,
-        out_shape=(shape((lanes, receivers), f32), shape((reach - 1, 2 * ROWS, SPAN), bf16)),
-        in_specs=[pl.BlockSpec(memory_space=pltpu.SMEM)] + vmem(2),
-        out_specs=tuple(vmem(2)),
+        out_shape=shape((lanes, receivers), f32),
+        in_specs=[smem] + vmem(2),
+        out_specs=vmem(1)[0],
         scratch_shapes=[pltpu.VMEM((pairs, 2 * ROWS, SPAN), bf16)],
         cost_estimate=pl.CostEstimate(
             flops=2 * lanes * receivers * SPAN, bytes_accessed=2 * receivers * samples, transcendentals=0
         ),
+        compiler_params=pltpu.CompilerParams(vmem_limit_bytes=12 << 20),
         name="own_spectra",
-    )(shot_fire_samples, jnp.asarray(dft_master()), record)
+    )(shot_fire_samples, table, record)
+    late = pl.pallas_call(
+        next_kernel,
+        grid=(1,),
+        out_shape=shape((2 * ROWS * (reach - 1), receivers), f32),
+        in_specs=[
+            smem,
+            pl.BlockSpec(table.shape, lambda i: (0, 0)),
+            pl.BlockSpec((receivers, WIN), lambda i: (0, 0)),
+        ],
+        out_specs=pl.BlockSpec((2 * ROWS * (reach - 1), receivers), lambda i: (0, 0)),
+        scratch_shapes=[pltpu.VMEM((reach - 1, 2 * ROWS, SPAN), bf16)],
+        compiler_params=pltpu.CompilerParams(vmem_limit_bytes=6 << 20),
+        name="next_spectra",
+    )(fire_before, table, record)
+    late = send(late, neighbour(-1))
     y0 = pl.pallas_call(
-        rim_kernel,
+        finish_kernel,
         out_shape=shape((QUARTERS, count, lanes), bf16),
-        in_specs=vmem(3),
+        in_specs=vmem(2),
         out_specs=vmem(1)[0],
         scratch_shapes=[pltpu.VMEM((lanes, receivers), f32)],
-        name="rim_spectra",
-    )(total, tables, rim)
+        compiler_params=pltpu.CompilerParams(vmem_limit_bytes=4 << 20),
+        name="finish_spectra",
+    )(total, late)
 
     ys = [send(y0, lambda e, z1, k, x, yl, m=m: (e, z1, k ^ m, x, yl)) for m in (1, 2, 3)]
     here, own = pl.pallas_call(
@@ -191,22 +222,25 @@
         out_shape=(shape((QUARTERS, QUARTERS, count, lanes), bf16), shape((QUARTERS, count, lanes), bf16)),
         in_specs=vmem(4),
         out_specs=tuple(vmem(2)),
+        compiler_params=pltpu.CompilerParams(vmem_limit_bytes=4 << 20),
         name="collect",
     )(y0, *ys)
 
     turn = {(1, 0): (0, 0), (0, 0): (0, 1), (0, 1): (1, 1), (1, 1): (1, 0)}
     ring = send(own, lambda e, z1, k, x, yl: (e, turn[z1, yl][0], k, x, turn[z1, yl][1]))
     cross = send(own, lambda e, z1, k, x, yl: (e, yl, k, x, z1) if z1 != yl else None)
-    there = send(here, lambda e, z1, k, x, yl: (e, 1 - z1, k, x, yl))
     q0 = pl.pallas_call(
         choose_kernel,
         out_shape=shape((2, QUARTERS, count, lanes), bf16),
         in_specs=vmem(3),
         out_specs=vmem(1)[0],
+        compiler_params=pltpu.CompilerParams(vmem_limit_bytes=4 << 20),
         name="choose",
     )(own, ring, cross)
+    here, q0 = lax.optimization_barrier((here, q0))
     qs = [send(q0, lambda e, z1, k, x, yl, t=t: (e, z1, k, (x - t) & 3, yl)) for t in (1, 3, 2)]
     q1, q3, q2 = qs
+    there = send(here, lambda e, z1, k, x, yl: (e, 1 - z1, k, x, yl))
 
     total_shots = shots * lax.axis_size("shot")
     rows = 2 * NF * count
@@ -219,6 +253,7 @@
             pltpu.VMEM((2, QUARTERS, 2 * receivers, lanes), bf16),
             pltpu.VMEM((QUARTERS, rows, receivers), f32),
         ],
+        compiler_params=pltpu.CompilerParams(vmem_limit_bytes=12 << 20),
         name="gram",
     )(here, there, q0, q1, q2, q3)
     sums = p0

time: 71.9 us -> 58 us (0.81)
  Pallas kernels: 11.8 us -> 4.2 us
  waiting for transfers between devices: 19.7 us -> 15.8 us
  local copies, waits for them, and re-layouts: 4.9 us -> 2.3 us
  starting transfers between devices: 33.2 us -> 34.6 us
  other arithmetic: 1.56 us -> 0.67 us
    ppermute x13 -> x14, waiting for transfers between devices: 19.7 us -> 15.8 us  [send(): return lax.ppermute(block, ('shot', 'rcv'), route)]
    pallas_call x2 -> x3, Pallas kernels: 5.43 us -> 2.79 us  [the longest x1 1.76 us: per_device(): pl.pallas_call(own_kernel, out_shape=shape((lanes, receivers), f32), in_s...]
    pallas_call x1, Pallas kernels: 3.29 us -> 1.38 us  [per_device(): pl.pallas_call(lambda *refs: gram_kernel(1.0 / total_shots, *refs), out_s...]
    unnamed x20 -> x10, local copies, waits for them, and re-layouts: 3.88 us -> 2.3 us
    pallas_call x1, Pallas kernels: 1.6 us -> 0.03 us  [per_device(): pl.pallas_call(collect_kernel, out_shape=(shape((QUARTERS, QUARTERS, coun...]
    pallas_call x1, Pallas kernels: 1.49 us -> 0.01 us  [per_device(): pl.pallas_call(choose_kernel, out_shape=shape((2, QUARTERS, count, lanes)...]
    ppermute x13 -> x14, starting transfers between devices: 33.2 us -> 34.6 us  [send(): return lax.ppermute(block, ('shot', 'rcv'), route)]
    slice x1 -> x0, local copies, waits for them, and re-layouts: 1.02 us -> none  [per_device(): rim = send(record[:, :WIN], before)]
  transfers between devices with their start and end apart: 13 -> 14, of which waited for: 7 -> 9; matrix products, arithmetic and copies ran while one was open for 0% -> 0% of each run, Pallas kernels for 7% -> 3%
where the time goes in v2:
time: 58 us; the launch traced here: 57.7 us
  starting transfers between devices  34.6 us (60%)
  waiting for transfers between devices  15.8 us (27%)
  Pallas kernels  4.2 us (7%)
  local copies, waits for them, and re-layouts  2.3 us (4%)
  other arithmetic  0.67 us (1%)
    ppermute x14, starting transfers between devices, send(): return lax.ppermute(block, ('shot', 'rcv'), route)  34.6 us
    ppermute x14, waiting for transfers between devices, send(): return lax.ppermute(block, ('shot', 'rcv'), route)  15.8 us
    unnamed x10, local copies, waits for them, and re-layouts  2.3 us
    pallas_call x1, Pallas kernels, per_device(): pl.pallas_call(own_kernel, out_shape=shape((lanes, receivers), f32), in_s...  1.76 us
    pallas_call x1, Pallas kernels, per_device(): pl.pallas_call(lambda *refs: gram_kernel(1.0 / total_shots, *refs), out_s...  1.38 us
  transfers between devices with their start and end apart: 14, of which 9 were waited for; matrix products, arithmetic and copies ran while one was open for 0% of the time, Pallas kernels for 3%

profile of v2, /device:TPU:4, one launch (start us, length us, event | category | flops | bytes accessed | tf_op | source)
XLA Modules:
  0.0 57.7 jit_solution(14845086670937792851)
XLA Ops:
  0.0 1.7 %collective-permute-start = (s32[32]{0:T(128)}, s32[32]{0:T(128)S(1)}, u32[]{:S(2)}, u32[]{:S(2)}) collective-permute-start(s32[32]{0:T(128)} %fire.1), channel_id=1, source_target_pairs={{0,8},{1,9},{2,10},{3,11},{4,12},{5,13},{6,14},{7,15},{8,16},{9,17... | collective-permute-start | bytes 392 | tf_op jit(solution)/shard_map/ppermute | solution.py:42
  1.7 0.9 %collective-permute-done.fire = s32[32]{0:T(128)S(1)} collective-permute-done((s32[32]{0:T(128)}, s32[32]{0:T(128)S(1)}, u32[]{:S(2)}, u32[]{:S(2)}) %collective-permute-start) | collective-permute-done | bytes 160 | tf_op jit(solution)/shard_map/ppermute | solution.py:42
  2.7 0.0 copy-start
  2.7 1.4 %copy-done = bf16[96,8192]{1,0:T(8,128)(2,1)S(1)} copy-done((bf16[96,8192]{1,0:T(8,128)(2,1)S(1)}, bf16[96,8192]{1,0:T(8,128)(2,1)}, u32[]{:S(2)}) %copy-start) | copy-done | bytes 1572888
  4.1 0.0 copy-start.2
  4.1 0.9 %copy-done.2 = f32[8,2560]{1,0:T(8,128)S(1)} copy-done((f32[8,2560]{1,0:T(8,128)S(1)}, f32[8,2560]{1,0:T(8,128)}, u32[]{:S(2)}) %copy-start.2) | copy-done | bytes 81944
  5.0 0.0 copy-start.1
  5.0 0.0 copy-start.3
  5.0 0.0 copy-start.4
  5.0 0.9 %next_spectra.1 = f32[64,96]{1,0:T(8,128)S(1)} custom-call(s32[32]{0:T(128)S(1)} %collective-permute-done.fire, f32[8,2560]{1,0:T(8,128)S(1)} %copy-done.2, bf16[96,8192]{1,0:T(8,128)(2,1)S(1)} %copy-done), custom_call_target="tpu_custom_call" | custom-call | tf_op jit(solution)/shard_map/next_spectra/pallas_call | solution.py:194
  5.9 1.3 %collective-permute-start.1 = (f32[64,96]{1,0:T(8,128)S(1)}, f32[64,96]{1,0:T(8,128)S(1)}, u32[]{:S(2)}, u32[]{:S(2)}) collective-permute-start(f32[64,96]{1,0:T(8,128)S(1)} %next_spectra.1), channel_id=1, source_target_pairs={{8,0},{9,1},{10,2},{11,3},{12,4},{13,5},{14,6},{15,7},{16,8},{17,9... | collective-permute-start | bytes 73736 | tf_op jit(solution)/shard_map/ppermute | solution.py:42
  7.2 0.0 copy-done.1
  7.2 0.0 copy-done.3
  7.2 0.0 copy-done.4
  7.2 1.8 %own_spectra.1.total = f32[256,96]{1,0:T(8,128)S(1)} custom-call(s32[32]{0:T(128)S(1)} %copy-done.4, f32[8,2560]{1,0:T(8,128)S(1)} %copy-done.3, bf16[96,8192]{1,0:T(8,128)(2,1)S(1)} %copy-done.1), custom_call_target="tpu_custom_call" | custom-call | flops 125829120 | bytes 1572864 | tf_op jit(solution)/shard_map/own_spectra/pallas_call | solution.py:182
  9.0 1.6 %collective-permute-done.1.late = f32[64,96]{1,0:T(8,128)S(1)} collective-permute-done((f32[64,96]{1,0:T(8,128)S(1)}, f32[64,96]{1,0:T(8,128)S(1)}, u32[]{:S(2)}, u32[]{:S(2)}) %collective-permute-start.1) | collective-permute-done | bytes 24608 | tf_op jit(solution)/shard_map/ppermute | solution.py:42
  10.6 0.1 finish_spectra.1.y0
  10.7 4.7 %collective-permute-start.4 = (bf16[4,24,256]{2,1,0:T(8,128)(2,1)S(1)}, bf16[4,24,256]{2,1,0:T(8,128)(2,1)S(1)}, u32[]{:S(2)}, u32[]{:S(2)}) collective-permute-start(bf16[4,24,256]{2,1,0:T(8,128)(2,1)S(1)} %finish_spectra.1.y0), channel_id=1, source_target_pairs={{0,24},{1,25},{2,26},{3,27},{4,28},{5,29},{6,30},{7,31},{8,16},{9,... | collective-permute-start | bytes 147464 | tf_op jit(solution)/shard_map/ppermute | solution.py:42
  15.5 0.1 collective-permute-start.3
  15.6 0.1 collective-permute-start.2
  15.7 1.8 %collective-permute-done.4.y3 = bf16[4,24,256]{2,1,0:T(8,128)(2,1)S(1)} collective-permute-done((bf16[4,24,256]{2,1,0:T(8,128)(2,1)S(1)}, bf16[4,24,256]{2,1,0:T(8,128)(2,1)S(1)}, u32[]{:S(2)}, u32[]{:S(2)}) %collective-permute-start.4) | collective-permute-done | bytes 49184 | tf_op jit(solution)/shard_map/ppermute | solution.py:42
  17.5 2.1 %collective-permute-done.3.y2 = bf16[4,24,256]{2,1,0:T(8,128)(2,1)S(1)} collective-permute-done((bf16[4,24,256]{2,1,0:T(8,128)(2,1)S(1)}, bf16[4,24,256]{2,1,0:T(8,128)(2,1)S(1)}, u32[]{:S(2)}, u32[]{:S(2)}) %collective-permute-start.3) | collective-permute-done | bytes 49184 | tf_op jit(solution)/shard_map/ppermute | solution.py:42
  19.6 0.0 collective-permute-done.2.y1
  19.6 0.7 %collective-permute-start.6 = (bf16[4,24,256]{2,1,0:T(8,128)(2,1)S(1)}, bf16[4,24,256]{2,1,0:T(8,128)(2,1)S(1)}, u32[]{:S(2)}, u32[]{:S(2)}) collective-permute-start(bf16[4,24,256]{2,1,0:T(8,128)(2,1)S(1)} %get-tuple-element.14.own), channel_id=1, source_target_pairs={{1,32},{3,34},{5,36},{7,38},{9,40},{11,42},{13,44},{15,46},{17,48}... | collective-permute-start | bytes 147464 | tf_op jit(solution)/shard_map/ppermute | solution.py:42
  20.3 8.5 %collective-permute-start.5 = (bf16[4,24,256]{2,1,0:T(8,128)(2,1)S(1)}, bf16[4,24,256]{2,1,0:T(8,128)(2,1)S(1)}, u32[]{:S(2)}, u32[]{:S(2)}) collective-permute-start(bf16[4,24,256]{2,1,0:T(8,128)(2,1)S(1)} %get-tuple-element.14.own), channel_id=1, source_target_pairs={{0,1},{1,33},{2,3},{3,35},{4,5},{5,37},{6,7},{7,39},{8,9},{9,41},{... | collective-permute-start | bytes 147464 | tf_op jit(solution)/shard_map/ppermute | solution.py:42
  28.7 0.0 collective-permute-done.6.cross
  28.7 2.1 %collective-permute-done.5.ring = bf16[4,24,256]{2,1,0:T(8,128)(2,1)S(1)} collective-permute-done((bf16[4,24,256]{2,1,0:T(8,128)(2,1)S(1)}, bf16[4,24,256]{2,1,0:T(8,128)(2,1)S(1)}, u32[]{:S(2)}, u32[]{:S(2)}) %collective-permute-start.5) | collective-permute-done | bytes 49184 | tf_op jit(solution)/shard_map/ppermute | solution.py:42
  30.8 2.4 %collective-permute-start.7 = (bf16[4,4,24,256]{3,2,1,0:T(8,128)(2,1)S(1)}, bf16[4,4,24,256]{3,2,1,0:T(8,128)(2,1)S(1)}, u32[]{:S(2)}, u32[]{:S(2)}) collective-permute-start(bf16[4,4,24,256]{3,2,1,0:T(8,128)(2,1)S(1)} %get-tuple-element.15.refs_0_), channel_id=1, source_target_pairs={{0,32},{1,33},{2,34},{3,35},{4,36},{5,37},{6,38},{7,39},{8,40},{9,... | collective-permute-start | bytes 589832 | tf_op jit(solution)/shard_map/ppermute | solution.py:42
  33.3 1.2 %collective-permute-start.10 = (bf16[2,4,24,256]{3,2,1,0:T(8,128)(2,1)S(1)}, bf16[2,4,24,256]{3,2,1,0:T(8,128)(2,1)S(1)}, u32[]{:S(2)}, u32[]{:S(2)}) collective-permute-start(bf16[2,4,24,256]{3,2,1,0:T(8,128)(2,1)S(1)} %choose.1.refs_2_), channel_id=1, source_target_pairs={{0,2},{1,3},{2,4},{3,5},{4,6},{5,7},{6,0},{7,1},{8,10},{9,11},{10,... | collective-permute-start | bytes 294920 | tf_op jit(solution)/shard_map/ppermute | solution.py:42
  34.5 0.8 %collective-permute-start.9 = (bf16[2,4,24,256]{3,2,1,0:T(8,128)(2,1)S(1)}, bf16[2,4,24,256]{3,2,1,0:T(8,128)(2,1)S(1)}, u32[]{:S(2)}, u32[]{:S(2)}) collective-permute-start(bf16[2,4,24,256]{3,2,1,0:T(8,128)(2,1)S(1)} %choose.1.refs_2_), channel_id=1, source_target_pairs={{0,4},{1,5},{2,6},{3,7},{4,0},{5,1},{6,2},{7,3},{8,12},{9,13},{10,... | collective-permute-start | bytes 294920 | tf_op jit(solution)/shard_map/ppermute | solution.py:42
  35.3 1.1 %collective-permute-start.8 = (bf16[2,4,24,256]{3,2,1,0:T(8,128)(2,1)S(1)}, bf16[2,4,24,256]{3,2,1,0:T(8,128)(2,1)S(1)}, u32[]{:S(2)}, u32[]{:S(2)}) collective-permute-start(bf16[2,4,24,256]{3,2,1,0:T(8,128)(2,1)S(1)} %choose.1.refs_2_), channel_id=1, source_target_pairs={{0,6},{1,7},{2,0},{3,1},{4,2},{5,3},{6,4},{7,5},{8,14},{9,15},{10,... | collective-permute-start | bytes 294920 | tf_op jit(solution)/shard_map/ppermute | solution.py:42
  36.4 1.5 %collective-permute-done.10.refs_5_ = bf16[2,4,24,256]{3,2,1,0:T(8,128)(2,1)S(1)} collective-permute-done((bf16[2,4,24,256]{3,2,1,0:T(8,128)(2,1)S(1)}, bf16[2,4,24,256]{3,2,1,0:T(8,128)(2,1)S(1)}, u32[]{:S(2)}, u32[]{:S(2)}) %collective-permute-start.10) | collective-permute-done | bytes 98336 | tf_op jit(solution)/shard_map/ppermute | solution.py:42
  37.9 2.7 %collective-permute-done.9.refs_4_ = bf16[2,4,24,256]{3,2,1,0:T(8,128)(2,1)S(1)} collective-permute-done((bf16[2,4,24,256]{3,2,1,0:T(8,128)(2,1)S(1)}, bf16[2,4,24,256]{3,2,1,0:T(8,128)(2,1)S(1)}, u32[]{:S(2)}, u32[]{:S(2)}) %collective-permute-start.9) | collective-permute-done | bytes 98336 | tf_op jit(solution)/shard_map/ppermute | solution.py:42
  40.6 0.5 collective-permute-done.8.refs_3_
  41.1 0.0 collective-permute-done.7.refs_1_
  41.1 1.4 %gram.1 = (f32[192,96]{1,0:T(8,128)S(1)}, bf16[192,96]{1,0:T(8,128)(2,1)S(1)}, bf16[192,96]{1,0:T(8,128)(2,1)S(1)}, bf16[192,96]{1,0:T(8,128)(2,1)S(1)}) custom-call(bf16[4,4,24,256]{3,2,1,0:T(8,128)(2,1)S(1)} %get-tuple-element.15.refs_0_, bf16[4,4,24,256]{3,2,1,0:T(8,128)(2,1)S(1)} %collective-permute-done.7.refs_1_, ...), custom_call_target="tpu_custom_call" | custom-call | tf_op jit(solution)/shard_map/gram/pallas_call | solution.py:247
  42.4 4.1 %collective-permute-start.11 = (bf16[192,96]{1,0:T(8,128)(2,1)S(1)}, bf16[192,96]{1,0:T(8,128)(2,1)S(1)}, u32[]{:S(2)}, u32[]{:S(2)}) collective-permute-start(bf16[192,96]{1,0:T(8,128)(2,1)S(1)} %get-tuple-element.18), channel_id=1, source_target_pairs={{0,64},{1,65},{2,66},{3,67},{4,68},{5,69},{6,70},{7,71},{8,72},{9,... | collective-permute-start | bytes 110600 | tf_op jit(solution)/shard_map/ppermute | solution.py:42
  46.5 2.5 %collective-permute-start.12 = (bf16[192,96]{1,0:T(8,128)(2,1)S(1)}, bf16[192,96]{1,0:T(8,128)(2,1)S(1)}, u32[]{:S(2)}, u32[]{:S(2)}) collective-permute-start(bf16[192,96]{1,0:T(8,128)(2,1)S(1)} %get-tuple-element.19), channel_id=1, source_target_pairs={{0,128},{1,129},{2,130},{3,131},{4,132},{5,133},{6,134},{7,135},{8... | collective-permute-start | bytes 110600 | tf_op jit(solution)/shard_map/ppermute | solution.py:42
  49.0 5.4 %collective-permute-start.13 = (bf16[192,96]{1,0:T(8,128)(2,1)S(1)}, bf16[192,96]{1,0:T(8,128)(2,1)S(1)}, u32[]{:S(2)}, u32[]{:S(2)}) collective-permute-start(bf16[192,96]{1,0:T(8,128)(2,1)S(1)} %get-tuple-element.20), channel_id=1, source_target_pairs={{0,192},{1,193},{2,194},{3,195},{4,196},{5,197},{6,198},{7,199},{8... | collective-permute-start | bytes 110600 | tf_op jit(solution)/shard_map/ppermute | solution.py:42
  54.4 0.0 collective-permute-done.11
  54.4 0.0 collective-permute-done.12
  54.4 2.6 %collective-permute-done.13 = bf16[192,96]{1,0:T(8,128)(2,1)S(1)} collective-permute-done((bf16[192,96]{1,0:T(8,128)(2,1)S(1)}, bf16[192,96]{1,0:T(8,128)(2,1)S(1)}, u32[]{:S(2)}, u32[]{:S(2)}) %collective-permute-start.13) | collective-permute-done | bytes 36896 | tf_op jit(solution)/shard_map/ppermute | solution.py:42
  57.0 0.7 %convert_add_fusion = f32[192,96]{1,0:T(8,128)} fusion(bf16[192,96]{1,0:T(8,128)(2,1)S(1)} %collective-permute-done.13, bf16[192,96]{1,0:T(8,128)(2,1)S(1)} %collective-permute-done.12, f32[192,96]{1,0:T(8,128)S(1)} %get-tuple-element.17, bf16[192,96]{1,0:T(8,128)(2,1)S(1)} %collective-permute-done.11), kind=kLoop, calls=%fused_computation | loop fusion | flops 110592 | bytes 258048 | tf_op jit(solution)/shard_map/add | solution.py:261
  (2 shorter events, 0.0 us)
Async XLA Ops:
  0.0 2.7 %collective-permute-start = (s32[32]{0:T(128)}, s32[32]{0:T(128)S(1)}, u32[]{:S(2)}, u32[]{:S(2)}) collective-permute-start(s32[32]{0:T(128)} %fire.1), channel_id=1, source_target_pairs={{0,8},{1,9},{2,10},{3,11},{4,12},{5,13},{6,14},{7,15},{8,16},{9,17... | collective-permute-start | bytes 392 | tf_op jit(solution)/shard_map/ppermute | solution.py:42
  2.7 1.4 %copy-start = (bf16[96,8192]{1,0:T(8,128)(2,1)S(1)}, bf16[96,8192]{1,0:T(8,128)(2,1)}, u32[]{:S(2)}) copy-start(bf16[96,8192]{1,0:T(8,128)(2,1)} %record.3) | copy-start | bytes 4718596
  4.1 0.9 %copy-start.2 = (f32[8,2560]{1,0:T(8,128)S(1)}, f32[8,2560]{1,0:T(8,128)}, u32[]{:S(2)}) copy-start(f32[8,2560]{1,0:T(8,128)} %constant.2.clone.table) | copy-start | bytes 245764
  5.0 2.2 %copy-start.1 = (bf16[96,8192]{1,0:T(8,128)(2,1)S(1)}, bf16[96,8192]{1,0:T(8,128)(2,1)}, u32[]{:S(2)}) copy-start(bf16[96,8192]{1,0:T(8,128)(2,1)} %record.3) | copy-start | bytes 4718596
  5.0 2.2 %copy-start.3 = (f32[8,2560]{1,0:T(8,128)S(1)}, f32[8,2560]{1,0:T(8,128)}, u32[]{:S(2)}) copy-start(f32[8,2560]{1,0:T(8,128)} %constant.2.clone.table) | copy-start | bytes 245764
  5.0 2.3 %copy-start.4 = (s32[32]{0:T(128)S(1)}, s32[32]{0:T(128)}, u32[]{:S(2)}) copy-start(s32[32]{0:T(128)} %fire.1) | copy-start | bytes 388
  5.9 4.7 %collective-permute-start.1 = (f32[64,96]{1,0:T(8,128)S(1)}, f32[64,96]{1,0:T(8,128)S(1)}, u32[]{:S(2)}, u32[]{:S(2)}) collective-permute-start(f32[64,96]{1,0:T(8,128)S(1)} %next_spectra.1), channel_id=1, source_target_pairs={{8,0},{9,1},{10,2},{11,3},{12,4},{13,5},{14,6},{15,7},{16,8},{17,9... | collective-permute-start | bytes 73736 | tf_op jit(solution)/shard_map/ppermute | solution.py:42
  10.7 6.7 %collective-permute-start.4 = (bf16[4,24,256]{2,1,0:T(8,128)(2,1)S(1)}, bf16[4,24,256]{2,1,0:T(8,128)(2,1)S(1)}, u32[]{:S(2)}, u32[]{:S(2)}) collective-permute-start(bf16[4,24,256]{2,1,0:T(8,128)(2,1)S(1)} %finish_spectra.1.y0), channel_id=1, source_target_pairs={{0,24},{1,25},{2,26},{3,27},{4,28},{5,29},{6,30},{7,31},{8,16},{9,... | collective-permute-start | bytes 147464 | tf_op jit(solution)/shard_map/ppermute | solution.py:42
  15.5 4.1 %collective-permute-start.3 = (bf16[4,24,256]{2,1,0:T(8,128)(2,1)S(1)}, bf16[4,24,256]{2,1,0:T(8,128)(2,1)S(1)}, u32[]{:S(2)}, u32[]{:S(2)}) collective-permute-start(bf16[4,24,256]{2,1,0:T(8,128)(2,1)S(1)} %finish_spectra.1.y0), channel_id=1, source_target_pairs={{0,16},{1,17},{2,18},{3,19},{4,20},{5,21},{6,22},{7,23},{8,24},{9,... | collective-permute-start | bytes 147464 | tf_op jit(solution)/shard_map/ppermute | solution.py:42
  15.6 4.0 %collective-permute-start.2 = (bf16[4,24,256]{2,1,0:T(8,128)(2,1)S(1)}, bf16[4,24,256]{2,1,0:T(8,128)(2,1)S(1)}, u32[]{:S(2)}, u32[]{:S(2)}) collective-permute-start(bf16[4,24,256]{2,1,0:T(8,128)(2,1)S(1)} %finish_spectra.1.y0), channel_id=1, source_target_pairs={{0,8},{1,9},{2,10},{3,11},{4,12},{5,13},{6,14},{7,15},{8,0},{9,1},... | collective-permute-start | bytes 147464 | tf_op jit(solution)/shard_map/ppermute | solution.py:42
  19.6 9.2 %collective-permute-start.6 = (bf16[4,24,256]{2,1,0:T(8,128)(2,1)S(1)}, bf16[4,24,256]{2,1,0:T(8,128)(2,1)S(1)}, u32[]{:S(2)}, u32[]{:S(2)}) collective-permute-start(bf16[4,24,256]{2,1,0:T(8,128)(2,1)S(1)} %get-tuple-element.14.own), channel_id=1, source_target_pairs={{1,32},{3,34},{5,36},{7,38},{9,40},{11,42},{13,44},{15,46},{17,48}... | collective-permute-start | bytes 147464 | tf_op jit(solution)/shard_map/ppermute | solution.py:42
  20.3 10.6 %collective-permute-start.5 = (bf16[4,24,256]{2,1,0:T(8,128)(2,1)S(1)}, bf16[4,24,256]{2,1,0:T(8,128)(2,1)S(1)}, u32[]{:S(2)}, u32[]{:S(2)}) collective-permute-start(bf16[4,24,256]{2,1,0:T(8,128)(2,1)S(1)} %get-tuple-element.14.own), channel_id=1, source_target_pairs={{0,1},{1,33},{2,3},{3,35},{4,5},{5,37},{6,7},{7,39},{8,9},{9,41},{... | collective-permute-start | bytes 147464 | tf_op jit(solution)/shard_map/ppermute | solution.py:42
  30.8 10.2 %collective-permute-start.7 = (bf16[4,4,24,256]{3,2,1,0:T(8,128)(2,1)S(1)}, bf16[4,4,24,256]{3,2,1,0:T(8,128)(2,1)S(1)}, u32[]{:S(2)}, u32[]{:S(2)}) collective-permute-start(bf16[4,4,24,256]{3,2,1,0:T(8,128)(2,1)S(1)} %get-tuple-element.15.refs_0_), channel_id=1, source_target_pairs={{0,32},{1,33},{2,34},{3,35},{4,36},{5,37},{6,38},{7,39},{8,40},{9,... | collective-permute-start | bytes 589832 | tf_op jit(solution)/shard_map/ppermute | solution.py:42
  33.3 4.6 %collective-permute-start.10 = (bf16[2,4,24,256]{3,2,1,0:T(8,128)(2,1)S(1)}, bf16[2,4,24,256]{3,2,1,0:T(8,128)(2,1)S(1)}, u32[]{:S(2)}, u32[]{:S(2)}) collective-permute-start(bf16[2,4,24,256]{3,2,1,0:T(8,128)(2,1)S(1)} %choose.1.refs_2_), channel_id=1, source_target_pairs={{0,2},{1,3},{2,4},{3,5},{4,6},{5,7},{6,0},{7,1},{8,10},{9,11},{10,... | collective-permute-start | bytes 294920 | tf_op jit(solution)/shard_map/ppermute | solution.py:42
  34.5 6.1 %collective-permute-start.9 = (bf16[2,4,24,256]{3,2,1,0:T(8,128)(2,1)S(1)}, bf16[2,4,24,256]{3,2,1,0:T(8,128)(2,1)S(1)}, u32[]{:S(2)}, u32[]{:S(2)}) collective-permute-start(bf16[2,4,24,256]{3,2,1,0:T(8,128)(2,1)S(1)} %choose.1.refs_2_), channel_id=1, source_target_pairs={{0,4},{1,5},{2,6},{3,7},{4,0},{5,1},{6,2},{7,3},{8,12},{9,13},{10,... | collective-permute-start | bytes 294920 | tf_op jit(solution)/shard_map/ppermute | solution.py:42
  35.3 5.8 %collective-permute-start.8 = (bf16[2,4,24,256]{3,2,1,0:T(8,128)(2,1)S(1)}, bf16[2,4,24,256]{3,2,1,0:T(8,128)(2,1)S(1)}, u32[]{:S(2)}, u32[]{:S(2)}) collective-permute-start(bf16[2,4,24,256]{3,2,1,0:T(8,128)(2,1)S(1)} %choose.1.refs_2_), channel_id=1, source_target_pairs={{0,6},{1,7},{2,0},{3,1},{4,2},{5,3},{6,4},{7,5},{8,14},{9,15},{10,... | collective-permute-start | bytes 294920 | tf_op jit(solution)/shard_map/ppermute | solution.py:42
  42.4 11.9 %collective-permute-start.11 = (bf16[192,96]{1,0:T(8,128)(2,1)S(1)}, bf16[192,96]{1,0:T(8,128)(2,1)S(1)}, u32[]{:S(2)}, u32[]{:S(2)}) collective-permute-start(bf16[192,96]{1,0:T(8,128)(2,1)S(1)} %get-tuple-element.18), channel_id=1, source_target_pairs={{0,64},{1,65},{2,66},{3,67},{4,68},{5,69},{6,70},{7,71},{8,72},{9,... | collective-permute-start | bytes 110600 | tf_op jit(solution)/shard_map/ppermute | solution.py:42
  46.5 7.8 %collective-permute-start.12 = (bf16[192,96]{1,0:T(8,128)(2,1)S(1)}, bf16[192,96]{1,0:T(8,128)(2,1)S(1)}, u32[]{:S(2)}, u32[]{:S(2)}) collective-permute-start(bf16[192,96]{1,0:T(8,128)(2,1)S(1)} %get-tuple-element.19), channel_id=1, source_target_pairs={{0,128},{1,129},{2,130},{3,131},{4,132},{5,133},{6,134},{7,135},{8... | collective-permute-start | bytes 110600 | tf_op jit(solution)/shard_map/ppermute | solution.py:42
  49.0 8.0 %collective-permute-start.13 = (bf16[192,96]{1,0:T(8,128)(2,1)S(1)}, bf16[192,96]{1,0:T(8,128)(2,1)S(1)}, u32[]{:S(2)}, u32[]{:S(2)}) collective-permute-start(bf16[192,96]{1,0:T(8,128)(2,1)S(1)} %get-tuple-element.20), channel_id=1, source_target_pairs={{0,192},{1,193},{2,194},{3,195},{4,196},{5,197},{6,198},{7,199},{8... | collective-permute-start | bytes 110600 | tf_op jit(solution)/shard_map/ppermute | solution.py:42

commit v3 on v1

v3 whole, which is shorter than its diff:
```python
import math

import jax
import jax.numpy as jnp
import numpy as np
from jax import lax
from jax.experimental import pallas as pl
from jax.experimental.pallas import tpu as pltpu
from jax.sharding import PartitionSpec as P

import ml_dtypes

WIN = 2048
SPACING = 256
PAIR = 2 * SPACING
SPAN = WIN + PAIR
FREQ_BINS = (24, 40, 56, 80)
NF = len(FREQ_BINS)
ROWS = 2 * NF

SHOT_DEVICES = 32
RCV_DEVICES = 8
QUARTERS = 4
LATE = WIN // SPACING


def dft_master():
    turns = np.arange(WIN)[None, :] * np.array(FREQ_BINS)[:, None] % WIN
    angle = 2.0 * math.pi / WIN * turns
    rows = np.concatenate([np.cos(angle), -np.sin(angle)], axis=0) / math.sqrt(WIN)
    rows = rows.astype(np.float32).astype(ml_dtypes.bfloat16).astype(np.float32)
    return np.concatenate([rows, np.zeros((ROWS, SPAN - WIN), np.float32)], axis=1)


def send(block, to):
    route = []
    for shot in range(SHOT_DEVICES):
        for rcv in range(RCV_DEVICES):
            target = to(shot >> 4, (shot >> 2) & 3, shot & 3, rcv >> 2, rcv & 3)
            if target is not None:
                yh, u, k, xh, v = target
                route.append((shot * RCV_DEVICES + rcv, (yh << 4 | u << 2 | k) * RCV_DEVICES + (xh << 2 | v)))
    return lax.ppermute(block, ("shot", "rcv"), route)


def shot_index():
    return lax.axis_index("shot")


def vmem(count):
    return [pl.BlockSpec(memory_space=pltpu.VMEM)] * count


def pair_tables(table, first, second):
    rows = [pltpu.roll(table, first, 1), pltpu.roll(table, second + SPACING, 1)]
    return jnp.concatenate(rows, axis=0).astype(jnp.bfloat16)


def delay(fire, shot):
    return fire[shot] & (SPACING - 1)


def add_products(total, tables, first_pair, blocks):
    reach = SPAN // PAIR
    last_pair = first_pair + tables.shape[0] - 1
    for u, samples in blocks:
        low, high = max(first_pair, u - reach + 1), min(u, last_pair)
        left = jnp.concatenate(
            [tables[p - first_pair, :, PAIR * (u - p) : PAIR * (u - p + 1)] for p in range(low, high + 1)], axis=0
        )
        part = lax.dot_general(left, samples, (((1,), (1,)), ((), ())), preferred_element_type=jnp.float32)
        total[2 * ROWS * (low - first_pair) : 2 * ROWS * (high + 1 - first_pair), :] += part


def tail_kernel(fire, table, record, message, tables, samples, sem):
    pairs = fire.shape[0] // 2
    late = LATE // 2
    start = record.shape[1] - samples.shape[1]
    copy = pltpu.make_async_copy(record.at[:, start:], samples, sem)
    copy.start()
    master = table[...]
    for p in range(late):
        shot = 2 * (pairs - late + p)
        tables[p] = pair_tables(master, delay(fire, shot), delay(fire, shot + 1))
    message[...] = jnp.zeros_like(message)
    row = lax.broadcasted_iota(jnp.int32, (LATE, message.shape[1]), 0)
    delays = jnp.zeros(row.shape, jnp.int32)
    for i in range(LATE):
        delays = jnp.where(row == i, delay(fire, 2 * (pairs - late) + i), delays)
    message[ROWS * LATE :, :] = delays.astype(jnp.float32)
    copy.wait()
    blocks = [(pairs - late + v, samples[:, PAIR * v : PAIR * (v + 1)]) for v in range(late)]
    add_products(message, tables, pairs - late, blocks)


def own_kernel(fire, table, record, total, head, tables, samples, sems):
    parts = sems.shape[0]
    width = record.shape[1] // parts
    copies = [
        pltpu.make_async_copy(
            record.at[:, width * i : width * (i + 1)], samples.at[:, width * i : width * (i + 1)], sems.at[i]
        )
        for i in range(parts)
    ]
    for copy in copies:
        copy.start()
    master = table[...]
    for p in range(tables.shape[0]):
        tables[p] = pair_tables(master, delay(fire, 2 * p), delay(fire, 2 * p + 1))
    total[...] = jnp.zeros_like(total)
    per = width // PAIR
    for i, copy in enumerate(copies):
        copy.wait()
        blocks = [(per * i + v, samples[:, PAIR * (per * i + v) : PAIR * (per * i + v + 1)]) for v in range(per)]
        add_products(total, tables, 0, blocks)
    head[...] = samples[:, : head.shape[1]]


def finish_kernel(total, head, table, message, out, scratch, tables):
    own_rows = total.shape[0]
    lanes = scratch.shape[0]
    late = LATE // 2
    follows = (shot_index() > 0).astype(jnp.float32)
    master = table[...]
    for p in range(late):
        rows = [message[ROWS * LATE + 2 * p + i : ROWS * LATE + 2 * p + i + 1, :] for i in range(2)]
        first, second = [jnp.max(r).astype(jnp.int32) for r in rows]
        tables[p] = pair_tables(master, first, second)
    scratch[:own_rows, :] = jnp.zeros_like(total)
    scratch[own_rows:, :] = jnp.zeros((lanes - own_rows, total.shape[1]), jnp.float32)
    blocks = [(late + v, head[:, PAIR * v : PAIR * (v + 1)]) for v in range(late)]
    add_products(scratch.at[own_rows:, :], tables, 0, blocks)
    scratch[own_rows:, :] = message[: ROWS * LATE, :] + follows * scratch[own_rows:, :]
    scratch[:own_rows, :] = total[...]
    ordered = jnp.concatenate([scratch[pl.ds(c, lanes // ROWS, stride=ROWS), :] for c in range(ROWS)], axis=0)
    turned = ordered.T
    count = out.shape[1]
    for k in range(QUARTERS):
        out[k] = turned[count * k : count * (k + 1), :].astype(out.dtype)


def pair_kernel(own, other, out):
    yh = shot_index() >> 4
    out[yh] = own[...]
    out[1 - yh] = other[...]


def collect_kernel(y0, y1, y2, y3, gathered, quarter):
    k = shot_index() & 3
    for m, y in enumerate((y0, y1, y2, y3)):
        gathered[k ^ m] = y[...]
        quarter[k ^ m] = y[:, k]


def choose_kernel(own, cross, out):
    straight = (shot_index() >> 4) == (lax.axis_index("rcv") >> 2)

    @pl.when(straight)
    def _():
        out[...] = own[...]

    @pl.when(jnp.logical_not(straight))
    def _():
        out[...] = cross[...]


def right_kernel(gathered, right):
    half = right.shape[2] // 2
    for k in range(QUARTERS):
        for yh in range(2):
            z = gathered[k, yh].astype(jnp.float32).reshape(right.shape[1] // 2, 2 * half)
            w = jnp.concatenate([-z[:, half:], z[:, :half]], axis=1)
            right[2 * k + yh] = jnp.concatenate([z, w], axis=0).astype(jnp.bfloat16)


def gram_kernel(scale, right, q0, q1, q2, q3, p0, p1, p2, p3, total):
    turn = ((shot_index() >> 2) ^ lax.axis_index("rcv")) & 3
    count, lanes = q0.shape[2:]
    half = lanes // 2
    span = right.shape[1] // 2
    per = half // NF
    lane = lax.broadcasted_iota(jnp.int32, (count, lanes), 1) % half // per
    for m, q in enumerate((q0, q1, q2, q3)):
        acc = jnp.zeros((NF * count, 2 * span), jnp.float32)
        for k in range(QUARTERS):
            for yh in range(2):
                rows = q[k, yh].astype(jnp.float32)
                left = jnp.concatenate([jnp.where(lane == f, rows, 0.0) for f in range(NF)], axis=0)
                acc = acc + lax.dot_general(
                    left.astype(jnp.bfloat16),
                    right[2 * k + yh],
                    (((1,), (1,)), ((), ())),
                    preferred_element_type=jnp.float32,
                )
        total[turn ^ m, : NF * count, :] = acc[:, :span] * scale
        total[turn ^ m, NF * count :, :] = acc[:, span:] * scale
    for n, out in enumerate((p0, p1, p2, p3)):
        out[...] = total[n].astype(out.dtype)


def local(kernel, name, out_shape, in_specs, scratch=(), limit=4):
    single = not isinstance(out_shape, tuple)
    return pl.pallas_call(
        kernel,
        out_shape=out_shape,
        in_specs=in_specs,
        out_specs=vmem(1)[0] if single else tuple(vmem(len(out_shape))),
        scratch_shapes=list(scratch),
        compiler_params=pltpu.CompilerParams(vmem_limit_bytes=limit << 20),
        name=name,
    )


def per_device(record, shot_fire_samples):
    receivers, samples = record.shape
    shots = shot_fire_samples.shape[0]
    pairs, late = shots // 2, LATE // 2
    lanes = ROWS * shots
    late_rows = ROWS * LATE
    count = receivers // QUARTERS
    bf16, f32 = jnp.bfloat16, jnp.float32
    shape = jax.ShapeDtypeStruct
    table = jnp.asarray(dft_master())
    smem, hbm = pl.BlockSpec(memory_space=pltpu.SMEM), pl.BlockSpec(memory_space=pltpu.HBM)

    message = local(
        tail_kernel,
        "tail_spectra",
        shape((late_rows + LATE, receivers), f32),
        [smem] + vmem(1) + [hbm],
        [pltpu.VMEM((late, 2 * ROWS, SPAN), bf16), pltpu.VMEM((receivers, WIN), bf16), pltpu.SemaphoreType.DMA],
        limit=63,
    )(shot_fire_samples, table, record)

    def following(yh, u, k, xh, v):
        shot = ((yh << 4 | u << 2 | k) + 1) % SHOT_DEVICES
        return shot >> 4, (shot >> 2) & 3, shot & 3, xh, v

    received = send(message, following)
    total, head = local(
        own_kernel,
        "own_spectra",
        (shape((lanes - late_rows, receivers), f32), shape((receivers, WIN), bf16)),
        [smem] + vmem(1) + [hbm],
        [
            pltpu.VMEM((pairs - late, 2 * ROWS, SPAN), bf16),
            pltpu.VMEM((receivers, samples), bf16),
            pltpu.SemaphoreType.DMA((4,)),
        ],
        limit=63,
    )(shot_fire_samples, table, record)
    y = local(
        finish_kernel,
        "finish_spectra",
        shape((QUARTERS, count, lanes), bf16),
        vmem(4),
        [pltpu.VMEM((lanes, receivers), f32), pltpu.VMEM((late, 2 * ROWS, SPAN), bf16)],
    )(total, head, table, received)

    y = local(pair_kernel, "both_halves", shape((2,) + y.shape, bf16), vmem(2))(
        y, send(y, lambda yh, u, k, xh, v: (1 - yh, u, k, xh, v))
    )
    ys = [send(y, lambda yh, u, k, xh, v, m=m: (yh, u, k ^ m, xh, v)) for m in (1, 2, 3)]
    gathered, quarter = local(
        collect_kernel,
        "collect",
        (shape((QUARTERS,) + y.shape, bf16), shape((QUARTERS, 2, count, lanes), bf16)),
        vmem(4),
    )(y, *ys)
    cross = send(quarter, lambda yh, u, k, xh, v: (yh, u, k, 1 - xh, v) if xh == yh else None)
    q = local(choose_kernel, "choose", shape(quarter.shape, bf16), vmem(2))(quarter, cross)
    qs = [q] + [send(q, lambda yh, u, k, xh, v, m=m: (yh, u, k, xh, v ^ m)) for m in (1, 2, 3)]
    right = local(right_kernel, "right_side", shape((2 * QUARTERS, 2 * receivers, lanes), bf16), vmem(1))(gathered)

    total_shots = shots * lax.axis_size("shot")
    rows = ROWS * count
    first, *others = local(
        lambda *refs: gram_kernel(1.0 / total_shots, *refs),
        "gram",
        (shape((rows, receivers), f32),) + (shape((rows, receivers), bf16),) * 3,
        vmem(5),
        [pltpu.VMEM((QUARTERS, rows, receivers), f32)],
        limit=8,
    )(right, *qs)
    sums = first
    for n, share in enumerate(others, 1):
        sums = sums + send(share, lambda yh, u, k, xh, v, n=n: (yh, u ^ n, k, xh, v)).astype(f32)
    return sums.reshape(2, NF, count, receivers).transpose(0, 1, 3, 2)


def solution(mesh):
    return jax.shard_map(
        per_device,
        mesh=mesh,
        in_specs=(P("rcv", "shot"), P("shot")),
        out_specs=P(None, None, "rcv", "shot"),
        check_vma=False,
    )
```

time: 71.9 us -> 56.2 us (0.78)
  starting transfers between devices: 33.2 us -> 14.2 us
  waiting for transfers between devices: 19.7 us -> 30 us
  local copies, waits for them, and re-layouts: 4.9 us -> 1.89 us
  Pallas kernels: 11.8 us -> 9.03 us
  other arithmetic: 1.56 us -> 0.66 us
    ppermute x13 -> x12, starting transfers between devices: 33.2 us -> 14.2 us  [send(): return lax.ppermute(block, ('shot', 'rcv'), route)]
    ppermute x13 -> x12, waiting for transfers between devices: 19.7 us -> 30 us  [send(): return lax.ppermute(block, ('shot', 'rcv'), route)]
    pallas_call x5 -> x8, Pallas kernels: 11.8 us -> 9.03 us  [the longest x1 4.09 us: per_device(): local(own_kernel, 'own_spectra', (shape((lanes - late_rows, receivers), f...]
    unnamed x20 -> x6, local copies, waits for them, and re-layouts: 3.88 us -> 1.89 us
    slice x1 -> x0, local copies, waits for them, and re-layouts: 1.02 us -> none  [per_device(): rim = send(record[:, :WIN], before)]
    add x1, other arithmetic: 1.56 us -> 0.66 us  [per_device(): sums + send(share, lambda yh, u, k, xh, v, n=n: (yh, u ^ n, k, xh, v)).as...]
  transfers between devices with their start and end apart: 13 -> 12, of which waited for: 7 -> 9; matrix products, arithmetic and copies ran while one was open for 0% -> 0% of each run, Pallas kernels for 7% -> 7%
where the time goes in v3:
time: 56.2 us; the launch traced here: 55.9 us
  waiting for transfers between devices  30 us (53%)
  starting transfers between devices  14.2 us (25%)
  Pallas kernels  9.03 us (16%)
  local copies, waits for them, and re-layouts  1.89 us (3%)
  other arithmetic  0.66 us (1%)
    ppermute x12, waiting for transfers between devices, send(): return lax.ppermute(block, ('shot', 'rcv'), route)  30 us
    ppermute x12, starting transfers between devices, send(): return lax.ppermute(block, ('shot', 'rcv'), route)  14.2 us
    pallas_call x1, Pallas kernels, per_device(): local(own_kernel, 'own_spectra', (shape((lanes - late_rows, receivers), f...  4.09 us
    pallas_call x1, Pallas kernels, per_device(): local(tail_kernel, 'tail_spectra', shape((late_rows + LATE, receivers), f...  2.94 us
    unnamed x6, local copies, waits for them, and re-layouts  1.89 us
    pallas_call x1, Pallas kernels, per_device(): local(lambda *refs: gram_kernel(1.0 / total_shots, *refs), 'gram', (shape...  1.26 us
  transfers between devices with their start and end apart: 12, of which 9 were waited for; matrix products, arithmetic and copies ran while one was open for 0% of the time, Pallas kernels for 7%

profile of v3, /device:TPU:4, one launch (start us, length us, event | category | flops | bytes accessed | tf_op | source)
XLA Modules:
  0.0 55.9 jit_solution(1888074448507055517)
XLA Ops:
  0.0 0.0 copy-start
  0.0 2.9 %tail_spectra.1 = f32[72,96]{1,0:T(8,128)} custom-call(s32[32]{0:T(128)} %fire.3, f32[8,2560]{1,0:T(8,128)} %constant.2.clone.table, bf16[96,8192]{1,0:T(8,128)(2,1)} %record.3), custom_call_target="tpu_custom_call" | custom-call | tf_op jit(solution)/shard_map/tail_spectra/pallas_call | solution.py:226
  2.9 0.1 collective-permute-start
  3.0 4.1 %own_spectra.1 = (f32[192,96]{1,0:T(8,128)}, bf16[96,2048]{1,0:T(8,128)(2,1)}) custom-call(s32[32]{0:T(128)} %fire.3, f32[8,2560]{1,0:T(8,128)} %constant.2.clone.table, bf16[96,8192]{1,0:T(8,128)(2,1)} %record.3), custom_call_target="tpu_custom_call" | custom-call | tf_op jit(solution)/shard_map/own_spectra/pallas_call | solution.py:240
  7.1 5.7 %collective-permute-done.message = f32[72,96]{1,0:T(8,128)S(1)} collective-permute-done((f32[72,96]{1,0:T(8,128)}, f32[72,96]{1,0:T(8,128)S(1)}, u32[]{:S(2)}, u32[]{:S(2)}) %collective-permute-start) | collective-permute-done | bytes 27680 | tf_op jit(solution)/shard_map/ppermute | solution.py:43
  12.8 0.0 copy-done
  12.8 0.0 copy-start.1
  12.8 1.0 %copy-done.1 = bf16[96,2048]{1,0:T(8,128)(2,1)S(1)} copy-done((bf16[96,2048]{1,0:T(8,128)(2,1)S(1)}, bf16[96,2048]{1,0:T(8,128)(2,1)}, u32[]{:S(2)}) %copy-start.1) | copy-done | bytes 393240
  13.8 0.0 copy-start.2
  13.8 0.9 %copy-done.2 = f32[192,96]{1,0:T(8,128)S(1)} copy-done((f32[192,96]{1,0:T(8,128)S(1)}, f32[192,96]{1,0:T(8,128)}, u32[]{:S(2)}) %copy-start.2) | copy-done | bytes 73752
  14.7 0.6 %finish_spectra.1.own = bf16[4,24,256]{2,1,0:T(8,128)(2,1)S(1)} custom-call(f32[192,96]{1,0:T(8,128)S(1)} %copy-done.2, bf16[96,2048]{1,0:T(8,128)(2,1)S(1)} %copy-done.1, f32[8,2560]{1,0:T(8,128)S(1)} %copy-done, f32[72,96]{1,0:T(8,128)S(1)} %collective-permute-done.message), custom_call_target="tpu_custom_call" | custom-call | tf_op jit(solution)/shard_map/finish_spectra/pallas_call | solution.py:252
  15.3 0.7 %collective-permute-start.1 = (bf16[4,24,256]{2,1,0:T(8,128)(2,1)S(1)}, bf16[4,24,256]{2,1,0:T(8,128)(2,1)S(1)}, u32[]{:S(2)}, u32[]{:S(2)}) collective-permute-start(bf16[4,24,256]{2,1,0:T(8,128)(2,1)S(1)} %finish_spectra.1.own), channel_id=1, source_target_pairs={{0,128},{1,129},{2,130},{3,131},{4,132},{5,133},{6,134},{7,135},{8... | collective-permute-start | bytes 147464 | tf_op jit(solution)/shard_map/ppermute | solution.py:43
  16.0 5.0 %collective-permute-done.1.other = bf16[4,24,256]{2,1,0:T(8,128)(2,1)S(1)} collective-permute-done((bf16[4,24,256]{2,1,0:T(8,128)(2,1)S(1)}, bf16[4,24,256]{2,1,0:T(8,128)(2,1)S(1)}, u32[]{:S(2)}, u32[]{:S(2)}) %collective-permute-start.1) | collective-permute-done | bytes 49184 | tf_op jit(solution)/shard_map/ppermute | solution.py:43
  21.0 0.1 collective-permute-start.2
  21.1 0.1 collective-permute-start.3
  21.2 1.8 %collective-permute-start.4 = (bf16[2,4,24,256]{3,2,1,0:T(8,128)(2,1)S(1)}, bf16[2,4,24,256]{3,2,1,0:T(8,128)(2,1)S(1)}, u32[]{:S(2)}, u32[]{:S(2)}) collective-permute-start(bf16[2,4,24,256]{3,2,1,0:T(8,128)(2,1)S(1)} %both_halves.1.y0), channel_id=1, source_target_pairs={{0,24},{1,25},{2,26},{3,27},{4,28},{5,29},{6,30},{7,31},{8,16},{9,... | collective-permute-start | bytes 294920 | tf_op jit(solution)/shard_map/ppermute | solution.py:43
  23.0 0.0 collective-permute-done.2.y1
  23.0 3.8 %collective-permute-done.3.y2 = bf16[2,4,24,256]{3,2,1,0:T(8,128)(2,1)S(1)} collective-permute-done((bf16[2,4,24,256]{3,2,1,0:T(8,128)(2,1)S(1)}, bf16[2,4,24,256]{3,2,1,0:T(8,128)(2,1)S(1)}, u32[]{:S(2)}, u32[]{:S(2)}) %collective-permute-start.3) | collective-permute-done | bytes 98336 | tf_op jit(solution)/shard_map/ppermute | solution.py:43
  26.8 1.2 %collective-permute-done.4.y3 = bf16[2,4,24,256]{3,2,1,0:T(8,128)(2,1)S(1)} collective-permute-done((bf16[2,4,24,256]{3,2,1,0:T(8,128)(2,1)S(1)}, bf16[2,4,24,256]{3,2,1,0:T(8,128)(2,1)S(1)}, u32[]{:S(2)}, u32[]{:S(2)}) %collective-permute-start.4) | collective-permute-done | bytes 98336 | tf_op jit(solution)/shard_map/ppermute | solution.py:43
  28.0 1.3 %collective-permute-start.5 = (bf16[4,2,24,256]{3,2,1,0:T(8,128)(2,1)S(1)}, bf16[4,2,24,256]{3,2,1,0:T(8,128)(2,1)S(1)}, u32[]{:S(2)}, u32[]{:S(2)}) collective-permute-start(bf16[4,2,24,256]{3,2,1,0:T(8,128)(2,1)S(1)} %get-tuple-element.16.own), channel_id=1, source_target_pairs={{0,4},{1,5},{2,6},{3,7},{8,12},{9,13},{10,14},{11,15},{16,20},{17,... | collective-permute-start | bytes 294920 | tf_op jit(solution)/shard_map/ppermute | solution.py:43
  29.3 7.1 %collective-permute-done.5.cross = bf16[4,2,24,256]{3,2,1,0:T(8,128)(2,1)S(1)} collective-permute-done((bf16[4,2,24,256]{3,2,1,0:T(8,128)(2,1)S(1)}, bf16[4,2,24,256]{3,2,1,0:T(8,128)(2,1)S(1)}, u32[]{:S(2)}, u32[]{:S(2)}) %collective-permute-start.5) | collective-permute-done | bytes 98336 | tf_op jit(solution)/shard_map/ppermute | solution.py:43
  36.4 0.8 %collective-permute-start.6 = (bf16[4,2,24,256]{3,2,1,0:T(8,128)(2,1)S(1)}, bf16[4,2,24,256]{3,2,1,0:T(8,128)(2,1)S(1)}, u32[]{:S(2)}, u32[]{:S(2)}) collective-permute-start(bf16[4,2,24,256]{3,2,1,0:T(8,128)(2,1)S(1)} %choose.1.refs_1_), channel_id=1, source_target_pairs={{0,1},{1,0},{2,3},{3,2},{4,5},{5,4},{6,7},{7,6},{8,9},{9,8},{10,11... | collective-permute-start | bytes 294920 | tf_op jit(solution)/shard_map/ppermute | solution.py:43
  37.2 1.2 %collective-permute-start.7 = (bf16[4,2,24,256]{3,2,1,0:T(8,128)(2,1)S(1)}, bf16[4,2,24,256]{3,2,1,0:T(8,128)(2,1)S(1)}, u32[]{:S(2)}, u32[]{:S(2)}) collective-permute-start(bf16[4,2,24,256]{3,2,1,0:T(8,128)(2,1)S(1)} %choose.1.refs_1_), channel_id=1, source_target_pairs={{0,2},{1,3},{2,0},{3,1},{4,6},{5,7},{6,4},{7,5},{8,10},{9,11},{10,... | collective-permute-start | bytes 294920 | tf_op jit(solution)/shard_map/ppermute | solution.py:43
  38.4 1.6 %collective-permute-start.8 = (bf16[4,2,24,256]{3,2,1,0:T(8,128)(2,1)S(1)}, bf16[4,2,24,256]{3,2,1,0:T(8,128)(2,1)S(1)}, u32[]{:S(2)}, u32[]{:S(2)}) collective-permute-start(bf16[4,2,24,256]{3,2,1,0:T(8,128)(2,1)S(1)} %choose.1.refs_1_), channel_id=1, source_target_pairs={{0,3},{1,2},{2,1},{3,0},{4,7},{5,6},{6,5},{7,4},{8,11},{9,10},{10,... | collective-permute-start | bytes 294920 | tf_op jit(solution)/shard_map/ppermute | solution.py:43
  40.0 0.1 right_side.1.refs_0_
  40.1 2.1 %collective-permute-done.6.refs_2_ = bf16[4,2,24,256]{3,2,1,0:T(8,128)(2,1)S(1)} collective-permute-done((bf16[4,2,24,256]{3,2,1,0:T(8,128)(2,1)S(1)}, bf16[4,2,24,256]{3,2,1,0:T(8,128)(2,1)S(1)}, u32[]{:S(2)}, u32[]{:S(2)}) %collective-permute-start.6) | collective-permute-done | bytes 98336 | tf_op jit(solution)/shard_map/ppermute | solution.py:43
  42.2 0.6 %collective-permute-done.7.refs_3_ = bf16[4,2,24,256]{3,2,1,0:T(8,128)(2,1)S(1)} collective-permute-done((bf16[4,2,24,256]{3,2,1,0:T(8,128)(2,1)S(1)}, bf16[4,2,24,256]{3,2,1,0:T(8,128)(2,1)S(1)}, u32[]{:S(2)}, u32[]{:S(2)}) %collective-permute-start.7) | collective-permute-done | bytes 98336 | tf_op jit(solution)/shard_map/ppermute | solution.py:43
  42.8 1.2 %collective-permute-done.8.refs_4_ = bf16[4,2,24,256]{3,2,1,0:T(8,128)(2,1)S(1)} collective-permute-done((bf16[4,2,24,256]{3,2,1,0:T(8,128)(2,1)S(1)}, bf16[4,2,24,256]{3,2,1,0:T(8,128)(2,1)S(1)}, u32[]{:S(2)}, u32[]{:S(2)}) %collective-permute-start.8) | collective-permute-done | bytes 98336 | tf_op jit(solution)/shard_map/ppermute | solution.py:43
  44.0 1.3 %gram.1 = (f32[192,96]{1,0:T(8,128)S(1)}, bf16[192,96]{1,0:T(8,128)(2,1)S(1)}, bf16[192,96]{1,0:T(8,128)(2,1)S(1)}, bf16[192,96]{1,0:T(8,128)(2,1)S(1)}) custom-call(bf16[8,192,256]{2,1,0:T(8,128)(2,1)S(1)} %right_side.1.refs_0_, bf16[4,2,24,256]{3,2,1,0:T(8,128)(2,1)S(1)} %choose.1.refs_1_, bf16[4,2,24,256]{3,2,1,0:T(8,128)(2,1)S(1)} %collective-permute-done.6.refs_2_, ...), custom_call_target="tpu_custom_call" | custom-call | tf_op jit(solution)/shard_map/gram/pallas_call | solution.py:277
  45.2 1.9 %collective-permute-start.11 = (bf16[192,96]{1,0:T(8,128)(2,1)S(1)}, bf16[192,96]{1,0:T(8,128)(2,1)S(1)}, u32[]{:S(2)}, u32[]{:S(2)}) collective-permute-start(bf16[192,96]{1,0:T(8,128)(2,1)S(1)} %get-tuple-element.20), channel_id=1, source_target_pairs={{0,96},{1,97},{2,98},{3,99},{4,100},{5,101},{6,102},{7,103},{8,104... | collective-permute-start | bytes 110600 | tf_op jit(solution)/shard_map/ppermute | solution.py:43
  47.1 2.3 %collective-permute-start.10 = (bf16[192,96]{1,0:T(8,128)(2,1)S(1)}, bf16[192,96]{1,0:T(8,128)(2,1)S(1)}, u32[]{:S(2)}, u32[]{:S(2)}) collective-permute-start(bf16[192,96]{1,0:T(8,128)(2,1)S(1)} %get-tuple-element.19), channel_id=1, source_target_pairs={{0,64},{1,65},{2,66},{3,67},{4,68},{5,69},{6,70},{7,71},{8,72},{9,... | collective-permute-start | bytes 110600 | tf_op jit(solution)/shard_map/ppermute | solution.py:43
  49.4 2.4 %collective-permute-start.9 = (bf16[192,96]{1,0:T(8,128)(2,1)S(1)}, bf16[192,96]{1,0:T(8,128)(2,1)S(1)}, u32[]{:S(2)}, u32[]{:S(2)}) collective-permute-start(bf16[192,96]{1,0:T(8,128)(2,1)S(1)} %get-tuple-element.18), channel_id=1, source_target_pairs={{0,32},{1,33},{2,34},{3,35},{4,36},{5,37},{6,38},{7,39},{8,40},{9,... | collective-permute-start | bytes 110600 | tf_op jit(solution)/shard_map/ppermute | solution.py:43
  51.8 0.0 collective-permute-done.11
  51.8 3.4 %collective-permute-done.10 = bf16[192,96]{1,0:T(8,128)(2,1)S(1)} collective-permute-done((bf16[192,96]{1,0:T(8,128)(2,1)S(1)}, bf16[192,96]{1,0:T(8,128)(2,1)S(1)}, u32[]{:S(2)}, u32[]{:S(2)}) %collective-permute-start.10) | collective-permute-done | bytes 36896 | tf_op jit(solution)/shard_map/ppermute | solution.py:43
  55.2 0.0 collective-permute-done.9
  55.2 0.7 %convert_add_fusion = f32[192,96]{1,0:T(8,128)} fusion(bf16[192,96]{1,0:T(8,128)(2,1)S(1)} %collective-permute-done.11, bf16[192,96]{1,0:T(8,128)(2,1)S(1)} %collective-permute-done.10, f32[192,96]{1,0:T(8,128)S(1)} %get-tuple-element.17, bf16[192,96]{1,0:T(8,128)(2,1)S(1)} %collective-permute-done.9), kind=kLoop, calls=%fused_computation | loop fusion | flops 110592 | bytes 258048 | tf_op jit(solution)/shard_map/add | solution.py:287
  (3 shorter events, 0.1 us)
Async XLA Ops:
  0.0 12.8 %copy-start = (f32[8,2560]{1,0:T(8,128)S(1)}, f32[8,2560]{1,0:T(8,128)}, u32[]{:S(2)}) copy-start(f32[8,2560]{1,0:T(8,128)} %constant.2.clone.table) | copy-start | bytes 245764
  2.9 9.9 %collective-permute-start = (f32[72,96]{1,0:T(8,128)}, f32[72,96]{1,0:T(8,128)S(1)}, u32[]{:S(2)}, u32[]{:S(2)}) collective-permute-start(f32[72,96]{1,0:T(8,128)} %tail_spectra.1), channel_id=1, source_target_pairs={{0,8},{1,9},{2,10},{3,11},{4,12},{5,13},{6,14},{7,15},{8,16},{9,17... | collective-permute-start | bytes 82952 | tf_op jit(solution)/shard_map/ppermute | solution.py:43
  12.8 1.0 %copy-start.1 = (bf16[96,2048]{1,0:T(8,128)(2,1)S(1)}, bf16[96,2048]{1,0:T(8,128)(2,1)}, u32[]{:S(2)}) copy-start(bf16[96,2048]{1,0:T(8,128)(2,1)} %get-tuple-element.14.head) | copy-start | bytes 1179652
  13.8 0.9 %copy-start.2 = (f32[192,96]{1,0:T(8,128)S(1)}, f32[192,96]{1,0:T(8,128)}, u32[]{:S(2)}) copy-start(f32[192,96]{1,0:T(8,128)} %get-tuple-element.13.total) | copy-start | bytes 221188
  15.3 5.7 %collective-permute-start.1 = (bf16[4,24,256]{2,1,0:T(8,128)(2,1)S(1)}, bf16[4,24,256]{2,1,0:T(8,128)(2,1)S(1)}, u32[]{:S(2)}, u32[]{:S(2)}) collective-permute-start(bf16[4,24,256]{2,1,0:T(8,128)(2,1)S(1)} %finish_spectra.1.own), channel_id=1, source_target_pairs={{0,128},{1,129},{2,130},{3,131},{4,132},{5,133},{6,134},{7,135},{8... | collective-permute-start | bytes 147464 | tf_op jit(solution)/shard_map/ppermute | solution.py:43
  21.0 2.0 %collective-permute-start.2 = (bf16[2,4,24,256]{3,2,1,0:T(8,128)(2,1)S(1)}, bf16[2,4,24,256]{3,2,1,0:T(8,128)(2,1)S(1)}, u32[]{:S(2)}, u32[]{:S(2)}) collective-permute-start(bf16[2,4,24,256]{3,2,1,0:T(8,128)(2,1)S(1)} %both_halves.1.y0), channel_id=1, source_target_pairs={{0,8},{1,9},{2,10},{3,11},{4,12},{5,13},{6,14},{7,15},{8,0},{9,1},... | collective-permute-start | bytes 294920 | tf_op jit(solution)/shard_map/ppermute | solution.py:43
  21.1 5.7 %collective-permute-start.3 = (bf16[2,4,24,256]{3,2,1,0:T(8,128)(2,1)S(1)}, bf16[2,4,24,256]{3,2,1,0:T(8,128)(2,1)S(1)}, u32[]{:S(2)}, u32[]{:S(2)}) collective-permute-start(bf16[2,4,24,256]{3,2,1,0:T(8,128)(2,1)S(1)} %both_halves.1.y0), channel_id=1, source_target_pairs={{0,16},{1,17},{2,18},{3,19},{4,20},{5,21},{6,22},{7,23},{8,24},{9,... | collective-permute-start | bytes 294920 | tf_op jit(solution)/shard_map/ppermute | solution.py:43
  21.2 6.7 %collective-permute-start.4 = (bf16[2,4,24,256]{3,2,1,0:T(8,128)(2,1)S(1)}, bf16[2,4,24,256]{3,2,1,0:T(8,128)(2,1)S(1)}, u32[]{:S(2)}, u32[]{:S(2)}) collective-permute-start(bf16[2,4,24,256]{3,2,1,0:T(8,128)(2,1)S(1)} %both_halves.1.y0), channel_id=1, source_target_pairs={{0,24},{1,25},{2,26},{3,27},{4,28},{5,29},{6,30},{7,31},{8,16},{9,... | collective-permute-start | bytes 294920 | tf_op jit(solution)/shard_map/ppermute | solution.py:43
  28.0 8.4 %collective-permute-start.5 = (bf16[4,2,24,256]{3,2,1,0:T(8,128)(2,1)S(1)}, bf16[4,2,24,256]{3,2,1,0:T(8,128)(2,1)S(1)}, u32[]{:S(2)}, u32[]{:S(2)}) collective-permute-start(bf16[4,2,24,256]{3,2,1,0:T(8,128)(2,1)S(1)} %get-tuple-element.16.own), channel_id=1, source_target_pairs={{0,4},{1,5},{2,6},{3,7},{8,12},{9,13},{10,14},{11,15},{16,20},{17,... | collective-permute-start | bytes 294920 | tf_op jit(solution)/shard_map/ppermute | solution.py:43
  36.4 5.8 %collective-permute-start.6 = (bf16[4,2,24,256]{3,2,1,0:T(8,128)(2,1)S(1)}, bf16[4,2,24,256]{3,2,1,0:T(8,128)(2,1)S(1)}, u32[]{:S(2)}, u32[]{:S(2)}) collective-permute-start(bf16[4,2,24,256]{3,2,1,0:T(8,128)(2,1)S(1)} %choose.1.refs_1_), channel_id=1, source_target_pairs={{0,1},{1,0},{2,3},{3,2},{4,5},{5,4},{6,7},{7,6},{8,9},{9,8},{10,11... | collective-permute-start | bytes 294920 | tf_op jit(solution)/shard_map/ppermute | solution.py:43
  37.2 5.6 %collective-permute-start.7 = (bf16[4,2,24,256]{3,2,1,0:T(8,128)(2,1)S(1)}, bf16[4,2,24,256]{3,2,1,0:T(8,128)(2,1)S(1)}, u32[]{:S(2)}, u32[]{:S(2)}) collective-permute-start(bf16[4,2,24,256]{3,2,1,0:T(8,128)(2,1)S(1)} %choose.1.refs_1_), channel_id=1, source_target_pairs={{0,2},{1,3},{2,0},{3,1},{4,6},{5,7},{6,4},{7,5},{8,10},{9,11},{10,... | collective-permute-start | bytes 294920 | tf_op jit(solution)/shard_map/ppermute | solution.py:43
  38.4 5.6 %collective-permute-start.8 = (bf16[4,2,24,256]{3,2,1,0:T(8,128)(2,1)S(1)}, bf16[4,2,24,256]{3,2,1,0:T(8,128)(2,1)S(1)}, u32[]{:S(2)}, u32[]{:S(2)}) collective-permute-start(bf16[4,2,24,256]{3,2,1,0:T(8,128)(2,1)S(1)} %choose.1.refs_1_), channel_id=1, source_target_pairs={{0,3},{1,2},{2,1},{3,0},{4,7},{5,6},{6,5},{7,4},{8,11},{9,10},{10,... | collective-permute-start | bytes 294920 | tf_op jit(solution)/shard_map/ppermute | solution.py:43
  45.2 6.6 %collective-permute-start.11 = (bf16[192,96]{1,0:T(8,128)(2,1)S(1)}, bf16[192,96]{1,0:T(8,128)(2,1)S(1)}, u32[]{:S(2)}, u32[]{:S(2)}) collective-permute-start(bf16[192,96]{1,0:T(8,128)(2,1)S(1)} %get-tuple-element.20), channel_id=1, source_target_pairs={{0,96},{1,97},{2,98},{3,99},{4,100},{5,101},{6,102},{7,103},{8,104... | collective-permute-start | bytes 110600 | tf_op jit(solution)/shard_map/ppermute | solution.py:43
  47.1 8.1 %collective-permute-start.10 = (bf16[192,96]{1,0:T(8,128)(2,1)S(1)}, bf16[192,96]{1,0:T(8,128)(2,1)S(1)}, u32[]{:S(2)}, u32[]{:S(2)}) collective-permute-start(bf16[192,96]{1,0:T(8,128)(2,1)S(1)} %get-tuple-element.19), channel_id=1, source_target_pairs={{0,64},{1,65},{2,66},{3,67},{4,68},{5,69},{6,70},{7,71},{8,72},{9,... | collective-permute-start | bytes 110600 | tf_op jit(solution)/shard_map/ppermute | solution.py:43
  49.4 5.8 %collective-permute-start.9 = (bf16[192,96]{1,0:T(8,128)(2,1)S(1)}, bf16[192,96]{1,0:T(8,128)(2,1)S(1)}, u32[]{:S(2)}, u32[]{:S(2)}) collective-permute-start(bf16[192,96]{1,0:T(8,128)(2,1)S(1)} %get-tuple-element.18), channel_id=1, source_target_pairs={{0,32},{1,33},{2,34},{3,35},{4,36},{5,37},{6,38},{7,39},{8,40},{9,... | collective-permute-start | bytes 110600 | tf_op jit(solution)/shard_map/ppermute | solution.py:43

commit v4 on v3

--- a/solution.py
+++ b/solution.py
@@ -72,48 +72,41 @@
         total[2 * ROWS * (low - first_pair) : 2 * ROWS * (high + 1 - first_pair), :] += part
 
 
-def tail_kernel(fire, table, record, message, tables, samples, sem):
+def tail_kernel(fire_hbm, table_hbm, record, message, fire, table, tables, samples, sems):
     pairs = fire.shape[0] // 2
     late = LATE // 2
     start = record.shape[1] - samples.shape[1]
-    copy = pltpu.make_async_copy(record.at[:, start:], samples, sem)
-    copy.start()
-    master = table[...]
-    for p in range(late):
-        shot = 2 * (pairs - late + p)
-        tables[p] = pair_tables(master, delay(fire, shot), delay(fire, shot + 1))
+    copies = [
+        pltpu.make_async_copy(fire_hbm, fire, sems.at[0]),
+        pltpu.make_async_copy(table_hbm, table, sems.at[1]),
+        pltpu.make_async_copy(record.at[:, start:], samples, sems.at[2]),
+    ]
+    for copy in copies:
+        copy.start()
     message[...] = jnp.zeros_like(message)
+    copies[0].wait()
     row = lax.broadcasted_iota(jnp.int32, (LATE, message.shape[1]), 0)
     delays = jnp.zeros(row.shape, jnp.int32)
     for i in range(LATE):
         delays = jnp.where(row == i, delay(fire, 2 * (pairs - late) + i), delays)
     message[ROWS * LATE :, :] = delays.astype(jnp.float32)
-    copy.wait()
+    copies[1].wait()
+    master = table[...]
+    for p in range(late):
+        shot = 2 * (pairs - late + p)
+        tables[p] = pair_tables(master, delay(fire, shot), delay(fire, shot + 1))
+    copies[2].wait()
     blocks = [(pairs - late + v, samples[:, PAIR * v : PAIR * (v + 1)]) for v in range(late)]
     add_products(message, tables, pairs - late, blocks)
 
 
-def own_kernel(fire, table, record, total, head, tables, samples, sems):
-    parts = sems.shape[0]
-    width = record.shape[1] // parts
-    copies = [
-        pltpu.make_async_copy(
-            record.at[:, width * i : width * (i + 1)], samples.at[:, width * i : width * (i + 1)], sems.at[i]
-        )
-        for i in range(parts)
-    ]
-    for copy in copies:
-        copy.start()
+def own_kernel(fire, table, record, total, tables):
+    pairs = record.shape[1] // PAIR
     master = table[...]
     for p in range(tables.shape[0]):
         tables[p] = pair_tables(master, delay(fire, 2 * p), delay(fire, 2 * p + 1))
     total[...] = jnp.zeros_like(total)
-    per = width // PAIR
-    for i, copy in enumerate(copies):
-        copy.wait()
-        blocks = [(per * i + v, samples[:, PAIR * (per * i + v) : PAIR * (per * i + v + 1)]) for v in range(per)]
-        add_products(total, tables, 0, blocks)
-    head[...] = samples[:, : head.shape[1]]
+    add_products(total, tables, 0, [(u, record[:, PAIR * u : PAIR * (u + 1)]) for u in range(pairs)])
 
 
 def finish_kernel(total, head, table, message, out, scratch, tables):
@@ -139,17 +132,19 @@
         out[k] = turned[count * k : count * (k + 1), :].astype(out.dtype)
 
 
-def pair_kernel(own, other, out):
-    yh = shot_index() >> 4
-    out[yh] = own[...]
-    out[1 - yh] = other[...]
-
-
-def collect_kernel(y0, y1, y2, y3, gathered, quarter):
+def join_kernel(place, own, other, out):
+    here = place(shot_index())
+    out[here] = own[...]
+    out[1 - here] = other[...]
+
+
+def collect_kernel(own, other, gathered, quarter):
     k = shot_index() & 3
-    for m, y in enumerate((y0, y1, y2, y3)):
-        gathered[k ^ m] = y[...]
-        quarter[k ^ m] = y[:, k]
+    here = k & 1
+    gathered[here] = own[...]
+    gathered[1 - here] = other[...]
+    quarter[here] = own[:, :, k]
+    quarter[1 - here] = other[:, :, k]
 
 
 def choose_kernel(own, cross, out):
@@ -166,32 +161,27 @@
 
 def right_kernel(gathered, right):
     half = right.shape[2] // 2
-    for k in range(QUARTERS):
-        for yh in range(2):
-            z = gathered[k, yh].astype(jnp.float32).reshape(right.shape[1] // 2, 2 * half)
-            w = jnp.concatenate([-z[:, half:], z[:, :half]], axis=1)
-            right[2 * k + yh] = jnp.concatenate([z, w], axis=0).astype(jnp.bfloat16)
+    for part in range(right.shape[0]):
+        z = gathered[part >> 2, (part >> 1) & 1, part & 1].astype(jnp.float32).reshape(right.shape[1] // 2, 2 * half)
+        w = jnp.concatenate([-z[:, half:], z[:, :half]], axis=1)
+        right[part] = jnp.concatenate([z, w], axis=0).astype(jnp.bfloat16)
 
 
 def gram_kernel(scale, right, q0, q1, q2, q3, p0, p1, p2, p3, total):
     turn = ((shot_index() >> 2) ^ lax.axis_index("rcv")) & 3
-    count, lanes = q0.shape[2:]
+    count, lanes = q0.shape[3:]
     half = lanes // 2
     span = right.shape[1] // 2
     per = half // NF
     lane = lax.broadcasted_iota(jnp.int32, (count, lanes), 1) % half // per
     for m, q in enumerate((q0, q1, q2, q3)):
         acc = jnp.zeros((NF * count, 2 * span), jnp.float32)
-        for k in range(QUARTERS):
-            for yh in range(2):
-                rows = q[k, yh].astype(jnp.float32)
-                left = jnp.concatenate([jnp.where(lane == f, rows, 0.0) for f in range(NF)], axis=0)
-                acc = acc + lax.dot_general(
-                    left.astype(jnp.bfloat16),
-                    right[2 * k + yh],
-                    (((1,), (1,)), ((), ())),
-                    preferred_element_type=jnp.float32,
-                )
+        for part in range(right.shape[0]):
+            rows = q[part >> 2, (part >> 1) & 1, part & 1].astype(jnp.float32)
+            left = jnp.concatenate([jnp.where(lane == f, rows, 0.0) for f in range(NF)], axis=0)
+            acc = acc + lax.dot_general(
+                left.astype(jnp.bfloat16), right[part], (((1,), (1,)), ((), ())), preferred_element_type=jnp.float32
+            )
         total[turn ^ m, : NF * count, :] = acc[:, :span] * scale
         total[turn ^ m, NF * count :, :] = acc[:, span:] * scale
     for n, out in enumerate((p0, p1, p2, p3)):
@@ -227,8 +217,14 @@
         tail_kernel,
         "tail_spectra",
         shape((late_rows + LATE, receivers), f32),
-        [smem] + vmem(1) + [hbm],
-        [pltpu.VMEM((late, 2 * ROWS, SPAN), bf16), pltpu.VMEM((receivers, WIN), bf16), pltpu.SemaphoreType.DMA],
+        [hbm] * 3,
+        [
+            pltpu.SMEM((shots,), jnp.int32),
+            pltpu.VMEM(table.shape, f32),
+            pltpu.VMEM((late, 2 * ROWS, SPAN), bf16),
+            pltpu.VMEM((receivers, WIN), bf16),
+            pltpu.SemaphoreType.DMA((3,)),
+        ],
         limit=63,
     )(shot_fire_samples, table, record)
 
@@ -237,36 +233,43 @@
         return shot >> 4, (shot >> 2) & 3, shot & 3, xh, v
 
     received = send(message, following)
-    total, head = local(
+    total = local(
         own_kernel,
         "own_spectra",
-        (shape((lanes - late_rows, receivers), f32), shape((receivers, WIN), bf16)),
-        [smem] + vmem(1) + [hbm],
-        [
-            pltpu.VMEM((pairs - late, 2 * ROWS, SPAN), bf16),
-            pltpu.VMEM((receivers, samples), bf16),
-            pltpu.SemaphoreType.DMA((4,)),
+        shape((lanes - late_rows, receivers), f32),
+        [smem] + vmem(2),
+        [pltpu.VMEM((pairs - late, 2 * ROWS, SPAN), bf16)],
+    )(shot_fire_samples, table, record)
+    y = pl.pallas_call(
+        finish_kernel,
+        grid=(1,),
+        out_shape=shape((QUARTERS, count, lanes), bf16),
+        in_specs=[
+            pl.BlockSpec(total.shape, lambda i: (0, 0)),
+            pl.BlockSpec((receivers, WIN), lambda i: (0, 0)),
+            pl.BlockSpec(table.shape, lambda i: (0, 0)),
+            pl.BlockSpec(received.shape, lambda i: (0, 0)),
         ],
-        limit=63,
-    )(shot_fire_samples, table, record)
-    y = local(
-        finish_kernel,
-        "finish_spectra",
-        shape((QUARTERS, count, lanes), bf16),
-        vmem(4),
-        [pltpu.VMEM((lanes, receivers), f32), pltpu.VMEM((late, 2 * ROWS, SPAN), bf16)],
-    )(total, head, table, received)
-
-    y = local(pair_kernel, "both_halves", shape((2,) + y.shape, bf16), vmem(2))(
-        y, send(y, lambda yh, u, k, xh, v: (1 - yh, u, k, xh, v))
-    )
-    ys = [send(y, lambda yh, u, k, xh, v, m=m: (yh, u, k ^ m, xh, v)) for m in (1, 2, 3)]
+        out_specs=pl.BlockSpec((QUARTERS, count, lanes), lambda i: (0, 0, 0)),
+        scratch_shapes=[pltpu.VMEM((lanes, receivers), f32), pltpu.VMEM((late, 2 * ROWS, SPAN), bf16)],
+        compiler_params=pltpu.CompilerParams(vmem_limit_bytes=4 << 20),
+        name="finish_spectra",
+    )(total, record, table, received)
+
+    def join(own, other, place, name):
+        return local(lambda *refs: join_kernel(place, *refs), name, shape((2,) + own.shape, bf16), vmem(2))(own, other)
+
+    other = send(y, lambda yh, u, k, xh, v: (yh, u, k ^ 2, xh, v))
+    y = join(y, other, lambda shot: (shot >> 1) & 1, "join_z0")
+    other = send(y, lambda yh, u, k, xh, v: (1 - yh, u, k, xh, v))
+    y = join(y, other, lambda shot: shot >> 4, "join_yh")
+    other = send(y, lambda yh, u, k, xh, v: (yh, u, k ^ 1, xh, v))
     gathered, quarter = local(
         collect_kernel,
         "collect",
-        (shape((QUARTERS,) + y.shape, bf16), shape((QUARTERS, 2, count, lanes), bf16)),
-        vmem(4),
-    )(y, *ys)
+        (shape((2,) + y.shape, bf16), shape((2,) + y.shape[:2] + (count, lanes), bf16)),
+        vmem(2),
+    )(y, other)
     cross = send(quarter, lambda yh, u, k, xh, v: (yh, u, k, 1 - xh, v) if xh == yh else None)
     q = local(choose_kernel, "choose", shape(quarter.shape, bf16), vmem(2))(quarter, cross)
     qs = [q] + [send(q, lambda yh, u, k, xh, v, m=m: (yh, u, k, xh, v ^ m)) for m in (1, 2, 3)]
@@ -283,8 +286,8 @@
         limit=8,
     )(right, *qs)
     sums = first
-    for n, share in enumerate(others, 1):
-        sums = sums + send(share, lambda yh, u, k, xh, v, n=n: (yh, u ^ n, k, xh, v)).astype(f32)
+    for n in (1, 3, 2):
+        sums = sums + send(others[n - 1], lambda yh, u, k, xh, v, n=n: (yh, u ^ n, k, xh, v)).astype(f32)
     return sums.reshape(2, NF, count, receivers).transpose(0, 1, 3, 2)
 
 

time: 56.2 us -> 51.8 us (0.922)
  Pallas kernels: 9.03 us -> 5.62 us
  starting transfers between devices: 14.2 us -> 12.4 us
  waiting for transfers between devices: 30 us -> 31.4 us
    pallas_call x4 -> x5, Pallas kernels: 4.75 us -> 2.23 us  [the longest x1 1.54 us: per_device(): local(own_kernel, 'own_spectra', shape((lanes - late_rows, receivers), f3...]
    ppermute x12 -> x11, starting transfers between devices: 14.2 us -> 12.4 us  [send(): return lax.ppermute(block, ('shot', 'rcv'), route)]
    ppermute x12 -> x11, waiting for transfers between devices: 30 us -> 31.4 us  [send(): return lax.ppermute(block, ('shot', 'rcv'), route)]
    pallas_call x1, Pallas kernels: 2.94 us -> 2.06 us  [per_device(): local(tail_kernel, 'tail_spectra', shape((late_rows + LATE, receivers), f...]
    unnamed x6 -> x8, local copies, waits for them, and re-layouts: 1.89 us -> 1.41 us
  transfers between devices with their start and end apart: 12 -> 11, of which waited for: 9 -> 10; matrix products, arithmetic and copies ran while one was open for 0% -> 0% of each run, Pallas kernels for 7% -> 3%
where the time goes in v4:
time: 51.8 us; the launch traced here: 51.6 us
  waiting for transfers between devices  31.4 us (61%)
  starting transfers between devices  12.4 us (24%)
  Pallas kernels  5.62 us (11%)
  local copies, waits for them, and re-layouts  1.41 us (3%)
  other arithmetic  0.66 us (1%)
    ppermute x11, waiting for transfers between devices, send(): return lax.ppermute(block, ('shot', 'rcv'), route)  31.4 us
    ppermute x11, starting transfers between devices, send(): return lax.ppermute(block, ('shot', 'rcv'), route)  12.4 us
    pallas_call x1, Pallas kernels, per_device(): local(tail_kernel, 'tail_spectra', shape((late_rows + LATE, receivers), f...  2.06 us
    pallas_call x1, Pallas kernels, per_device(): local(own_kernel, 'own_spectra', shape((lanes - late_rows, receivers), f3...  1.54 us
    unnamed x8, local copies, waits for them, and re-layouts  1.41 us
    pallas_call x1, Pallas kernels, per_device(): local(lambda *refs: gram_kernel(1.0 / total_shots, *refs), 'gram', (shape...  1.26 us
  transfers between devices with their start and end apart: 11, of which 10 were waited for; matrix products, arithmetic and copies ran while one was open for 0% of the time, Pallas kernels for 3%

profile of v4, /device:TPU:4, one launch (start us, length us, event | category | flops | bytes accessed | tf_op | source)
XLA Modules:
  0.0 51.6 jit_solution(10942418238833458277)
XLA Ops:
  0.0 0.0 copy-start.2
  0.0 0.0 copy-start.3
  0.0 2.1 %tail_spectra.1 = f32[72,96]{1,0:T(8,128)} custom-call(s32[32]{0:T(128)} %fire_hbm.1, f32[8,2560]{1,0:T(8,128)} %constant.2.clone.table.table_hbm, bf16[96,8192]{1,0:T(8,128)(2,1)} %head.1), custom_call_target="tpu_custom_call" | custom-call | tf_op jit(solution)/shard_map/tail_spectra/pallas_call | solution.py:216
  2.1 0.1 collective-permute-start
  2.2 0.0 copy-done.2
  2.2 0.0 copy-done.3
  2.2 0.0 copy-start
  2.2 1.4 %copy-done = bf16[96,8192]{1,0:T(8,128)(2,1)S(1)} copy-done((bf16[96,8192]{1,0:T(8,128)(2,1)S(1)}, bf16[96,8192]{1,0:T(8,128)(2,1)}, u32[]{:S(2)}) %copy-start) | copy-done | bytes 1572888
  3.6 0.0 copy-start.1
  3.6 1.5 %own_spectra.1.total = f32[192,96]{1,0:T(8,128)S(1)} custom-call(s32[32]{0:T(128)S(1)} %copy-done.3, f32[8,2560]{1,0:T(8,128)S(1)} %copy-done.2, bf16[96,8192]{1,0:T(8,128)(2,1)S(1)} %copy-done), custom_call_target="tpu_custom_call" | custom-call | tf_op jit(solution)/shard_map/own_spectra/pallas_call | solution.py:236
  5.1 6.8 %collective-permute-done.message = f32[72,96]{1,0:T(8,128)S(1)} collective-permute-done((f32[72,96]{1,0:T(8,128)}, f32[72,96]{1,0:T(8,128)S(1)}, u32[]{:S(2)}, u32[]{:S(2)}) %collective-permute-start) | collective-permute-done | bytes 27680 | tf_op jit(solution)/shard_map/ppermute | solution.py:43
  11.9 0.0 copy-done.1
  11.9 0.6 %finish_spectra.1.refs_0_ = bf16[4,24,256]{2,1,0:T(8,128)(2,1)S(1)} custom-call(f32[192,96]{1,0:T(8,128)S(1)} %own_spectra.1.total, bf16[96,8192]{1,0:T(8,128)(2,1)S(1)} %copy-done.1, f32[8,2560]{1,0:T(8,128)S(1)} %copy-done.2, f32[72,96]{1,0:T(8,128)S(1)} %collective-permute-done.message), custom_call_target="tpu_custom_call" | custom-call | tf_op jit(solution)/shard_map/finish_spectra/pallas_call | solution.py:243
  12.5 0.1 collective-permute-start.1
  12.6 4.1 %collective-permute-done.1.refs_1_ = bf16[4,24,256]{2,1,0:T(8,128)(2,1)S(1)} collective-permute-done((bf16[4,24,256]{2,1,0:T(8,128)(2,1)S(1)}, bf16[4,24,256]{2,1,0:T(8,128)(2,1)S(1)}, u32[]{:S(2)}, u32[]{:S(2)}) %collective-permute-start.1) | collective-permute-done | bytes 49184 | tf_op jit(solution)/shard_map/ppermute | solution.py:43
  16.7 0.7 %collective-permute-start.2 = (bf16[2,4,24,256]{3,2,1,0:T(8,128)(2,1)S(1)}, bf16[2,4,24,256]{3,2,1,0:T(8,128)(2,1)S(1)}, u32[]{:S(2)}, u32[]{:S(2)}) collective-permute-start(bf16[2,4,24,256]{3,2,1,0:T(8,128)(2,1)S(1)} %join_z0.1.refs_0_), channel_id=1, source_target_pairs={{0,128},{1,129},{2,130},{3,131},{4,132},{5,133},{6,134},{7,135},{8... | collective-permute-start | bytes 294920 | tf_op jit(solution)/shard_map/ppermute | solution.py:43
  17.4 5.5 %collective-permute-done.2.refs_1_ = bf16[2,4,24,256]{3,2,1,0:T(8,128)(2,1)S(1)} collective-permute-done((bf16[2,4,24,256]{3,2,1,0:T(8,128)(2,1)S(1)}, bf16[2,4,24,256]{3,2,1,0:T(8,128)(2,1)S(1)}, u32[]{:S(2)}, u32[]{:S(2)}) %collective-permute-start.2) | collective-permute-done | bytes 98336 | tf_op jit(solution)/shard_map/ppermute | solution.py:43
  23.0 0.1 collective-permute-start.3
  23.1 1.4 %collective-permute-done.3.other = bf16[2,2,4,24,256]{4,3,2,1,0:T(8,128)(2,1)S(1)} collective-permute-done((bf16[2,2,4,24,256]{4,3,2,1,0:T(8,128)(2,1)S(1)}, bf16[2,2,4,24,256]{4,3,2,1,0:T(8,128)(2,1)S(1)}, u32[]{:S(2)}, u32[]{:S(2)}) %collective-permute-start.3) | collective-permute-done | bytes 196640 | tf_op jit(solution)/shard_map/ppermute | solution.py:43
  24.5 1.3 %collective-permute-start.4 = (bf16[2,2,2,24,256]{4,3,2,1,0:T(8,128)(2,1)S(1)}, bf16[2,2,2,24,256]{4,3,2,1,0:T(8,128)(2,1)S(1)}, u32[]{:S(2)}, u32[]{:S(2)}) collective-permute-start(bf16[2,2,2,24,256]{4,3,2,1,0:T(8,128)(2,1)S(1)} %get-tuple-element.12.own), channel_id=1, source_target_pairs={{0,4},{1,5},{2,6},{3,7},{8,12},{9,13},{10,14},{11,15},{16,20},{17,... | collective-permute-start | bytes 294920 | tf_op jit(solution)/shard_map/ppermute | solution.py:43
  25.8 6.9 %collective-permute-done.4.cross = bf16[2,2,2,24,256]{4,3,2,1,0:T(8,128)(2,1)S(1)} collective-permute-done((bf16[2,2,2,24,256]{4,3,2,1,0:T(8,128)(2,1)S(1)}, bf16[2,2,2,24,256]{4,3,2,1,0:T(8,128)(2,1)S(1)}, u32[]{:S(2)}, u32[]{:S(2)}) %collective-permute-start.4) | collective-permute-done | bytes 98336 | tf_op jit(solution)/shard_map/ppermute | solution.py:43
  32.8 0.8 %collective-permute-start.5 = (bf16[2,2,2,24,256]{4,3,2,1,0:T(8,128)(2,1)S(1)}, bf16[2,2,2,24,256]{4,3,2,1,0:T(8,128)(2,1)S(1)}, u32[]{:S(2)}, u32[]{:S(2)}) collective-permute-start(bf16[2,2,2,24,256]{4,3,2,1,0:T(8,128)(2,1)S(1)} %choose.1.refs_1_), channel_id=1, source_target_pairs={{0,1},{1,0},{2,3},{3,2},{4,5},{5,4},{6,7},{7,6},{8,9},{9,8},{10,11... | collective-permute-start | bytes 294920 | tf_op jit(solution)/shard_map/ppermute | solution.py:43
  33.6 1.2 %collective-permute-start.6 = (bf16[2,2,2,24,256]{4,3,2,1,0:T(8,128)(2,1)S(1)}, bf16[2,2,2,24,256]{4,3,2,1,0:T(8,128)(2,1)S(1)}, u32[]{:S(2)}, u32[]{:S(2)}) collective-permute-start(bf16[2,2,2,24,256]{4,3,2,1,0:T(8,128)(2,1)S(1)} %choose.1.refs_1_), channel_id=1, source_target_pairs={{0,2},{1,3},{2,0},{3,1},{4,6},{5,7},{6,4},{7,5},{8,10},{9,11},{10,... | collective-permute-start | bytes 294920 | tf_op jit(solution)/shard_map/ppermute | solution.py:43
  34.8 1.6 %collective-permute-start.7 = (bf16[2,2,2,24,256]{4,3,2,1,0:T(8,128)(2,1)S(1)}, bf16[2,2,2,24,256]{4,3,2,1,0:T(8,128)(2,1)S(1)}, u32[]{:S(2)}, u32[]{:S(2)}) collective-permute-start(bf16[2,2,2,24,256]{4,3,2,1,0:T(8,128)(2,1)S(1)} %choose.1.refs_1_), channel_id=1, source_target_pairs={{0,3},{1,2},{2,1},{3,0},{4,7},{5,6},{6,5},{7,4},{8,11},{9,10},{10,... | collective-permute-start | bytes 294920 | tf_op jit(solution)/shard_map/ppermute | solution.py:43
  36.4 0.1 right_side.1.refs_0_
  36.4 2.1 %collective-permute-done.5.refs_2_ = bf16[2,2,2,24,256]{4,3,2,1,0:T(8,128)(2,1)S(1)} collective-permute-done((bf16[2,2,2,24,256]{4,3,2,1,0:T(8,128)(2,1)S(1)}, bf16[2,2,2,24,256]{4,3,2,1,0:T(8,128)(2,1)S(1)}, u32[]{:S(2)}, u32[]{:S(2)}) %collective-permute-start.5) | collective-permute-done | bytes 98336 | tf_op jit(solution)/shard_map/ppermute | solution.py:43
  38.6 0.4 collective-permute-done.6.refs_3_
  39.0 1.3 %collective-permute-done.7.refs_4_ = bf16[2,2,2,24,256]{4,3,2,1,0:T(8,128)(2,1)S(1)} collective-permute-done((bf16[2,2,2,24,256]{4,3,2,1,0:T(8,128)(2,1)S(1)}, bf16[2,2,2,24,256]{4,3,2,1,0:T(8,128)(2,1)S(1)}, u32[]{:S(2)}, u32[]{:S(2)}) %collective-permute-start.7) | collective-permute-done | bytes 98336 | tf_op jit(solution)/shard_map/ppermute | solution.py:43
  40.3 1.3 %gram.1 = (f32[192,96]{1,0:T(8,128)S(1)}, bf16[192,96]{1,0:T(8,128)(2,1)S(1)}, bf16[192,96]{1,0:T(8,128)(2,1)S(1)}, bf16[192,96]{1,0:T(8,128)(2,1)S(1)}) custom-call(bf16[8,192,256]{2,1,0:T(8,128)(2,1)S(1)} %right_side.1.refs_0_, bf16[2,2,2,24,256]{4,3,2,1,0:T(8,128)(2,1)S(1)} %choose.1.refs_1_, ...), custom_call_target="tpu_custom_call" | custom-call | tf_op jit(solution)/shard_map/gram/pallas_call | solution.py:280
  41.5 3.2 %collective-permute-start.10 = (bf16[192,96]{1,0:T(8,128)(2,1)S(1)}, bf16[192,96]{1,0:T(8,128)(2,1)S(1)}, u32[]{:S(2)}, u32[]{:S(2)}) collective-permute-start(bf16[192,96]{1,0:T(8,128)(2,1)S(1)} %get-tuple-element.16), channel_id=1, source_target_pairs={{0,64},{1,65},{2,66},{3,67},{4,68},{5,69},{6,70},{7,71},{8,72},{9,... | collective-permute-start | bytes 110600 | tf_op jit(solution)/shard_map/ppermute | solution.py:43
  44.7 0.0 collective-permute-start.9
  44.7 3.4 %collective-permute-start.8 = (bf16[192,96]{1,0:T(8,128)(2,1)S(1)}, bf16[192,96]{1,0:T(8,128)(2,1)S(1)}, u32[]{:S(2)}, u32[]{:S(2)}) collective-permute-start(bf16[192,96]{1,0:T(8,128)(2,1)S(1)} %get-tuple-element.14), channel_id=1, source_target_pairs={{0,32},{1,33},{2,34},{3,35},{4,36},{5,37},{6,38},{7,39},{8,40},{9,... | collective-permute-start | bytes 110600 | tf_op jit(solution)/shard_map/ppermute | solution.py:43
  48.1 1.6 %collective-permute-done.10 = bf16[192,96]{1,0:T(8,128)(2,1)S(1)} collective-permute-done((bf16[192,96]{1,0:T(8,128)(2,1)S(1)}, bf16[192,96]{1,0:T(8,128)(2,1)S(1)}, u32[]{:S(2)}, u32[]{:S(2)}) %collective-permute-start.10) | collective-permute-done | bytes 36896 | tf_op jit(solution)/shard_map/ppermute | solution.py:43
  49.7 1.2 %collective-permute-done.9 = bf16[192,96]{1,0:T(8,128)(2,1)S(1)} collective-permute-done((bf16[192,96]{1,0:T(8,128)(2,1)S(1)}, bf16[192,96]{1,0:T(8,128)(2,1)S(1)}, u32[]{:S(2)}, u32[]{:S(2)}) %collective-permute-start.9) | collective-permute-done | bytes 36896 | tf_op jit(solution)/shard_map/ppermute | solution.py:43
  50.9 0.0 collective-permute-done.8
  50.9 0.7 %convert_add_fusion = f32[192,96]{1,0:T(8,128)} fusion(bf16[192,96]{1,0:T(8,128)(2,1)S(1)} %collective-permute-done.10, bf16[192,96]{1,0:T(8,128)(2,1)S(1)} %collective-permute-done.9, f32[192,96]{1,0:T(8,128)S(1)} %get-tuple-element.13, bf16[192,96]{1,0:T(8,128)(2,1)S(1)} %collective-permute-done.8), kind=kLoop, calls=%fused_computation | loop fusion | flops 110592 | bytes 258048 | tf_op jit(solution)/shard_map/add | solution.py:290
  (4 shorter events, 0.1 us)
Async XLA Ops:
  0.0 2.2 %copy-start.2 = (f32[8,2560]{1,0:T(8,128)S(1)}, f32[8,2560]{1,0:T(8,128)}, u32[]{:S(2)}) copy-start(f32[8,2560]{1,0:T(8,128)} %constant.2.clone.table.table_hbm) | copy-start | bytes 245764
  0.0 2.2 %copy-start.3 = (s32[32]{0:T(128)S(1)}, s32[32]{0:T(128)}, u32[]{:S(2)}) copy-start(s32[32]{0:T(128)} %fire_hbm.1) | copy-start | bytes 388
  2.1 9.9 %collective-permute-start = (f32[72,96]{1,0:T(8,128)}, f32[72,96]{1,0:T(8,128)S(1)}, u32[]{:S(2)}, u32[]{:S(2)}) collective-permute-start(f32[72,96]{1,0:T(8,128)} %tail_spectra.1), channel_id=1, source_target_pairs={{0,8},{1,9},{2,10},{3,11},{4,12},{5,13},{6,14},{7,15},{8,16},{9,17... | collective-permute-start | bytes 82952 | tf_op jit(solution)/shard_map/ppermute | solution.py:43
  2.2 1.4 %copy-start = (bf16[96,8192]{1,0:T(8,128)(2,1)S(1)}, bf16[96,8192]{1,0:T(8,128)(2,1)}, u32[]{:S(2)}) copy-start(bf16[96,8192]{1,0:T(8,128)(2,1)} %head.1) | copy-start | bytes 4718596
  3.6 8.3 %copy-start.1 = (bf16[96,8192]{1,0:T(8,128)(2,1)S(1)}, bf16[96,8192]{1,0:T(8,128)(2,1)}, u32[]{:S(2)}) copy-start(bf16[96,8192]{1,0:T(8,128)(2,1)} %head.1) | copy-start | bytes 4718596
  12.5 4.2 %collective-permute-start.1 = (bf16[4,24,256]{2,1,0:T(8,128)(2,1)S(1)}, bf16[4,24,256]{2,1,0:T(8,128)(2,1)S(1)}, u32[]{:S(2)}, u32[]{:S(2)}) collective-permute-start(bf16[4,24,256]{2,1,0:T(8,128)(2,1)S(1)} %finish_spectra.1.refs_0_), channel_id=1, source_target_pairs={{0,16},{1,17},{2,18},{3,19},{4,20},{5,21},{6,22},{7,23},{8,24},{9,... | collective-permute-start | bytes 147464 | tf_op jit(solution)/shard_map/ppermute | solution.py:43
  16.7 6.2 %collective-permute-start.2 = (bf16[2,4,24,256]{3,2,1,0:T(8,128)(2,1)S(1)}, bf16[2,4,24,256]{3,2,1,0:T(8,128)(2,1)S(1)}, u32[]{:S(2)}, u32[]{:S(2)}) collective-permute-start(bf16[2,4,24,256]{3,2,1,0:T(8,128)(2,1)S(1)} %join_z0.1.refs_0_), channel_id=1, source_target_pairs={{0,128},{1,129},{2,130},{3,131},{4,132},{5,133},{6,134},{7,135},{8... | collective-permute-start | bytes 294920 | tf_op jit(solution)/shard_map/ppermute | solution.py:43
  23.0 1.5 %collective-permute-start.3 = (bf16[2,2,4,24,256]{4,3,2,1,0:T(8,128)(2,1)S(1)}, bf16[2,2,4,24,256]{4,3,2,1,0:T(8,128)(2,1)S(1)}, u32[]{:S(2)}, u32[]{:S(2)}) collective-permute-start(bf16[2,2,4,24,256]{4,3,2,1,0:T(8,128)(2,1)S(1)} %join_yh.1.own), channel_id=1, source_target_pairs={{0,8},{1,9},{2,10},{3,11},{4,12},{5,13},{6,14},{7,15},{8,0},{9,1},... | collective-permute-start | bytes 589832 | tf_op jit(solution)/shard_map/ppermute | solution.py:43
  24.5 8.2 %collective-permute-start.4 = (bf16[2,2,2,24,256]{4,3,2,1,0:T(8,128)(2,1)S(1)}, bf16[2,2,2,24,256]{4,3,2,1,0:T(8,128)(2,1)S(1)}, u32[]{:S(2)}, u32[]{:S(2)}) collective-permute-start(bf16[2,2,2,24,256]{4,3,2,1,0:T(8,128)(2,1)S(1)} %get-tuple-element.12.own), channel_id=1, source_target_pairs={{0,4},{1,5},{2,6},{3,7},{8,12},{9,13},{10,14},{11,15},{16,20},{17,... | collective-permute-start | bytes 294920 | tf_op jit(solution)/shard_map/ppermute | solution.py:43
  32.8 5.8 %collective-permute-start.5 = (bf16[2,2,2,24,256]{4,3,2,1,0:T(8,128)(2,1)S(1)}, bf16[2,2,2,24,256]{4,3,2,1,0:T(8,128)(2,1)S(1)}, u32[]{:S(2)}, u32[]{:S(2)}) collective-permute-start(bf16[2,2,2,24,256]{4,3,2,1,0:T(8,128)(2,1)S(1)} %choose.1.refs_1_), channel_id=1, source_target_pairs={{0,1},{1,0},{2,3},{3,2},{4,5},{5,4},{6,7},{7,6},{8,9},{9,8},{10,11... | collective-permute-start | bytes 294920 | tf_op jit(solution)/shard_map/ppermute | solution.py:43
  33.6 5.4 %collective-permute-start.6 = (bf16[2,2,2,24,256]{4,3,2,1,0:T(8,128)(2,1)S(1)}, bf16[2,2,2,24,256]{4,3,2,1,0:T(8,128)(2,1)S(1)}, u32[]{:S(2)}, u32[]{:S(2)}) collective-permute-start(bf16[2,2,2,24,256]{4,3,2,1,0:T(8,128)(2,1)S(1)} %choose.1.refs_1_), channel_id=1, source_target_pairs={{0,2},{1,3},{2,0},{3,1},{4,6},{5,7},{6,4},{7,5},{8,10},{9,11},{10,... | collective-permute-start | bytes 294920 | tf_op jit(solution)/shard_map/ppermute | solution.py:43
  34.8 5.5 %collective-permute-start.7 = (bf16[2,2,2,24,256]{4,3,2,1,0:T(8,128)(2,1)S(1)}, bf16[2,2,2,24,256]{4,3,2,1,0:T(8,128)(2,1)S(1)}, u32[]{:S(2)}, u32[]{:S(2)}) collective-permute-start(bf16[2,2,2,24,256]{4,3,2,1,0:T(8,128)(2,1)S(1)} %choose.1.refs_1_), channel_id=1, source_target_pairs={{0,3},{1,2},{2,1},{3,0},{4,7},{5,6},{6,5},{7,4},{8,11},{9,10},{10,... | collective-permute-start | bytes 294920 | tf_op jit(solution)/shard_map/ppermute | solution.py:43
  41.5 8.2 %collective-permute-start.10 = (bf16[192,96]{1,0:T(8,128)(2,1)S(1)}, bf16[192,96]{1,0:T(8,128)(2,1)S(1)}, u32[]{:S(2)}, u32[]{:S(2)}) collective-permute-start(bf16[192,96]{1,0:T(8,128)(2,1)S(1)} %get-tuple-element.16), channel_id=1, source_target_pairs={{0,64},{1,65},{2,66},{3,67},{4,68},{5,69},{6,70},{7,71},{8,72},{9,... | collective-permute-start | bytes 110600 | tf_op jit(solution)/shard_map/ppermute | solution.py:43
  44.7 6.2 %collective-permute-start.9 = (bf16[192,96]{1,0:T(8,128)(2,1)S(1)}, bf16[192,96]{1,0:T(8,128)(2,1)S(1)}, u32[]{:S(2)}, u32[]{:S(2)}) collective-permute-start(bf16[192,96]{1,0:T(8,128)(2,1)S(1)} %get-tuple-element.15), channel_id=1, source_target_pairs={{0,96},{1,97},{2,98},{3,99},{4,100},{5,101},{6,102},{7,103},{8,104... | collective-permute-start | bytes 110600 | tf_op jit(solution)/shard_map/ppermute | solution.py:43
  44.7 6.2 %collective-permute-start.8 = (bf16[192,96]{1,0:T(8,128)(2,1)S(1)}, bf16[192,96]{1,0:T(8,128)(2,1)S(1)}, u32[]{:S(2)}, u32[]{:S(2)}) collective-permute-start(bf16[192,96]{1,0:T(8,128)(2,1)S(1)} %get-tuple-element.14), channel_id=1, source_target_pairs={{0,32},{1,33},{2,34},{3,35},{4,36},{5,37},{6,38},{7,39},{8,40},{9,... | collective-permute-start | bytes 110600 | tf_op jit(solution)/shard_map/ppermute | solution.py:43

commit v5 on v4

--- a/solution.py
+++ b/solution.py
@@ -41,6 +41,9 @@
                 yh, u, k, xh, v = target
                 route.append((shot * RCV_DEVICES + rcv, (yh << 4 | u << 2 | k) * RCV_DEVICES + (xh << 2 | v)))
     return lax.ppermute(block, ("shot", "rcv"), route)
+
+
+shape = jax.ShapeDtypeStruct
 
 
 def shot_index():
@@ -125,26 +128,47 @@
     add_products(scratch.at[own_rows:, :], tables, 0, blocks)
     scratch[own_rows:, :] = message[: ROWS * LATE, :] + follows * scratch[own_rows:, :]
     scratch[:own_rows, :] = total[...]
-    ordered = jnp.concatenate([scratch[pl.ds(c, lanes // ROWS, stride=ROWS), :] for c in range(ROWS)], axis=0)
+    turn_over(scratch, out)
+
+
+def turn_over(scratch, out):
+    shots = scratch.shape[0] // ROWS
+    ordered = jnp.concatenate([scratch[pl.ds(c, shots, stride=ROWS), :] for c in range(ROWS)], axis=0)
     turned = ordered.T
     count = out.shape[1]
     for k in range(QUARTERS):
         out[k] = turned[count * k : count * (k + 1), :].astype(out.dtype)
 
 
-def join_kernel(place, own, other, out):
-    here = place(shot_index())
-    out[here] = own[...]
-    out[1 - here] = other[...]
-
-
-def collect_kernel(own, other, gathered, quarter):
+def wrap_kernel(message, out, scratch):
+    late_rows = ROWS * LATE
+    own_rows = scratch.shape[0] - late_rows
+    scratch[:own_rows, :] = jnp.zeros((own_rows, scratch.shape[1]), jnp.float32)
+    scratch[own_rows:, :] = message[:late_rows, :]
+    turn_over(scratch, out)
+
+
+def yh_kernel(own, other, extra1, extra0, out):
+    yh = shot_index() >> 4
+    out[yh] = own[...]
+    out[1 - yh] = other[...]
+    extra = extra1[...].astype(jnp.float32) + extra0[...].astype(jnp.float32)
+    out[0] = (out[0].astype(jnp.float32) + extra).astype(out.dtype)
+
+
+def z0_kernel(own, other, out, mine, theirs):
     k = shot_index() & 3
-    here = k & 1
-    gathered[here] = own[...]
-    gathered[1 - here] = other[...]
-    quarter[here] = own[:, :, k]
-    quarter[1 - here] = other[:, :, k]
+    z0 = k >> 1
+    for here, block in ((z0, own), (1 - z0, other)):
+        out[here] = block[...]
+        mine[here] = block[:, k]
+        theirs[here] = block[:, k ^ 1]
+
+
+def core_kernel(own, other, out):
+    c = shot_index() & 1
+    out[c] = own[...]
+    out[1 - c] = other[...]
 
 
 def choose_kernel(own, cross, out):
@@ -159,31 +183,42 @@
         out[...] = cross[...]
 
 
-def right_kernel(gathered, right):
+def right_kernel(own, other, right):
+    c = shot_index() & 1
     half = right.shape[2] // 2
-    for part in range(right.shape[0]):
-        z = gathered[part >> 2, (part >> 1) & 1, part & 1].astype(jnp.float32).reshape(right.shape[1] // 2, 2 * half)
-        w = jnp.concatenate([-z[:, half:], z[:, :half]], axis=1)
-        right[part] = jnp.concatenate([z, w], axis=0).astype(jnp.bfloat16)
-
-
-def gram_kernel(scale, right, q0, q1, q2, q3, p0, p1, p2, p3, total):
-    turn = ((shot_index() >> 2) ^ lax.axis_index("rcv")) & 3
-    count, lanes = q0.shape[3:]
+    parts = right.shape[0] // 2
+    for here, block in ((c, own), (1 - c, other)):
+        for part in range(parts):
+            z = block[part >> 1, part & 1].astype(jnp.float32).reshape(right.shape[1] // 2, 2 * half)
+            w = jnp.concatenate([-z[:, half:], z[:, :half]], axis=1)
+            right[parts * here + part] = jnp.concatenate([z, w], axis=0).astype(jnp.bfloat16)
+
+
+def products(scale, right, q):
+    count, lanes = q.shape[3:]
     half = lanes // 2
     span = right.shape[1] // 2
-    per = half // NF
-    lane = lax.broadcasted_iota(jnp.int32, (count, lanes), 1) % half // per
-    for m, q in enumerate((q0, q1, q2, q3)):
-        acc = jnp.zeros((NF * count, 2 * span), jnp.float32)
-        for part in range(right.shape[0]):
-            rows = q[part >> 2, (part >> 1) & 1, part & 1].astype(jnp.float32)
-            left = jnp.concatenate([jnp.where(lane == f, rows, 0.0) for f in range(NF)], axis=0)
-            acc = acc + lax.dot_general(
-                left.astype(jnp.bfloat16), right[part], (((1,), (1,)), ((), ())), preferred_element_type=jnp.float32
-            )
-        total[turn ^ m, : NF * count, :] = acc[:, :span] * scale
-        total[turn ^ m, NF * count :, :] = acc[:, span:] * scale
+    lane = lax.broadcasted_iota(jnp.int32, (count, lanes), 1) % half // (half // NF)
+    acc = jnp.zeros((NF * count, 2 * span), jnp.float32)
+    for part in range(right.shape[0]):
+        rows = q[part >> 2, (part >> 1) & 1, part & 1].astype(jnp.float32)
+        left = jnp.concatenate([jnp.where(lane == f, rows, 0.0) for f in range(NF)], axis=0)
+        acc = acc + lax.dot_general(
+            left.astype(jnp.bfloat16), right[part], (((1,), (1,)), ((), ())), preferred_element_type=jnp.float32
+        )
+    return jnp.concatenate([acc[:, :span] * scale, acc[:, span:] * scale], axis=0)
+
+
+def gram_kernel(scale, right, q, before, out):
+    out[...] = products(scale, right, q)
+
+
+def last_kernel(scale, right, q, g0, g3, g1, p0, p1, p2, p3, total):
+    turn = ((shot_index() >> 2) ^ lax.axis_index("rcv")) & 3
+    total[turn] = g0[...]
+    total[turn ^ 3] = g3[...]
+    total[turn ^ 1] = g1[...]
+    total[turn ^ 2] = products(scale, right, q)
     for n, out in enumerate((p0, p1, p2, p3)):
         out[...] = total[n].astype(out.dtype)
 
@@ -209,7 +244,6 @@
     late_rows = ROWS * LATE
     count = receivers // QUARTERS
     bf16, f32 = jnp.bfloat16, jnp.float32
-    shape = jax.ShapeDtypeStruct
     table = jnp.asarray(dft_master())
     smem, hbm = pl.BlockSpec(memory_space=pltpu.SMEM), pl.BlockSpec(memory_space=pltpu.HBM)
 
@@ -229,10 +263,21 @@
     )(shot_fire_samples, table, record)
 
     def following(yh, u, k, xh, v):
-        shot = ((yh << 4 | u << 2 | k) + 1) % SHOT_DEVICES
-        return shot >> 4, (shot >> 2) & 3, shot & 3, xh, v
+        shot = (yh << 4 | u << 2 | k) + 1
+        return (shot >> 4, (shot >> 2) & 3, shot & 3, xh, v) if shot < SHOT_DEVICES else None
 
     received = send(message, following)
+    block = local(
+        wrap_kernel,
+        "wrap_spectra",
+        shape((QUARTERS, count, lanes), bf16),
+        vmem(1),
+        [pltpu.VMEM((lanes, receivers), f32)],
+    )(message)
+    extras = [
+        send(block, lambda yh, u, k, xh, v, to=to: (to, 0, 0, xh, v) if (yh, u, k) == (1, 3, 3) else None)
+        for to in (1, 0)
+    ]
     total = local(
         own_kernel,
         "own_spectra",
@@ -256,38 +301,47 @@
         name="finish_spectra",
     )(total, record, table, received)
 
-    def join(own, other, place, name):
-        return local(lambda *refs: join_kernel(place, *refs), name, shape((2,) + own.shape, bf16), vmem(2))(own, other)
-
+    other = send(y, lambda yh, u, k, xh, v: (1 - yh, u, k, xh, v))
+    y = local(yh_kernel, "join_yh", shape((2,) + y.shape, bf16), vmem(4))(y, other, *extras)
     other = send(y, lambda yh, u, k, xh, v: (yh, u, k ^ 2, xh, v))
-    y = join(y, other, lambda shot: (shot >> 1) & 1, "join_z0")
-    other = send(y, lambda yh, u, k, xh, v: (1 - yh, u, k, xh, v))
-    y = join(y, other, lambda shot: shot >> 4, "join_yh")
-    other = send(y, lambda yh, u, k, xh, v: (yh, u, k ^ 1, xh, v))
-    gathered, quarter = local(
-        collect_kernel,
-        "collect",
-        (shape((2,) + y.shape, bf16), shape((2,) + y.shape[:2] + (count, lanes), bf16)),
-        vmem(2),
-    )(y, other)
+    slices = shape((2, 2, count, lanes), bf16)
+    y, mine, theirs = local(z0_kernel, "join_z0", (shape((2,) + y.shape, bf16), slices, slices), vmem(2))(y, other)
+
+    def to_partner(yh, u, k, xh, v):
+        return yh, u, k ^ 1, xh, v
+
+    quarter = local(core_kernel, "join_core", shape((2,) + mine.shape, bf16), vmem(2))(mine, send(theirs, to_partner))
     cross = send(quarter, lambda yh, u, k, xh, v: (yh, u, k, 1 - xh, v) if xh == yh else None)
     q = local(choose_kernel, "choose", shape(quarter.shape, bf16), vmem(2))(quarter, cross)
     qs = [q] + [send(q, lambda yh, u, k, xh, v, m=m: (yh, u, k, xh, v ^ m)) for m in (1, 2, 3)]
-    right = local(right_kernel, "right_side", shape((2 * QUARTERS, 2 * receivers, lanes), bf16), vmem(1))(gathered)
+    right = local(right_kernel, "right_side", shape((2 * QUARTERS, 2 * receivers, lanes), bf16), vmem(2))(
+        y, send(y, to_partner)
+    )
 
     total_shots = shots * lax.axis_size("shot")
     rows = ROWS * count
-    first, *others = local(
-        lambda *refs: gram_kernel(1.0 / total_shots, *refs),
-        "gram",
-        (shape((rows, receivers), f32),) + (shape((rows, receivers), bf16),) * 3,
+    scale = 1.0 / total_shots
+    share = shape((rows, receivers), f32)
+    wire = shape((rows, receivers), bf16)
+    early = []
+    for m in (0, 3, 1):
+        early += [
+            local(
+                lambda *refs: gram_kernel(scale, *refs),
+                "gram",
+                share,
+                vmem(2) + [pl.BlockSpec(memory_space=pl.ANY)],
+            )(right, qs[m], early[-1] if early else right)
+        ]
+    sums, p1, p2, p3 = local(
+        lambda *refs: last_kernel(scale, *refs),
+        "last_gram",
+        (share, wire, wire, wire),
         vmem(5),
         [pltpu.VMEM((QUARTERS, rows, receivers), f32)],
-        limit=8,
-    )(right, *qs)
-    sums = first
-    for n in (1, 3, 2):
-        sums = sums + send(others[n - 1], lambda yh, u, k, xh, v, n=n: (yh, u ^ n, k, xh, v)).astype(f32)
+    )(right, qs[2], *early)
+    for n, p in ((2, p2), (3, p3), (1, p1)):
+        sums = sums + send(p, lambda yh, u, k, xh, v, n=n: (yh, u ^ n, k, xh, v)).astype(f32)
     return sums.reshape(2, NF, count, receivers).transpose(0, 1, 3, 2)
 
 

time: 51.8 us -> 53.3 us (1.029)
  waiting for transfers between devices: 31.4 us -> 22.2 us
  starting transfers between devices: 12.4 us -> 21.2 us
  local copies, waits for them, and re-layouts: 1.41 us -> 2.18 us
  Pallas kernels: 5.62 us -> 6.29 us
    ppermute x11 -> x14, waiting for transfers between devices: 31.4 us -> 22.2 us  [send(): return lax.ppermute(block, ('shot', 'rcv'), route)]
    ppermute x11 -> x14, starting transfers between devices: 12.4 us -> 21.2 us  [send(): return lax.ppermute(block, ('shot', 'rcv'), route)]
    unnamed x8 -> x10, local copies, waits for them, and re-layouts: 1.41 us -> 2.18 us
    pallas_call x4 -> x8, Pallas kernels: 1.34 us -> 1.99 us  [the longest x3 1.34 us: per_device(): local(lambda *refs: gram_kernel(scale, *refs), 'gram', share, vmem(2) + [...]
  transfers between devices with their start and end apart: 11 -> 14, of which waited for: 10 -> 8; matrix products, arithmetic and copies ran while one was open for 0% -> 0% of each run, Pallas kernels for 3% -> 7%
where the time goes in v5:
time: 53.3 us; the launch traced here: 52.7 us
  waiting for transfers between devices  22.2 us (42%)
  starting transfers between devices  21.2 us (40%)
  Pallas kernels  6.29 us (12%)
  local copies, waits for them, and re-layouts  2.18 us (4%)
  other arithmetic  0.66 us (1%)
    ppermute x14, waiting for transfers between devices, send(): return lax.ppermute(block, ('shot', 'rcv'), route)  22.2 us
    ppermute x14, starting transfers between devices, send(): return lax.ppermute(block, ('shot', 'rcv'), route)  21.2 us
    unnamed x10, local copies, waits for them, and re-layouts  2.18 us
    pallas_call x1, Pallas kernels, per_device(): local(tail_kernel, 'tail_spectra', shape((late_rows + LATE, receivers), f...  2.06 us
    pallas_call x1, Pallas kernels, per_device(): local(own_kernel, 'own_spectra', shape((lanes - late_rows, receivers), f3...  1.55 us
    pallas_call x3, Pallas kernels, per_device(): local(lambda *refs: gram_kernel(scale, *refs), 'gram', share, vmem(2) + [...  1.34 us
  transfers between devices with their start and end apart: 14, of which 8 were waited for; matrix products, arithmetic and copies ran while one was open for 0% of the time, Pallas kernels for 7%

profile of v5, /device:TPU:4, one launch (start us, length us, event | category | flops | bytes accessed | tf_op | source)
XLA Modules:
  0.0 52.7 jit_solution(10593892369434689813)
XLA Ops:
  0.0 0.0 copy-start.2
  0.0 0.0 copy-start.4
  0.0 2.1 %tail_spectra.1.message = f32[72,96]{1,0:T(8,128)} custom-call(s32[32]{0:T(128)} %fire_hbm.1, f32[8,2560]{1,0:T(8,128)} %constant.2.clone.table.table_hbm, bf16[96,8192]{1,0:T(8,128)(2,1)} %head.1), custom_call_target="tpu_custom_call" | custom-call | tf_op jit(solution)/shard_map/tail_spectra/pallas_call | solution.py:250
  2.1 1.7 %collective-permute-start = (f32[72,96]{1,0:T(8,128)}, f32[72,96]{1,0:T(8,128)S(1)}, u32[]{:S(2)}, u32[]{:S(2)}) collective-permute-start(f32[72,96]{1,0:T(8,128)} %tail_spectra.1.message), channel_id=1, source_target_pairs={{0,8},{1,9},{2,10},{3,11},{4,12},{5,13},{6,14},{7,15},{8,16},{9,17... | collective-permute-start | bytes 82952 | tf_op jit(solution)/shard_map/ppermute | solution.py:43
  3.8 0.0 copy-start.3
  3.8 0.8 %copy-done.3 = f32[72,96]{1,0:T(8,128)S(1)} copy-done((f32[72,96]{1,0:T(8,128)S(1)}, f32[72,96]{1,0:T(8,128)}, u32[]{:S(2)}) %copy-start.3) | copy-done | bytes 27672
  4.6 0.1 wrap_spectra.1
  4.7 0.7 %collective-permute-start.2 = (bf16[4,24,256]{2,1,0:T(8,128)(2,1)S(1)}, bf16[4,24,256]{2,1,0:T(8,128)(2,1)S(1)}, u32[]{:S(2)}, u32[]{:S(2)}) collective-permute-start(bf16[4,24,256]{2,1,0:T(8,128)(2,1)S(1)} %wrap_spectra.1), channel_id=1, source_target_pairs={{248,128},{249,129},{250,130},{251,131},{252,132},{253,133},{254,1... | collective-permute-start | bytes 147464 | tf_op jit(solution)/shard_map/ppermute | solution.py:43
  5.4 1.3 %collective-permute-start.3 = (bf16[4,24,256]{2,1,0:T(8,128)(2,1)S(1)}, bf16[4,24,256]{2,1,0:T(8,128)(2,1)S(1)}, u32[]{:S(2)}, u32[]{:S(2)}) collective-permute-start(bf16[4,24,256]{2,1,0:T(8,128)(2,1)S(1)} %wrap_spectra.1), channel_id=1, source_target_pairs={{248,0},{249,1},{250,2},{251,3},{252,4},{253,5},{254,6},{255,7}} | collective-permute-start | bytes 147464 | tf_op jit(solution)/shard_map/ppermute | solution.py:43
  6.7 0.0 copy-done.2
  6.7 0.0 copy-done.4
  6.7 0.0 copy-start
  6.7 1.4 %copy-done = bf16[96,8192]{1,0:T(8,128)(2,1)S(1)} copy-done((bf16[96,8192]{1,0:T(8,128)(2,1)S(1)}, bf16[96,8192]{1,0:T(8,128)(2,1)}, u32[]{:S(2)}) %copy-start) | copy-done | bytes 1572888
  8.1 0.0 copy-start.1
  8.1 1.5 %own_spectra.1.total = f32[192,96]{1,0:T(8,128)S(1)} custom-call(s32[32]{0:T(128)S(1)} %copy-done.4, f32[8,2560]{1,0:T(8,128)S(1)} %copy-done.2, bf16[96,8192]{1,0:T(8,128)(2,1)S(1)} %copy-done), custom_call_target="tpu_custom_call" | custom-call | tf_op jit(solution)/shard_map/own_spectra/pallas_call | solution.py:281
  9.6 0.0 collective-permute-done.message
  9.6 0.0 copy-done.1
  9.7 0.6 %finish_spectra.1.own = bf16[4,24,256]{2,1,0:T(8,128)(2,1)S(1)} custom-call(f32[192,96]{1,0:T(8,128)S(1)} %own_spectra.1.total, bf16[96,8192]{1,0:T(8,128)(2,1)S(1)} %copy-done.1, f32[8,2560]{1,0:T(8,128)S(1)} %copy-done.2, f32[72,96]{1,0:T(8,128)S(1)} %collective-permute-done.message), custom_call_target="tpu_custom_call" | custom-call | tf_op jit(solution)/shard_map/finish_spectra/pallas_call | solution.py:288
  10.3 4.8 %collective-permute-start.1 = (bf16[4,24,256]{2,1,0:T(8,128)(2,1)S(1)}, bf16[4,24,256]{2,1,0:T(8,128)(2,1)S(1)}, u32[]{:S(2)}, u32[]{:S(2)}) collective-permute-start(bf16[4,24,256]{2,1,0:T(8,128)(2,1)S(1)} %finish_spectra.1.own), channel_id=1, source_target_pairs={{0,128},{1,129},{2,130},{3,131},{4,132},{5,133},{6,134},{7,135},{8... | collective-permute-start | bytes 147464 | tf_op jit(solution)/shard_map/ppermute | solution.py:43
  15.1 0.0 collective-permute-done.2.extra1
  15.1 1.5 %collective-permute-done.3.extra0 = bf16[4,24,256]{2,1,0:T(8,128)(2,1)S(1)} collective-permute-done((bf16[4,24,256]{2,1,0:T(8,128)(2,1)S(1)}, bf16[4,24,256]{2,1,0:T(8,128)(2,1)S(1)}, u32[]{:S(2)}, u32[]{:S(2)}) %collective-permute-start.3) | collective-permute-done | bytes 49184 | tf_op jit(solution)/shard_map/ppermute | solution.py:43
  16.6 1.0 %collective-permute-done.1.other = bf16[4,24,256]{2,1,0:T(8,128)(2,1)S(1)} collective-permute-done((bf16[4,24,256]{2,1,0:T(8,128)(2,1)S(1)}, bf16[4,24,256]{2,1,0:T(8,128)(2,1)S(1)}, u32[]{:S(2)}, u32[]{:S(2)}) %collective-permute-start.1) | collective-permute-done | bytes 49184 | tf_op jit(solution)/shard_map/ppermute | solution.py:43
  17.6 0.1 collective-permute-start.4
  17.7 4.7 %collective-permute-done.4.other = bf16[2,4,24,256]{3,2,1,0:T(8,128)(2,1)S(1)} collective-permute-done((bf16[2,4,24,256]{3,2,1,0:T(8,128)(2,1)S(1)}, bf16[2,4,24,256]{3,2,1,0:T(8,128)(2,1)S(1)}, u32[]{:S(2)}, u32[]{:S(2)}) %collective-permute-start.4) | collective-permute-done | bytes 98336 | tf_op jit(solution)/shard_map/ppermute | solution.py:43
  22.5 0.1 collective-permute-start.6
  22.6 0.5 collective-permute-start.5
  23.1 0.7 %collective-permute-done.6.other = bf16[2,2,24,256]{3,2,1,0:T(8,128)(2,1)S(1)} collective-permute-done((bf16[2,2,24,256]{3,2,1,0:T(8,128)(2,1)S(1)}, bf16[2,2,24,256]{3,2,1,0:T(8,128)(2,1)S(1)}, u32[]{:S(2)}, u32[]{:S(2)}) %collective-permute-start.6) | collective-permute-done | bytes 49184 | tf_op jit(solution)/shard_map/ppermute | solution.py:43
  23.8 1.3 %collective-permute-start.7 = (bf16[2,2,2,24,256]{4,3,2,1,0:T(8,128)(2,1)S(1)}, bf16[2,2,2,24,256]{4,3,2,1,0:T(8,128)(2,1)S(1)}, u32[]{:S(2)}, u32[]{:S(2)}) collective-permute-start(bf16[2,2,2,24,256]{4,3,2,1,0:T(8,128)(2,1)S(1)} %join_core.1.own), channel_id=1, source_target_pairs={{0,4},{1,5},{2,6},{3,7},{8,12},{9,13},{10,14},{11,15},{16,20},{17,... | collective-permute-start | bytes 294920 | tf_op jit(solution)/shard_map/ppermute | solution.py:43
  25.1 7.0 %collective-permute-done.7.cross = bf16[2,2,2,24,256]{4,3,2,1,0:T(8,128)(2,1)S(1)} collective-permute-done((bf16[2,2,2,24,256]{4,3,2,1,0:T(8,128)(2,1)S(1)}, bf16[2,2,2,24,256]{4,3,2,1,0:T(8,128)(2,1)S(1)}, u32[]{:S(2)}, u32[]{:S(2)}) %collective-permute-start.7) | collective-permute-done | bytes 98336 | tf_op jit(solution)/shard_map/ppermute | solution.py:43
  32.1 1.7 %collective-permute-start.9 = (bf16[2,2,2,24,256]{4,3,2,1,0:T(8,128)(2,1)S(1)}, bf16[2,2,2,24,256]{4,3,2,1,0:T(8,128)(2,1)S(1)}, u32[]{:S(2)}, u32[]{:S(2)}) collective-permute-start(bf16[2,2,2,24,256]{4,3,2,1,0:T(8,128)(2,1)S(1)} %choose.1.refs_1_), channel_id=1, source_target_pairs={{0,3},{1,2},{2,1},{3,0},{4,7},{5,6},{6,5},{7,4},{8,11},{9,10},{10,... | collective-permute-start | bytes 294920 | tf_op jit(solution)/shard_map/ppermute | solution.py:43
  33.8 1.0 %collective-permute-start.10 = (bf16[2,2,2,24,256]{4,3,2,1,0:T(8,128)(2,1)S(1)}, bf16[2,2,2,24,256]{4,3,2,1,0:T(8,128)(2,1)S(1)}, u32[]{:S(2)}, u32[]{:S(2)}) collective-permute-start(bf16[2,2,2,24,256]{4,3,2,1,0:T(8,128)(2,1)S(1)} %choose.1.refs_1_), channel_id=1, source_target_pairs={{0,1},{1,0},{2,3},{3,2},{4,5},{5,4},{6,7},{7,6},{8,9},{9,8},{10,11... | collective-permute-start | bytes 294920 | tf_op jit(solution)/shard_map/ppermute | solution.py:43
  34.8 0.8 %collective-permute-start.8 = (bf16[2,2,2,24,256]{4,3,2,1,0:T(8,128)(2,1)S(1)}, bf16[2,2,2,24,256]{4,3,2,1,0:T(8,128)(2,1)S(1)}, u32[]{:S(2)}, u32[]{:S(2)}) collective-permute-start(bf16[2,2,2,24,256]{4,3,2,1,0:T(8,128)(2,1)S(1)} %choose.1.refs_1_), channel_id=1, source_target_pairs={{0,2},{1,3},{2,0},{3,1},{4,6},{5,7},{6,4},{7,5},{8,10},{9,11},{10,... | collective-permute-start | bytes 294920 | tf_op jit(solution)/shard_map/ppermute | solution.py:43
  35.6 0.0 collective-permute-done.5.other
  35.6 0.1 right_side.1.refs_0_.refs_2_
  35.7 0.4 gram.3.refs_2_
  36.2 2.5 %collective-permute-done.9.refs_1_ = bf16[2,2,2,24,256]{4,3,2,1,0:T(8,128)(2,1)S(1)} collective-permute-done((bf16[2,2,2,24,256]{4,3,2,1,0:T(8,128)(2,1)S(1)}, bf16[2,2,2,24,256]{4,3,2,1,0:T(8,128)(2,1)S(1)}, u32[]{:S(2)}, u32[]{:S(2)}) %collective-permute-start.9) | collective-permute-done | bytes 98336 | tf_op jit(solution)/shard_map/ppermute | solution.py:43
  38.7 0.4 gram.4.refs_2_.refs_3_
  39.2 0.0 collective-permute-done.10.refs_1_
  39.2 0.4 gram.5.refs_4_
  39.6 0.0 collective-permute-done.8.refs_1_
  39.6 0.5 last_gram.1
  40.1 5.7 %collective-permute-start.11 = (bf16[192,96]{1,0:T(8,128)(2,1)S(1)}, bf16[192,96]{1,0:T(8,128)(2,1)S(1)}, u32[]{:S(2)}, u32[]{:S(2)}) collective-permute-start(bf16[192,96]{1,0:T(8,128)(2,1)S(1)} %get-tuple-element.16), channel_id=1, source_target_pairs={{0,64},{1,65},{2,66},{3,67},{4,68},{5,69},{6,70},{7,71},{8,72},{9,... | collective-permute-start | bytes 110600 | tf_op jit(solution)/shard_map/ppermute | solution.py:43
  45.8 0.3 collective-permute-start.12
  46.1 1.2 %collective-permute-start.13 = (bf16[192,96]{1,0:T(8,128)(2,1)S(1)}, bf16[192,96]{1,0:T(8,128)(2,1)S(1)}, u32[]{:S(2)}, u32[]{:S(2)}) collective-permute-start(bf16[192,96]{1,0:T(8,128)(2,1)S(1)} %get-tuple-element.18), channel_id=1, source_target_pairs={{0,32},{1,33},{2,34},{3,35},{4,36},{5,37},{6,38},{7,39},{8,40},{9,... | collective-permute-start | bytes 110600 | tf_op jit(solution)/shard_map/ppermute | solution.py:43
  47.3 1.0 %collective-permute-done.11 = bf16[192,96]{1,0:T(8,128)(2,1)S(1)} collective-permute-done((bf16[192,96]{1,0:T(8,128)(2,1)S(1)}, bf16[192,96]{1,0:T(8,128)(2,1)S(1)}, u32[]{:S(2)}, u32[]{:S(2)}) %collective-permute-start.11) | collective-permute-done | bytes 36896 | tf_op jit(solution)/shard_map/ppermute | solution.py:43
  48.3 3.8 %collective-permute-done.12 = bf16[192,96]{1,0:T(8,128)(2,1)S(1)} collective-permute-done((bf16[192,96]{1,0:T(8,128)(2,1)S(1)}, bf16[192,96]{1,0:T(8,128)(2,1)S(1)}, u32[]{:S(2)}, u32[]{:S(2)}) %collective-permute-start.12) | collective-permute-done | bytes 36896 | tf_op jit(solution)/shard_map/ppermute | solution.py:43
  52.1 0.0 collective-permute-done.13
  52.1 0.7 %convert_add_fusion = f32[192,96]{1,0:T(8,128)} fusion(bf16[192,96]{1,0:T(8,128)(2,1)S(1)} %collective-permute-done.13, bf16[192,96]{1,0:T(8,128)(2,1)S(1)} %collective-permute-done.12, f32[192,96]{1,0:T(8,128)S(1)} %get-tuple-element.15, bf16[192,96]{1,0:T(8,128)(2,1)S(1)} %collective-permute-done.11), kind=kLoop, calls=%fused_computation | loop fusion | flops 110592 | bytes 258048 | tf_op jit(solution)/shard_map/add | solution.py:344
  (4 shorter events, 0.1 us)
Async XLA Ops:
  0.0 6.7 %copy-start.2 = (f32[8,2560]{1,0:T(8,128)S(1)}, f32[8,2560]{1,0:T(8,128)}, u32[]{:S(2)}) copy-start(f32[8,2560]{1,0:T(8,128)} %constant.2.clone.table.table_hbm) | copy-start | bytes 245764
  0.0 6.7 %copy-start.4 = (s32[32]{0:T(128)S(1)}, s32[32]{0:T(128)}, u32[]{:S(2)}) copy-start(s32[32]{0:T(128)} %fire_hbm.1) | copy-start | bytes 388
  2.1 7.6 %collective-permute-start = (f32[72,96]{1,0:T(8,128)}, f32[72,96]{1,0:T(8,128)S(1)}, u32[]{:S(2)}, u32[]{:S(2)}) collective-permute-start(f32[72,96]{1,0:T(8,128)} %tail_spectra.1.message), channel_id=1, source_target_pairs={{0,8},{1,9},{2,10},{3,11},{4,12},{5,13},{6,14},{7,15},{8,16},{9,17... | collective-permute-start | bytes 82952 | tf_op jit(solution)/shard_map/ppermute | solution.py:43
  3.8 0.8 %copy-start.3 = (f32[72,96]{1,0:T(8,128)S(1)}, f32[72,96]{1,0:T(8,128)}, u32[]{:S(2)}) copy-start(f32[72,96]{1,0:T(8,128)} %tail_spectra.1.message) | copy-start | bytes 82948
  4.7 10.4 %collective-permute-start.2 = (bf16[4,24,256]{2,1,0:T(8,128)(2,1)S(1)}, bf16[4,24,256]{2,1,0:T(8,128)(2,1)S(1)}, u32[]{:S(2)}, u32[]{:S(2)}) collective-permute-start(bf16[4,24,256]{2,1,0:T(8,128)(2,1)S(1)} %wrap_spectra.1), channel_id=1, source_target_pairs={{248,128},{249,129},{250,130},{251,131},{252,132},{253,133},{254,1... | collective-permute-start | bytes 147464 | tf_op jit(solution)/shard_map/ppermute | solution.py:43
  5.4 11.2 %collective-permute-start.3 = (bf16[4,24,256]{2,1,0:T(8,128)(2,1)S(1)}, bf16[4,24,256]{2,1,0:T(8,128)(2,1)S(1)}, u32[]{:S(2)}, u32[]{:S(2)}) collective-permute-start(bf16[4,24,256]{2,1,0:T(8,128)(2,1)S(1)} %wrap_spectra.1), channel_id=1, source_target_pairs={{248,0},{249,1},{250,2},{251,3},{252,4},{253,5},{254,6},{255,7}} | collective-permute-start | bytes 147464 | tf_op jit(solution)/shard_map/ppermute | solution.py:43
  6.7 1.4 %copy-start = (bf16[96,8192]{1,0:T(8,128)(2,1)S(1)}, bf16[96,8192]{1,0:T(8,128)(2,1)}, u32[]{:S(2)}) copy-start(bf16[96,8192]{1,0:T(8,128)(2,1)} %head.1) | copy-start | bytes 4718596
  8.1 1.6 %copy-start.1 = (bf16[96,8192]{1,0:T(8,128)(2,1)S(1)}, bf16[96,8192]{1,0:T(8,128)(2,1)}, u32[]{:S(2)}) copy-start(bf16[96,8192]{1,0:T(8,128)(2,1)} %head.1) | copy-start | bytes 4718596
  10.3 7.3 %collective-permute-start.1 = (bf16[4,24,256]{2,1,0:T(8,128)(2,1)S(1)}, bf16[4,24,256]{2,1,0:T(8,128)(2,1)S(1)}, u32[]{:S(2)}, u32[]{:S(2)}) collective-permute-start(bf16[4,24,256]{2,1,0:T(8,128)(2,1)S(1)} %finish_spectra.1.own), channel_id=1, source_target_pairs={{0,128},{1,129},{2,130},{3,131},{4,132},{5,133},{6,134},{7,135},{8... | collective-permute-start | bytes 147464 | tf_op jit(solution)/shard_map/ppermute | solution.py:43
  17.6 4.8 %collective-permute-start.4 = (bf16[2,4,24,256]{3,2,1,0:T(8,128)(2,1)S(1)}, bf16[2,4,24,256]{3,2,1,0:T(8,128)(2,1)S(1)}, u32[]{:S(2)}, u32[]{:S(2)}) collective-permute-start(bf16[2,4,24,256]{3,2,1,0:T(8,128)(2,1)S(1)} %join_yh.1.own), channel_id=1, source_target_pairs={{0,16},{1,17},{2,18},{3,19},{4,20},{5,21},{6,22},{7,23},{8,24},{9,... | collective-permute-start | bytes 294920 | tf_op jit(solution)/shard_map/ppermute | solution.py:43
  22.5 1.3 %collective-permute-start.6 = (bf16[2,2,24,256]{3,2,1,0:T(8,128)(2,1)S(1)}, bf16[2,2,24,256]{3,2,1,0:T(8,128)(2,1)S(1)}, u32[]{:S(2)}, u32[]{:S(2)}) collective-permute-start(bf16[2,2,24,256]{3,2,1,0:T(8,128)(2,1)S(1)} %get-tuple-element.14), channel_id=1, source_target_pairs={{0,8},{1,9},{2,10},{3,11},{4,12},{5,13},{6,14},{7,15},{8,0},{9,1},... | collective-permute-start | bytes 147464 | tf_op jit(solution)/shard_map/ppermute | solution.py:43
  22.6 13.1 %collective-permute-start.5 = (bf16[2,2,4,24,256]{4,3,2,1,0:T(8,128)(2,1)S(1)}, bf16[2,2,4,24,256]{4,3,2,1,0:T(8,128)(2,1)S(1)}, u32[]{:S(2)}, u32[]{:S(2)}) collective-permute-start(bf16[2,2,4,24,256]{4,3,2,1,0:T(8,128)(2,1)S(1)} %get-tuple-element.12.own), channel_id=1, source_target_pairs={{0,8},{1,9},{2,10},{3,11},{4,12},{5,13},{6,14},{7,15},{8,0},{9,1},... | collective-permute-start | bytes 589832 | tf_op jit(solution)/shard_map/ppermute | solution.py:43
  23.8 8.3 %collective-permute-start.7 = (bf16[2,2,2,24,256]{4,3,2,1,0:T(8,128)(2,1)S(1)}, bf16[2,2,2,24,256]{4,3,2,1,0:T(8,128)(2,1)S(1)}, u32[]{:S(2)}, u32[]{:S(2)}) collective-permute-start(bf16[2,2,2,24,256]{4,3,2,1,0:T(8,128)(2,1)S(1)} %join_core.1.own), channel_id=1, source_target_pairs={{0,4},{1,5},{2,6},{3,7},{8,12},{9,13},{10,14},{11,15},{16,20},{17,... | collective-permute-start | bytes 294920 | tf_op jit(solution)/shard_map/ppermute | solution.py:43
  32.1 6.7 %collective-permute-start.9 = (bf16[2,2,2,24,256]{4,3,2,1,0:T(8,128)(2,1)S(1)}, bf16[2,2,2,24,256]{4,3,2,1,0:T(8,128)(2,1)S(1)}, u32[]{:S(2)}, u32[]{:S(2)}) collective-permute-start(bf16[2,2,2,24,256]{4,3,2,1,0:T(8,128)(2,1)S(1)} %choose.1.refs_1_), channel_id=1, source_target_pairs={{0,3},{1,2},{2,1},{3,0},{4,7},{5,6},{6,5},{7,4},{8,11},{9,10},{10,... | collective-permute-start | bytes 294920 | tf_op jit(solution)/shard_map/ppermute | solution.py:43
  33.8 5.4 %collective-permute-start.10 = (bf16[2,2,2,24,256]{4,3,2,1,0:T(8,128)(2,1)S(1)}, bf16[2,2,2,24,256]{4,3,2,1,0:T(8,128)(2,1)S(1)}, u32[]{:S(2)}, u32[]{:S(2)}) collective-permute-start(bf16[2,2,2,24,256]{4,3,2,1,0:T(8,128)(2,1)S(1)} %choose.1.refs_1_), channel_id=1, source_target_pairs={{0,1},{1,0},{2,3},{3,2},{4,5},{5,4},{6,7},{7,6},{8,9},{9,8},{10,11... | collective-permute-start | bytes 294920 | tf_op jit(solution)/shard_map/ppermute | solution.py:43
  34.8 4.8 %collective-permute-start.8 = (bf16[2,2,2,24,256]{4,3,2,1,0:T(8,128)(2,1)S(1)}, bf16[2,2,2,24,256]{4,3,2,1,0:T(8,128)(2,1)S(1)}, u32[]{:S(2)}, u32[]{:S(2)}) collective-permute-start(bf16[2,2,2,24,256]{4,3,2,1,0:T(8,128)(2,1)S(1)} %choose.1.refs_1_), channel_id=1, source_target_pairs={{0,2},{1,3},{2,0},{3,1},{4,6},{5,7},{6,4},{7,5},{8,10},{9,11},{10,... | collective-permute-start | bytes 294920 | tf_op jit(solution)/shard_map/ppermute | solution.py:43
  40.1 8.2 %collective-permute-start.11 = (bf16[192,96]{1,0:T(8,128)(2,1)S(1)}, bf16[192,96]{1,0:T(8,128)(2,1)S(1)}, u32[]{:S(2)}, u32[]{:S(2)}) collective-permute-start(bf16[192,96]{1,0:T(8,128)(2,1)S(1)} %get-tuple-element.16), channel_id=1, source_target_pairs={{0,64},{1,65},{2,66},{3,67},{4,68},{5,69},{6,70},{7,71},{8,72},{9,... | collective-permute-start | bytes 110600 | tf_op jit(solution)/shard_map/ppermute | solution.py:43
  45.8 6.3 %collective-permute-start.12 = (bf16[192,96]{1,0:T(8,128)(2,1)S(1)}, bf16[192,96]{1,0:T(8,128)(2,1)S(1)}, u32[]{:S(2)}, u32[]{:S(2)}) collective-permute-start(bf16[192,96]{1,0:T(8,128)(2,1)S(1)} %get-tuple-element.17), channel_id=1, source_target_pairs={{0,96},{1,97},{2,98},{3,99},{4,100},{5,101},{6,102},{7,103},{8,104... | collective-permute-start | bytes 110600 | tf_op jit(solution)/shard_map/ppermute | solution.py:43
  46.1 6.0 %collective-permute-start.13 = (bf16[192,96]{1,0:T(8,128)(2,1)S(1)}, bf16[192,96]{1,0:T(8,128)(2,1)S(1)}, u32[]{:S(2)}, u32[]{:S(2)}) collective-permute-start(bf16[192,96]{1,0:T(8,128)(2,1)S(1)} %get-tuple-element.18), channel_id=1, source_target_pairs={{0,32},{1,33},{2,34},{3,35},{4,36},{5,37},{6,38},{7,39},{8,40},{9,... | collective-permute-start | bytes 110600 | tf_op jit(solution)/shard_map/ppermute | solution.py:43

commit v6 on v5

--- a/solution.py
+++ b/solution.py
@@ -140,20 +140,10 @@
         out[k] = turned[count * k : count * (k + 1), :].astype(out.dtype)
 
 
-def wrap_kernel(message, out, scratch):
-    late_rows = ROWS * LATE
-    own_rows = scratch.shape[0] - late_rows
-    scratch[:own_rows, :] = jnp.zeros((own_rows, scratch.shape[1]), jnp.float32)
-    scratch[own_rows:, :] = message[:late_rows, :]
-    turn_over(scratch, out)
-
-
-def yh_kernel(own, other, extra1, extra0, out):
+def yh_kernel(own, other, out):
     yh = shot_index() >> 4
     out[yh] = own[...]
     out[1 - yh] = other[...]
-    extra = extra1[...].astype(jnp.float32) + extra0[...].astype(jnp.float32)
-    out[0] = (out[0].astype(jnp.float32) + extra).astype(out.dtype)
 
 
 def z0_kernel(own, other, out, mine, theirs):
@@ -263,21 +253,10 @@
     )(shot_fire_samples, table, record)
 
     def following(yh, u, k, xh, v):
-        shot = (yh << 4 | u << 2 | k) + 1
-        return (shot >> 4, (shot >> 2) & 3, shot & 3, xh, v) if shot < SHOT_DEVICES else None
+        shot = ((yh << 4 | u << 2 | k) + 1) % SHOT_DEVICES
+        return shot >> 4, (shot >> 2) & 3, shot & 3, xh, v
 
     received = send(message, following)
-    block = local(
-        wrap_kernel,
-        "wrap_spectra",
-        shape((QUARTERS, count, lanes), bf16),
-        vmem(1),
-        [pltpu.VMEM((lanes, receivers), f32)],
-    )(message)
-    extras = [
-        send(block, lambda yh, u, k, xh, v, to=to: (to, 0, 0, xh, v) if (yh, u, k) == (1, 3, 3) else None)
-        for to in (1, 0)
-    ]
     total = local(
         own_kernel,
         "own_spectra",
@@ -302,7 +281,7 @@
     )(total, record, table, received)
 
     other = send(y, lambda yh, u, k, xh, v: (1 - yh, u, k, xh, v))
-    y = local(yh_kernel, "join_yh", shape((2,) + y.shape, bf16), vmem(4))(y, other, *extras)
+    y = local(yh_kernel, "join_yh", shape((2,) + y.shape, bf16), vmem(2))(y, other)
     other = send(y, lambda yh, u, k, xh, v: (yh, u, k ^ 2, xh, v))
     slices = shape((2, 2, count, lanes), bf16)
     y, mine, theirs = local(z0_kernel, "join_z0", (shape((2,) + y.shape, bf16), slices, slices), vmem(2))(y, other)
@@ -311,7 +290,7 @@
         return yh, u, k ^ 1, xh, v
 
     quarter = local(core_kernel, "join_core", shape((2,) + mine.shape, bf16), vmem(2))(mine, send(theirs, to_partner))
-    cross = send(quarter, lambda yh, u, k, xh, v: (yh, u, k, 1 - xh, v) if xh == yh else None)
+    cross = send(quarter, lambda yh, u, k, xh, v: (yh, u, k, 1 - xh, v))
     q = local(choose_kernel, "choose", shape(quarter.shape, bf16), vmem(2))(quarter, cross)
     qs = [q] + [send(q, lambda yh, u, k, xh, v, m=m: (yh, u, k, xh, v ^ m)) for m in (1, 2, 3)]
     right = local(right_kernel, "right_side", shape((2 * QUARTERS, 2 * receivers, lanes), bf16), vmem(2))(
@@ -340,7 +319,7 @@
         vmem(5),
         [pltpu.VMEM((QUARTERS, rows, receivers), f32)],
     )(right, qs[2], *early)
-    for n, p in ((2, p2), (3, p3), (1, p1)):
+    for n, p in ((1, p1), (2, p2), (3, p3)):
         sums = sums + send(p, lambda yh, u, k, xh, v, n=n: (yh, u ^ n, k, xh, v)).astype(f32)
     return sums.reshape(2, NF, count, receivers).transpose(0, 1, 3, 2)
 

time: 53.3 us -> 48.9 us (0.917)
  starting transfers between devices: 21.2 us -> 12.2 us
  waiting for transfers between devices: 22.2 us -> 28.2 us
  local copies, waits for them, and re-layouts: 2.18 us -> 1.41 us
    ppermute x14 -> x12, starting transfers between devices: 21.2 us -> 12.2 us  [send(): return lax.ppermute(block, ('shot', 'rcv'), route)]
    ppermute x14 -> x12, waiting for transfers between devices: 22.2 us -> 28.2 us  [send(): return lax.ppermute(block, ('shot', 'rcv'), route)]
    unnamed x10 -> x8, local copies, waits for them, and re-layouts: 2.18 us -> 1.41 us
  transfers between devices with their start and end apart: 14 -> 12, of which waited for: 8 -> 8; matrix products, arithmetic and copies ran while one was open for 0% -> 0% of each run, Pallas kernels for 7% -> 6%
where the time goes in v6:
time: 48.9 us; the launch traced here: 48.8 us
  waiting for transfers between devices  28.2 us (58%)
  starting transfers between devices  12.2 us (25%)
  Pallas kernels  6.22 us (13%)
  local copies, waits for them, and re-layouts  1.41 us (3%)
  other arithmetic  0.67 us (1%)
    ppermute x12, waiting for transfers between devices, send(): return lax.ppermute(block, ('shot', 'rcv'), route)  28.2 us
    ppermute x12, starting transfers between devices, send(): return lax.ppermute(block, ('shot', 'rcv'), route)  12.2 us
    pallas_call x1, Pallas kernels, per_device(): local(tail_kernel, 'tail_spectra', shape((late_rows + LATE, receivers), f...  2.06 us
    pallas_call x1, Pallas kernels, per_device(): local(own_kernel, 'own_spectra', shape((lanes - late_rows, receivers), f3...  1.59 us
    unnamed x8, local copies, waits for them, and re-layouts  1.41 us
    pallas_call x3, Pallas kernels, per_device(): local(lambda *refs: gram_kernel(scale, *refs), 'gram', share, vmem(2) + [...  1.34 us
  transfers between devices with their start and end apart: 12, of which 8 were waited for; matrix products, arithmetic and copies ran while one was open for 0% of the time, Pallas kernels for 6%

profile of v6, /device:TPU:4, one launch (start us, length us, event | category | flops | bytes accessed | tf_op | source)
XLA Modules:
  0.0 48.8 jit_solution(18390005566518138188)
XLA Ops:
  0.0 0.0 copy-start.2
  0.0 0.0 copy-start.3
  0.0 2.1 %tail_spectra.1 = f32[72,96]{1,0:T(8,128)} custom-call(s32[32]{0:T(128)} %fire_hbm.1, f32[8,2560]{1,0:T(8,128)} %constant.2.clone.table.table_hbm, bf16[96,8192]{1,0:T(8,128)(2,1)} %head.1), custom_call_target="tpu_custom_call" | custom-call | tf_op jit(solution)/shard_map/tail_spectra/pallas_call | solution.py:240
  2.1 0.1 collective-permute-start
  2.2 0.0 copy-done.2
  2.2 0.0 copy-done.3
  2.2 0.0 copy-start
  2.2 1.4 %copy-done = bf16[96,8192]{1,0:T(8,128)(2,1)S(1)} copy-done((bf16[96,8192]{1,0:T(8,128)(2,1)S(1)}, bf16[96,8192]{1,0:T(8,128)(2,1)}, u32[]{:S(2)}) %copy-start) | copy-done | bytes 1572888
  3.6 0.0 copy-start.1
  3.6 1.6 %own_spectra.1.total = f32[192,96]{1,0:T(8,128)S(1)} custom-call(s32[32]{0:T(128)S(1)} %copy-done.3, f32[8,2560]{1,0:T(8,128)S(1)} %copy-done.2, bf16[96,8192]{1,0:T(8,128)(2,1)S(1)} %copy-done), custom_call_target="tpu_custom_call" | custom-call | tf_op jit(solution)/shard_map/own_spectra/pallas_call | solution.py:260
  5.2 6.7 %collective-permute-done.message = f32[72,96]{1,0:T(8,128)S(1)} collective-permute-done((f32[72,96]{1,0:T(8,128)}, f32[72,96]{1,0:T(8,128)S(1)}, u32[]{:S(2)}, u32[]{:S(2)}) %collective-permute-start) | collective-permute-done | bytes 27680 | tf_op jit(solution)/shard_map/ppermute | solution.py:43
  11.9 0.0 copy-done.1
  11.9 0.6 %finish_spectra.1.own = bf16[4,24,256]{2,1,0:T(8,128)(2,1)S(1)} custom-call(f32[192,96]{1,0:T(8,128)S(1)} %own_spectra.1.total, bf16[96,8192]{1,0:T(8,128)(2,1)S(1)} %copy-done.1, f32[8,2560]{1,0:T(8,128)S(1)} %copy-done.2, f32[72,96]{1,0:T(8,128)S(1)} %collective-permute-done.message), custom_call_target="tpu_custom_call" | custom-call | tf_op jit(solution)/shard_map/finish_spectra/pallas_call | solution.py:267
  12.5 0.7 %collective-permute-start.1 = (bf16[4,24,256]{2,1,0:T(8,128)(2,1)S(1)}, bf16[4,24,256]{2,1,0:T(8,128)(2,1)S(1)}, u32[]{:S(2)}, u32[]{:S(2)}) collective-permute-start(bf16[4,24,256]{2,1,0:T(8,128)(2,1)S(1)} %finish_spectra.1.own), channel_id=1, source_target_pairs={{0,128},{1,129},{2,130},{3,131},{4,132},{5,133},{6,134},{7,135},{8... | collective-permute-start | bytes 147464 | tf_op jit(solution)/shard_map/ppermute | solution.py:43
  13.3 5.0 %collective-permute-done.1.other = bf16[4,24,256]{2,1,0:T(8,128)(2,1)S(1)} collective-permute-done((bf16[4,24,256]{2,1,0:T(8,128)(2,1)S(1)}, bf16[4,24,256]{2,1,0:T(8,128)(2,1)S(1)}, u32[]{:S(2)}, u32[]{:S(2)}) %collective-permute-start.1) | collective-permute-done | bytes 49184 | tf_op jit(solution)/shard_map/ppermute | solution.py:43
  18.2 0.1 collective-permute-start.2
  18.3 4.6 %collective-permute-done.2.other = bf16[2,4,24,256]{3,2,1,0:T(8,128)(2,1)S(1)} collective-permute-done((bf16[2,4,24,256]{3,2,1,0:T(8,128)(2,1)S(1)}, bf16[2,4,24,256]{3,2,1,0:T(8,128)(2,1)S(1)}, u32[]{:S(2)}, u32[]{:S(2)}) %collective-permute-start.2) | collective-permute-done | bytes 98336 | tf_op jit(solution)/shard_map/ppermute | solution.py:43
  23.0 0.1 collective-permute-start.4
  23.1 0.5 %collective-permute-start.3 = (bf16[2,2,4,24,256]{4,3,2,1,0:T(8,128)(2,1)S(1)}, bf16[2,2,4,24,256]{4,3,2,1,0:T(8,128)(2,1)S(1)}, u32[]{:S(2)}, u32[]{:S(2)}) collective-permute-start(bf16[2,2,4,24,256]{4,3,2,1,0:T(8,128)(2,1)S(1)} %get-tuple-element.12.own), channel_id=1, source_target_pairs={{0,8},{1,9},{2,10},{3,11},{4,12},{5,13},{6,14},{7,15},{8,0},{9,1},... | collective-permute-start | bytes 589832 | tf_op jit(solution)/shard_map/ppermute | solution.py:43
  23.6 0.7 %collective-permute-done.4.other = bf16[2,2,24,256]{3,2,1,0:T(8,128)(2,1)S(1)} collective-permute-done((bf16[2,2,24,256]{3,2,1,0:T(8,128)(2,1)S(1)}, bf16[2,2,24,256]{3,2,1,0:T(8,128)(2,1)S(1)}, u32[]{:S(2)}, u32[]{:S(2)}) %collective-permute-start.4) | collective-permute-done | bytes 49184 | tf_op jit(solution)/shard_map/ppermute | solution.py:43
  24.3 0.6 %collective-permute-start.5 = (bf16[2,2,2,24,256]{4,3,2,1,0:T(8,128)(2,1)S(1)}, bf16[2,2,2,24,256]{4,3,2,1,0:T(8,128)(2,1)S(1)}, u32[]{:S(2)}, u32[]{:S(2)}) collective-permute-start(bf16[2,2,2,24,256]{4,3,2,1,0:T(8,128)(2,1)S(1)} %join_core.1.own), channel_id=1, source_target_pairs={{0,4},{1,5},{2,6},{3,7},{4,0},{5,1},{6,2},{7,3},{8,12},{9,13},{10,... | collective-permute-start | bytes 294920 | tf_op jit(solution)/shard_map/ppermute | solution.py:43
  24.9 5.9 %collective-permute-done.5.cross = bf16[2,2,2,24,256]{4,3,2,1,0:T(8,128)(2,1)S(1)} collective-permute-done((bf16[2,2,2,24,256]{4,3,2,1,0:T(8,128)(2,1)S(1)}, bf16[2,2,2,24,256]{4,3,2,1,0:T(8,128)(2,1)S(1)}, u32[]{:S(2)}, u32[]{:S(2)}) %collective-permute-start.5) | collective-permute-done | bytes 98336 | tf_op jit(solution)/shard_map/ppermute | solution.py:43
  30.8 1.4 %collective-permute-start.7 = (bf16[2,2,2,24,256]{4,3,2,1,0:T(8,128)(2,1)S(1)}, bf16[2,2,2,24,256]{4,3,2,1,0:T(8,128)(2,1)S(1)}, u32[]{:S(2)}, u32[]{:S(2)}) collective-permute-start(bf16[2,2,2,24,256]{4,3,2,1,0:T(8,128)(2,1)S(1)} %choose.1.refs_1_), channel_id=1, source_target_pairs={{0,3},{1,2},{2,1},{3,0},{4,7},{5,6},{6,5},{7,4},{8,11},{9,10},{10,... | collective-permute-start | bytes 294920 | tf_op jit(solution)/shard_map/ppermute | solution.py:43
  32.2 1.3 %collective-permute-start.8 = (bf16[2,2,2,24,256]{4,3,2,1,0:T(8,128)(2,1)S(1)}, bf16[2,2,2,24,256]{4,3,2,1,0:T(8,128)(2,1)S(1)}, u32[]{:S(2)}, u32[]{:S(2)}) collective-permute-start(bf16[2,2,2,24,256]{4,3,2,1,0:T(8,128)(2,1)S(1)} %choose.1.refs_1_), channel_id=1, source_target_pairs={{0,1},{1,0},{2,3},{3,2},{4,5},{5,4},{6,7},{7,6},{8,9},{9,8},{10,11... | collective-permute-start | bytes 294920 | tf_op jit(solution)/shard_map/ppermute | solution.py:43
  33.5 0.8 %collective-permute-start.6 = (bf16[2,2,2,24,256]{4,3,2,1,0:T(8,128)(2,1)S(1)}, bf16[2,2,2,24,256]{4,3,2,1,0:T(8,128)(2,1)S(1)}, u32[]{:S(2)}, u32[]{:S(2)}) collective-permute-start(bf16[2,2,2,24,256]{4,3,2,1,0:T(8,128)(2,1)S(1)} %choose.1.refs_1_), channel_id=1, source_target_pairs={{0,2},{1,3},{2,0},{3,1},{4,6},{5,7},{6,4},{7,5},{8,10},{9,11},{10,... | collective-permute-start | bytes 294920 | tf_op jit(solution)/shard_map/ppermute | solution.py:43
  34.4 0.0 collective-permute-done.3.other
  34.4 0.1 right_side.1.refs_0_.refs_2_
  34.4 0.4 gram.3.refs_2_
  34.9 2.3 %collective-permute-done.7.refs_1_ = bf16[2,2,2,24,256]{4,3,2,1,0:T(8,128)(2,1)S(1)} collective-permute-done((bf16[2,2,2,24,256]{4,3,2,1,0:T(8,128)(2,1)S(1)}, bf16[2,2,2,24,256]{4,3,2,1,0:T(8,128)(2,1)S(1)}, u32[]{:S(2)}, u32[]{:S(2)}) %collective-permute-start.7) | collective-permute-done | bytes 98336 | tf_op jit(solution)/shard_map/ppermute | solution.py:43
  37.2 0.4 gram.4.refs_2_.refs_3_
  37.7 0.2 collective-permute-done.8.refs_1_
  37.9 0.4 gram.5.refs_4_
  38.3 0.0 collective-permute-done.6.refs_1_
  38.4 0.5 last_gram.1
  38.8 2.3 %collective-permute-start.10 = (bf16[192,96]{1,0:T(8,128)(2,1)S(1)}, bf16[192,96]{1,0:T(8,128)(2,1)S(1)}, u32[]{:S(2)}, u32[]{:S(2)}) collective-permute-start(bf16[192,96]{1,0:T(8,128)(2,1)S(1)} %get-tuple-element.17), channel_id=1, source_target_pairs={{0,64},{1,65},{2,66},{3,67},{4,68},{5,69},{6,70},{7,71},{8,72},{9,... | collective-permute-start | bytes 110600 | tf_op jit(solution)/shard_map/ppermute | solution.py:43
  41.2 0.0 collective-permute-start.11
  41.2 4.3 %collective-permute-start.9 = (bf16[192,96]{1,0:T(8,128)(2,1)S(1)}, bf16[192,96]{1,0:T(8,128)(2,1)S(1)}, u32[]{:S(2)}, u32[]{:S(2)}) collective-permute-start(bf16[192,96]{1,0:T(8,128)(2,1)S(1)} %get-tuple-element.16), channel_id=1, source_target_pairs={{0,32},{1,33},{2,34},{3,35},{4,36},{5,37},{6,38},{7,39},{8,40},{9,... | collective-permute-start | bytes 110600 | tf_op jit(solution)/shard_map/ppermute | solution.py:43
  45.4 2.7 %collective-permute-done.10 = bf16[192,96]{1,0:T(8,128)(2,1)S(1)} collective-permute-done((bf16[192,96]{1,0:T(8,128)(2,1)S(1)}, bf16[192,96]{1,0:T(8,128)(2,1)S(1)}, u32[]{:S(2)}, u32[]{:S(2)}) %collective-permute-start.10) | collective-permute-done | bytes 36896 | tf_op jit(solution)/shard_map/ppermute | solution.py:43
  48.1 0.0 collective-permute-done.11
  48.1 0.0 collective-permute-done.9
  48.2 0.7 %convert_add_fusion = f32[192,96]{1,0:T(8,128)} fusion(bf16[192,96]{1,0:T(8,128)(2,1)S(1)} %collective-permute-done.11, bf16[192,96]{1,0:T(8,128)(2,1)S(1)} %collective-permute-done.10, f32[192,96]{1,0:T(8,128)S(1)} %get-tuple-element.15, bf16[192,96]{1,0:T(8,128)(2,1)S(1)} %collective-permute-done.9), kind=kLoop, calls=%fused_computation | loop fusion | flops 110592 | bytes 258048 | tf_op jit(solution)/shard_map/add | solution.py:323
  (4 shorter events, 0.1 us)
Async XLA Ops:
  0.0 2.2 %copy-start.2 = (f32[8,2560]{1,0:T(8,128)S(1)}, f32[8,2560]{1,0:T(8,128)}, u32[]{:S(2)}) copy-start(f32[8,2560]{1,0:T(8,128)} %constant.2.clone.table.table_hbm) | copy-start | bytes 245764
  0.0 2.2 %copy-start.3 = (s32[32]{0:T(128)S(1)}, s32[32]{0:T(128)}, u32[]{:S(2)}) copy-start(s32[32]{0:T(128)} %fire_hbm.1) | copy-start | bytes 388
  2.1 9.9 %collective-permute-start = (f32[72,96]{1,0:T(8,128)}, f32[72,96]{1,0:T(8,128)S(1)}, u32[]{:S(2)}, u32[]{:S(2)}) collective-permute-start(f32[72,96]{1,0:T(8,128)} %tail_spectra.1), channel_id=1, source_target_pairs={{0,8},{1,9},{2,10},{3,11},{4,12},{5,13},{6,14},{7,15},{8,16},{9,17... | collective-permute-start | bytes 82952 | tf_op jit(solution)/shard_map/ppermute | solution.py:43
  2.2 1.4 %copy-start = (bf16[96,8192]{1,0:T(8,128)(2,1)S(1)}, bf16[96,8192]{1,0:T(8,128)(2,1)}, u32[]{:S(2)}) copy-start(bf16[96,8192]{1,0:T(8,128)(2,1)} %head.1) | copy-start | bytes 4718596
  3.6 8.3 %copy-start.1 = (bf16[96,8192]{1,0:T(8,128)(2,1)S(1)}, bf16[96,8192]{1,0:T(8,128)(2,1)}, u32[]{:S(2)}) copy-start(bf16[96,8192]{1,0:T(8,128)(2,1)} %head.1) | copy-start | bytes 4718596
  12.5 5.7 %collective-permute-start.1 = (bf16[4,24,256]{2,1,0:T(8,128)(2,1)S(1)}, bf16[4,24,256]{2,1,0:T(8,128)(2,1)S(1)}, u32[]{:S(2)}, u32[]{:S(2)}) collective-permute-start(bf16[4,24,256]{2,1,0:T(8,128)(2,1)S(1)} %finish_spectra.1.own), channel_id=1, source_target_pairs={{0,128},{1,129},{2,130},{3,131},{4,132},{5,133},{6,134},{7,135},{8... | collective-permute-start | bytes 147464 | tf_op jit(solution)/shard_map/ppermute | solution.py:43
  18.2 4.7 %collective-permute-start.2 = (bf16[2,4,24,256]{3,2,1,0:T(8,128)(2,1)S(1)}, bf16[2,4,24,256]{3,2,1,0:T(8,128)(2,1)S(1)}, u32[]{:S(2)}, u32[]{:S(2)}) collective-permute-start(bf16[2,4,24,256]{3,2,1,0:T(8,128)(2,1)S(1)} %join_yh.1.own), channel_id=1, source_target_pairs={{0,16},{1,17},{2,18},{3,19},{4,20},{5,21},{6,22},{7,23},{8,24},{9,... | collective-permute-start | bytes 294920 | tf_op jit(solution)/shard_map/ppermute | solution.py:43
  23.0 1.3 %collective-permute-start.4 = (bf16[2,2,24,256]{3,2,1,0:T(8,128)(2,1)S(1)}, bf16[2,2,24,256]{3,2,1,0:T(8,128)(2,1)S(1)}, u32[]{:S(2)}, u32[]{:S(2)}) collective-permute-start(bf16[2,2,24,256]{3,2,1,0:T(8,128)(2,1)S(1)} %get-tuple-element.14), channel_id=1, source_target_pairs={{0,8},{1,9},{2,10},{3,11},{4,12},{5,13},{6,14},{7,15},{8,0},{9,1},... | collective-permute-start | bytes 147464 | tf_op jit(solution)/shard_map/ppermute | solution.py:43
  23.1 11.3 %collective-permute-start.3 = (bf16[2,2,4,24,256]{4,3,2,1,0:T(8,128)(2,1)S(1)}, bf16[2,2,4,24,256]{4,3,2,1,0:T(8,128)(2,1)S(1)}, u32[]{:S(2)}, u32[]{:S(2)}) collective-permute-start(bf16[2,2,4,24,256]{4,3,2,1,0:T(8,128)(2,1)S(1)} %get-tuple-element.12.own), channel_id=1, source_target_pairs={{0,8},{1,9},{2,10},{3,11},{4,12},{5,13},{6,14},{7,15},{8,0},{9,1},... | collective-permute-start | bytes 589832 | tf_op jit(solution)/shard_map/ppermute | solution.py:43
  24.3 6.5 %collective-permute-start.5 = (bf16[2,2,2,24,256]{4,3,2,1,0:T(8,128)(2,1)S(1)}, bf16[2,2,2,24,256]{4,3,2,1,0:T(8,128)(2,1)S(1)}, u32[]{:S(2)}, u32[]{:S(2)}) collective-permute-start(bf16[2,2,2,24,256]{4,3,2,1,0:T(8,128)(2,1)S(1)} %join_core.1.own), channel_id=1, source_target_pairs={{0,4},{1,5},{2,6},{3,7},{4,0},{5,1},{6,2},{7,3},{8,12},{9,13},{10,... | collective-permute-start | bytes 294920 | tf_op jit(solution)/shard_map/ppermute | solution.py:43
  30.8 6.4 %collective-permute-start.7 = (bf16[2,2,2,24,256]{4,3,2,1,0:T(8,128)(2,1)S(1)}, bf16[2,2,2,24,256]{4,3,2,1,0:T(8,128)(2,1)S(1)}, u32[]{:S(2)}, u32[]{:S(2)}) collective-permute-start(bf16[2,2,2,24,256]{4,3,2,1,0:T(8,128)(2,1)S(1)} %choose.1.refs_1_), channel_id=1, source_target_pairs={{0,3},{1,2},{2,1},{3,0},{4,7},{5,6},{6,5},{7,4},{8,11},{9,10},{10,... | collective-permute-start | bytes 294920 | tf_op jit(solution)/shard_map/ppermute | solution.py:43
  32.2 5.7 %collective-permute-start.8 = (bf16[2,2,2,24,256]{4,3,2,1,0:T(8,128)(2,1)S(1)}, bf16[2,2,2,24,256]{4,3,2,1,0:T(8,128)(2,1)S(1)}, u32[]{:S(2)}, u32[]{:S(2)}) collective-permute-start(bf16[2,2,2,24,256]{4,3,2,1,0:T(8,128)(2,1)S(1)} %choose.1.refs_1_), channel_id=1, source_target_pairs={{0,1},{1,0},{2,3},{3,2},{4,5},{5,4},{6,7},{7,6},{8,9},{9,8},{10,11... | collective-permute-start | bytes 294920 | tf_op jit(solution)/shard_map/ppermute | solution.py:43
  33.5 4.8 %collective-permute-start.6 = (bf16[2,2,2,24,256]{4,3,2,1,0:T(8,128)(2,1)S(1)}, bf16[2,2,2,24,256]{4,3,2,1,0:T(8,128)(2,1)S(1)}, u32[]{:S(2)}, u32[]{:S(2)}) collective-permute-start(bf16[2,2,2,24,256]{4,3,2,1,0:T(8,128)(2,1)S(1)} %choose.1.refs_1_), channel_id=1, source_target_pairs={{0,2},{1,3},{2,0},{3,1},{4,6},{5,7},{6,4},{7,5},{8,10},{9,11},{10,... | collective-permute-start | bytes 294920 | tf_op jit(solution)/shard_map/ppermute | solution.py:43
  38.8 9.3 %collective-permute-start.10 = (bf16[192,96]{1,0:T(8,128)(2,1)S(1)}, bf16[192,96]{1,0:T(8,128)(2,1)S(1)}, u32[]{:S(2)}, u32[]{:S(2)}) collective-permute-start(bf16[192,96]{1,0:T(8,128)(2,1)S(1)} %get-tuple-element.17), channel_id=1, source_target_pairs={{0,64},{1,65},{2,66},{3,67},{4,68},{5,69},{6,70},{7,71},{8,72},{9,... | collective-permute-start | bytes 110600 | tf_op jit(solution)/shard_map/ppermute | solution.py:43
  41.2 7.0 %collective-permute-start.11 = (bf16[192,96]{1,0:T(8,128)(2,1)S(1)}, bf16[192,96]{1,0:T(8,128)(2,1)S(1)}, u32[]{:S(2)}, u32[]{:S(2)}) collective-permute-start(bf16[192,96]{1,0:T(8,128)(2,1)S(1)} %get-tuple-element.18), channel_id=1, source_target_pairs={{0,96},{1,97},{2,98},{3,99},{4,100},{5,101},{6,102},{7,103},{8,104... | collective-permute-start | bytes 110600 | tf_op jit(solution)/shard_map/ppermute | solution.py:43
  41.2 7.0 %collective-permute-start.9 = (bf16[192,96]{1,0:T(8,128)(2,1)S(1)}, bf16[192,96]{1,0:T(8,128)(2,1)S(1)}, u32[]{:S(2)}, u32[]{:S(2)}) collective-permute-start(bf16[192,96]{1,0:T(8,128)(2,1)S(1)} %get-tuple-element.16), channel_id=1, source_target_pairs={{0,32},{1,33},{2,34},{3,35},{4,36},{5,37},{6,38},{7,39},{8,40},{9,... | collective-permute-start | bytes 110600 | tf_op jit(solution)/shard_map/ppermute | solution.py:43

commit v7 on v6

--- a/solution.py
+++ b/solution.py
@@ -54,8 +54,10 @@
     return [pl.BlockSpec(memory_space=pltpu.VMEM)] * count
 
 
-def pair_tables(table, first, second):
-    rows = [pltpu.roll(table, first, 1), pltpu.roll(table, second + SPACING, 1)]
+def pair_tables(table, first, second, length=SPAN):
+    if length < SPAN:
+        table = jnp.concatenate([table[:, :length], jnp.zeros((ROWS, PAIR), table.dtype)], axis=1)
+    rows = [pltpu.roll(table, first, 1)[:, :length], pltpu.roll(table, second + SPACING, 1)[:, :length]]
     return jnp.concatenate(rows, axis=0).astype(jnp.bfloat16)
 
 
@@ -97,7 +99,8 @@
     master = table[...]
     for p in range(late):
         shot = 2 * (pairs - late + p)
-        tables[p] = pair_tables(master, delay(fire, shot), delay(fire, shot + 1))
+        length = PAIR * (late - p)
+        tables[p, :, :length] = pair_tables(master, delay(fire, shot), delay(fire, shot + 1), length)
     copies[2].wait()
     blocks = [(pairs - late + v, samples[:, PAIR * v : PAIR * (v + 1)]) for v in range(late)]
     add_products(message, tables, pairs - late, blocks)
@@ -249,8 +252,7 @@
             pltpu.VMEM((receivers, WIN), bf16),
             pltpu.SemaphoreType.DMA((3,)),
         ],
-        limit=63,
-    )(shot_fire_samples, table, record)
+    )(*(pltpu.with_memory_space_constraint(a, pltpu.HBM) for a in (shot_fire_samples, table, record)))
 
     def following(yh, u, k, xh, v):
         shot = ((yh << 4 | u << 2 | k) + 1) % SHOT_DEVICES

time: 48.9 us -> 48 us (0.982)
  local copies, waits for them, and re-layouts: 1.41 us -> 0.06 us
  waiting for transfers between devices: 28.2 us -> 29.3 us
  Pallas kernels: 6.22 us -> 5.59 us
    unnamed x8 -> x6, local copies, waits for them, and re-layouts: 1.41 us -> 0.06 us
    ppermute x12, waiting for transfers between devices: 28.2 us -> 29.3 us  [send(): return lax.ppermute(block, ('shot', 'rcv'), route)]
    pallas_call x1, Pallas kernels: 2.06 us -> 1.44 us  [per_device(): local(tail_kernel, 'tail_spectra', shape((late_rows + LATE, receivers), f...]
where the time goes in v7:
time: 48 us; the launch traced here: 47.9 us
  waiting for transfers between devices  29.3 us (61%)
  starting transfers between devices  12.2 us (25%)
  Pallas kernels  5.59 us (12%)
  other arithmetic  0.67 us (1%)
    ppermute x12, waiting for transfers between devices, send(): return lax.ppermute(block, ('shot', 'rcv'), route)  29.3 us
    ppermute x12, starting transfers between devices, send(): return lax.ppermute(block, ('shot', 'rcv'), route)  12.2 us
    pallas_call x1, Pallas kernels, per_device(): local(own_kernel, 'own_spectra', shape((lanes - late_rows, receivers), f3...  1.58 us
    pallas_call x1, Pallas kernels, per_device(): local(tail_kernel, 'tail_spectra', shape((late_rows + LATE, receivers), f...  1.44 us
    pallas_call x3, Pallas kernels, per_device(): local(lambda *refs: gram_kernel(scale, *refs), 'gram', share, vmem(2) + [...  1.33 us
  transfers between devices with their start and end apart: 12, of which 8 were waited for; matrix products, arithmetic and copies ran while one was open for 0% of the time, Pallas kernels for 6%

profile of v7, /device:TPU:4, one launch (start us, length us, event | category | flops | bytes accessed | tf_op | source)
XLA Modules:
  0.0 47.9 jit_solution(18049241479114896115)
XLA Ops:
  0.0 0.0 copy-start.1
  0.0 0.0 copy-start
  0.0 0.0 copy-start.2
  0.0 1.4 %tail_spectra.1 = f32[72,96]{1,0:T(8,128)S(1)} custom-call(s32[32]{0:T(128)} %fire_hbm.1, f32[8,2560]{1,0:T(8,128)} %constant.2.clone.table.table_hbm, bf16[96,8192]{1,0:T(8,128)(2,1)} %head.1), custom_call_target="tpu_custom_call" | custom-call | tf_op jit(solution)/shard_map/tail_spectra/pallas_call | solution.py:243
  1.5 0.1 collective-permute-start
  1.6 0.0 copy-done.1
  1.6 0.1 copy-done
  1.6 0.0 copy-done.2
  1.6 1.6 %own_spectra.1.total = f32[192,96]{1,0:T(8,128)S(1)} custom-call(s32[32]{0:T(128)S(1)} %copy-done.2, f32[8,2560]{1,0:T(8,128)S(1)} %copy-done.1, bf16[96,8192]{1,0:T(8,128)(2,1)S(1)} %copy-done), custom_call_target="tpu_custom_call" | custom-call | tf_op jit(solution)/shard_map/own_spectra/pallas_call | solution.py:262
  3.2 7.9 %collective-permute-done.message = f32[72,96]{1,0:T(8,128)S(1)} collective-permute-done((f32[72,96]{1,0:T(8,128)S(1)}, f32[72,96]{1,0:T(8,128)S(1)}, u32[]{:S(2)}, u32[]{:S(2)}) %collective-permute-start) | collective-permute-done | bytes 27680 | tf_op jit(solution)/shard_map/ppermute | solution.py:43
  11.1 0.6 %finish_spectra.1.own = bf16[4,24,256]{2,1,0:T(8,128)(2,1)S(1)} custom-call(f32[192,96]{1,0:T(8,128)S(1)} %own_spectra.1.total, bf16[96,8192]{1,0:T(8,128)(2,1)S(1)} %copy-done, f32[8,2560]{1,0:T(8,128)S(1)} %copy-done.1, f32[72,96]{1,0:T(8,128)S(1)} %collective-permute-done.message), custom_call_target="tpu_custom_call" | custom-call | tf_op jit(solution)/shard_map/finish_spectra/pallas_call | solution.py:269
  11.7 0.7 %collective-permute-start.1 = (bf16[4,24,256]{2,1,0:T(8,128)(2,1)S(1)}, bf16[4,24,256]{2,1,0:T(8,128)(2,1)S(1)}, u32[]{:S(2)}, u32[]{:S(2)}) collective-permute-start(bf16[4,24,256]{2,1,0:T(8,128)(2,1)S(1)} %finish_spectra.1.own), channel_id=1, source_target_pairs={{0,128},{1,129},{2,130},{3,131},{4,132},{5,133},{6,134},{7,135},{8... | collective-permute-start | bytes 147464 | tf_op jit(solution)/shard_map/ppermute | solution.py:43
  12.4 5.0 %collective-permute-done.1.other = bf16[4,24,256]{2,1,0:T(8,128)(2,1)S(1)} collective-permute-done((bf16[4,24,256]{2,1,0:T(8,128)(2,1)S(1)}, bf16[4,24,256]{2,1,0:T(8,128)(2,1)S(1)}, u32[]{:S(2)}, u32[]{:S(2)}) %collective-permute-start.1) | collective-permute-done | bytes 49184 | tf_op jit(solution)/shard_map/ppermute | solution.py:43
  17.4 0.1 collective-permute-start.2
  17.5 4.6 %collective-permute-done.2.other = bf16[2,4,24,256]{3,2,1,0:T(8,128)(2,1)S(1)} collective-permute-done((bf16[2,4,24,256]{3,2,1,0:T(8,128)(2,1)S(1)}, bf16[2,4,24,256]{3,2,1,0:T(8,128)(2,1)S(1)}, u32[]{:S(2)}, u32[]{:S(2)}) %collective-permute-start.2) | collective-permute-done | bytes 98336 | tf_op jit(solution)/shard_map/ppermute | solution.py:43
  22.2 0.1 collective-permute-start.4
  22.3 0.5 %collective-permute-start.3 = (bf16[2,2,4,24,256]{4,3,2,1,0:T(8,128)(2,1)S(1)}, bf16[2,2,4,24,256]{4,3,2,1,0:T(8,128)(2,1)S(1)}, u32[]{:S(2)}, u32[]{:S(2)}) collective-permute-start(bf16[2,2,4,24,256]{4,3,2,1,0:T(8,128)(2,1)S(1)} %get-tuple-element.12.own), channel_id=1, source_target_pairs={{0,8},{1,9},{2,10},{3,11},{4,12},{5,13},{6,14},{7,15},{8,0},{9,1},... | collective-permute-start | bytes 589832 | tf_op jit(solution)/shard_map/ppermute | solution.py:43
  22.8 0.7 %collective-permute-done.4.other = bf16[2,2,24,256]{3,2,1,0:T(8,128)(2,1)S(1)} collective-permute-done((bf16[2,2,24,256]{3,2,1,0:T(8,128)(2,1)S(1)}, bf16[2,2,24,256]{3,2,1,0:T(8,128)(2,1)S(1)}, u32[]{:S(2)}, u32[]{:S(2)}) %collective-permute-start.4) | collective-permute-done | bytes 49184 | tf_op jit(solution)/shard_map/ppermute | solution.py:43
  23.5 0.6 %collective-permute-start.5 = (bf16[2,2,2,24,256]{4,3,2,1,0:T(8,128)(2,1)S(1)}, bf16[2,2,2,24,256]{4,3,2,1,0:T(8,128)(2,1)S(1)}, u32[]{:S(2)}, u32[]{:S(2)}) collective-permute-start(bf16[2,2,2,24,256]{4,3,2,1,0:T(8,128)(2,1)S(1)} %join_core.1.own), channel_id=1, source_target_pairs={{0,4},{1,5},{2,6},{3,7},{4,0},{5,1},{6,2},{7,3},{8,12},{9,13},{10,... | collective-permute-start | bytes 294920 | tf_op jit(solution)/shard_map/ppermute | solution.py:43
  24.1 5.9 %collective-permute-done.5.cross = bf16[2,2,2,24,256]{4,3,2,1,0:T(8,128)(2,1)S(1)} collective-permute-done((bf16[2,2,2,24,256]{4,3,2,1,0:T(8,128)(2,1)S(1)}, bf16[2,2,2,24,256]{4,3,2,1,0:T(8,128)(2,1)S(1)}, u32[]{:S(2)}, u32[]{:S(2)}) %collective-permute-start.5) | collective-permute-done | bytes 98336 | tf_op jit(solution)/shard_map/ppermute | solution.py:43
  30.0 1.4 %collective-permute-start.7 = (bf16[2,2,2,24,256]{4,3,2,1,0:T(8,128)(2,1)S(1)}, bf16[2,2,2,24,256]{4,3,2,1,0:T(8,128)(2,1)S(1)}, u32[]{:S(2)}, u32[]{:S(2)}) collective-permute-start(bf16[2,2,2,24,256]{4,3,2,1,0:T(8,128)(2,1)S(1)} %choose.1.refs_1_), channel_id=1, source_target_pairs={{0,3},{1,2},{2,1},{3,0},{4,7},{5,6},{6,5},{7,4},{8,11},{9,10},{10,... | collective-permute-start | bytes 294920 | tf_op jit(solution)/shard_map/ppermute | solution.py:43
  31.4 1.3 %collective-permute-start.8 = (bf16[2,2,2,24,256]{4,3,2,1,0:T(8,128)(2,1)S(1)}, bf16[2,2,2,24,256]{4,3,2,1,0:T(8,128)(2,1)S(1)}, u32[]{:S(2)}, u32[]{:S(2)}) collective-permute-start(bf16[2,2,2,24,256]{4,3,2,1,0:T(8,128)(2,1)S(1)} %choose.1.refs_1_), channel_id=1, source_target_pairs={{0,1},{1,0},{2,3},{3,2},{4,5},{5,4},{6,7},{7,6},{8,9},{9,8},{10,11... | collective-permute-start | bytes 294920 | tf_op jit(solution)/shard_map/ppermute | solution.py:43
  32.7 0.8 %collective-permute-start.6 = (bf16[2,2,2,24,256]{4,3,2,1,0:T(8,128)(2,1)S(1)}, bf16[2,2,2,24,256]{4,3,2,1,0:T(8,128)(2,1)S(1)}, u32[]{:S(2)}, u32[]{:S(2)}) collective-permute-start(bf16[2,2,2,24,256]{4,3,2,1,0:T(8,128)(2,1)S(1)} %choose.1.refs_1_), channel_id=1, source_target_pairs={{0,2},{1,3},{2,0},{3,1},{4,6},{5,7},{6,4},{7,5},{8,10},{9,11},{10,... | collective-permute-start | bytes 294920 | tf_op jit(solution)/shard_map/ppermute | solution.py:43
  33.5 0.0 collective-permute-done.3.other
  33.5 0.1 right_side.1.refs_0_.refs_2_
  33.6 0.4 gram.3.refs_2_
  34.1 2.3 %collective-permute-done.7.refs_1_ = bf16[2,2,2,24,256]{4,3,2,1,0:T(8,128)(2,1)S(1)} collective-permute-done((bf16[2,2,2,24,256]{4,3,2,1,0:T(8,128)(2,1)S(1)}, bf16[2,2,2,24,256]{4,3,2,1,0:T(8,128)(2,1)S(1)}, u32[]{:S(2)}, u32[]{:S(2)}) %collective-permute-start.7) | collective-permute-done | bytes 98336 | tf_op jit(solution)/shard_map/ppermute | solution.py:43
  36.4 0.4 gram.4.refs_2_.refs_3_
  36.9 0.2 collective-permute-done.8.refs_1_
  37.1 0.4 gram.5.refs_4_
  37.5 0.0 collective-permute-done.6.refs_1_
  37.5 0.5 %last_gram.1 = (f32[192,96]{1,0:T(8,128)S(1)}, bf16[192,96]{1,0:T(8,128)(2,1)S(1)}, bf16[192,96]{1,0:T(8,128)(2,1)S(1)}, bf16[192,96]{1,0:T(8,128)(2,1)S(1)}) custom-call(bf16[8,192,256]{2,1,0:T(8,128)(2,1)S(1)} %right_side.1.refs_0_.refs_2_, bf16[2,2,2,24,256]{4,3,2,1,0:T(8,128)(2,1)S(1)} %collective-permute-done.6.refs_1_, f32[192,96]{1,0:T(8,128)S(1)} %gram.3.refs_2_, ...), custom_call_target="tpu_custom_call" | custom-call | tf_op jit(solution)/shard_map/last_gram/pallas_call | solution.py:317
  38.0 2.3 %collective-permute-start.10 = (bf16[192,96]{1,0:T(8,128)(2,1)S(1)}, bf16[192,96]{1,0:T(8,128)(2,1)S(1)}, u32[]{:S(2)}, u32[]{:S(2)}) collective-permute-start(bf16[192,96]{1,0:T(8,128)(2,1)S(1)} %get-tuple-element.17), channel_id=1, source_target_pairs={{0,64},{1,65},{2,66},{3,67},{4,68},{5,69},{6,70},{7,71},{8,72},{9,... | collective-permute-start | bytes 110600 | tf_op jit(solution)/shard_map/ppermute | solution.py:43
  40.3 0.0 collective-permute-start.11
  40.3 4.3 %collective-permute-start.9 = (bf16[192,96]{1,0:T(8,128)(2,1)S(1)}, bf16[192,96]{1,0:T(8,128)(2,1)S(1)}, u32[]{:S(2)}, u32[]{:S(2)}) collective-permute-start(bf16[192,96]{1,0:T(8,128)(2,1)S(1)} %get-tuple-element.16), channel_id=1, source_target_pairs={{0,32},{1,33},{2,34},{3,35},{4,36},{5,37},{6,38},{7,39},{8,40},{9,... | collective-permute-start | bytes 110600 | tf_op jit(solution)/shard_map/ppermute | solution.py:43
  44.6 2.6 %collective-permute-done.10 = bf16[192,96]{1,0:T(8,128)(2,1)S(1)} collective-permute-done((bf16[192,96]{1,0:T(8,128)(2,1)S(1)}, bf16[192,96]{1,0:T(8,128)(2,1)S(1)}, u32[]{:S(2)}, u32[]{:S(2)}) %collective-permute-start.10) | collective-permute-done | bytes 36896 | tf_op jit(solution)/shard_map/ppermute | solution.py:43
  47.3 0.0 collective-permute-done.11
  47.3 0.0 collective-permute-done.9
  47.3 0.7 %convert_add_fusion = f32[192,96]{1,0:T(8,128)} fusion(bf16[192,96]{1,0:T(8,128)(2,1)S(1)} %collective-permute-done.11, bf16[192,96]{1,0:T(8,128)(2,1)S(1)} %collective-permute-done.10, f32[192,96]{1,0:T(8,128)S(1)} %get-tuple-element.15, bf16[192,96]{1,0:T(8,128)(2,1)S(1)} %collective-permute-done.9), kind=kLoop, calls=%fused_computation | loop fusion | flops 110592 | bytes 258048 | tf_op jit(solution)/shard_map/add | solution.py:325
  (4 shorter events, 0.1 us)
Async XLA Ops:
  0.0 1.6 %copy-start.1 = (f32[8,2560]{1,0:T(8,128)S(1)}, f32[8,2560]{1,0:T(8,128)}, u32[]{:S(2)}) copy-start(f32[8,2560]{1,0:T(8,128)} %constant.2.clone.table.table_hbm) | copy-start | bytes 245764
  0.0 1.6 %copy-start = (bf16[96,8192]{1,0:T(8,128)(2,1)S(1)}, bf16[96,8192]{1,0:T(8,128)(2,1)}, u32[]{:S(2)}) copy-start(bf16[96,8192]{1,0:T(8,128)(2,1)} %head.1) | copy-start | bytes 4718596
  0.0 1.6 %copy-start.2 = (s32[32]{0:T(128)S(1)}, s32[32]{0:T(128)}, u32[]{:S(2)}) copy-start(s32[32]{0:T(128)} %fire_hbm.1) | copy-start | bytes 388
  1.5 9.6 %collective-permute-start = (f32[72,96]{1,0:T(8,128)S(1)}, f32[72,96]{1,0:T(8,128)S(1)}, u32[]{:S(2)}, u32[]{:S(2)}) collective-permute-start(f32[72,96]{1,0:T(8,128)S(1)} %tail_spectra.1), channel_id=1, source_target_pairs={{0,8},{1,9},{2,10},{3,11},{4,12},{5,13},{6,14},{7,15},{8,16},{9,17... | collective-permute-start | bytes 82952 | tf_op jit(solution)/shard_map/ppermute | solution.py:43
  11.7 5.7 %collective-permute-start.1 = (bf16[4,24,256]{2,1,0:T(8,128)(2,1)S(1)}, bf16[4,24,256]{2,1,0:T(8,128)(2,1)S(1)}, u32[]{:S(2)}, u32[]{:S(2)}) collective-permute-start(bf16[4,24,256]{2,1,0:T(8,128)(2,1)S(1)} %finish_spectra.1.own), channel_id=1, source_target_pairs={{0,128},{1,129},{2,130},{3,131},{4,132},{5,133},{6,134},{7,135},{8... | collective-permute-start | bytes 147464 | tf_op jit(solution)/shard_map/ppermute | solution.py:43
  17.4 4.7 %collective-permute-start.2 = (bf16[2,4,24,256]{3,2,1,0:T(8,128)(2,1)S(1)}, bf16[2,4,24,256]{3,2,1,0:T(8,128)(2,1)S(1)}, u32[]{:S(2)}, u32[]{:S(2)}) collective-permute-start(bf16[2,4,24,256]{3,2,1,0:T(8,128)(2,1)S(1)} %join_yh.1.own), channel_id=1, source_target_pairs={{0,16},{1,17},{2,18},{3,19},{4,20},{5,21},{6,22},{7,23},{8,24},{9,... | collective-permute-start | bytes 294920 | tf_op jit(solution)/shard_map/ppermute | solution.py:43
  22.2 1.3 %collective-permute-start.4 = (bf16[2,2,24,256]{3,2,1,0:T(8,128)(2,1)S(1)}, bf16[2,2,24,256]{3,2,1,0:T(8,128)(2,1)S(1)}, u32[]{:S(2)}, u32[]{:S(2)}) collective-permute-start(bf16[2,2,24,256]{3,2,1,0:T(8,128)(2,1)S(1)} %get-tuple-element.14), channel_id=1, source_target_pairs={{0,8},{1,9},{2,10},{3,11},{4,12},{5,13},{6,14},{7,15},{8,0},{9,1},... | collective-permute-start | bytes 147464 | tf_op jit(solution)/shard_map/ppermute | solution.py:43
  22.3 11.3 %collective-permute-start.3 = (bf16[2,2,4,24,256]{4,3,2,1,0:T(8,128)(2,1)S(1)}, bf16[2,2,4,24,256]{4,3,2,1,0:T(8,128)(2,1)S(1)}, u32[]{:S(2)}, u32[]{:S(2)}) collective-permute-start(bf16[2,2,4,24,256]{4,3,2,1,0:T(8,128)(2,1)S(1)} %get-tuple-element.12.own), channel_id=1, source_target_pairs={{0,8},{1,9},{2,10},{3,11},{4,12},{5,13},{6,14},{7,15},{8,0},{9,1},... | collective-permute-start | bytes 589832 | tf_op jit(solution)/shard_map/ppermute | solution.py:43
  23.5 6.5 %collective-permute-start.5 = (bf16[2,2,2,24,256]{4,3,2,1,0:T(8,128)(2,1)S(1)}, bf16[2,2,2,24,256]{4,3,2,1,0:T(8,128)(2,1)S(1)}, u32[]{:S(2)}, u32[]{:S(2)}) collective-permute-start(bf16[2,2,2,24,256]{4,3,2,1,0:T(8,128)(2,1)S(1)} %join_core.1.own), channel_id=1, source_target_pairs={{0,4},{1,5},{2,6},{3,7},{4,0},{5,1},{6,2},{7,3},{8,12},{9,13},{10,... | collective-permute-start | bytes 294920 | tf_op jit(solution)/shard_map/ppermute | solution.py:43
  30.0 6.5 %collective-permute-start.7 = (bf16[2,2,2,24,256]{4,3,2,1,0:T(8,128)(2,1)S(1)}, bf16[2,2,2,24,256]{4,3,2,1,0:T(8,128)(2,1)S(1)}, u32[]{:S(2)}, u32[]{:S(2)}) collective-permute-start(bf16[2,2,2,24,256]{4,3,2,1,0:T(8,128)(2,1)S(1)} %choose.1.refs_1_), channel_id=1, source_target_pairs={{0,3},{1,2},{2,1},{3,0},{4,7},{5,6},{6,5},{7,4},{8,11},{9,10},{10,... | collective-permute-start | bytes 294920 | tf_op jit(solution)/shard_map/ppermute | solution.py:43
  31.4 5.7 %collective-permute-start.8 = (bf16[2,2,2,24,256]{4,3,2,1,0:T(8,128)(2,1)S(1)}, bf16[2,2,2,24,256]{4,3,2,1,0:T(8,128)(2,1)S(1)}, u32[]{:S(2)}, u32[]{:S(2)}) collective-permute-start(bf16[2,2,2,24,256]{4,3,2,1,0:T(8,128)(2,1)S(1)} %choose.1.refs_1_), channel_id=1, source_target_pairs={{0,1},{1,0},{2,3},{3,2},{4,5},{5,4},{6,7},{7,6},{8,9},{9,8},{10,11... | collective-permute-start | bytes 294920 | tf_op jit(solution)/shard_map/ppermute | solution.py:43
  32.7 4.8 %collective-permute-start.6 = (bf16[2,2,2,24,256]{4,3,2,1,0:T(8,128)(2,1)S(1)}, bf16[2,2,2,24,256]{4,3,2,1,0:T(8,128)(2,1)S(1)}, u32[]{:S(2)}, u32[]{:S(2)}) collective-permute-start(bf16[2,2,2,24,256]{4,3,2,1,0:T(8,128)(2,1)S(1)} %choose.1.refs_1_), channel_id=1, source_target_pairs={{0,2},{1,3},{2,0},{3,1},{4,6},{5,7},{6,4},{7,5},{8,10},{9,11},{10,... | collective-permute-start | bytes 294920 | tf_op jit(solution)/shard_map/ppermute | solution.py:43
  38.0 9.2 %collective-permute-start.10 = (bf16[192,96]{1,0:T(8,128)(2,1)S(1)}, bf16[192,96]{1,0:T(8,128)(2,1)S(1)}, u32[]{:S(2)}, u32[]{:S(2)}) collective-permute-start(bf16[192,96]{1,0:T(8,128)(2,1)S(1)} %get-tuple-element.17), channel_id=1, source_target_pairs={{0,64},{1,65},{2,66},{3,67},{4,68},{5,69},{6,70},{7,71},{8,72},{9,... | collective-permute-start | bytes 110600 | tf_op jit(solution)/shard_map/ppermute | solution.py:43
  40.3 6.9 %collective-permute-start.11 = (bf16[192,96]{1,0:T(8,128)(2,1)S(1)}, bf16[192,96]{1,0:T(8,128)(2,1)S(1)}, u32[]{:S(2)}, u32[]{:S(2)}) collective-permute-start(bf16[192,96]{1,0:T(8,128)(2,1)S(1)} %get-tuple-element.18), channel_id=1, source_target_pairs={{0,96},{1,97},{2,98},{3,99},{4,100},{5,101},{6,102},{7,103},{8,104... | collective-permute-start | bytes 110600 | tf_op jit(solution)/shard_map/ppermute | solution.py:43
  40.3 6.9 %collective-permute-start.9 = (bf16[192,96]{1,0:T(8,128)(2,1)S(1)}, bf16[192,96]{1,0:T(8,128)(2,1)S(1)}, u32[]{:S(2)}, u32[]{:S(2)}) collective-permute-start(bf16[192,96]{1,0:T(8,128)(2,1)S(1)} %get-tuple-element.16), channel_id=1, source_target_pairs={{0,32},{1,33},{2,34},{3,35},{4,36},{5,37},{6,38},{7,39},{8,40},{9,... | collective-permute-start | bytes 110600 | tf_op jit(solution)/shard_map/ppermute | solution.py:43

commit v8 on v7

--- a/solution.py
+++ b/solution.py
@@ -143,19 +143,15 @@
         out[k] = turned[count * k : count * (k + 1), :].astype(out.dtype)
 
 
-def yh_kernel(own, other, out):
-    yh = shot_index() >> 4
-    out[yh] = own[...]
-    out[1 - yh] = other[...]
-
-
-def z0_kernel(own, other, out, mine, theirs):
-    k = shot_index() & 3
+def join_kernel(y3, y2, y1, y0, out, mine, theirs):
+    shot = shot_index()
+    yh, k = shot >> 4, shot & 3
     z0 = k >> 1
-    for here, block in ((z0, own), (1 - z0, other)):
-        out[here] = block[...]
-        mine[here] = block[:, k]
-        theirs[here] = block[:, k ^ 1]
+    for m, block in enumerate((y0, y1, y2, y3)):
+        place = z0 ^ (m & 1), yh ^ (m >> 1)
+        out[place] = block[...]
+        mine[place] = block[k]
+        theirs[place] = block[k ^ 1]
 
 
 def core_kernel(own, other, out):
@@ -282,11 +278,11 @@
         name="finish_spectra",
     )(total, record, table, received)
 
-    other = send(y, lambda yh, u, k, xh, v: (1 - yh, u, k, xh, v))
-    y = local(yh_kernel, "join_yh", shape((2,) + y.shape, bf16), vmem(2))(y, other)
-    other = send(y, lambda yh, u, k, xh, v: (yh, u, k ^ 2, xh, v))
+    y3, y2, y1 = [send(y, lambda yh, u, k, xh, v, m=m: (yh ^ m >> 1, u, k ^ (m & 1) << 1, xh, v)) for m in (3, 2, 1)]
     slices = shape((2, 2, count, lanes), bf16)
-    y, mine, theirs = local(z0_kernel, "join_z0", (shape((2,) + y.shape, bf16), slices, slices), vmem(2))(y, other)
+    y, mine, theirs = local(join_kernel, "join", (shape((2, 2) + y.shape, bf16), slices, slices), vmem(4))(
+        y3, y2, y1, y
+    )
 
     def to_partner(yh, u, k, xh, v):
         return yh, u, k ^ 1, xh, v

time: 48 us -> 46.5 us (0.969)
  waiting for transfers between devices: 29.3 us -> 23.5 us
  starting transfers between devices: 12.2 us -> 16.5 us
    ppermute x12 -> x13, waiting for transfers between devices: 29.3 us -> 23.5 us  [send(): return lax.ppermute(block, ('shot', 'rcv'), route)]
    ppermute x12 -> x13, starting transfers between devices: 12.2 us -> 16.5 us  [send(): return lax.ppermute(block, ('shot', 'rcv'), route)]
  transfers between devices with their start and end apart: 12 -> 13, of which waited for: 8 -> 9; matrix products, arithmetic and copies ran while one was open for 0% -> 0% of each run, Pallas kernels for 6% -> 7%
where the time goes in v8:
time: 46.5 us; the launch traced here: 46.4 us
  waiting for transfers between devices  23.5 us (51%)
  starting transfers between devices  16.5 us (35%)
  Pallas kernels  5.58 us (12%)
  other arithmetic  0.66 us (1%)
    ppermute x13, waiting for transfers between devices, send(): return lax.ppermute(block, ('shot', 'rcv'), route)  23.5 us
    ppermute x13, starting transfers between devices, send(): return lax.ppermute(block, ('shot', 'rcv'), route)  16.5 us
    pallas_call x1, Pallas kernels, per_device(): local(own_kernel, 'own_spectra', shape((lanes - late_rows, receivers), f3...  1.58 us
    pallas_call x1, Pallas kernels, per_device(): local(tail_kernel, 'tail_spectra', shape((late_rows + LATE, receivers), f...  1.44 us
    pallas_call x3, Pallas kernels, per_device(): local(lambda *refs: gram_kernel(scale, *refs), 'gram', share, vmem(2) + [...  1.34 us
  transfers between devices with their start and end apart: 13, of which 9 were waited for; matrix products, arithmetic and copies ran while one was open for 0% of the time, Pallas kernels for 7%

profile of v8, /device:TPU:4, one launch (start us, length us, event | category | flops | bytes accessed | tf_op | source)
XLA Modules:
  0.0 46.4 jit_solution(12600615373744824741)
XLA Ops:
  0.0 0.0 copy-start.1
  0.0 0.0 copy-start
  0.0 0.0 copy-start.2
  0.0 1.4 %tail_spectra.1 = f32[72,96]{1,0:T(8,128)S(1)} custom-call(s32[32]{0:T(128)} %fire_hbm.1, f32[8,2560]{1,0:T(8,128)} %constant.2.clone.table.table_hbm, bf16[96,8192]{1,0:T(8,128)(2,1)} %head.1), custom_call_target="tpu_custom_call" | custom-call | tf_op jit(solution)/shard_map/tail_spectra/pallas_call | solution.py:239
  1.5 0.1 collective-permute-start
  1.6 0.0 copy-done.1
  1.6 0.1 copy-done
  1.6 0.0 copy-done.2
  1.6 1.6 %own_spectra.1.total = f32[192,96]{1,0:T(8,128)S(1)} custom-call(s32[32]{0:T(128)S(1)} %copy-done.2, f32[8,2560]{1,0:T(8,128)S(1)} %copy-done.1, bf16[96,8192]{1,0:T(8,128)(2,1)S(1)} %copy-done), custom_call_target="tpu_custom_call" | custom-call | tf_op jit(solution)/shard_map/own_spectra/pallas_call | solution.py:258
  3.2 7.9 %collective-permute-done.message = f32[72,96]{1,0:T(8,128)S(1)} collective-permute-done((f32[72,96]{1,0:T(8,128)S(1)}, f32[72,96]{1,0:T(8,128)S(1)}, u32[]{:S(2)}, u32[]{:S(2)}) %collective-permute-start) | collective-permute-done | bytes 27680 | tf_op jit(solution)/shard_map/ppermute | solution.py:43
  11.1 0.6 %finish_spectra.1.y0 = bf16[4,24,256]{2,1,0:T(8,128)(2,1)S(1)} custom-call(f32[192,96]{1,0:T(8,128)S(1)} %own_spectra.1.total, bf16[96,8192]{1,0:T(8,128)(2,1)S(1)} %copy-done, f32[8,2560]{1,0:T(8,128)S(1)} %copy-done.1, f32[72,96]{1,0:T(8,128)S(1)} %collective-permute-done.message), custom_call_target="tpu_custom_call" | custom-call | tf_op jit(solution)/shard_map/finish_spectra/pallas_call | solution.py:265
  11.7 0.1 collective-permute-start.1
  11.8 0.7 %collective-permute-start.2 = (bf16[4,24,256]{2,1,0:T(8,128)(2,1)S(1)}, bf16[4,24,256]{2,1,0:T(8,128)(2,1)S(1)}, u32[]{:S(2)}, u32[]{:S(2)}) collective-permute-start(bf16[4,24,256]{2,1,0:T(8,128)(2,1)S(1)} %finish_spectra.1.y0), channel_id=1, source_target_pairs={{0,128},{1,129},{2,130},{3,131},{4,132},{5,133},{6,134},{7,135},{8... | collective-permute-start | bytes 147464 | tf_op jit(solution)/shard_map/ppermute | solution.py:43
  12.5 4.3 %collective-permute-start.3 = (bf16[4,24,256]{2,1,0:T(8,128)(2,1)S(1)}, bf16[4,24,256]{2,1,0:T(8,128)(2,1)S(1)}, u32[]{:S(2)}, u32[]{:S(2)}) collective-permute-start(bf16[4,24,256]{2,1,0:T(8,128)(2,1)S(1)} %finish_spectra.1.y0), channel_id=1, source_target_pairs={{0,16},{1,17},{2,18},{3,19},{4,20},{5,21},{6,22},{7,23},{8,24},{9,... | collective-permute-start | bytes 147464 | tf_op jit(solution)/shard_map/ppermute | solution.py:43
  16.8 1.5 %collective-permute-done.1.y3 = bf16[4,24,256]{2,1,0:T(8,128)(2,1)S(1)} collective-permute-done((bf16[4,24,256]{2,1,0:T(8,128)(2,1)S(1)}, bf16[4,24,256]{2,1,0:T(8,128)(2,1)S(1)}, u32[]{:S(2)}, u32[]{:S(2)}) %collective-permute-start.1) | collective-permute-done | bytes 49184 | tf_op jit(solution)/shard_map/ppermute | solution.py:43
  18.3 0.0 collective-permute-done.2.y2
  18.3 0.6 %collective-permute-done.3.y1 = bf16[4,24,256]{2,1,0:T(8,128)(2,1)S(1)} collective-permute-done((bf16[4,24,256]{2,1,0:T(8,128)(2,1)S(1)}, bf16[4,24,256]{2,1,0:T(8,128)(2,1)S(1)}, u32[]{:S(2)}, u32[]{:S(2)}) %collective-permute-start.3) | collective-permute-done | bytes 49184 | tf_op jit(solution)/shard_map/ppermute | solution.py:43
  18.9 0.1 collective-permute-start.5
  19.0 0.5 %collective-permute-start.4 = (bf16[2,2,4,24,256]{4,3,2,1,0:T(8,128)(2,1)S(1)}, bf16[2,2,4,24,256]{4,3,2,1,0:T(8,128)(2,1)S(1)}, u32[]{:S(2)}, u32[]{:S(2)}) collective-permute-start(bf16[2,2,4,24,256]{4,3,2,1,0:T(8,128)(2,1)S(1)} %get-tuple-element.12.own), channel_id=1, source_target_pairs={{0,8},{1,9},{2,10},{3,11},{4,12},{5,13},{6,14},{7,15},{8,0},{9,1},... | collective-permute-start | bytes 589832 | tf_op jit(solution)/shard_map/ppermute | solution.py:43
  19.5 0.7 %collective-permute-done.5.other = bf16[2,2,24,256]{3,2,1,0:T(8,128)(2,1)S(1)} collective-permute-done((bf16[2,2,24,256]{3,2,1,0:T(8,128)(2,1)S(1)}, bf16[2,2,24,256]{3,2,1,0:T(8,128)(2,1)S(1)}, u32[]{:S(2)}, u32[]{:S(2)}) %collective-permute-start.5) | collective-permute-done | bytes 49184 | tf_op jit(solution)/shard_map/ppermute | solution.py:43
  20.2 0.6 %collective-permute-start.6 = (bf16[2,2,2,24,256]{4,3,2,1,0:T(8,128)(2,1)S(1)}, bf16[2,2,2,24,256]{4,3,2,1,0:T(8,128)(2,1)S(1)}, u32[]{:S(2)}, u32[]{:S(2)}) collective-permute-start(bf16[2,2,2,24,256]{4,3,2,1,0:T(8,128)(2,1)S(1)} %join_core.1.own), channel_id=1, source_target_pairs={{0,4},{1,5},{2,6},{3,7},{4,0},{5,1},{6,2},{7,3},{8,12},{9,13},{10,... | collective-permute-start | bytes 294920 | tf_op jit(solution)/shard_map/ppermute | solution.py:43
  20.8 5.9 %collective-permute-done.6.cross = bf16[2,2,2,24,256]{4,3,2,1,0:T(8,128)(2,1)S(1)} collective-permute-done((bf16[2,2,2,24,256]{4,3,2,1,0:T(8,128)(2,1)S(1)}, bf16[2,2,2,24,256]{4,3,2,1,0:T(8,128)(2,1)S(1)}, u32[]{:S(2)}, u32[]{:S(2)}) %collective-permute-start.6) | collective-permute-done | bytes 98336 | tf_op jit(solution)/shard_map/ppermute | solution.py:43
  26.7 1.4 %collective-permute-start.8 = (bf16[2,2,2,24,256]{4,3,2,1,0:T(8,128)(2,1)S(1)}, bf16[2,2,2,24,256]{4,3,2,1,0:T(8,128)(2,1)S(1)}, u32[]{:S(2)}, u32[]{:S(2)}) collective-permute-start(bf16[2,2,2,24,256]{4,3,2,1,0:T(8,128)(2,1)S(1)} %choose.1.refs_1_), channel_id=1, source_target_pairs={{0,3},{1,2},{2,1},{3,0},{4,7},{5,6},{6,5},{7,4},{8,11},{9,10},{10,... | collective-permute-start | bytes 294920 | tf_op jit(solution)/shard_map/ppermute | solution.py:43
  28.1 1.3 %collective-permute-start.9 = (bf16[2,2,2,24,256]{4,3,2,1,0:T(8,128)(2,1)S(1)}, bf16[2,2,2,24,256]{4,3,2,1,0:T(8,128)(2,1)S(1)}, u32[]{:S(2)}, u32[]{:S(2)}) collective-permute-start(bf16[2,2,2,24,256]{4,3,2,1,0:T(8,128)(2,1)S(1)} %choose.1.refs_1_), channel_id=1, source_target_pairs={{0,1},{1,0},{2,3},{3,2},{4,5},{5,4},{6,7},{7,6},{8,9},{9,8},{10,11... | collective-permute-start | bytes 294920 | tf_op jit(solution)/shard_map/ppermute | solution.py:43
  29.5 0.8 %collective-permute-start.7 = (bf16[2,2,2,24,256]{4,3,2,1,0:T(8,128)(2,1)S(1)}, bf16[2,2,2,24,256]{4,3,2,1,0:T(8,128)(2,1)S(1)}, u32[]{:S(2)}, u32[]{:S(2)}) collective-permute-start(bf16[2,2,2,24,256]{4,3,2,1,0:T(8,128)(2,1)S(1)} %choose.1.refs_1_), channel_id=1, source_target_pairs={{0,2},{1,3},{2,0},{3,1},{4,6},{5,7},{6,4},{7,5},{8,10},{9,11},{10,... | collective-permute-start | bytes 294920 | tf_op jit(solution)/shard_map/ppermute | solution.py:43
  30.3 0.0 collective-permute-done.4.other
  30.3 0.1 right_side.1.refs_0_.refs_2_
  30.4 0.4 gram.3.refs_2_
  30.8 2.3 %collective-permute-done.8.refs_1_ = bf16[2,2,2,24,256]{4,3,2,1,0:T(8,128)(2,1)S(1)} collective-permute-done((bf16[2,2,2,24,256]{4,3,2,1,0:T(8,128)(2,1)S(1)}, bf16[2,2,2,24,256]{4,3,2,1,0:T(8,128)(2,1)S(1)}, u32[]{:S(2)}, u32[]{:S(2)}) %collective-permute-start.8) | collective-permute-done | bytes 98336 | tf_op jit(solution)/shard_map/ppermute | solution.py:43
  33.1 0.4 gram.4.refs_2_.refs_3_
  33.6 0.2 collective-permute-done.9.refs_1_
  33.8 0.4 gram.5.refs_4_
  34.3 0.0 collective-permute-done.7.refs_1_
  34.3 0.5 %last_gram.1 = (f32[192,96]{1,0:T(8,128)S(1)}, bf16[192,96]{1,0:T(8,128)(2,1)S(1)}, bf16[192,96]{1,0:T(8,128)(2,1)S(1)}, bf16[192,96]{1,0:T(8,128)(2,1)S(1)}) custom-call(bf16[8,192,256]{2,1,0:T(8,128)(2,1)S(1)} %right_side.1.refs_0_.refs_2_, bf16[2,2,2,24,256]{4,3,2,1,0:T(8,128)(2,1)S(1)} %collective-permute-done.7.refs_1_, f32[192,96]{1,0:T(8,128)S(1)} %gram.3.refs_2_, ...), custom_call_target="tpu_custom_call" | custom-call | tf_op jit(solution)/shard_map/last_gram/pallas_call | solution.py:313
  34.8 0.6 %collective-permute-start.10 = (bf16[192,96]{1,0:T(8,128)(2,1)S(1)}, bf16[192,96]{1,0:T(8,128)(2,1)S(1)}, u32[]{:S(2)}, u32[]{:S(2)}) collective-permute-start(bf16[192,96]{1,0:T(8,128)(2,1)S(1)} %get-tuple-element.16), channel_id=1, source_target_pairs={{0,32},{1,33},{2,34},{3,35},{4,36},{5,37},{6,38},{7,39},{8,40},{9,... | collective-permute-start | bytes 110600 | tf_op jit(solution)/shard_map/ppermute | solution.py:43
  35.4 4.2 %collective-permute-start.11 = (bf16[192,96]{1,0:T(8,128)(2,1)S(1)}, bf16[192,96]{1,0:T(8,128)(2,1)S(1)}, u32[]{:S(2)}, u32[]{:S(2)}) collective-permute-start(bf16[192,96]{1,0:T(8,128)(2,1)S(1)} %get-tuple-element.17), channel_id=1, source_target_pairs={{0,64},{1,65},{2,66},{3,67},{4,68},{5,69},{6,70},{7,71},{8,72},{9,... | collective-permute-start | bytes 110600 | tf_op jit(solution)/shard_map/ppermute | solution.py:43
  39.5 1.8 %collective-permute-start.12 = (bf16[192,96]{1,0:T(8,128)(2,1)S(1)}, bf16[192,96]{1,0:T(8,128)(2,1)S(1)}, u32[]{:S(2)}, u32[]{:S(2)}) collective-permute-start(bf16[192,96]{1,0:T(8,128)(2,1)S(1)} %get-tuple-element.18), channel_id=1, source_target_pairs={{0,96},{1,97},{2,98},{3,99},{4,100},{5,101},{6,102},{7,103},{8,104... | collective-permute-start | bytes 110600 | tf_op jit(solution)/shard_map/ppermute | solution.py:43
  41.4 0.0 collective-permute-done.10
  41.4 2.2 %collective-permute-done.11 = bf16[192,96]{1,0:T(8,128)(2,1)S(1)} collective-permute-done((bf16[192,96]{1,0:T(8,128)(2,1)S(1)}, bf16[192,96]{1,0:T(8,128)(2,1)S(1)}, u32[]{:S(2)}, u32[]{:S(2)}) %collective-permute-start.11) | collective-permute-done | bytes 36896 | tf_op jit(solution)/shard_map/ppermute | solution.py:43
  43.6 2.2 %collective-permute-done.12 = bf16[192,96]{1,0:T(8,128)(2,1)S(1)} collective-permute-done((bf16[192,96]{1,0:T(8,128)(2,1)S(1)}, bf16[192,96]{1,0:T(8,128)(2,1)S(1)}, u32[]{:S(2)}, u32[]{:S(2)}) %collective-permute-start.12) | collective-permute-done | bytes 36896 | tf_op jit(solution)/shard_map/ppermute | solution.py:43
  45.7 0.7 %convert_add_fusion = f32[192,96]{1,0:T(8,128)} fusion(bf16[192,96]{1,0:T(8,128)(2,1)S(1)} %collective-permute-done.12, bf16[192,96]{1,0:T(8,128)(2,1)S(1)} %collective-permute-done.11, f32[192,96]{1,0:T(8,128)S(1)} %get-tuple-element.15, bf16[192,96]{1,0:T(8,128)(2,1)S(1)} %collective-permute-done.10), kind=kLoop, calls=%fused_computation | loop fusion | flops 110592 | bytes 258048 | tf_op jit(solution)/shard_map/add | solution.py:321
  (3 shorter events, 0.0 us)
Async XLA Ops:
  0.0 1.6 %copy-start.1 = (f32[8,2560]{1,0:T(8,128)S(1)}, f32[8,2560]{1,0:T(8,128)}, u32[]{:S(2)}) copy-start(f32[8,2560]{1,0:T(8,128)} %constant.2.clone.table.table_hbm) | copy-start | bytes 245764
  0.0 1.6 %copy-start = (bf16[96,8192]{1,0:T(8,128)(2,1)S(1)}, bf16[96,8192]{1,0:T(8,128)(2,1)}, u32[]{:S(2)}) copy-start(bf16[96,8192]{1,0:T(8,128)(2,1)} %head.1) | copy-start | bytes 4718596
  0.0 1.6 %copy-start.2 = (s32[32]{0:T(128)S(1)}, s32[32]{0:T(128)}, u32[]{:S(2)}) copy-start(s32[32]{0:T(128)} %fire_hbm.1) | copy-start | bytes 388
  1.5 9.6 %collective-permute-start = (f32[72,96]{1,0:T(8,128)S(1)}, f32[72,96]{1,0:T(8,128)S(1)}, u32[]{:S(2)}, u32[]{:S(2)}) collective-permute-start(f32[72,96]{1,0:T(8,128)S(1)} %tail_spectra.1), channel_id=1, source_target_pairs={{0,8},{1,9},{2,10},{3,11},{4,12},{5,13},{6,14},{7,15},{8,16},{9,17... | collective-permute-start | bytes 82952 | tf_op jit(solution)/shard_map/ppermute | solution.py:43
  11.7 6.6 %collective-permute-start.1 = (bf16[4,24,256]{2,1,0:T(8,128)(2,1)S(1)}, bf16[4,24,256]{2,1,0:T(8,128)(2,1)S(1)}, u32[]{:S(2)}, u32[]{:S(2)}) collective-permute-start(bf16[4,24,256]{2,1,0:T(8,128)(2,1)S(1)} %finish_spectra.1.y0), channel_id=1, source_target_pairs={{0,144},{1,145},{2,146},{3,147},{4,148},{5,149},{6,150},{7,151},{8... | collective-permute-start | bytes 147464 | tf_op jit(solution)/shard_map/ppermute | solution.py:43
  11.8 6.5 %collective-permute-start.2 = (bf16[4,24,256]{2,1,0:T(8,128)(2,1)S(1)}, bf16[4,24,256]{2,1,0:T(8,128)(2,1)S(1)}, u32[]{:S(2)}, u32[]{:S(2)}) collective-permute-start(bf16[4,24,256]{2,1,0:T(8,128)(2,1)S(1)} %finish_spectra.1.y0), channel_id=1, source_target_pairs={{0,128},{1,129},{2,130},{3,131},{4,132},{5,133},{6,134},{7,135},{8... | collective-permute-start | bytes 147464 | tf_op jit(solution)/shard_map/ppermute | solution.py:43
  12.5 6.3 %collective-permute-start.3 = (bf16[4,24,256]{2,1,0:T(8,128)(2,1)S(1)}, bf16[4,24,256]{2,1,0:T(8,128)(2,1)S(1)}, u32[]{:S(2)}, u32[]{:S(2)}) collective-permute-start(bf16[4,24,256]{2,1,0:T(8,128)(2,1)S(1)} %finish_spectra.1.y0), channel_id=1, source_target_pairs={{0,16},{1,17},{2,18},{3,19},{4,20},{5,21},{6,22},{7,23},{8,24},{9,... | collective-permute-start | bytes 147464 | tf_op jit(solution)/shard_map/ppermute | solution.py:43
  18.9 1.3 %collective-permute-start.5 = (bf16[2,2,24,256]{3,2,1,0:T(8,128)(2,1)S(1)}, bf16[2,2,24,256]{3,2,1,0:T(8,128)(2,1)S(1)}, u32[]{:S(2)}, u32[]{:S(2)}) collective-permute-start(bf16[2,2,24,256]{3,2,1,0:T(8,128)(2,1)S(1)} %get-tuple-element.14), channel_id=1, source_target_pairs={{0,8},{1,9},{2,10},{3,11},{4,12},{5,13},{6,14},{7,15},{8,0},{9,1},... | collective-permute-start | bytes 147464 | tf_op jit(solution)/shard_map/ppermute | solution.py:43
  19.0 11.3 %collective-permute-start.4 = (bf16[2,2,4,24,256]{4,3,2,1,0:T(8,128)(2,1)S(1)}, bf16[2,2,4,24,256]{4,3,2,1,0:T(8,128)(2,1)S(1)}, u32[]{:S(2)}, u32[]{:S(2)}) collective-permute-start(bf16[2,2,4,24,256]{4,3,2,1,0:T(8,128)(2,1)S(1)} %get-tuple-element.12.own), channel_id=1, source_target_pairs={{0,8},{1,9},{2,10},{3,11},{4,12},{5,13},{6,14},{7,15},{8,0},{9,1},... | collective-permute-start | bytes 589832 | tf_op jit(solution)/shard_map/ppermute | solution.py:43
  20.2 6.5 %collective-permute-start.6 = (bf16[2,2,2,24,256]{4,3,2,1,0:T(8,128)(2,1)S(1)}, bf16[2,2,2,24,256]{4,3,2,1,0:T(8,128)(2,1)S(1)}, u32[]{:S(2)}, u32[]{:S(2)}) collective-permute-start(bf16[2,2,2,24,256]{4,3,2,1,0:T(8,128)(2,1)S(1)} %join_core.1.own), channel_id=1, source_target_pairs={{0,4},{1,5},{2,6},{3,7},{4,0},{5,1},{6,2},{7,3},{8,12},{9,13},{10,... | collective-permute-start | bytes 294920 | tf_op jit(solution)/shard_map/ppermute | solution.py:43
  26.7 6.4 %collective-permute-start.8 = (bf16[2,2,2,24,256]{4,3,2,1,0:T(8,128)(2,1)S(1)}, bf16[2,2,2,24,256]{4,3,2,1,0:T(8,128)(2,1)S(1)}, u32[]{:S(2)}, u32[]{:S(2)}) collective-permute-start(bf16[2,2,2,24,256]{4,3,2,1,0:T(8,128)(2,1)S(1)} %choose.1.refs_1_), channel_id=1, source_target_pairs={{0,3},{1,2},{2,1},{3,0},{4,7},{5,6},{6,5},{7,4},{8,11},{9,10},{10,... | collective-permute-start | bytes 294920 | tf_op jit(solution)/shard_map/ppermute | solution.py:43
  28.1 5.7 %collective-permute-start.9 = (bf16[2,2,2,24,256]{4,3,2,1,0:T(8,128)(2,1)S(1)}, bf16[2,2,2,24,256]{4,3,2,1,0:T(8,128)(2,1)S(1)}, u32[]{:S(2)}, u32[]{:S(2)}) collective-permute-start(bf16[2,2,2,24,256]{4,3,2,1,0:T(8,128)(2,1)S(1)} %choose.1.refs_1_), channel_id=1, source_target_pairs={{0,1},{1,0},{2,3},{3,2},{4,5},{5,4},{6,7},{7,6},{8,9},{9,8},{10,11... | collective-permute-start | bytes 294920 | tf_op jit(solution)/shard_map/ppermute | solution.py:43
  29.5 4.8 %collective-permute-start.7 = (bf16[2,2,2,24,256]{4,3,2,1,0:T(8,128)(2,1)S(1)}, bf16[2,2,2,24,256]{4,3,2,1,0:T(8,128)(2,1)S(1)}, u32[]{:S(2)}, u32[]{:S(2)}) collective-permute-start(bf16[2,2,2,24,256]{4,3,2,1,0:T(8,128)(2,1)S(1)} %choose.1.refs_1_), channel_id=1, source_target_pairs={{0,2},{1,3},{2,0},{3,1},{4,6},{5,7},{6,4},{7,5},{8,10},{9,11},{10,... | collective-permute-start | bytes 294920 | tf_op jit(solution)/shard_map/ppermute | solution.py:43
  34.8 6.6 %collective-permute-start.10 = (bf16[192,96]{1,0:T(8,128)(2,1)S(1)}, bf16[192,96]{1,0:T(8,128)(2,1)S(1)}, u32[]{:S(2)}, u32[]{:S(2)}) collective-permute-start(bf16[192,96]{1,0:T(8,128)(2,1)S(1)} %get-tuple-element.16), channel_id=1, source_target_pairs={{0,32},{1,33},{2,34},{3,35},{4,36},{5,37},{6,38},{7,39},{8,40},{9,... | collective-permute-start | bytes 110600 | tf_op jit(solution)/shard_map/ppermute | solution.py:43
  35.4 8.2 %collective-permute-start.11 = (bf16[192,96]{1,0:T(8,128)(2,1)S(1)}, bf16[192,96]{1,0:T(8,128)(2,1)S(1)}, u32[]{:S(2)}, u32[]{:S(2)}) collective-permute-start(bf16[192,96]{1,0:T(8,128)(2,1)S(1)} %get-tuple-element.17), channel_id=1, source_target_pairs={{0,64},{1,65},{2,66},{3,67},{4,68},{5,69},{6,70},{7,71},{8,72},{9,... | collective-permute-start | bytes 110600 | tf_op jit(solution)/shard_map/ppermute | solution.py:43
  39.5 6.2 %collective-permute-start.12 = (bf16[192,96]{1,0:T(8,128)(2,1)S(1)}, bf16[192,96]{1,0:T(8,128)(2,1)S(1)}, u32[]{:S(2)}, u32[]{:S(2)}) collective-permute-start(bf16[192,96]{1,0:T(8,128)(2,1)S(1)} %get-tuple-element.18), channel_id=1, source_target_pairs={{0,96},{1,97},{2,98},{3,99},{4,100},{5,101},{6,102},{7,103},{8,104... | collective-permute-start | bytes 110600 | tf_op jit(solution)/shard_map/ppermute | solution.py:43

commit v9 on v8

--- a/solution.py
+++ b/solution.py
@@ -208,8 +208,28 @@
     total[turn ^ 3] = g3[...]
     total[turn ^ 1] = g1[...]
     total[turn ^ 2] = products(scale, right, q)
-    for n, out in enumerate((p0, p1, p2, p3)):
-        out[...] = total[n].astype(out.dtype)
+    p0[...] = total[0]
+    for n, out in ((1, p1), (2, p2), (3, p3)):
+        pack(total[n], out)
+
+
+def pack(share, out):
+    rows, width = out.shape
+    lanes = share.shape[1]
+    rest = width - lanes
+    out[:, :lanes] = share[:rows].astype(out.dtype)
+    pieces = [share[rows:, rest * g : rest * (g + 1)] for g in range(lanes // rest)]
+    out[:, lanes:] = jnp.concatenate(pieces, axis=0).astype(out.dtype)
+
+
+def sum_kernel(r2, r3, r1, p0, out):
+    shares = r1[...].astype(jnp.float32) + r2[...].astype(jnp.float32) + r3[...].astype(jnp.float32)
+    rows = shares.shape[0]
+    lanes = out.shape[1]
+    high = out.shape[0] - rows
+    out[:rows] = p0[:rows] + shares[:, :lanes]
+    pieces = [shares[high * g : high * (g + 1), lanes:] for g in range(rows // high)]
+    out[rows:] = p0[rows:] + jnp.concatenate(pieces, axis=1)
 
 
 def local(kernel, name, out_shape, in_specs, scratch=(), limit=4):
@@ -299,7 +319,8 @@
     rows = ROWS * count
     scale = 1.0 / total_shots
     share = shape((rows, receivers), f32)
-    wire = shape((rows, receivers), bf16)
+    width = 128
+    wire = shape((rows * receivers // width, width), bf16)
     early = []
     for m in (0, 3, 1):
         early += [
@@ -310,15 +331,15 @@
                 vmem(2) + [pl.BlockSpec(memory_space=pl.ANY)],
             )(right, qs[m], early[-1] if early else right)
         ]
-    sums, p1, p2, p3 = local(
+    p0, p1, p2, p3 = local(
         lambda *refs: last_kernel(scale, *refs),
         "last_gram",
         (share, wire, wire, wire),
         vmem(5),
         [pltpu.VMEM((QUARTERS, rows, receivers), f32)],
     )(right, qs[2], *early)
-    for n, p in ((1, p1), (2, p2), (3, p3)):
-        sums = sums + send(p, lambda yh, u, k, xh, v, n=n: (yh, u ^ n, k, xh, v)).astype(f32)
+    r1, r2, r3 = [send(p, lambda yh, u, k, xh, v, n=n: (yh, u ^ n, k, xh, v)) for n, p in ((1, p1), (2, p2), (3, p3))]
+    sums = local(sum_kernel, "sum", share, vmem(4))(r2, r3, r1, p0)
     return sums.reshape(2, NF, count, receivers).transpose(0, 1, 3, 2)
 
 

time: 46.5 us -> 45.5 us (0.978)
  waiting for transfers between devices: 23.5 us -> 21.9 us
  Pallas kernels: 5.58 us -> 6.49 us
  other arithmetic: 0.66 us -> 0 us
    ppermute x13, waiting for transfers between devices: 23.5 us -> 21.9 us  [send(): return lax.ppermute(block, ('shot', 'rcv'), route)]
    pallas_call x0 -> x1, Pallas kernels: none -> 0.74 us  [per_device(): sums = local(sum_kernel, 'sum', share, vmem(4))(r2, r3, r1, p0)]
    add x1 -> x0, other arithmetic: 0.66 us -> none  [per_device(): sums + send(p, lambda yh, u, k, xh, v, n=n: (yh, u ^ n, k, xh, v)).astype...]
where the time goes in v9:
time: 45.5 us; the launch traced here: 45 us
  waiting for transfers between devices  21.9 us (48%)
  starting transfers between devices  16.5 us (36%)
  Pallas kernels  6.49 us (14%)
    ppermute x13, waiting for transfers between devices, send(): return lax.ppermute(block, ('shot', 'rcv'), route)  21.9 us
    ppermute x13, starting transfers between devices, send(): return lax.ppermute(block, ('shot', 'rcv'), route)  16.5 us
    pallas_call x1, Pallas kernels, per_device(): local(own_kernel, 'own_spectra', shape((lanes - late_rows, receivers), f3...  1.58 us
    pallas_call x1, Pallas kernels, per_device(): local(tail_kernel, 'tail_spectra', shape((late_rows + LATE, receivers), f...  1.44 us
    pallas_call x3, Pallas kernels, per_device(): local(lambda *refs: gram_kernel(scale, *refs), 'gram', share, vmem(2) + [...  1.34 us
  transfers between devices with their start and end apart: 13, of which 9 were waited for; matrix products, arithmetic and copies ran while one was open for 0% of the time, Pallas kernels for 7%

profile of v9, /device:TPU:4, one launch (start us, length us, event | category | flops | bytes accessed | tf_op | source)
XLA Modules:
  0.0 45.0 jit_solution(18080929211359038383)
XLA Ops:
  0.0 0.0 copy-start.1
  0.0 0.0 copy-start
  0.0 0.0 copy-start.2
  0.0 1.4 %tail_spectra.1 = f32[72,96]{1,0:T(8,128)S(1)} custom-call(s32[32]{0:T(128)} %fire_hbm.1, f32[8,2560]{1,0:T(8,128)} %constant.2.clone.table.table_hbm, bf16[96,8192]{1,0:T(8,128)(2,1)} %head.1), custom_call_target="tpu_custom_call" | custom-call | tf_op jit(solution)/shard_map/tail_spectra/pallas_call | solution.py:259
  1.5 0.1 collective-permute-start
  1.6 0.0 copy-done.1
  1.6 0.1 copy-done
  1.6 0.0 copy-done.2
  1.6 1.6 %own_spectra.1.total = f32[192,96]{1,0:T(8,128)S(1)} custom-call(s32[32]{0:T(128)S(1)} %copy-done.2, f32[8,2560]{1,0:T(8,128)S(1)} %copy-done.1, bf16[96,8192]{1,0:T(8,128)(2,1)S(1)} %copy-done), custom_call_target="tpu_custom_call" | custom-call | tf_op jit(solution)/shard_map/own_spectra/pallas_call | solution.py:278
  3.2 7.9 %collective-permute-done.message = f32[72,96]{1,0:T(8,128)S(1)} collective-permute-done((f32[72,96]{1,0:T(8,128)S(1)}, f32[72,96]{1,0:T(8,128)S(1)}, u32[]{:S(2)}, u32[]{:S(2)}) %collective-permute-start) | collective-permute-done | bytes 27680 | tf_op jit(solution)/shard_map/ppermute | solution.py:43
  11.1 0.6 %finish_spectra.1.y0 = bf16[4,24,256]{2,1,0:T(8,128)(2,1)S(1)} custom-call(f32[192,96]{1,0:T(8,128)S(1)} %own_spectra.1.total, bf16[96,8192]{1,0:T(8,128)(2,1)S(1)} %copy-done, f32[8,2560]{1,0:T(8,128)S(1)} %copy-done.1, f32[72,96]{1,0:T(8,128)S(1)} %collective-permute-done.message), custom_call_target="tpu_custom_call" | custom-call | tf_op jit(solution)/shard_map/finish_spectra/pallas_call | solution.py:285
  11.7 0.1 collective-permute-start.1
  11.8 0.7 %collective-permute-start.2 = (bf16[4,24,256]{2,1,0:T(8,128)(2,1)S(1)}, bf16[4,24,256]{2,1,0:T(8,128)(2,1)S(1)}, u32[]{:S(2)}, u32[]{:S(2)}) collective-permute-start(bf16[4,24,256]{2,1,0:T(8,128)(2,1)S(1)} %finish_spectra.1.y0), channel_id=1, source_target_pairs={{0,128},{1,129},{2,130},{3,131},{4,132},{5,133},{6,134},{7,135},{8... | collective-permute-start | bytes 147464 | tf_op jit(solution)/shard_map/ppermute | solution.py:43
  12.5 4.3 %collective-permute-start.3 = (bf16[4,24,256]{2,1,0:T(8,128)(2,1)S(1)}, bf16[4,24,256]{2,1,0:T(8,128)(2,1)S(1)}, u32[]{:S(2)}, u32[]{:S(2)}) collective-permute-start(bf16[4,24,256]{2,1,0:T(8,128)(2,1)S(1)} %finish_spectra.1.y0), channel_id=1, source_target_pairs={{0,16},{1,17},{2,18},{3,19},{4,20},{5,21},{6,22},{7,23},{8,24},{9,... | collective-permute-start | bytes 147464 | tf_op jit(solution)/shard_map/ppermute | solution.py:43
  16.8 1.5 %collective-permute-done.1.y3 = bf16[4,24,256]{2,1,0:T(8,128)(2,1)S(1)} collective-permute-done((bf16[4,24,256]{2,1,0:T(8,128)(2,1)S(1)}, bf16[4,24,256]{2,1,0:T(8,128)(2,1)S(1)}, u32[]{:S(2)}, u32[]{:S(2)}) %collective-permute-start.1) | collective-permute-done | bytes 49184 | tf_op jit(solution)/shard_map/ppermute | solution.py:43
  18.3 0.0 collective-permute-done.2.y2
  18.3 0.6 %collective-permute-done.3.y1 = bf16[4,24,256]{2,1,0:T(8,128)(2,1)S(1)} collective-permute-done((bf16[4,24,256]{2,1,0:T(8,128)(2,1)S(1)}, bf16[4,24,256]{2,1,0:T(8,128)(2,1)S(1)}, u32[]{:S(2)}, u32[]{:S(2)}) %collective-permute-start.3) | collective-permute-done | bytes 49184 | tf_op jit(solution)/shard_map/ppermute | solution.py:43
  18.9 0.1 collective-permute-start.5
  19.0 0.5 %collective-permute-start.4 = (bf16[2,2,4,24,256]{4,3,2,1,0:T(8,128)(2,1)S(1)}, bf16[2,2,4,24,256]{4,3,2,1,0:T(8,128)(2,1)S(1)}, u32[]{:S(2)}, u32[]{:S(2)}) collective-permute-start(bf16[2,2,4,24,256]{4,3,2,1,0:T(8,128)(2,1)S(1)} %get-tuple-element.12.own), channel_id=1, source_target_pairs={{0,8},{1,9},{2,10},{3,11},{4,12},{5,13},{6,14},{7,15},{8,0},{9,1},... | collective-permute-start | bytes 589832 | tf_op jit(solution)/shard_map/ppermute | solution.py:43
  19.5 0.7 %collective-permute-done.5.other = bf16[2,2,24,256]{3,2,1,0:T(8,128)(2,1)S(1)} collective-permute-done((bf16[2,2,24,256]{3,2,1,0:T(8,128)(2,1)S(1)}, bf16[2,2,24,256]{3,2,1,0:T(8,128)(2,1)S(1)}, u32[]{:S(2)}, u32[]{:S(2)}) %collective-permute-start.5) | collective-permute-done | bytes 49184 | tf_op jit(solution)/shard_map/ppermute | solution.py:43
  20.2 0.6 %collective-permute-start.6 = (bf16[2,2,2,24,256]{4,3,2,1,0:T(8,128)(2,1)S(1)}, bf16[2,2,2,24,256]{4,3,2,1,0:T(8,128)(2,1)S(1)}, u32[]{:S(2)}, u32[]{:S(2)}) collective-permute-start(bf16[2,2,2,24,256]{4,3,2,1,0:T(8,128)(2,1)S(1)} %join_core.1.own), channel_id=1, source_target_pairs={{0,4},{1,5},{2,6},{3,7},{4,0},{5,1},{6,2},{7,3},{8,12},{9,13},{10,... | collective-permute-start | bytes 294920 | tf_op jit(solution)/shard_map/ppermute | solution.py:43
  20.8 5.9 %collective-permute-done.6.cross = bf16[2,2,2,24,256]{4,3,2,1,0:T(8,128)(2,1)S(1)} collective-permute-done((bf16[2,2,2,24,256]{4,3,2,1,0:T(8,128)(2,1)S(1)}, bf16[2,2,2,24,256]{4,3,2,1,0:T(8,128)(2,1)S(1)}, u32[]{:S(2)}, u32[]{:S(2)}) %collective-permute-start.6) | collective-permute-done | bytes 98336 | tf_op jit(solution)/shard_map/ppermute | solution.py:43
  26.7 1.4 %collective-permute-start.8 = (bf16[2,2,2,24,256]{4,3,2,1,0:T(8,128)(2,1)S(1)}, bf16[2,2,2,24,256]{4,3,2,1,0:T(8,128)(2,1)S(1)}, u32[]{:S(2)}, u32[]{:S(2)}) collective-permute-start(bf16[2,2,2,24,256]{4,3,2,1,0:T(8,128)(2,1)S(1)} %choose.1.refs_1_), channel_id=1, source_target_pairs={{0,3},{1,2},{2,1},{3,0},{4,7},{5,6},{6,5},{7,4},{8,11},{9,10},{10,... | collective-permute-start | bytes 294920 | tf_op jit(solution)/shard_map/ppermute | solution.py:43
  28.1 1.3 %collective-permute-start.9 = (bf16[2,2,2,24,256]{4,3,2,1,0:T(8,128)(2,1)S(1)}, bf16[2,2,2,24,256]{4,3,2,1,0:T(8,128)(2,1)S(1)}, u32[]{:S(2)}, u32[]{:S(2)}) collective-permute-start(bf16[2,2,2,24,256]{4,3,2,1,0:T(8,128)(2,1)S(1)} %choose.1.refs_1_), channel_id=1, source_target_pairs={{0,1},{1,0},{2,3},{3,2},{4,5},{5,4},{6,7},{7,6},{8,9},{9,8},{10,11... | collective-permute-start | bytes 294920 | tf_op jit(solution)/shard_map/ppermute | solution.py:43
  29.5 0.8 %collective-permute-start.7 = (bf16[2,2,2,24,256]{4,3,2,1,0:T(8,128)(2,1)S(1)}, bf16[2,2,2,24,256]{4,3,2,1,0:T(8,128)(2,1)S(1)}, u32[]{:S(2)}, u32[]{:S(2)}) collective-permute-start(bf16[2,2,2,24,256]{4,3,2,1,0:T(8,128)(2,1)S(1)} %choose.1.refs_1_), channel_id=1, source_target_pairs={{0,2},{1,3},{2,0},{3,1},{4,6},{5,7},{6,4},{7,5},{8,10},{9,11},{10,... | collective-permute-start | bytes 294920 | tf_op jit(solution)/shard_map/ppermute | solution.py:43
  30.3 0.0 collective-permute-done.4.other
  30.3 0.1 right_side.1.refs_0_.refs_2_
  30.4 0.5 %gram.3.refs_2_ = f32[192,96]{1,0:T(8,128)S(1)} custom-call(bf16[8,192,256]{2,1,0:T(8,128)(2,1)S(1)} %right_side.1.refs_0_.refs_2_, bf16[2,2,2,24,256]{4,3,2,1,0:T(8,128)(2,1)S(1)} %choose.1.refs_1_, bf16[8,192,256]{2,1,0:T(8,128)(2,1)S(1)} %right_side.1.refs_0_.refs_2_), custom_call_target="tpu_custom_call" | custom-call | tf_op jit(solution)/shard_map/gram/pallas_call | solution.py:327
  30.8 2.3 %collective-permute-done.8.refs_1_ = bf16[2,2,2,24,256]{4,3,2,1,0:T(8,128)(2,1)S(1)} collective-permute-done((bf16[2,2,2,24,256]{4,3,2,1,0:T(8,128)(2,1)S(1)}, bf16[2,2,2,24,256]{4,3,2,1,0:T(8,128)(2,1)S(1)}, u32[]{:S(2)}, u32[]{:S(2)}) %collective-permute-start.8) | collective-permute-done | bytes 98336 | tf_op jit(solution)/shard_map/ppermute | solution.py:43
  33.1 0.4 gram.4.refs_2_.refs_3_
  33.6 0.2 collective-permute-done.9.refs_1_
  33.8 0.4 gram.5.refs_4_
  34.3 0.0 collective-permute-done.7.refs_1_
  34.3 0.6 %last_gram.1 = (f32[192,96]{1,0:T(8,128)S(1)}, bf16[144,128]{1,0:T(8,128)(2,1)S(1)}, bf16[144,128]{1,0:T(8,128)(2,1)S(1)}, bf16[144,128]{1,0:T(8,128)(2,1)S(1)}) custom-call(bf16[8,192,256]{2,1,0:T(8,128)(2,1)S(1)} %right_side.1.refs_0_.refs_2_, bf16[2,2,2,24,256]{4,3,2,1,0:T(8,128)(2,1)S(1)} %collective-permute-done.7.refs_1_, f32[192,96]{1,0:T(8,128)S(1)} %gram.3.refs_2_, ...), custom_call_target="tpu_custom_call" | custom-call | tf_op jit(solution)/shard_map/last_gram/pallas_call | solution.py:334
  34.9 3.3 %collective-permute-start.10 = (bf16[144,128]{1,0:T(8,128)(2,1)S(1)}, bf16[144,128]{1,0:T(8,128)(2,1)S(1)}, u32[]{:S(2)}, u32[]{:S(2)}) collective-permute-start(bf16[144,128]{1,0:T(8,128)(2,1)S(1)} %get-tuple-element.15), channel_id=1, source_target_pairs={{0,64},{1,65},{2,66},{3,67},{4,68},{5,69},{6,70},{7,71},{8,72},{9,... | collective-permute-start | bytes 110600 | tf_op jit(solution)/shard_map/ppermute | solution.py:43
  38.2 0.9 %collective-permute-start.11 = (bf16[144,128]{1,0:T(8,128)(2,1)S(1)}, bf16[144,128]{1,0:T(8,128)(2,1)S(1)}, u32[]{:S(2)}, u32[]{:S(2)}) collective-permute-start(bf16[144,128]{1,0:T(8,128)(2,1)S(1)} %get-tuple-element.16), channel_id=1, source_target_pairs={{0,96},{1,97},{2,98},{3,99},{4,100},{5,101},{6,102},{7,103},{8,104... | collective-permute-start | bytes 110600 | tf_op jit(solution)/shard_map/ppermute | solution.py:43
  39.1 2.4 %collective-permute-start.12 = (bf16[144,128]{1,0:T(8,128)(2,1)S(1)}, bf16[144,128]{1,0:T(8,128)(2,1)S(1)}, u32[]{:S(2)}, u32[]{:S(2)}) collective-permute-start(bf16[144,128]{1,0:T(8,128)(2,1)S(1)} %get-tuple-element.17), channel_id=1, source_target_pairs={{0,32},{1,33},{2,34},{3,35},{4,36},{5,37},{6,38},{7,39},{8,40},{9,... | collective-permute-start | bytes 110600 | tf_op jit(solution)/shard_map/ppermute | solution.py:43
  41.5 1.5 %collective-permute-done.10.r2 = bf16[144,128]{1,0:T(8,128)(2,1)S(1)} collective-permute-done((bf16[144,128]{1,0:T(8,128)(2,1)S(1)}, bf16[144,128]{1,0:T(8,128)(2,1)S(1)}, u32[]{:S(2)}, u32[]{:S(2)}) %collective-permute-start.10) | collective-permute-done | bytes 36896 | tf_op jit(solution)/shard_map/ppermute | solution.py:43
  43.0 1.3 %collective-permute-done.11.r3 = bf16[144,128]{1,0:T(8,128)(2,1)S(1)} collective-permute-done((bf16[144,128]{1,0:T(8,128)(2,1)S(1)}, bf16[144,128]{1,0:T(8,128)(2,1)S(1)}, u32[]{:S(2)}, u32[]{:S(2)}) %collective-permute-start.11) | collective-permute-done | bytes 36896 | tf_op jit(solution)/shard_map/ppermute | solution.py:43
  44.3 0.0 collective-permute-done.12.r1
  44.3 0.7 %sum.1 = f32[192,96]{1,0:T(8,128)} custom-call(bf16[144,128]{1,0:T(8,128)(2,1)S(1)} %collective-permute-done.10.r2, bf16[144,128]{1,0:T(8,128)(2,1)S(1)} %collective-permute-done.11.r3, bf16[144,128]{1,0:T(8,128)(2,1)S(1)} %collective-permute-done.12.r1, f32[192,96]{1,0:T(8,128)S(1)} %get-tuple-element.18.p0), custom_call_target="tpu_custom_call" | custom-call | tf_op jit(solution)/shard_map/sum/pallas_call | solution.py:342
  (3 shorter events, 0.0 us)
Async XLA Ops:
  0.0 1.6 %copy-start.1 = (f32[8,2560]{1,0:T(8,128)S(1)}, f32[8,2560]{1,0:T(8,128)}, u32[]{:S(2)}) copy-start(f32[8,2560]{1,0:T(8,128)} %constant.2.clone.table.table_hbm) | copy-start | bytes 245764
  0.0 1.6 %copy-start = (bf16[96,8192]{1,0:T(8,128)(2,1)S(1)}, bf16[96,8192]{1,0:T(8,128)(2,1)}, u32[]{:S(2)}) copy-start(bf16[96,8192]{1,0:T(8,128)(2,1)} %head.1) | copy-start | bytes 4718596
  0.0 1.6 %copy-start.2 = (s32[32]{0:T(128)S(1)}, s32[32]{0:T(128)}, u32[]{:S(2)}) copy-start(s32[32]{0:T(128)} %fire_hbm.1) | copy-start | bytes 388
  1.5 9.6 %collective-permute-start = (f32[72,96]{1,0:T(8,128)S(1)}, f32[72,96]{1,0:T(8,128)S(1)}, u32[]{:S(2)}, u32[]{:S(2)}) collective-permute-start(f32[72,96]{1,0:T(8,128)S(1)} %tail_spectra.1), channel_id=1, source_target_pairs={{0,8},{1,9},{2,10},{3,11},{4,12},{5,13},{6,14},{7,15},{8,16},{9,17... | collective-permute-start | bytes 82952 | tf_op jit(solution)/shard_map/ppermute | solution.py:43
  11.7 6.6 %collective-permute-start.1 = (bf16[4,24,256]{2,1,0:T(8,128)(2,1)S(1)}, bf16[4,24,256]{2,1,0:T(8,128)(2,1)S(1)}, u32[]{:S(2)}, u32[]{:S(2)}) collective-permute-start(bf16[4,24,256]{2,1,0:T(8,128)(2,1)S(1)} %finish_spectra.1.y0), channel_id=1, source_target_pairs={{0,144},{1,145},{2,146},{3,147},{4,148},{5,149},{6,150},{7,151},{8... | collective-permute-start | bytes 147464 | tf_op jit(solution)/shard_map/ppermute | solution.py:43
  11.8 6.5 %collective-permute-start.2 = (bf16[4,24,256]{2,1,0:T(8,128)(2,1)S(1)}, bf16[4,24,256]{2,1,0:T(8,128)(2,1)S(1)}, u32[]{:S(2)}, u32[]{:S(2)}) collective-permute-start(bf16[4,24,256]{2,1,0:T(8,128)(2,1)S(1)} %finish_spectra.1.y0), channel_id=1, source_target_pairs={{0,128},{1,129},{2,130},{3,131},{4,132},{5,133},{6,134},{7,135},{8... | collective-permute-start | bytes 147464 | tf_op jit(solution)/shard_map/ppermute | solution.py:43
  12.5 6.3 %collective-permute-start.3 = (bf16[4,24,256]{2,1,0:T(8,128)(2,1)S(1)}, bf16[4,24,256]{2,1,0:T(8,128)(2,1)S(1)}, u32[]{:S(2)}, u32[]{:S(2)}) collective-permute-start(bf16[4,24,256]{2,1,0:T(8,128)(2,1)S(1)} %finish_spectra.1.y0), channel_id=1, source_target_pairs={{0,16},{1,17},{2,18},{3,19},{4,20},{5,21},{6,22},{7,23},{8,24},{9,... | collective-permute-start | bytes 147464 | tf_op jit(solution)/shard_map/ppermute | solution.py:43
  18.9 1.3 %collective-permute-start.5 = (bf16[2,2,24,256]{3,2,1,0:T(8,128)(2,1)S(1)}, bf16[2,2,24,256]{3,2,1,0:T(8,128)(2,1)S(1)}, u32[]{:S(2)}, u32[]{:S(2)}) collective-permute-start(bf16[2,2,24,256]{3,2,1,0:T(8,128)(2,1)S(1)} %get-tuple-element.14), channel_id=1, source_target_pairs={{0,8},{1,9},{2,10},{3,11},{4,12},{5,13},{6,14},{7,15},{8,0},{9,1},... | collective-permute-start | bytes 147464 | tf_op jit(solution)/shard_map/ppermute | solution.py:43
  19.0 11.3 %collective-permute-start.4 = (bf16[2,2,4,24,256]{4,3,2,1,0:T(8,128)(2,1)S(1)}, bf16[2,2,4,24,256]{4,3,2,1,0:T(8,128)(2,1)S(1)}, u32[]{:S(2)}, u32[]{:S(2)}) collective-permute-start(bf16[2,2,4,24,256]{4,3,2,1,0:T(8,128)(2,1)S(1)} %get-tuple-element.12.own), channel_id=1, source_target_pairs={{0,8},{1,9},{2,10},{3,11},{4,12},{5,13},{6,14},{7,15},{8,0},{9,1},... | collective-permute-start | bytes 589832 | tf_op jit(solution)/shard_map/ppermute | solution.py:43
  20.2 6.5 %collective-permute-start.6 = (bf16[2,2,2,24,256]{4,3,2,1,0:T(8,128)(2,1)S(1)}, bf16[2,2,2,24,256]{4,3,2,1,0:T(8,128)(2,1)S(1)}, u32[]{:S(2)}, u32[]{:S(2)}) collective-permute-start(bf16[2,2,2,24,256]{4,3,2,1,0:T(8,128)(2,1)S(1)} %join_core.1.own), channel_id=1, source_target_pairs={{0,4},{1,5},{2,6},{3,7},{4,0},{5,1},{6,2},{7,3},{8,12},{9,13},{10,... | collective-permute-start | bytes 294920 | tf_op jit(solution)/shard_map/ppermute | solution.py:43
  26.7 6.4 %collective-permute-start.8 = (bf16[2,2,2,24,256]{4,3,2,1,0:T(8,128)(2,1)S(1)}, bf16[2,2,2,24,256]{4,3,2,1,0:T(8,128)(2,1)S(1)}, u32[]{:S(2)}, u32[]{:S(2)}) collective-permute-start(bf16[2,2,2,24,256]{4,3,2,1,0:T(8,128)(2,1)S(1)} %choose.1.refs_1_), channel_id=1, source_target_pairs={{0,3},{1,2},{2,1},{3,0},{4,7},{5,6},{6,5},{7,4},{8,11},{9,10},{10,... | collective-permute-start | bytes 294920 | tf_op jit(solution)/shard_map/ppermute | solution.py:43
  28.1 5.7 %collective-permute-start.9 = (bf16[2,2,2,24,256]{4,3,2,1,0:T(8,128)(2,1)S(1)}, bf16[2,2,2,24,256]{4,3,2,1,0:T(8,128)(2,1)S(1)}, u32[]{:S(2)}, u32[]{:S(2)}) collective-permute-start(bf16[2,2,2,24,256]{4,3,2,1,0:T(8,128)(2,1)S(1)} %choose.1.refs_1_), channel_id=1, source_target_pairs={{0,1},{1,0},{2,3},{3,2},{4,5},{5,4},{6,7},{7,6},{8,9},{9,8},{10,11... | collective-permute-start | bytes 294920 | tf_op jit(solution)/shard_map/ppermute | solution.py:43
  29.5 4.8 %collective-permute-start.7 = (bf16[2,2,2,24,256]{4,3,2,1,0:T(8,128)(2,1)S(1)}, bf16[2,2,2,24,256]{4,3,2,1,0:T(8,128)(2,1)S(1)}, u32[]{:S(2)}, u32[]{:S(2)}) collective-permute-start(bf16[2,2,2,24,256]{4,3,2,1,0:T(8,128)(2,1)S(1)} %choose.1.refs_1_), channel_id=1, source_target_pairs={{0,2},{1,3},{2,0},{3,1},{4,6},{5,7},{6,4},{7,5},{8,10},{9,11},{10,... | collective-permute-start | bytes 294920 | tf_op jit(solution)/shard_map/ppermute | solution.py:43
  34.9 8.1 %collective-permute-start.10 = (bf16[144,128]{1,0:T(8,128)(2,1)S(1)}, bf16[144,128]{1,0:T(8,128)(2,1)S(1)}, u32[]{:S(2)}, u32[]{:S(2)}) collective-permute-start(bf16[144,128]{1,0:T(8,128)(2,1)S(1)} %get-tuple-element.15), channel_id=1, source_target_pairs={{0,64},{1,65},{2,66},{3,67},{4,68},{5,69},{6,70},{7,71},{8,72},{9,... | collective-permute-start | bytes 110600 | tf_op jit(solution)/shard_map/ppermute | solution.py:43
  38.2 6.1 %collective-permute-start.11 = (bf16[144,128]{1,0:T(8,128)(2,1)S(1)}, bf16[144,128]{1,0:T(8,128)(2,1)S(1)}, u32[]{:S(2)}, u32[]{:S(2)}) collective-permute-start(bf16[144,128]{1,0:T(8,128)(2,1)S(1)} %get-tuple-element.16), channel_id=1, source_target_pairs={{0,96},{1,97},{2,98},{3,99},{4,100},{5,101},{6,102},{7,103},{8,104... | collective-permute-start | bytes 110600 | tf_op jit(solution)/shard_map/ppermute | solution.py:43
  39.1 5.2 %collective-permute-start.12 = (bf16[144,128]{1,0:T(8,128)(2,1)S(1)}, bf16[144,128]{1,0:T(8,128)(2,1)S(1)}, u32[]{:S(2)}, u32[]{:S(2)}) collective-permute-start(bf16[144,128]{1,0:T(8,128)(2,1)S(1)} %get-tuple-element.17), channel_id=1, source_target_pairs={{0,32},{1,33},{2,34},{3,35},{4,36},{5,37},{6,38},{7,39},{8,40},{9,... | collective-permute-start | bytes 110600 | tf_op jit(solution)/shard_map/ppermute | solution.py:43

commit v10 on v9

--- a/solution.py
+++ b/solution.py
@@ -198,19 +198,23 @@
     return jnp.concatenate([acc[:, :span] * scale, acc[:, span:] * scale], axis=0)
 
 
-def gram_kernel(scale, right, q, before, out):
+def gram_kernel(scale, right, q, before, out, packed):
     out[...] = products(scale, right, q)
-
-
-def last_kernel(scale, right, q, g0, g3, g1, p0, p1, p2, p3, total):
+    pack(out, packed)
+
+
+def last_kernel(scale, right, q, *refs):
+    early, (p0, p1, p2, p3, total, wire) = refs[:-6], refs[-6:]
     turn = ((shot_index() >> 2) ^ lax.axis_index("rcv")) & 3
-    total[turn] = g0[...]
-    total[turn ^ 3] = g3[...]
-    total[turn ^ 1] = g1[...]
-    total[turn ^ 2] = products(scale, right, q)
+    for m in range(QUARTERS - 1):
+        total[turn ^ m] = early[2 * m][...]
+        wire[turn ^ m] = early[2 * m + 1][...]
+    last = turn ^ (QUARTERS - 1)
+    total[last] = products(scale, right, q)
+    pack(total.at[last], wire.at[last])
     p0[...] = total[0]
     for n, out in ((1, p1), (2, p2), (3, p3)):
-        pack(total[n], out)
+        out[...] = wire[n]
 
 
 def pack(share, out):
@@ -322,22 +326,20 @@
     width = 128
     wire = shape((rows * receivers // width, width), bf16)
     early = []
-    for m in (0, 3, 1):
-        early += [
-            local(
-                lambda *refs: gram_kernel(scale, *refs),
-                "gram",
-                share,
-                vmem(2) + [pl.BlockSpec(memory_space=pl.ANY)],
-            )(right, qs[m], early[-1] if early else right)
-        ]
+    for m in range(QUARTERS - 1):
+        early += local(
+            lambda *refs: gram_kernel(scale, *refs),
+            "gram",
+            (share, wire),
+            vmem(2) + [pl.BlockSpec(memory_space=pl.ANY)],
+        )(right, qs[m], early[-2] if early else right)
     p0, p1, p2, p3 = local(
         lambda *refs: last_kernel(scale, *refs),
         "last_gram",
         (share, wire, wire, wire),
-        vmem(5),
-        [pltpu.VMEM((QUARTERS, rows, receivers), f32)],
-    )(right, qs[2], *early)
+        vmem(2 + len(early)),
+        [pltpu.VMEM((QUARTERS,) + share.shape, f32), pltpu.VMEM((QUARTERS,) + wire.shape, bf16)],
+    )(right, qs[3], *early)
     r1, r2, r3 = [send(p, lambda yh, u, k, xh, v, n=n: (yh, u ^ n, k, xh, v)) for n, p in ((1, p1), (2, p2), (3, p3))]
     sums = local(sum_kernel, "sum", share, vmem(4))(r2, r3, r1, p0)
     return sums.reshape(2, NF, count, receivers).transpose(0, 1, 3, 2)

time: 45.5 us -> 45.6 us (level)
    pallas_call x3, Pallas kernels: 1.34 us -> 1.82 us  [per_device(): local(lambda *refs: gram_kernel(scale, *refs), 'gram', (share, wire), vme...]
  transfers between devices with their start and end apart: 13 -> 13, of which waited for: 9 -> 9; matrix products, arithmetic and copies ran while one was open for 0% -> 0% of each run, Pallas kernels for 7% -> 8%
where the time goes in v10:
time: 45.6 us; the launch traced here: 45.1 us
  waiting for transfers between devices  21.5 us (47%)
  starting transfers between devices  16.5 us (36%)
  Pallas kernels  6.94 us (15%)
    ppermute x13, waiting for transfers between devices, send(): return lax.ppermute(block, ('shot', 'rcv'), route)  21.5 us
    ppermute x13, starting transfers between devices, send(): return lax.ppermute(block, ('shot', 'rcv'), route)  16.5 us
    pallas_call x3, Pallas kernels, per_device(): local(lambda *refs: gram_kernel(scale, *refs), 'gram', (share, wire), vme...  1.82 us
    pallas_call x1, Pallas kernels, per_device(): local(own_kernel, 'own_spectra', shape((lanes - late_rows, receivers), f3...  1.58 us
    pallas_call x1, Pallas kernels, per_device(): local(tail_kernel, 'tail_spectra', shape((late_rows + LATE, receivers), f...  1.44 us
  transfers between devices with their start and end apart: 13, of which 9 were waited for; matrix products, arithmetic and copies ran while one was open for 0% of the time, Pallas kernels for 8%

profile of v10, /device:TPU:4, one launch (start us, length us, event | category | flops | bytes accessed | tf_op | source)
XLA Modules:
  0.0 45.1 jit_solution(5663117179749281814)
XLA Ops:
  0.0 0.0 copy-start.1
  0.0 0.0 copy-start
  0.0 0.0 copy-start.2
  0.0 1.4 %tail_spectra.1 = f32[72,96]{1,0:T(8,128)S(1)} custom-call(s32[32]{0:T(128)} %fire_hbm.1, f32[8,2560]{1,0:T(8,128)} %constant.2.clone.table.table_hbm, bf16[96,8192]{1,0:T(8,128)(2,1)} %head.1), custom_call_target="tpu_custom_call" | custom-call | tf_op jit(solution)/shard_map/tail_spectra/pallas_call | solution.py:263
  1.5 0.1 collective-permute-start
  1.6 0.0 copy-done.1
  1.6 0.1 copy-done
  1.6 0.0 copy-done.2
  1.6 1.6 %own_spectra.1.total = f32[192,96]{1,0:T(8,128)S(1)} custom-call(s32[32]{0:T(128)S(1)} %copy-done.2, f32[8,2560]{1,0:T(8,128)S(1)} %copy-done.1, bf16[96,8192]{1,0:T(8,128)(2,1)S(1)} %copy-done), custom_call_target="tpu_custom_call" | custom-call | tf_op jit(solution)/shard_map/own_spectra/pallas_call | solution.py:282
  3.2 7.9 %collective-permute-done.message = f32[72,96]{1,0:T(8,128)S(1)} collective-permute-done((f32[72,96]{1,0:T(8,128)S(1)}, f32[72,96]{1,0:T(8,128)S(1)}, u32[]{:S(2)}, u32[]{:S(2)}) %collective-permute-start) | collective-permute-done | bytes 27680 | tf_op jit(solution)/shard_map/ppermute | solution.py:43
  11.1 0.6 %finish_spectra.1.y0 = bf16[4,24,256]{2,1,0:T(8,128)(2,1)S(1)} custom-call(f32[192,96]{1,0:T(8,128)S(1)} %own_spectra.1.total, bf16[96,8192]{1,0:T(8,128)(2,1)S(1)} %copy-done, f32[8,2560]{1,0:T(8,128)S(1)} %copy-done.1, f32[72,96]{1,0:T(8,128)S(1)} %collective-permute-done.message), custom_call_target="tpu_custom_call" | custom-call | tf_op jit(solution)/shard_map/finish_spectra/pallas_call | solution.py:289
  11.7 0.1 collective-permute-start.1
  11.8 0.7 %collective-permute-start.2 = (bf16[4,24,256]{2,1,0:T(8,128)(2,1)S(1)}, bf16[4,24,256]{2,1,0:T(8,128)(2,1)S(1)}, u32[]{:S(2)}, u32[]{:S(2)}) collective-permute-start(bf16[4,24,256]{2,1,0:T(8,128)(2,1)S(1)} %finish_spectra.1.y0), channel_id=1, source_target_pairs={{0,128},{1,129},{2,130},{3,131},{4,132},{5,133},{6,134},{7,135},{8... | collective-permute-start | bytes 147464 | tf_op jit(solution)/shard_map/ppermute | solution.py:43
  12.5 4.3 %collective-permute-start.3 = (bf16[4,24,256]{2,1,0:T(8,128)(2,1)S(1)}, bf16[4,24,256]{2,1,0:T(8,128)(2,1)S(1)}, u32[]{:S(2)}, u32[]{:S(2)}) collective-permute-start(bf16[4,24,256]{2,1,0:T(8,128)(2,1)S(1)} %finish_spectra.1.y0), channel_id=1, source_target_pairs={{0,16},{1,17},{2,18},{3,19},{4,20},{5,21},{6,22},{7,23},{8,24},{9,... | collective-permute-start | bytes 147464 | tf_op jit(solution)/shard_map/ppermute | solution.py:43
  16.8 1.5 %collective-permute-done.1.y3 = bf16[4,24,256]{2,1,0:T(8,128)(2,1)S(1)} collective-permute-done((bf16[4,24,256]{2,1,0:T(8,128)(2,1)S(1)}, bf16[4,24,256]{2,1,0:T(8,128)(2,1)S(1)}, u32[]{:S(2)}, u32[]{:S(2)}) %collective-permute-start.1) | collective-permute-done | bytes 49184 | tf_op jit(solution)/shard_map/ppermute | solution.py:43
  18.3 0.0 collective-permute-done.2.y2
  18.3 0.6 %collective-permute-done.3.y1 = bf16[4,24,256]{2,1,0:T(8,128)(2,1)S(1)} collective-permute-done((bf16[4,24,256]{2,1,0:T(8,128)(2,1)S(1)}, bf16[4,24,256]{2,1,0:T(8,128)(2,1)S(1)}, u32[]{:S(2)}, u32[]{:S(2)}) %collective-permute-start.3) | collective-permute-done | bytes 49184 | tf_op jit(solution)/shard_map/ppermute | solution.py:43
  18.9 0.1 collective-permute-start.5
  19.0 0.5 %collective-permute-start.4 = (bf16[2,2,4,24,256]{4,3,2,1,0:T(8,128)(2,1)S(1)}, bf16[2,2,4,24,256]{4,3,2,1,0:T(8,128)(2,1)S(1)}, u32[]{:S(2)}, u32[]{:S(2)}) collective-permute-start(bf16[2,2,4,24,256]{4,3,2,1,0:T(8,128)(2,1)S(1)} %get-tuple-element.18.own), channel_id=1, source_target_pairs={{0,8},{1,9},{2,10},{3,11},{4,12},{5,13},{6,14},{7,15},{8,0},{9,1},... | collective-permute-start | bytes 589832 | tf_op jit(solution)/shard_map/ppermute | solution.py:43
  19.5 0.7 %collective-permute-done.5.other = bf16[2,2,24,256]{3,2,1,0:T(8,128)(2,1)S(1)} collective-permute-done((bf16[2,2,24,256]{3,2,1,0:T(8,128)(2,1)S(1)}, bf16[2,2,24,256]{3,2,1,0:T(8,128)(2,1)S(1)}, u32[]{:S(2)}, u32[]{:S(2)}) %collective-permute-start.5) | collective-permute-done | bytes 49184 | tf_op jit(solution)/shard_map/ppermute | solution.py:43
  20.2 0.6 %collective-permute-start.6 = (bf16[2,2,2,24,256]{4,3,2,1,0:T(8,128)(2,1)S(1)}, bf16[2,2,2,24,256]{4,3,2,1,0:T(8,128)(2,1)S(1)}, u32[]{:S(2)}, u32[]{:S(2)}) collective-permute-start(bf16[2,2,2,24,256]{4,3,2,1,0:T(8,128)(2,1)S(1)} %join_core.1.own), channel_id=1, source_target_pairs={{0,4},{1,5},{2,6},{3,7},{4,0},{5,1},{6,2},{7,3},{8,12},{9,13},{10,... | collective-permute-start | bytes 294920 | tf_op jit(solution)/shard_map/ppermute | solution.py:43
  20.8 5.9 %collective-permute-done.6.cross = bf16[2,2,2,24,256]{4,3,2,1,0:T(8,128)(2,1)S(1)} collective-permute-done((bf16[2,2,2,24,256]{4,3,2,1,0:T(8,128)(2,1)S(1)}, bf16[2,2,2,24,256]{4,3,2,1,0:T(8,128)(2,1)S(1)}, u32[]{:S(2)}, u32[]{:S(2)}) %collective-permute-start.6) | collective-permute-done | bytes 98336 | tf_op jit(solution)/shard_map/ppermute | solution.py:43
  26.7 0.8 %collective-permute-start.8 = (bf16[2,2,2,24,256]{4,3,2,1,0:T(8,128)(2,1)S(1)}, bf16[2,2,2,24,256]{4,3,2,1,0:T(8,128)(2,1)S(1)}, u32[]{:S(2)}, u32[]{:S(2)}) collective-permute-start(bf16[2,2,2,24,256]{4,3,2,1,0:T(8,128)(2,1)S(1)} %choose.1.refs_1_), channel_id=1, source_target_pairs={{0,1},{1,0},{2,3},{3,2},{4,5},{5,4},{6,7},{7,6},{8,9},{9,8},{10,11... | collective-permute-start | bytes 294920 | tf_op jit(solution)/shard_map/ppermute | solution.py:43
  27.5 1.2 %collective-permute-start.9 = (bf16[2,2,2,24,256]{4,3,2,1,0:T(8,128)(2,1)S(1)}, bf16[2,2,2,24,256]{4,3,2,1,0:T(8,128)(2,1)S(1)}, u32[]{:S(2)}, u32[]{:S(2)}) collective-permute-start(bf16[2,2,2,24,256]{4,3,2,1,0:T(8,128)(2,1)S(1)} %choose.1.refs_1_), channel_id=1, source_target_pairs={{0,2},{1,3},{2,0},{3,1},{4,6},{5,7},{6,4},{7,5},{8,10},{9,11},{10,... | collective-permute-start | bytes 294920 | tf_op jit(solution)/shard_map/ppermute | solution.py:43
  28.7 1.6 %collective-permute-start.7 = (bf16[2,2,2,24,256]{4,3,2,1,0:T(8,128)(2,1)S(1)}, bf16[2,2,2,24,256]{4,3,2,1,0:T(8,128)(2,1)S(1)}, u32[]{:S(2)}, u32[]{:S(2)}) collective-permute-start(bf16[2,2,2,24,256]{4,3,2,1,0:T(8,128)(2,1)S(1)} %choose.1.refs_1_), channel_id=1, source_target_pairs={{0,3},{1,2},{2,1},{3,0},{4,7},{5,6},{6,5},{7,4},{8,11},{9,10},{10,... | collective-permute-start | bytes 294920 | tf_op jit(solution)/shard_map/ppermute | solution.py:43
  30.3 0.0 collective-permute-done.4.other
  30.3 0.1 right_side.1.refs_0_.refs_2_
  30.4 0.6 %gram.3 = (f32[192,96]{1,0:T(8,128)S(1)}, bf16[144,128]{1,0:T(8,128)(2,1)S(1)}) custom-call(bf16[8,192,256]{2,1,0:T(8,128)(2,1)S(1)} %right_side.1.refs_0_.refs_2_, bf16[2,2,2,24,256]{4,3,2,1,0:T(8,128)(2,1)S(1)} %choose.1.refs_1_, bf16[8,192,256]{2,1,0:T(8,128)(2,1)S(1)} %right_side.1.refs_0_.refs_2_), custom_call_target="tpu_custom_call" | custom-call | tf_op jit(solution)/shard_map/gram/pallas_call | solution.py:330
  31.0 1.5 %collective-permute-done.8.refs_1_ = bf16[2,2,2,24,256]{4,3,2,1,0:T(8,128)(2,1)S(1)} collective-permute-done((bf16[2,2,2,24,256]{4,3,2,1,0:T(8,128)(2,1)S(1)}, bf16[2,2,2,24,256]{4,3,2,1,0:T(8,128)(2,1)S(1)}, u32[]{:S(2)}, u32[]{:S(2)}) %collective-permute-start.8) | collective-permute-done | bytes 98336 | tf_op jit(solution)/shard_map/ppermute | solution.py:43
  32.5 0.6 %gram.4 = (f32[192,96]{1,0:T(8,128)S(1)}, bf16[144,128]{1,0:T(8,128)(2,1)S(1)}) custom-call(bf16[8,192,256]{2,1,0:T(8,128)(2,1)S(1)} %right_side.1.refs_0_.refs_2_, bf16[2,2,2,24,256]{4,3,2,1,0:T(8,128)(2,1)S(1)} %collective-permute-done.8.refs_1_, f32[192,96]{1,0:T(8,128)S(1)} %get-tuple-element.21.refs_2_), custom_call_target="tpu_custom_call" | custom-call | tf_op jit(solution)/shard_map/gram/pallas_call | solution.py:330
  33.1 0.0 collective-permute-done.9.refs_1_
  33.1 0.6 %gram.5 = (f32[192,96]{1,0:T(8,128)S(1)}, bf16[144,128]{1,0:T(8,128)(2,1)S(1)}) custom-call(bf16[8,192,256]{2,1,0:T(8,128)(2,1)S(1)} %right_side.1.refs_0_.refs_2_, bf16[2,2,2,24,256]{4,3,2,1,0:T(8,128)(2,1)S(1)} %collective-permute-done.9.refs_1_, f32[192,96]{1,0:T(8,128)S(1)} %get-tuple-element.23.refs_2_.refs_4_), custom_call_target="tpu_custom_call" | custom-call | tf_op jit(solution)/shard_map/gram/pallas_call | solution.py:330
  33.7 0.5 %collective-permute-done.7.refs_1_ = bf16[2,2,2,24,256]{4,3,2,1,0:T(8,128)(2,1)S(1)} collective-permute-done((bf16[2,2,2,24,256]{4,3,2,1,0:T(8,128)(2,1)S(1)}, bf16[2,2,2,24,256]{4,3,2,1,0:T(8,128)(2,1)S(1)}, u32[]{:S(2)}, u32[]{:S(2)}) %collective-permute-start.7) | collective-permute-done | bytes 98336 | tf_op jit(solution)/shard_map/ppermute | solution.py:43
  34.2 0.6 %last_gram.1 = (f32[192,96]{1,0:T(8,128)S(1)}, bf16[144,128]{1,0:T(8,128)(2,1)S(1)}, bf16[144,128]{1,0:T(8,128)(2,1)S(1)}, bf16[144,128]{1,0:T(8,128)(2,1)S(1)}) custom-call(bf16[8,192,256]{2,1,0:T(8,128)(2,1)S(1)} %right_side.1.refs_0_.refs_2_, bf16[2,2,2,24,256]{4,3,2,1,0:T(8,128)(2,1)S(1)} %collective-permute-done.7.refs_1_, ...), custom_call_target="tpu_custom_call" | custom-call | tf_op jit(solution)/shard_map/last_gram/pallas_call | solution.py:336
  34.8 3.5 %collective-permute-start.10 = (bf16[144,128]{1,0:T(8,128)(2,1)S(1)}, bf16[144,128]{1,0:T(8,128)(2,1)S(1)}, u32[]{:S(2)}, u32[]{:S(2)}) collective-permute-start(bf16[144,128]{1,0:T(8,128)(2,1)S(1)} %get-tuple-element.27), channel_id=1, source_target_pairs={{0,64},{1,65},{2,66},{3,67},{4,68},{5,69},{6,70},{7,71},{8,72},{9,... | collective-permute-start | bytes 110600 | tf_op jit(solution)/shard_map/ppermute | solution.py:43
  38.3 0.7 %collective-permute-start.11 = (bf16[144,128]{1,0:T(8,128)(2,1)S(1)}, bf16[144,128]{1,0:T(8,128)(2,1)S(1)}, u32[]{:S(2)}, u32[]{:S(2)}) collective-permute-start(bf16[144,128]{1,0:T(8,128)(2,1)S(1)} %get-tuple-element.28), channel_id=1, source_target_pairs={{0,96},{1,97},{2,98},{3,99},{4,100},{5,101},{6,102},{7,103},{8,104... | collective-permute-start | bytes 110600 | tf_op jit(solution)/shard_map/ppermute | solution.py:43
  39.0 2.4 %collective-permute-start.12 = (bf16[144,128]{1,0:T(8,128)(2,1)S(1)}, bf16[144,128]{1,0:T(8,128)(2,1)S(1)}, u32[]{:S(2)}, u32[]{:S(2)}) collective-permute-start(bf16[144,128]{1,0:T(8,128)(2,1)S(1)} %get-tuple-element.29), channel_id=1, source_target_pairs={{0,32},{1,33},{2,34},{3,35},{4,36},{5,37},{6,38},{7,39},{8,40},{9,... | collective-permute-start | bytes 110600 | tf_op jit(solution)/shard_map/ppermute | solution.py:43
  41.4 1.4 %collective-permute-done.10.r2 = bf16[144,128]{1,0:T(8,128)(2,1)S(1)} collective-permute-done((bf16[144,128]{1,0:T(8,128)(2,1)S(1)}, bf16[144,128]{1,0:T(8,128)(2,1)S(1)}, u32[]{:S(2)}, u32[]{:S(2)}) %collective-permute-start.10) | collective-permute-done | bytes 36896 | tf_op jit(solution)/shard_map/ppermute | solution.py:43
  42.8 1.6 %collective-permute-done.11.r3 = bf16[144,128]{1,0:T(8,128)(2,1)S(1)} collective-permute-done((bf16[144,128]{1,0:T(8,128)(2,1)S(1)}, bf16[144,128]{1,0:T(8,128)(2,1)S(1)}, u32[]{:S(2)}, u32[]{:S(2)}) %collective-permute-start.11) | collective-permute-done | bytes 36896 | tf_op jit(solution)/shard_map/ppermute | solution.py:43
  44.4 0.0 collective-permute-done.12.r1
  44.4 0.7 %sum.1 = f32[192,96]{1,0:T(8,128)} custom-call(bf16[144,128]{1,0:T(8,128)(2,1)S(1)} %collective-permute-done.10.r2, bf16[144,128]{1,0:T(8,128)(2,1)S(1)} %collective-permute-done.11.r3, bf16[144,128]{1,0:T(8,128)(2,1)S(1)} %collective-permute-done.12.r1, f32[192,96]{1,0:T(8,128)S(1)} %get-tuple-element.30.p0), custom_call_target="tpu_custom_call" | custom-call | tf_op jit(solution)/shard_map/sum/pallas_call | solution.py:344
  (3 shorter events, 0.0 us)
Async XLA Ops:
  0.0 1.6 %copy-start.1 = (f32[8,2560]{1,0:T(8,128)S(1)}, f32[8,2560]{1,0:T(8,128)}, u32[]{:S(2)}) copy-start(f32[8,2560]{1,0:T(8,128)} %constant.2.clone.table.table_hbm) | copy-start | bytes 245764
  0.0 1.6 %copy-start = (bf16[96,8192]{1,0:T(8,128)(2,1)S(1)}, bf16[96,8192]{1,0:T(8,128)(2,1)}, u32[]{:S(2)}) copy-start(bf16[96,8192]{1,0:T(8,128)(2,1)} %head.1) | copy-start | bytes 4718596
  0.0 1.6 %copy-start.2 = (s32[32]{0:T(128)S(1)}, s32[32]{0:T(128)}, u32[]{:S(2)}) copy-start(s32[32]{0:T(128)} %fire_hbm.1) | copy-start | bytes 388
  1.5 9.6 %collective-permute-start = (f32[72,96]{1,0:T(8,128)S(1)}, f32[72,96]{1,0:T(8,128)S(1)}, u32[]{:S(2)}, u32[]{:S(2)}) collective-permute-start(f32[72,96]{1,0:T(8,128)S(1)} %tail_spectra.1), channel_id=1, source_target_pairs={{0,8},{1,9},{2,10},{3,11},{4,12},{5,13},{6,14},{7,15},{8,16},{9,17... | collective-permute-start | bytes 82952 | tf_op jit(solution)/shard_map/ppermute | solution.py:43
  11.7 6.6 %collective-permute-start.1 = (bf16[4,24,256]{2,1,0:T(8,128)(2,1)S(1)}, bf16[4,24,256]{2,1,0:T(8,128)(2,1)S(1)}, u32[]{:S(2)}, u32[]{:S(2)}) collective-permute-start(bf16[4,24,256]{2,1,0:T(8,128)(2,1)S(1)} %finish_spectra.1.y0), channel_id=1, source_target_pairs={{0,144},{1,145},{2,146},{3,147},{4,148},{5,149},{6,150},{7,151},{8... | collective-permute-start | bytes 147464 | tf_op jit(solution)/shard_map/ppermute | solution.py:43
  11.8 6.5 %collective-permute-start.2 = (bf16[4,24,256]{2,1,0:T(8,128)(2,1)S(1)}, bf16[4,24,256]{2,1,0:T(8,128)(2,1)S(1)}, u32[]{:S(2)}, u32[]{:S(2)}) collective-permute-start(bf16[4,24,256]{2,1,0:T(8,128)(2,1)S(1)} %finish_spectra.1.y0), channel_id=1, source_target_pairs={{0,128},{1,129},{2,130},{3,131},{4,132},{5,133},{6,134},{7,135},{8... | collective-permute-start | bytes 147464 | tf_op jit(solution)/shard_map/ppermute | solution.py:43
  12.5 6.3 %collective-permute-start.3 = (bf16[4,24,256]{2,1,0:T(8,128)(2,1)S(1)}, bf16[4,24,256]{2,1,0:T(8,128)(2,1)S(1)}, u32[]{:S(2)}, u32[]{:S(2)}) collective-permute-start(bf16[4,24,256]{2,1,0:T(8,128)(2,1)S(1)} %finish_spectra.1.y0), channel_id=1, source_target_pairs={{0,16},{1,17},{2,18},{3,19},{4,20},{5,21},{6,22},{7,23},{8,24},{9,... | collective-permute-start | bytes 147464 | tf_op jit(solution)/shard_map/ppermute | solution.py:43
  18.9 1.3 %collective-permute-start.5 = (bf16[2,2,24,256]{3,2,1,0:T(8,128)(2,1)S(1)}, bf16[2,2,24,256]{3,2,1,0:T(8,128)(2,1)S(1)}, u32[]{:S(2)}, u32[]{:S(2)}) collective-permute-start(bf16[2,2,24,256]{3,2,1,0:T(8,128)(2,1)S(1)} %get-tuple-element.20), channel_id=1, source_target_pairs={{0,8},{1,9},{2,10},{3,11},{4,12},{5,13},{6,14},{7,15},{8,0},{9,1},... | collective-permute-start | bytes 147464 | tf_op jit(solution)/shard_map/ppermute | solution.py:43
  19.0 11.3 %collective-permute-start.4 = (bf16[2,2,4,24,256]{4,3,2,1,0:T(8,128)(2,1)S(1)}, bf16[2,2,4,24,256]{4,3,2,1,0:T(8,128)(2,1)S(1)}, u32[]{:S(2)}, u32[]{:S(2)}) collective-permute-start(bf16[2,2,4,24,256]{4,3,2,1,0:T(8,128)(2,1)S(1)} %get-tuple-element.18.own), channel_id=1, source_target_pairs={{0,8},{1,9},{2,10},{3,11},{4,12},{5,13},{6,14},{7,15},{8,0},{9,1},... | collective-permute-start | bytes 589832 | tf_op jit(solution)/shard_map/ppermute | solution.py:43
  20.2 6.5 %collective-permute-start.6 = (bf16[2,2,2,24,256]{4,3,2,1,0:T(8,128)(2,1)S(1)}, bf16[2,2,2,24,256]{4,3,2,1,0:T(8,128)(2,1)S(1)}, u32[]{:S(2)}, u32[]{:S(2)}) collective-permute-start(bf16[2,2,2,24,256]{4,3,2,1,0:T(8,128)(2,1)S(1)} %join_core.1.own), channel_id=1, source_target_pairs={{0,4},{1,5},{2,6},{3,7},{4,0},{5,1},{6,2},{7,3},{8,12},{9,13},{10,... | collective-permute-start | bytes 294920 | tf_op jit(solution)/shard_map/ppermute | solution.py:43
  26.7 5.8 %collective-permute-start.8 = (bf16[2,2,2,24,256]{4,3,2,1,0:T(8,128)(2,1)S(1)}, bf16[2,2,2,24,256]{4,3,2,1,0:T(8,128)(2,1)S(1)}, u32[]{:S(2)}, u32[]{:S(2)}) collective-permute-start(bf16[2,2,2,24,256]{4,3,2,1,0:T(8,128)(2,1)S(1)} %choose.1.refs_1_), channel_id=1, source_target_pairs={{0,1},{1,0},{2,3},{3,2},{4,5},{5,4},{6,7},{7,6},{8,9},{9,8},{10,11... | collective-permute-start | bytes 294920 | tf_op jit(solution)/shard_map/ppermute | solution.py:43
  27.5 5.6 %collective-permute-start.9 = (bf16[2,2,2,24,256]{4,3,2,1,0:T(8,128)(2,1)S(1)}, bf16[2,2,2,24,256]{4,3,2,1,0:T(8,128)(2,1)S(1)}, u32[]{:S(2)}, u32[]{:S(2)}) collective-permute-start(bf16[2,2,2,24,256]{4,3,2,1,0:T(8,128)(2,1)S(1)} %choose.1.refs_1_), channel_id=1, source_target_pairs={{0,2},{1,3},{2,0},{3,1},{4,6},{5,7},{6,4},{7,5},{8,10},{9,11},{10,... | collective-permute-start | bytes 294920 | tf_op jit(solution)/shard_map/ppermute | solution.py:43
  28.7 5.5 %collective-permute-start.7 = (bf16[2,2,2,24,256]{4,3,2,1,0:T(8,128)(2,1)S(1)}, bf16[2,2,2,24,256]{4,3,2,1,0:T(8,128)(2,1)S(1)}, u32[]{:S(2)}, u32[]{:S(2)}) collective-permute-start(bf16[2,2,2,24,256]{4,3,2,1,0:T(8,128)(2,1)S(1)} %choose.1.refs_1_), channel_id=1, source_target_pairs={{0,3},{1,2},{2,1},{3,0},{4,7},{5,6},{6,5},{7,4},{8,11},{9,10},{10,... | collective-permute-start | bytes 294920 | tf_op jit(solution)/shard_map/ppermute | solution.py:43
  34.8 8.0 %collective-permute-start.10 = (bf16[144,128]{1,0:T(8,128)(2,1)S(1)}, bf16[144,128]{1,0:T(8,128)(2,1)S(1)}, u32[]{:S(2)}, u32[]{:S(2)}) collective-permute-start(bf16[144,128]{1,0:T(8,128)(2,1)S(1)} %get-tuple-element.27), channel_id=1, source_target_pairs={{0,64},{1,65},{2,66},{3,67},{4,68},{5,69},{6,70},{7,71},{8,72},{9,... | collective-permute-start | bytes 110600 | tf_op jit(solution)/shard_map/ppermute | solution.py:43
  38.3 6.1 %collective-permute-start.11 = (bf16[144,128]{1,0:T(8,128)(2,1)S(1)}, bf16[144,128]{1,0:T(8,128)(2,1)S(1)}, u32[]{:S(2)}, u32[]{:S(2)}) collective-permute-start(bf16[144,128]{1,0:T(8,128)(2,1)S(1)} %get-tuple-element.28), channel_id=1, source_target_pairs={{0,96},{1,97},{2,98},{3,99},{4,100},{5,101},{6,102},{7,103},{8,104... | collective-permute-start | bytes 110600 | tf_op jit(solution)/shard_map/ppermute | solution.py:43
  39.0 5.4 %collective-permute-start.12 = (bf16[144,128]{1,0:T(8,128)(2,1)S(1)}, bf16[144,128]{1,0:T(8,128)(2,1)S(1)}, u32[]{:S(2)}, u32[]{:S(2)}) collective-permute-start(bf16[144,128]{1,0:T(8,128)(2,1)S(1)} %get-tuple-element.29), channel_id=1, source_target_pairs={{0,32},{1,33},{2,34},{3,35},{4,36},{5,37},{6,38},{7,39},{8,40},{9,... | collective-permute-start | bytes 110600 | tf_op jit(solution)/shard_map/ppermute | solution.py:43

commit v11 on v10

--- a/solution.py
+++ b/solution.py
@@ -22,6 +22,7 @@
 RCV_DEVICES = 8
 QUARTERS = 4
 LATE = WIN // SPACING
+MIDDLE = SHOT_DEVICES // 2
 
 
 def dft_master():
@@ -106,31 +107,33 @@
     add_products(message, tables, pairs - late, blocks)
 
 
-def own_kernel(fire, table, record, total, tables):
+def own_kernel(fire, table, record, total, first, tables):
     pairs = record.shape[1] // PAIR
     master = table[...]
     for p in range(tables.shape[0]):
         tables[p] = pair_tables(master, delay(fire, 2 * p), delay(fire, 2 * p + 1))
     total[...] = jnp.zeros_like(total)
     add_products(total, tables, 0, [(u, record[:, PAIR * u : PAIR * (u + 1)]) for u in range(pairs)])
-
-
-def finish_kernel(total, head, table, message, out, scratch, tables):
+    first[...] = total[: first.shape[0], :]
+
+
+def finish_kernel(total, head, table, received, moved, given, out, scratch, tables, message):
     own_rows = total.shape[0]
-    lanes = scratch.shape[0]
+    late_rows = ROWS * LATE
     late = LATE // 2
-    follows = (shot_index() > 0).astype(jnp.float32)
+    shot = shot_index()
     master = table[...]
+    message[...] = jnp.where(shot == MIDDLE - 1, moved[...], received[...])
     for p in range(late):
-        rows = [message[ROWS * LATE + 2 * p + i : ROWS * LATE + 2 * p + i + 1, :] for i in range(2)]
+        rows = [message[late_rows + 2 * p + i : late_rows + 2 * p + i + 1, :] for i in range(2)]
         first, second = [jnp.max(r).astype(jnp.int32) for r in rows]
         tables[p] = pair_tables(master, first, second)
-    scratch[:own_rows, :] = jnp.zeros_like(total)
-    scratch[own_rows:, :] = jnp.zeros((lanes - own_rows, total.shape[1]), jnp.float32)
+    scratch[own_rows:, :] = message[:late_rows, :]
     blocks = [(late + v, head[:, PAIR * v : PAIR * (v + 1)]) for v in range(late)]
     add_products(scratch.at[own_rows:, :], tables, 0, blocks)
-    scratch[own_rows:, :] = message[: ROWS * LATE, :] + follows * scratch[own_rows:, :]
-    scratch[:own_rows, :] = total[...]
+    scratch[own_rows:, :] = jnp.where(shot == 0, given[...], scratch[own_rows:, :])
+    scratch[late_rows:own_rows, :] = total[late_rows:, :]
+    scratch[:late_rows, :] = jnp.where(shot == MIDDLE, moved[:late_rows, :], total[:late_rows, :])
     turn_over(scratch, out)
 
 
@@ -274,18 +277,24 @@
         ],
     )(*(pltpu.with_memory_space_constraint(a, pltpu.HBM) for a in (shot_fire_samples, table, record)))
 
-    def following(yh, u, k, xh, v):
-        shot = ((yh << 4 | u << 2 | k) + 1) % SHOT_DEVICES
-        return shot >> 4, (shot >> 2) & 3, shot & 3, xh, v
-
-    received = send(message, following)
-    total = local(
+    def chain(route):
+        def to(yh, u, k, xh, v):
+            shot = route(yh << 4 | u << 2 | k)
+            return None if shot is None else (shot >> 4, (shot >> 2) & 3, shot & 3, xh, v)
+
+        return to
+
+    ends = {MIDDLE - 2: 0, SHOT_DEVICES - 1: MIDDLE - 1}
+    received = send(message, chain(lambda shot: ends.get(shot, shot + 1)))
+    moved = send(message, chain({MIDDLE - 2: MIDDLE - 1, SHOT_DEVICES - 1: MIDDLE}.get))
+    total, first = local(
         own_kernel,
         "own_spectra",
-        shape((lanes - late_rows, receivers), f32),
+        (shape((lanes - late_rows, receivers), f32), shape((late_rows, receivers), f32)),
         [smem] + vmem(2),
         [pltpu.VMEM((pairs - late, 2 * ROWS, SPAN), bf16)],
     )(shot_fire_samples, table, record)
+    given = send(first, chain({MIDDLE: 0}.get))
     y = pl.pallas_call(
         finish_kernel,
         grid=(1,),
@@ -295,12 +304,18 @@
             pl.BlockSpec((receivers, WIN), lambda i: (0, 0)),
             pl.BlockSpec(table.shape, lambda i: (0, 0)),
             pl.BlockSpec(received.shape, lambda i: (0, 0)),
+            pl.BlockSpec(moved.shape, lambda i: (0, 0)),
+            pl.BlockSpec(given.shape, lambda i: (0, 0)),
         ],
         out_specs=pl.BlockSpec((QUARTERS, count, lanes), lambda i: (0, 0, 0)),
-        scratch_shapes=[pltpu.VMEM((lanes, receivers), f32), pltpu.VMEM((late, 2 * ROWS, SPAN), bf16)],
+        scratch_shapes=[
+            pltpu.VMEM((lanes, receivers), f32),
+            pltpu.VMEM((late, 2 * ROWS, SPAN), bf16),
+            pltpu.VMEM(message.shape, f32),
+        ],
         compiler_params=pltpu.CompilerParams(vmem_limit_bytes=4 << 20),
         name="finish_spectra",
-    )(total, record, table, received)
+    )(total, record, table, received, moved, given)
 
     y3, y2, y1 = [send(y, lambda yh, u, k, xh, v, m=m: (yh ^ m >> 1, u, k ^ (m & 1) << 1, xh, v)) for m in (3, 2, 1)]
     slices = shape((2, 2, count, lanes), bf16)

time: 45.6 us -> 46.6 us (1.022)
  starting transfers between devices: 16.5 us -> 20.7 us
  waiting for transfers between devices: 21.5 us -> 18.2 us
    ppermute x13 -> x15, starting transfers between devices: 16.5 us -> 20.7 us  [send(): return lax.ppermute(block, ('shot', 'rcv'), route)]
    ppermute x13 -> x15, waiting for transfers between devices: 21.5 us -> 18.2 us  [send(): return lax.ppermute(block, ('shot', 'rcv'), route)]
  transfers between devices with their start and end apart: 13 -> 15, of which waited for: 9 -> 11; matrix products, arithmetic and copies ran while one was open for 0% -> 0% of each run, Pallas kernels for 8% -> 8%
where the time goes in v11:
time: 46.6 us; the launch traced here: 46.1 us
  starting transfers between devices  20.7 us (44%)
  waiting for transfers between devices  18.2 us (39%)
  Pallas kernels  6.96 us (15%)
    ppermute x15, starting transfers between devices, send(): return lax.ppermute(block, ('shot', 'rcv'), route)  20.7 us
    ppermute x15, waiting for transfers between devices, send(): return lax.ppermute(block, ('shot', 'rcv'), route)  18.2 us
    pallas_call x3, Pallas kernels, per_device(): local(lambda *refs: gram_kernel(scale, *refs), 'gram', (share, wire), vme...  1.8 us
    pallas_call x1, Pallas kernels, per_device(): local(own_kernel, 'own_spectra', (shape((lanes - late_rows, receivers), f...  1.59 us
    pallas_call x1, Pallas kernels, per_device(): local(tail_kernel, 'tail_spectra', shape((late_rows + LATE, receivers), f...  1.44 us
  transfers between devices with their start and end apart: 15, of which 11 were waited for; matrix products, arithmetic and copies ran while one was open for 0% of the time, Pallas kernels for 8%

profile of v11, /device:TPU:4, one launch (start us, length us, event | category | flops | bytes accessed | tf_op | source)
XLA Modules:
  0.0 46.1 jit_solution(14157592141462754758)
XLA Ops:
  0.0 0.0 copy-start.1
  0.0 0.0 copy-start
  0.0 0.0 copy-start.2
  0.0 1.4 %tail_spectra.1 = f32[72,96]{1,0:T(8,128)S(1)} custom-call(s32[32]{0:T(128)} %fire_hbm.1, f32[8,2560]{1,0:T(8,128)} %constant.2.clone.table.table_hbm, bf16[96,8192]{1,0:T(8,128)(2,1)} %head.1), custom_call_target="tpu_custom_call" | custom-call | tf_op jit(solution)/shard_map/tail_spectra/pallas_call | solution.py:266
  1.5 0.1 collective-permute-start
  1.6 0.7 %collective-permute-start.1 = (f32[72,96]{1,0:T(8,128)S(1)}, f32[72,96]{1,0:T(8,128)S(1)}, u32[]{:S(2)}, u32[]{:S(2)}) collective-permute-start(f32[72,96]{1,0:T(8,128)S(1)} %tail_spectra.1), channel_id=1, source_target_pairs={{112,120},{113,121},{114,122},{115,123},{116,124},{117,125},{118,1... | collective-permute-start | bytes 82952 | tf_op jit(solution)/shard_map/ppermute | solution.py:44
  2.2 0.0 copy-done.1
  2.2 0.0 copy-done
  2.3 0.0 copy-done.2
  2.3 1.6 %own_spectra.1 = (f32[192,96]{1,0:T(8,128)S(1)}, f32[64,96]{1,0:T(8,128)S(1)}) custom-call(s32[32]{0:T(128)S(1)} %copy-done.2, f32[8,2560]{1,0:T(8,128)S(1)} %copy-done.1, bf16[96,8192]{1,0:T(8,128)(2,1)S(1)} %copy-done), custom_call_target="tpu_custom_call" | custom-call | tf_op jit(solution)/shard_map/own_spectra/pallas_call | solution.py:290
  3.9 1.3 %collective-permute-start.2 = (f32[64,96]{1,0:T(8,128)S(1)}, f32[64,96]{1,0:T(8,128)S(1)}, u32[]{:S(2)}, u32[]{:S(2)}) collective-permute-start(f32[64,96]{1,0:T(8,128)S(1)} %get-tuple-element.21), channel_id=1, source_target_pairs={{128,0},{129,1},{130,2},{131,3},{132,4},{133,5},{134,6},{135,7}} | collective-permute-start | bytes 73736 | tf_op jit(solution)/shard_map/ppermute | solution.py:44
  5.2 6.0 %collective-permute-done.2.given = f32[64,96]{1,0:T(8,128)S(1)} collective-permute-done((f32[64,96]{1,0:T(8,128)S(1)}, f32[64,96]{1,0:T(8,128)S(1)}, u32[]{:S(2)}, u32[]{:S(2)}) %collective-permute-start.2) | collective-permute-done | bytes 24608 | tf_op jit(solution)/shard_map/ppermute | solution.py:44
  11.2 0.0 collective-permute-done.received
  11.2 0.0 collective-permute-done.1.moved
  11.2 0.6 %finish_spectra.1.y0 = bf16[4,24,256]{2,1,0:T(8,128)(2,1)S(1)} custom-call(f32[192,96]{1,0:T(8,128)S(1)} %get-tuple-element.20.total, bf16[96,8192]{1,0:T(8,128)(2,1)S(1)} %copy-done, f32[8,2560]{1,0:T(8,128)S(1)} %copy-done.1, f32[72,96]{1,0:T(8,128)S(1)} %collective-permute-done.received, f32[72,96]{1,0:T(8,128)S(1)} %collective-permute-done.1.moved, ...), custom_call_target="tpu_custom_call" | custom-call | tf_op jit(solution)/shard_map/finish_spectra/pallas_call | solution.py:298
  11.8 0.1 collective-permute-start.3
  11.9 1.9 %collective-permute-start.4 = (bf16[4,24,256]{2,1,0:T(8,128)(2,1)S(1)}, bf16[4,24,256]{2,1,0:T(8,128)(2,1)S(1)}, u32[]{:S(2)}, u32[]{:S(2)}) collective-permute-start(bf16[4,24,256]{2,1,0:T(8,128)(2,1)S(1)} %finish_spectra.1.y0), channel_id=1, source_target_pairs={{0,128},{1,129},{2,130},{3,131},{4,132},{5,133},{6,134},{7,135},{8... | collective-permute-start | bytes 147464 | tf_op jit(solution)/shard_map/ppermute | solution.py:44
  13.8 3.1 %collective-permute-start.5 = (bf16[4,24,256]{2,1,0:T(8,128)(2,1)S(1)}, bf16[4,24,256]{2,1,0:T(8,128)(2,1)S(1)}, u32[]{:S(2)}, u32[]{:S(2)}) collective-permute-start(bf16[4,24,256]{2,1,0:T(8,128)(2,1)S(1)} %finish_spectra.1.y0), channel_id=1, source_target_pairs={{0,16},{1,17},{2,18},{3,19},{4,20},{5,21},{6,22},{7,23},{8,24},{9,... | collective-permute-start | bytes 147464 | tf_op jit(solution)/shard_map/ppermute | solution.py:44
  16.9 1.5 %collective-permute-done.3.y3 = bf16[4,24,256]{2,1,0:T(8,128)(2,1)S(1)} collective-permute-done((bf16[4,24,256]{2,1,0:T(8,128)(2,1)S(1)}, bf16[4,24,256]{2,1,0:T(8,128)(2,1)S(1)}, u32[]{:S(2)}, u32[]{:S(2)}) %collective-permute-start.3) | collective-permute-done | bytes 49184 | tf_op jit(solution)/shard_map/ppermute | solution.py:44
  18.4 0.0 collective-permute-done.4.y2
  18.4 0.6 %collective-permute-done.5.y1 = bf16[4,24,256]{2,1,0:T(8,128)(2,1)S(1)} collective-permute-done((bf16[4,24,256]{2,1,0:T(8,128)(2,1)S(1)}, bf16[4,24,256]{2,1,0:T(8,128)(2,1)S(1)}, u32[]{:S(2)}, u32[]{:S(2)}) %collective-permute-start.5) | collective-permute-done | bytes 49184 | tf_op jit(solution)/shard_map/ppermute | solution.py:44
  19.0 0.1 collective-permute-start.7
  19.1 0.5 %collective-permute-start.6 = (bf16[2,2,4,24,256]{4,3,2,1,0:T(8,128)(2,1)S(1)}, bf16[2,2,4,24,256]{4,3,2,1,0:T(8,128)(2,1)S(1)}, u32[]{:S(2)}, u32[]{:S(2)}) collective-permute-start(bf16[2,2,4,24,256]{4,3,2,1,0:T(8,128)(2,1)S(1)} %get-tuple-element.22.own), channel_id=1, source_target_pairs={{0,8},{1,9},{2,10},{3,11},{4,12},{5,13},{6,14},{7,15},{8,0},{9,1},... | collective-permute-start | bytes 589832 | tf_op jit(solution)/shard_map/ppermute | solution.py:44
  19.6 0.7 %collective-permute-done.7.other = bf16[2,2,24,256]{3,2,1,0:T(8,128)(2,1)S(1)} collective-permute-done((bf16[2,2,24,256]{3,2,1,0:T(8,128)(2,1)S(1)}, bf16[2,2,24,256]{3,2,1,0:T(8,128)(2,1)S(1)}, u32[]{:S(2)}, u32[]{:S(2)}) %collective-permute-start.7) | collective-permute-done | bytes 49184 | tf_op jit(solution)/shard_map/ppermute | solution.py:44
  20.3 2.9 %collective-permute-start.8 = (bf16[2,2,2,24,256]{4,3,2,1,0:T(8,128)(2,1)S(1)}, bf16[2,2,2,24,256]{4,3,2,1,0:T(8,128)(2,1)S(1)}, u32[]{:S(2)}, u32[]{:S(2)}) collective-permute-start(bf16[2,2,2,24,256]{4,3,2,1,0:T(8,128)(2,1)S(1)} %join_core.1.own), channel_id=1, source_target_pairs={{0,4},{1,5},{2,6},{3,7},{4,0},{5,1},{6,2},{7,3},{8,12},{9,13},{10,... | collective-permute-start | bytes 294920 | tf_op jit(solution)/shard_map/ppermute | solution.py:44
  23.2 3.6 %collective-permute-done.8.cross = bf16[2,2,2,24,256]{4,3,2,1,0:T(8,128)(2,1)S(1)} collective-permute-done((bf16[2,2,2,24,256]{4,3,2,1,0:T(8,128)(2,1)S(1)}, bf16[2,2,2,24,256]{4,3,2,1,0:T(8,128)(2,1)S(1)}, u32[]{:S(2)}, u32[]{:S(2)}) %collective-permute-start.8) | collective-permute-done | bytes 98336 | tf_op jit(solution)/shard_map/ppermute | solution.py:44
  26.8 1.7 %collective-permute-start.10 = (bf16[2,2,2,24,256]{4,3,2,1,0:T(8,128)(2,1)S(1)}, bf16[2,2,2,24,256]{4,3,2,1,0:T(8,128)(2,1)S(1)}, u32[]{:S(2)}, u32[]{:S(2)}) collective-permute-start(bf16[2,2,2,24,256]{4,3,2,1,0:T(8,128)(2,1)S(1)} %choose.1.refs_1_), channel_id=1, source_target_pairs={{0,1},{1,0},{2,3},{3,2},{4,5},{5,4},{6,7},{7,6},{8,9},{9,8},{10,11... | collective-permute-start | bytes 294920 | tf_op jit(solution)/shard_map/ppermute | solution.py:44
  28.5 1.2 %collective-permute-start.11 = (bf16[2,2,2,24,256]{4,3,2,1,0:T(8,128)(2,1)S(1)}, bf16[2,2,2,24,256]{4,3,2,1,0:T(8,128)(2,1)S(1)}, u32[]{:S(2)}, u32[]{:S(2)}) collective-permute-start(bf16[2,2,2,24,256]{4,3,2,1,0:T(8,128)(2,1)S(1)} %choose.1.refs_1_), channel_id=1, source_target_pairs={{0,2},{1,3},{2,0},{3,1},{4,6},{5,7},{6,4},{7,5},{8,10},{9,11},{10,... | collective-permute-start | bytes 294920 | tf_op jit(solution)/shard_map/ppermute | solution.py:44
  29.7 0.7 %collective-permute-start.9 = (bf16[2,2,2,24,256]{4,3,2,1,0:T(8,128)(2,1)S(1)}, bf16[2,2,2,24,256]{4,3,2,1,0:T(8,128)(2,1)S(1)}, u32[]{:S(2)}, u32[]{:S(2)}) collective-permute-start(bf16[2,2,2,24,256]{4,3,2,1,0:T(8,128)(2,1)S(1)} %choose.1.refs_1_), channel_id=1, source_target_pairs={{0,3},{1,2},{2,1},{3,0},{4,7},{5,6},{6,5},{7,4},{8,11},{9,10},{10,... | collective-permute-start | bytes 294920 | tf_op jit(solution)/shard_map/ppermute | solution.py:44
  30.4 0.0 collective-permute-done.6.other
  30.4 0.1 right_side.1.refs_0_.refs_2_
  30.5 0.6 %gram.3 = (f32[192,96]{1,0:T(8,128)S(1)}, bf16[144,128]{1,0:T(8,128)(2,1)S(1)}) custom-call(bf16[8,192,256]{2,1,0:T(8,128)(2,1)S(1)} %right_side.1.refs_0_.refs_2_, bf16[2,2,2,24,256]{4,3,2,1,0:T(8,128)(2,1)S(1)} %choose.1.refs_1_, bf16[8,192,256]{2,1,0:T(8,128)(2,1)S(1)} %right_side.1.refs_0_.refs_2_), custom_call_target="tpu_custom_call" | custom-call | tf_op jit(solution)/shard_map/gram/pallas_call | solution.py:345
  31.1 0.6 %collective-permute-done.10.refs_1_ = bf16[2,2,2,24,256]{4,3,2,1,0:T(8,128)(2,1)S(1)} collective-permute-done((bf16[2,2,2,24,256]{4,3,2,1,0:T(8,128)(2,1)S(1)}, bf16[2,2,2,24,256]{4,3,2,1,0:T(8,128)(2,1)S(1)}, u32[]{:S(2)}, u32[]{:S(2)}) %collective-permute-start.10) | collective-permute-done | bytes 98336 | tf_op jit(solution)/shard_map/ppermute | solution.py:44
  31.7 0.6 %gram.4 = (f32[192,96]{1,0:T(8,128)S(1)}, bf16[144,128]{1,0:T(8,128)(2,1)S(1)}) custom-call(bf16[8,192,256]{2,1,0:T(8,128)(2,1)S(1)} %right_side.1.refs_0_.refs_2_, bf16[2,2,2,24,256]{4,3,2,1,0:T(8,128)(2,1)S(1)} %collective-permute-done.10.refs_1_, f32[192,96]{1,0:T(8,128)S(1)} %get-tuple-element.25.refs_2_), custom_call_target="tpu_custom_call" | custom-call | tf_op jit(solution)/shard_map/gram/pallas_call | solution.py:345
  32.3 1.0 %collective-permute-done.11.refs_1_ = bf16[2,2,2,24,256]{4,3,2,1,0:T(8,128)(2,1)S(1)} collective-permute-done((bf16[2,2,2,24,256]{4,3,2,1,0:T(8,128)(2,1)S(1)}, bf16[2,2,2,24,256]{4,3,2,1,0:T(8,128)(2,1)S(1)}, u32[]{:S(2)}, u32[]{:S(2)}) %collective-permute-start.11) | collective-permute-done | bytes 98336 | tf_op jit(solution)/shard_map/ppermute | solution.py:44
  33.3 0.6 %gram.5 = (f32[192,96]{1,0:T(8,128)S(1)}, bf16[144,128]{1,0:T(8,128)(2,1)S(1)}) custom-call(bf16[8,192,256]{2,1,0:T(8,128)(2,1)S(1)} %right_side.1.refs_0_.refs_2_, bf16[2,2,2,24,256]{4,3,2,1,0:T(8,128)(2,1)S(1)} %collective-permute-done.11.refs_1_, f32[192,96]{1,0:T(8,128)S(1)} %get-tuple-element.27.refs_2_.refs_4_), custom_call_target="tpu_custom_call" | custom-call | tf_op jit(solution)/shard_map/gram/pallas_call | solution.py:345
  33.9 1.3 %collective-permute-done.9.refs_1_ = bf16[2,2,2,24,256]{4,3,2,1,0:T(8,128)(2,1)S(1)} collective-permute-done((bf16[2,2,2,24,256]{4,3,2,1,0:T(8,128)(2,1)S(1)}, bf16[2,2,2,24,256]{4,3,2,1,0:T(8,128)(2,1)S(1)}, u32[]{:S(2)}, u32[]{:S(2)}) %collective-permute-start.9) | collective-permute-done | bytes 98336 | tf_op jit(solution)/shard_map/ppermute | solution.py:44
  35.2 0.6 %last_gram.1 = (f32[192,96]{1,0:T(8,128)S(1)}, bf16[144,128]{1,0:T(8,128)(2,1)S(1)}, bf16[144,128]{1,0:T(8,128)(2,1)S(1)}, bf16[144,128]{1,0:T(8,128)(2,1)S(1)}) custom-call(bf16[8,192,256]{2,1,0:T(8,128)(2,1)S(1)} %right_side.1.refs_0_.refs_2_, bf16[2,2,2,24,256]{4,3,2,1,0:T(8,128)(2,1)S(1)} %collective-permute-done.9.refs_1_, ...), custom_call_target="tpu_custom_call" | custom-call | tf_op jit(solution)/shard_map/last_gram/pallas_call | solution.py:351
  35.8 2.7 %collective-permute-start.12 = (bf16[144,128]{1,0:T(8,128)(2,1)S(1)}, bf16[144,128]{1,0:T(8,128)(2,1)S(1)}, u32[]{:S(2)}, u32[]{:S(2)}) collective-permute-start(bf16[144,128]{1,0:T(8,128)(2,1)S(1)} %get-tuple-element.31), channel_id=1, source_target_pairs={{0,64},{1,65},{2,66},{3,67},{4,68},{5,69},{6,70},{7,71},{8,72},{9,... | collective-permute-start | bytes 110600 | tf_op jit(solution)/shard_map/ppermute | solution.py:44
  38.5 1.5 %collective-permute-start.13 = (bf16[144,128]{1,0:T(8,128)(2,1)S(1)}, bf16[144,128]{1,0:T(8,128)(2,1)S(1)}, u32[]{:S(2)}, u32[]{:S(2)}) collective-permute-start(bf16[144,128]{1,0:T(8,128)(2,1)S(1)} %get-tuple-element.32), channel_id=1, source_target_pairs={{0,96},{1,97},{2,98},{3,99},{4,100},{5,101},{6,102},{7,103},{8,104... | collective-permute-start | bytes 110600 | tf_op jit(solution)/shard_map/ppermute | solution.py:44
  40.1 2.3 %collective-permute-start.14 = (bf16[144,128]{1,0:T(8,128)(2,1)S(1)}, bf16[144,128]{1,0:T(8,128)(2,1)S(1)}, u32[]{:S(2)}, u32[]{:S(2)}) collective-permute-start(bf16[144,128]{1,0:T(8,128)(2,1)S(1)} %get-tuple-element.33), channel_id=1, source_target_pairs={{0,32},{1,33},{2,34},{3,35},{4,36},{5,37},{6,38},{7,39},{8,40},{9,... | collective-permute-start | bytes 110600 | tf_op jit(solution)/shard_map/ppermute | solution.py:44
  42.4 1.8 %collective-permute-done.12.r2 = bf16[144,128]{1,0:T(8,128)(2,1)S(1)} collective-permute-done((bf16[144,128]{1,0:T(8,128)(2,1)S(1)}, bf16[144,128]{1,0:T(8,128)(2,1)S(1)}, u32[]{:S(2)}, u32[]{:S(2)}) %collective-permute-start.12) | collective-permute-done | bytes 36896 | tf_op jit(solution)/shard_map/ppermute | solution.py:44
  44.2 0.6 %collective-permute-done.13.r3 = bf16[144,128]{1,0:T(8,128)(2,1)S(1)} collective-permute-done((bf16[144,128]{1,0:T(8,128)(2,1)S(1)}, bf16[144,128]{1,0:T(8,128)(2,1)S(1)}, u32[]{:S(2)}, u32[]{:S(2)}) %collective-permute-start.13) | collective-permute-done | bytes 36896 | tf_op jit(solution)/shard_map/ppermute | solution.py:44
  44.7 0.6 %collective-permute-done.14.r1 = bf16[144,128]{1,0:T(8,128)(2,1)S(1)} collective-permute-done((bf16[144,128]{1,0:T(8,128)(2,1)S(1)}, bf16[144,128]{1,0:T(8,128)(2,1)S(1)}, u32[]{:S(2)}, u32[]{:S(2)}) %collective-permute-start.14) | collective-permute-done | bytes 36896 | tf_op jit(solution)/shard_map/ppermute | solution.py:44
  45.3 0.7 %sum.1 = f32[192,96]{1,0:T(8,128)} custom-call(bf16[144,128]{1,0:T(8,128)(2,1)S(1)} %collective-permute-done.12.r2, bf16[144,128]{1,0:T(8,128)(2,1)S(1)} %collective-permute-done.13.r3, bf16[144,128]{1,0:T(8,128)(2,1)S(1)} %collective-permute-done.14.r1, f32[192,96]{1,0:T(8,128)S(1)} %get-tuple-element.34.p0), custom_call_target="tpu_custom_call" | custom-call | tf_op jit(solution)/shard_map/sum/pallas_call | solution.py:359
  (3 shorter events, 0.0 us)
Async XLA Ops:
  0.0 2.2 %copy-start.1 = (f32[8,2560]{1,0:T(8,128)S(1)}, f32[8,2560]{1,0:T(8,128)}, u32[]{:S(2)}) copy-start(f32[8,2560]{1,0:T(8,128)} %constant.2.clone.table.table_hbm) | copy-start | bytes 245764
  0.0 2.2 %copy-start = (bf16[96,8192]{1,0:T(8,128)(2,1)S(1)}, bf16[96,8192]{1,0:T(8,128)(2,1)}, u32[]{:S(2)}) copy-start(bf16[96,8192]{1,0:T(8,128)(2,1)} %head.1) | copy-start | bytes 4718596
  0.0 2.3 %copy-start.2 = (s32[32]{0:T(128)S(1)}, s32[32]{0:T(128)}, u32[]{:S(2)}) copy-start(s32[32]{0:T(128)} %fire_hbm.1) | copy-start | bytes 388
  1.5 9.7 %collective-permute-start = (f32[72,96]{1,0:T(8,128)S(1)}, f32[72,96]{1,0:T(8,128)S(1)}, u32[]{:S(2)}, u32[]{:S(2)}) collective-permute-start(f32[72,96]{1,0:T(8,128)S(1)} %tail_spectra.1), channel_id=1, source_target_pairs={{0,8},{1,9},{2,10},{3,11},{4,12},{5,13},{6,14},{7,15},{8,16},{9,17... | collective-permute-start | bytes 82952 | tf_op jit(solution)/shard_map/ppermute | solution.py:44
  1.6 9.6 %collective-permute-start.1 = (f32[72,96]{1,0:T(8,128)S(1)}, f32[72,96]{1,0:T(8,128)S(1)}, u32[]{:S(2)}, u32[]{:S(2)}) collective-permute-start(f32[72,96]{1,0:T(8,128)S(1)} %tail_spectra.1), channel_id=1, source_target_pairs={{112,120},{113,121},{114,122},{115,123},{116,124},{117,125},{118,1... | collective-permute-start | bytes 82952 | tf_op jit(solution)/shard_map/ppermute | solution.py:44
  3.9 7.3 %collective-permute-start.2 = (f32[64,96]{1,0:T(8,128)S(1)}, f32[64,96]{1,0:T(8,128)S(1)}, u32[]{:S(2)}, u32[]{:S(2)}) collective-permute-start(f32[64,96]{1,0:T(8,128)S(1)} %get-tuple-element.21), channel_id=1, source_target_pairs={{128,0},{129,1},{130,2},{131,3},{132,4},{133,5},{134,6},{135,7}} | collective-permute-start | bytes 73736 | tf_op jit(solution)/shard_map/ppermute | solution.py:44
  11.8 6.6 %collective-permute-start.3 = (bf16[4,24,256]{2,1,0:T(8,128)(2,1)S(1)}, bf16[4,24,256]{2,1,0:T(8,128)(2,1)S(1)}, u32[]{:S(2)}, u32[]{:S(2)}) collective-permute-start(bf16[4,24,256]{2,1,0:T(8,128)(2,1)S(1)} %finish_spectra.1.y0), channel_id=1, source_target_pairs={{0,144},{1,145},{2,146},{3,147},{4,148},{5,149},{6,150},{7,151},{8... | collective-permute-start | bytes 147464 | tf_op jit(solution)/shard_map/ppermute | solution.py:44
  11.9 6.5 %collective-permute-start.4 = (bf16[4,24,256]{2,1,0:T(8,128)(2,1)S(1)}, bf16[4,24,256]{2,1,0:T(8,128)(2,1)S(1)}, u32[]{:S(2)}, u32[]{:S(2)}) collective-permute-start(bf16[4,24,256]{2,1,0:T(8,128)(2,1)S(1)} %finish_spectra.1.y0), channel_id=1, source_target_pairs={{0,128},{1,129},{2,130},{3,131},{4,132},{5,133},{6,134},{7,135},{8... | collective-permute-start | bytes 147464 | tf_op jit(solution)/shard_map/ppermute | solution.py:44
  13.8 5.1 %collective-permute-start.5 = (bf16[4,24,256]{2,1,0:T(8,128)(2,1)S(1)}, bf16[4,24,256]{2,1,0:T(8,128)(2,1)S(1)}, u32[]{:S(2)}, u32[]{:S(2)}) collective-permute-start(bf16[4,24,256]{2,1,0:T(8,128)(2,1)S(1)} %finish_spectra.1.y0), channel_id=1, source_target_pairs={{0,16},{1,17},{2,18},{3,19},{4,20},{5,21},{6,22},{7,23},{8,24},{9,... | collective-permute-start | bytes 147464 | tf_op jit(solution)/shard_map/ppermute | solution.py:44
  19.0 1.3 %collective-permute-start.7 = (bf16[2,2,24,256]{3,2,1,0:T(8,128)(2,1)S(1)}, bf16[2,2,24,256]{3,2,1,0:T(8,128)(2,1)S(1)}, u32[]{:S(2)}, u32[]{:S(2)}) collective-permute-start(bf16[2,2,24,256]{3,2,1,0:T(8,128)(2,1)S(1)} %get-tuple-element.24), channel_id=1, source_target_pairs={{0,8},{1,9},{2,10},{3,11},{4,12},{5,13},{6,14},{7,15},{8,0},{9,1},... | collective-permute-start | bytes 147464 | tf_op jit(solution)/shard_map/ppermute | solution.py:44
  19.1 11.3 %collective-permute-start.6 = (bf16[2,2,4,24,256]{4,3,2,1,0:T(8,128)(2,1)S(1)}, bf16[2,2,4,24,256]{4,3,2,1,0:T(8,128)(2,1)S(1)}, u32[]{:S(2)}, u32[]{:S(2)}) collective-permute-start(bf16[2,2,4,24,256]{4,3,2,1,0:T(8,128)(2,1)S(1)} %get-tuple-element.22.own), channel_id=1, source_target_pairs={{0,8},{1,9},{2,10},{3,11},{4,12},{5,13},{6,14},{7,15},{8,0},{9,1},... | collective-permute-start | bytes 589832 | tf_op jit(solution)/shard_map/ppermute | solution.py:44
  20.3 6.5 %collective-permute-start.8 = (bf16[2,2,2,24,256]{4,3,2,1,0:T(8,128)(2,1)S(1)}, bf16[2,2,2,24,256]{4,3,2,1,0:T(8,128)(2,1)S(1)}, u32[]{:S(2)}, u32[]{:S(2)}) collective-permute-start(bf16[2,2,2,24,256]{4,3,2,1,0:T(8,128)(2,1)S(1)} %join_core.1.own), channel_id=1, source_target_pairs={{0,4},{1,5},{2,6},{3,7},{4,0},{5,1},{6,2},{7,3},{8,12},{9,13},{10,... | collective-permute-start | bytes 294920 | tf_op jit(solution)/shard_map/ppermute | solution.py:44
  26.8 4.9 %collective-permute-start.10 = (bf16[2,2,2,24,256]{4,3,2,1,0:T(8,128)(2,1)S(1)}, bf16[2,2,2,24,256]{4,3,2,1,0:T(8,128)(2,1)S(1)}, u32[]{:S(2)}, u32[]{:S(2)}) collective-permute-start(bf16[2,2,2,24,256]{4,3,2,1,0:T(8,128)(2,1)S(1)} %choose.1.refs_1_), channel_id=1, source_target_pairs={{0,1},{1,0},{2,3},{3,2},{4,5},{5,4},{6,7},{7,6},{8,9},{9,8},{10,11... | collective-permute-start | bytes 294920 | tf_op jit(solution)/shard_map/ppermute | solution.py:44
  28.5 4.8 %collective-permute-start.11 = (bf16[2,2,2,24,256]{4,3,2,1,0:T(8,128)(2,1)S(1)}, bf16[2,2,2,24,256]{4,3,2,1,0:T(8,128)(2,1)S(1)}, u32[]{:S(2)}, u32[]{:S(2)}) collective-permute-start(bf16[2,2,2,24,256]{4,3,2,1,0:T(8,128)(2,1)S(1)} %choose.1.refs_1_), channel_id=1, source_target_pairs={{0,2},{1,3},{2,0},{3,1},{4,6},{5,7},{6,4},{7,5},{8,10},{9,11},{10,... | collective-permute-start | bytes 294920 | tf_op jit(solution)/shard_map/ppermute | solution.py:44
  29.7 5.5 %collective-permute-start.9 = (bf16[2,2,2,24,256]{4,3,2,1,0:T(8,128)(2,1)S(1)}, bf16[2,2,2,24,256]{4,3,2,1,0:T(8,128)(2,1)S(1)}, u32[]{:S(2)}, u32[]{:S(2)}) collective-permute-start(bf16[2,2,2,24,256]{4,3,2,1,0:T(8,128)(2,1)S(1)} %choose.1.refs_1_), channel_id=1, source_target_pairs={{0,3},{1,2},{2,1},{3,0},{4,7},{5,6},{6,5},{7,4},{8,11},{9,10},{10,... | collective-permute-start | bytes 294920 | tf_op jit(solution)/shard_map/ppermute | solution.py:44
  35.8 8.4 %collective-permute-start.12 = (bf16[144,128]{1,0:T(8,128)(2,1)S(1)}, bf16[144,128]{1,0:T(8,128)(2,1)S(1)}, u32[]{:S(2)}, u32[]{:S(2)}) collective-permute-start(bf16[144,128]{1,0:T(8,128)(2,1)S(1)} %get-tuple-element.31), channel_id=1, source_target_pairs={{0,64},{1,65},{2,66},{3,67},{4,68},{5,69},{6,70},{7,71},{8,72},{9,... | collective-permute-start | bytes 110600 | tf_op jit(solution)/shard_map/ppermute | solution.py:44
  38.5 6.2 %collective-permute-start.13 = (bf16[144,128]{1,0:T(8,128)(2,1)S(1)}, bf16[144,128]{1,0:T(8,128)(2,1)S(1)}, u32[]{:S(2)}, u32[]{:S(2)}) collective-permute-start(bf16[144,128]{1,0:T(8,128)(2,1)S(1)} %get-tuple-element.32), channel_id=1, source_target_pairs={{0,96},{1,97},{2,98},{3,99},{4,100},{5,101},{6,102},{7,103},{8,104... | collective-permute-start | bytes 110600 | tf_op jit(solution)/shard_map/ppermute | solution.py:44
  40.1 5.3 %collective-permute-start.14 = (bf16[144,128]{1,0:T(8,128)(2,1)S(1)}, bf16[144,128]{1,0:T(8,128)(2,1)S(1)}, u32[]{:S(2)}, u32[]{:S(2)}) collective-permute-start(bf16[144,128]{1,0:T(8,128)(2,1)S(1)} %get-tuple-element.33), channel_id=1, source_target_pairs={{0,32},{1,33},{2,34},{3,35},{4,36},{5,37},{6,38},{7,39},{8,40},{9,... | collective-permute-start | bytes 110600 | tf_op jit(solution)/shard_map/ppermute | solution.py:44

commit v12 on v10

--- a/solution.py
+++ b/solution.py
@@ -21,6 +21,7 @@
 SHOT_DEVICES = 32
 RCV_DEVICES = 8
 QUARTERS = 4
+BLOCK = 128
 LATE = WIN // SPACING
 
 
@@ -29,7 +30,7 @@
     angle = 2.0 * math.pi / WIN * turns
     rows = np.concatenate([np.cos(angle), -np.sin(angle)], axis=0) / math.sqrt(WIN)
     rows = rows.astype(np.float32).astype(ml_dtypes.bfloat16).astype(np.float32)
-    return np.concatenate([rows, np.zeros((ROWS, SPAN - WIN), np.float32)], axis=1)
+    return rows
 
 
 def send(block, to):
@@ -54,10 +55,20 @@
     return [pl.BlockSpec(memory_space=pltpu.VMEM)] * count
 
 
-def pair_tables(table, first, second, length=SPAN):
-    if length < SPAN:
-        table = jnp.concatenate([table[:, :length], jnp.zeros((ROWS, PAIR), table.dtype)], axis=1)
-    rows = [pltpu.roll(table, first, 1)[:, :length], pltpu.roll(table, second + SPACING, 1)[:, :length]]
+def shifted_blocks(table, by):
+    rest, whole = by & (BLOCK - 1), by >= BLOCK
+    zero = jnp.zeros((ROWS, BLOCK), table.dtype)
+    turned = [pltpu.roll(table[:, BLOCK * i : BLOCK * (i + 1)], rest, 1) for i in range(WIN // BLOCK)]
+    early = lax.broadcasted_iota(jnp.int32, zero.shape, 1) < rest
+    part = [jnp.where(early, a, b) for a, b in zip([zero, *turned], [*turned, zero])]
+    return [jnp.where(whole, a, b) for a, b in zip([zero, *part], [*part, zero])]
+
+
+def pair_tables(table, first, second, low=0, high=SPAN):
+    zero = jnp.zeros((ROWS, BLOCK), table.dtype)
+    ahead = [zero] * (SPACING // BLOCK)
+    rows = [shifted_blocks(table, first) + ahead, ahead + shifted_blocks(table, second)]
+    rows = [jnp.concatenate(blocks[low // BLOCK : high // BLOCK], axis=1) for blocks in rows]
     return jnp.concatenate(rows, axis=0).astype(jnp.bfloat16)
 
 
@@ -100,7 +111,7 @@
     for p in range(late):
         shot = 2 * (pairs - late + p)
         length = PAIR * (late - p)
-        tables[p, :, :length] = pair_tables(master, delay(fire, shot), delay(fire, shot + 1), length)
+        tables[p, :, :length] = pair_tables(master, delay(fire, shot), delay(fire, shot + 1), 0, length)
     copies[2].wait()
     blocks = [(pairs - late + v, samples[:, PAIR * v : PAIR * (v + 1)]) for v in range(late)]
     add_products(message, tables, pairs - late, blocks)
@@ -124,8 +135,8 @@
     for p in range(late):
         rows = [message[ROWS * LATE + 2 * p + i : ROWS * LATE + 2 * p + i + 1, :] for i in range(2)]
         first, second = [jnp.max(r).astype(jnp.int32) for r in rows]
-        tables[p] = pair_tables(master, first, second)
-    scratch[:own_rows, :] = jnp.zeros_like(total)
+        low = PAIR * (late - p)
+        tables[p, :, low:] = pair_tables(master, first, second, low)
     scratch[own_rows:, :] = jnp.zeros((lanes - own_rows, total.shape[1]), jnp.float32)
     blocks = [(late + v, head[:, PAIR * v : PAIR * (v + 1)]) for v in range(late)]
     add_products(scratch.at[own_rows:, :], tables, 0, blocks)

time: 45.6 us -> 45.5 us (level)
  Pallas kernels: 6.94 us -> 6.47 us
  transfers between devices with their start and end apart: 13 -> 13, of which waited for: 9 -> 9; matrix products, arithmetic and copies ran while one was open for 0% -> 0% of each run, Pallas kernels for 8% -> 7%
where the time goes in v12:
time: 45.5 us; the launch traced here: 44.8 us
  waiting for transfers between devices  21.6 us (47%)
  starting transfers between devices  16.5 us (36%)
  Pallas kernels  6.47 us (14%)
    ppermute x13, waiting for transfers between devices, send(): return lax.ppermute(block, ('shot', 'rcv'), route)  21.6 us
    ppermute x13, starting transfers between devices, send(): return lax.ppermute(block, ('shot', 'rcv'), route)  16.5 us
    pallas_call x3, Pallas kernels, per_device(): local(lambda *refs: gram_kernel(scale, *refs), 'gram', (share, wire), vme...  1.81 us
    pallas_call x1, Pallas kernels, per_device(): local(tail_kernel, 'tail_spectra', shape((late_rows + LATE, receivers), f...  1.42 us
    pallas_call x1, Pallas kernels, per_device(): local(own_kernel, 'own_spectra', shape((lanes - late_rows, receivers), f3...  1.24 us
  transfers between devices with their start and end apart: 13, of which 9 were waited for; matrix products, arithmetic and copies ran while one was open for 0% of the time, Pallas kernels for 7%

profile of v12, /device:TPU:4, one launch (start us, length us, event | category | flops | bytes accessed | tf_op | source)
XLA Modules:
  0.0 44.8 jit_solution(3066981088779010630)
XLA Ops:
  0.0 0.0 copy-start.1
  0.0 0.0 copy-start
  0.0 0.0 copy-start.2
  0.0 1.4 %tail_spectra.1 = f32[72,96]{1,0:T(8,128)S(1)} custom-call(s32[32]{0:T(128)} %fire_hbm.1, f32[8,2048]{1,0:T(8,128)} %constant.2.clone.table.table_hbm, bf16[96,8192]{1,0:T(8,128)(2,1)} %head.1), custom_call_target="tpu_custom_call" | custom-call | tf_op jit(solution)/shard_map/tail_spectra/pallas_call | solution.py:274
  1.4 0.1 collective-permute-start
  1.5 0.0 copy-done.1
  1.5 0.1 copy-done
  1.6 0.0 copy-done.2
  1.6 1.2 %own_spectra.1.total = f32[192,96]{1,0:T(8,128)S(1)} custom-call(s32[32]{0:T(128)S(1)} %copy-done.2, f32[8,2048]{1,0:T(8,128)S(1)} %copy-done.1, bf16[96,8192]{1,0:T(8,128)(2,1)S(1)} %copy-done), custom_call_target="tpu_custom_call" | custom-call | tf_op jit(solution)/shard_map/own_spectra/pallas_call | solution.py:293
  2.8 8.5 %collective-permute-done.message = f32[72,96]{1,0:T(8,128)S(1)} collective-permute-done((f32[72,96]{1,0:T(8,128)S(1)}, f32[72,96]{1,0:T(8,128)S(1)}, u32[]{:S(2)}, u32[]{:S(2)}) %collective-permute-start) | collective-permute-done | bytes 27680 | tf_op jit(solution)/shard_map/ppermute | solution.py:44
  11.4 0.5 %finish_spectra.1.y0 = bf16[4,24,256]{2,1,0:T(8,128)(2,1)S(1)} custom-call(f32[192,96]{1,0:T(8,128)S(1)} %own_spectra.1.total, bf16[96,8192]{1,0:T(8,128)(2,1)S(1)} %copy-done, f32[8,2048]{1,0:T(8,128)S(1)} %copy-done.1, f32[72,96]{1,0:T(8,128)S(1)} %collective-permute-done.message), custom_call_target="tpu_custom_call" | custom-call | tf_op jit(solution)/shard_map/finish_spectra/pallas_call | solution.py:300
  11.9 0.1 collective-permute-start.1
  12.0 0.4 collective-permute-start.2
  12.4 4.5 %collective-permute-start.3 = (bf16[4,24,256]{2,1,0:T(8,128)(2,1)S(1)}, bf16[4,24,256]{2,1,0:T(8,128)(2,1)S(1)}, u32[]{:S(2)}, u32[]{:S(2)}) collective-permute-start(bf16[4,24,256]{2,1,0:T(8,128)(2,1)S(1)} %finish_spectra.1.y0), channel_id=1, source_target_pairs={{0,16},{1,17},{2,18},{3,19},{4,20},{5,21},{6,22},{7,23},{8,24},{9,... | collective-permute-start | bytes 147464 | tf_op jit(solution)/shard_map/ppermute | solution.py:44
  16.9 1.5 %collective-permute-done.1.y3 = bf16[4,24,256]{2,1,0:T(8,128)(2,1)S(1)} collective-permute-done((bf16[4,24,256]{2,1,0:T(8,128)(2,1)S(1)}, bf16[4,24,256]{2,1,0:T(8,128)(2,1)S(1)}, u32[]{:S(2)}, u32[]{:S(2)}) %collective-permute-start.1) | collective-permute-done | bytes 49184 | tf_op jit(solution)/shard_map/ppermute | solution.py:44
  18.4 0.0 collective-permute-done.2.y2
  18.4 0.6 %collective-permute-done.3.y1 = bf16[4,24,256]{2,1,0:T(8,128)(2,1)S(1)} collective-permute-done((bf16[4,24,256]{2,1,0:T(8,128)(2,1)S(1)}, bf16[4,24,256]{2,1,0:T(8,128)(2,1)S(1)}, u32[]{:S(2)}, u32[]{:S(2)}) %collective-permute-start.3) | collective-permute-done | bytes 49184 | tf_op jit(solution)/shard_map/ppermute | solution.py:44
  19.1 0.1 collective-permute-start.5
  19.2 0.5 %collective-permute-start.4 = (bf16[2,2,4,24,256]{4,3,2,1,0:T(8,128)(2,1)S(1)}, bf16[2,2,4,24,256]{4,3,2,1,0:T(8,128)(2,1)S(1)}, u32[]{:S(2)}, u32[]{:S(2)}) collective-permute-start(bf16[2,2,4,24,256]{4,3,2,1,0:T(8,128)(2,1)S(1)} %get-tuple-element.18.own), channel_id=1, source_target_pairs={{0,8},{1,9},{2,10},{3,11},{4,12},{5,13},{6,14},{7,15},{8,0},{9,1},... | collective-permute-start | bytes 589832 | tf_op jit(solution)/shard_map/ppermute | solution.py:44
  19.6 0.7 %collective-permute-done.5.other = bf16[2,2,24,256]{3,2,1,0:T(8,128)(2,1)S(1)} collective-permute-done((bf16[2,2,24,256]{3,2,1,0:T(8,128)(2,1)S(1)}, bf16[2,2,24,256]{3,2,1,0:T(8,128)(2,1)S(1)}, u32[]{:S(2)}, u32[]{:S(2)}) %collective-permute-start.5) | collective-permute-done | bytes 49184 | tf_op jit(solution)/shard_map/ppermute | solution.py:44
  20.4 0.6 %collective-permute-start.6 = (bf16[2,2,2,24,256]{4,3,2,1,0:T(8,128)(2,1)S(1)}, bf16[2,2,2,24,256]{4,3,2,1,0:T(8,128)(2,1)S(1)}, u32[]{:S(2)}, u32[]{:S(2)}) collective-permute-start(bf16[2,2,2,24,256]{4,3,2,1,0:T(8,128)(2,1)S(1)} %join_core.1.own), channel_id=1, source_target_pairs={{0,4},{1,5},{2,6},{3,7},{4,0},{5,1},{6,2},{7,3},{8,12},{9,13},{10,... | collective-permute-start | bytes 294920 | tf_op jit(solution)/shard_map/ppermute | solution.py:44
  21.0 5.9 %collective-permute-done.6.cross = bf16[2,2,2,24,256]{4,3,2,1,0:T(8,128)(2,1)S(1)} collective-permute-done((bf16[2,2,2,24,256]{4,3,2,1,0:T(8,128)(2,1)S(1)}, bf16[2,2,2,24,256]{4,3,2,1,0:T(8,128)(2,1)S(1)}, u32[]{:S(2)}, u32[]{:S(2)}) %collective-permute-start.6) | collective-permute-done | bytes 98336 | tf_op jit(solution)/shard_map/ppermute | solution.py:44
  26.8 0.5 %collective-permute-start.8 = (bf16[2,2,2,24,256]{4,3,2,1,0:T(8,128)(2,1)S(1)}, bf16[2,2,2,24,256]{4,3,2,1,0:T(8,128)(2,1)S(1)}, u32[]{:S(2)}, u32[]{:S(2)}) collective-permute-start(bf16[2,2,2,24,256]{4,3,2,1,0:T(8,128)(2,1)S(1)} %choose.1.refs_1_), channel_id=1, source_target_pairs={{0,1},{1,0},{2,3},{3,2},{4,5},{5,4},{6,7},{7,6},{8,9},{9,8},{10,11... | collective-permute-start | bytes 294920 | tf_op jit(solution)/shard_map/ppermute | solution.py:44
  27.3 1.2 %collective-permute-start.9 = (bf16[2,2,2,24,256]{4,3,2,1,0:T(8,128)(2,1)S(1)}, bf16[2,2,2,24,256]{4,3,2,1,0:T(8,128)(2,1)S(1)}, u32[]{:S(2)}, u32[]{:S(2)}) collective-permute-start(bf16[2,2,2,24,256]{4,3,2,1,0:T(8,128)(2,1)S(1)} %choose.1.refs_1_), channel_id=1, source_target_pairs={{0,2},{1,3},{2,0},{3,1},{4,6},{5,7},{6,4},{7,5},{8,10},{9,11},{10,... | collective-permute-start | bytes 294920 | tf_op jit(solution)/shard_map/ppermute | solution.py:44
  28.5 1.9 %collective-permute-start.7 = (bf16[2,2,2,24,256]{4,3,2,1,0:T(8,128)(2,1)S(1)}, bf16[2,2,2,24,256]{4,3,2,1,0:T(8,128)(2,1)S(1)}, u32[]{:S(2)}, u32[]{:S(2)}) collective-permute-start(bf16[2,2,2,24,256]{4,3,2,1,0:T(8,128)(2,1)S(1)} %choose.1.refs_1_), channel_id=1, source_target_pairs={{0,3},{1,2},{2,1},{3,0},{4,7},{5,6},{6,5},{7,4},{8,11},{9,10},{10,... | collective-permute-start | bytes 294920 | tf_op jit(solution)/shard_map/ppermute | solution.py:44
  30.4 0.0 collective-permute-done.4.other
  30.4 0.1 right_side.1.refs_0_.refs_2_
  30.5 0.6 %gram.3 = (f32[192,96]{1,0:T(8,128)S(1)}, bf16[144,128]{1,0:T(8,128)(2,1)S(1)}) custom-call(bf16[8,192,256]{2,1,0:T(8,128)(2,1)S(1)} %right_side.1.refs_0_.refs_2_, bf16[2,2,2,24,256]{4,3,2,1,0:T(8,128)(2,1)S(1)} %choose.1.refs_1_, bf16[8,192,256]{2,1,0:T(8,128)(2,1)S(1)} %right_side.1.refs_0_.refs_2_), custom_call_target="tpu_custom_call" | custom-call | tf_op jit(solution)/shard_map/gram/pallas_call | solution.py:341
  31.1 1.5 %collective-permute-done.8.refs_1_ = bf16[2,2,2,24,256]{4,3,2,1,0:T(8,128)(2,1)S(1)} collective-permute-done((bf16[2,2,2,24,256]{4,3,2,1,0:T(8,128)(2,1)S(1)}, bf16[2,2,2,24,256]{4,3,2,1,0:T(8,128)(2,1)S(1)}, u32[]{:S(2)}, u32[]{:S(2)}) %collective-permute-start.8) | collective-permute-done | bytes 98336 | tf_op jit(solution)/shard_map/ppermute | solution.py:44
  32.6 0.6 %gram.4 = (f32[192,96]{1,0:T(8,128)S(1)}, bf16[144,128]{1,0:T(8,128)(2,1)S(1)}) custom-call(bf16[8,192,256]{2,1,0:T(8,128)(2,1)S(1)} %right_side.1.refs_0_.refs_2_, bf16[2,2,2,24,256]{4,3,2,1,0:T(8,128)(2,1)S(1)} %collective-permute-done.8.refs_1_, f32[192,96]{1,0:T(8,128)S(1)} %get-tuple-element.21.refs_2_), custom_call_target="tpu_custom_call" | custom-call | tf_op jit(solution)/shard_map/gram/pallas_call | solution.py:341
  33.2 0.0 collective-permute-done.9.refs_1_
  33.2 0.6 %gram.5 = (f32[192,96]{1,0:T(8,128)S(1)}, bf16[144,128]{1,0:T(8,128)(2,1)S(1)}) custom-call(bf16[8,192,256]{2,1,0:T(8,128)(2,1)S(1)} %right_side.1.refs_0_.refs_2_, bf16[2,2,2,24,256]{4,3,2,1,0:T(8,128)(2,1)S(1)} %collective-permute-done.9.refs_1_, f32[192,96]{1,0:T(8,128)S(1)} %get-tuple-element.23.refs_2_.refs_4_), custom_call_target="tpu_custom_call" | custom-call | tf_op jit(solution)/shard_map/gram/pallas_call | solution.py:341
  33.8 0.4 collective-permute-done.7.refs_1_
  34.3 0.6 %last_gram.1 = (f32[192,96]{1,0:T(8,128)S(1)}, bf16[144,128]{1,0:T(8,128)(2,1)S(1)}, bf16[144,128]{1,0:T(8,128)(2,1)S(1)}, bf16[144,128]{1,0:T(8,128)(2,1)S(1)}) custom-call(bf16[8,192,256]{2,1,0:T(8,128)(2,1)S(1)} %right_side.1.refs_0_.refs_2_, bf16[2,2,2,24,256]{4,3,2,1,0:T(8,128)(2,1)S(1)} %collective-permute-done.7.refs_1_, ...), custom_call_target="tpu_custom_call" | custom-call | tf_op jit(solution)/shard_map/last_gram/pallas_call | solution.py:347
  34.9 3.1 %collective-permute-start.10 = (bf16[144,128]{1,0:T(8,128)(2,1)S(1)}, bf16[144,128]{1,0:T(8,128)(2,1)S(1)}, u32[]{:S(2)}, u32[]{:S(2)}) collective-permute-start(bf16[144,128]{1,0:T(8,128)(2,1)S(1)} %get-tuple-element.27), channel_id=1, source_target_pairs={{0,64},{1,65},{2,66},{3,67},{4,68},{5,69},{6,70},{7,71},{8,72},{9,... | collective-permute-start | bytes 110600 | tf_op jit(solution)/shard_map/ppermute | solution.py:44
  38.0 1.0 %collective-permute-start.11 = (bf16[144,128]{1,0:T(8,128)(2,1)S(1)}, bf16[144,128]{1,0:T(8,128)(2,1)S(1)}, u32[]{:S(2)}, u32[]{:S(2)}) collective-permute-start(bf16[144,128]{1,0:T(8,128)(2,1)S(1)} %get-tuple-element.28), channel_id=1, source_target_pairs={{0,96},{1,97},{2,98},{3,99},{4,100},{5,101},{6,102},{7,103},{8,104... | collective-permute-start | bytes 110600 | tf_op jit(solution)/shard_map/ppermute | solution.py:44
  38.9 2.5 %collective-permute-start.12 = (bf16[144,128]{1,0:T(8,128)(2,1)S(1)}, bf16[144,128]{1,0:T(8,128)(2,1)S(1)}, u32[]{:S(2)}, u32[]{:S(2)}) collective-permute-start(bf16[144,128]{1,0:T(8,128)(2,1)S(1)} %get-tuple-element.29), channel_id=1, source_target_pairs={{0,32},{1,33},{2,34},{3,35},{4,36},{5,37},{6,38},{7,39},{8,40},{9,... | collective-permute-start | bytes 110600 | tf_op jit(solution)/shard_map/ppermute | solution.py:44
  41.5 1.6 %collective-permute-done.10.r2 = bf16[144,128]{1,0:T(8,128)(2,1)S(1)} collective-permute-done((bf16[144,128]{1,0:T(8,128)(2,1)S(1)}, bf16[144,128]{1,0:T(8,128)(2,1)S(1)}, u32[]{:S(2)}, u32[]{:S(2)}) %collective-permute-start.10) | collective-permute-done | bytes 36896 | tf_op jit(solution)/shard_map/ppermute | solution.py:44
  43.0 1.0 %collective-permute-done.11.r3 = bf16[144,128]{1,0:T(8,128)(2,1)S(1)} collective-permute-done((bf16[144,128]{1,0:T(8,128)(2,1)S(1)}, bf16[144,128]{1,0:T(8,128)(2,1)S(1)}, u32[]{:S(2)}, u32[]{:S(2)}) %collective-permute-start.11) | collective-permute-done | bytes 36896 | tf_op jit(solution)/shard_map/ppermute | solution.py:44
  44.0 0.0 collective-permute-done.12.r1
  44.0 0.7 %sum.1 = f32[192,96]{1,0:T(8,128)} custom-call(bf16[144,128]{1,0:T(8,128)(2,1)S(1)} %collective-permute-done.10.r2, bf16[144,128]{1,0:T(8,128)(2,1)S(1)} %collective-permute-done.11.r3, bf16[144,128]{1,0:T(8,128)(2,1)S(1)} %collective-permute-done.12.r1, f32[192,96]{1,0:T(8,128)S(1)} %get-tuple-element.30.p0), custom_call_target="tpu_custom_call" | custom-call | tf_op jit(solution)/shard_map/sum/pallas_call | solution.py:355
  (3 shorter events, 0.0 us)
Async XLA Ops:
  0.0 1.5 %copy-start.1 = (f32[8,2048]{1,0:T(8,128)S(1)}, f32[8,2048]{1,0:T(8,128)}, u32[]{:S(2)}) copy-start(f32[8,2048]{1,0:T(8,128)} %constant.2.clone.table.table_hbm) | copy-start | bytes 196612
  0.0 1.6 %copy-start = (bf16[96,8192]{1,0:T(8,128)(2,1)S(1)}, bf16[96,8192]{1,0:T(8,128)(2,1)}, u32[]{:S(2)}) copy-start(bf16[96,8192]{1,0:T(8,128)(2,1)} %head.1) | copy-start | bytes 4718596
  0.0 1.6 %copy-start.2 = (s32[32]{0:T(128)S(1)}, s32[32]{0:T(128)}, u32[]{:S(2)}) copy-start(s32[32]{0:T(128)} %fire_hbm.1) | copy-start | bytes 388
  1.4 9.9 %collective-permute-start = (f32[72,96]{1,0:T(8,128)S(1)}, f32[72,96]{1,0:T(8,128)S(1)}, u32[]{:S(2)}, u32[]{:S(2)}) collective-permute-start(f32[72,96]{1,0:T(8,128)S(1)} %tail_spectra.1), channel_id=1, source_target_pairs={{0,8},{1,9},{2,10},{3,11},{4,12},{5,13},{6,14},{7,15},{8,16},{9,17... | collective-permute-start | bytes 82952 | tf_op jit(solution)/shard_map/ppermute | solution.py:44
  11.9 6.6 %collective-permute-start.1 = (bf16[4,24,256]{2,1,0:T(8,128)(2,1)S(1)}, bf16[4,24,256]{2,1,0:T(8,128)(2,1)S(1)}, u32[]{:S(2)}, u32[]{:S(2)}) collective-permute-start(bf16[4,24,256]{2,1,0:T(8,128)(2,1)S(1)} %finish_spectra.1.y0), channel_id=1, source_target_pairs={{0,144},{1,145},{2,146},{3,147},{4,148},{5,149},{6,150},{7,151},{8... | collective-permute-start | bytes 147464 | tf_op jit(solution)/shard_map/ppermute | solution.py:44
  12.0 6.5 %collective-permute-start.2 = (bf16[4,24,256]{2,1,0:T(8,128)(2,1)S(1)}, bf16[4,24,256]{2,1,0:T(8,128)(2,1)S(1)}, u32[]{:S(2)}, u32[]{:S(2)}) collective-permute-start(bf16[4,24,256]{2,1,0:T(8,128)(2,1)S(1)} %finish_spectra.1.y0), channel_id=1, source_target_pairs={{0,128},{1,129},{2,130},{3,131},{4,132},{5,133},{6,134},{7,135},{8... | collective-permute-start | bytes 147464 | tf_op jit(solution)/shard_map/ppermute | solution.py:44
  12.4 6.6 %collective-permute-start.3 = (bf16[4,24,256]{2,1,0:T(8,128)(2,1)S(1)}, bf16[4,24,256]{2,1,0:T(8,128)(2,1)S(1)}, u32[]{:S(2)}, u32[]{:S(2)}) collective-permute-start(bf16[4,24,256]{2,1,0:T(8,128)(2,1)S(1)} %finish_spectra.1.y0), channel_id=1, source_target_pairs={{0,16},{1,17},{2,18},{3,19},{4,20},{5,21},{6,22},{7,23},{8,24},{9,... | collective-permute-start | bytes 147464 | tf_op jit(solution)/shard_map/ppermute | solution.py:44
  19.1 1.3 %collective-permute-start.5 = (bf16[2,2,24,256]{3,2,1,0:T(8,128)(2,1)S(1)}, bf16[2,2,24,256]{3,2,1,0:T(8,128)(2,1)S(1)}, u32[]{:S(2)}, u32[]{:S(2)}) collective-permute-start(bf16[2,2,24,256]{3,2,1,0:T(8,128)(2,1)S(1)} %get-tuple-element.20), channel_id=1, source_target_pairs={{0,8},{1,9},{2,10},{3,11},{4,12},{5,13},{6,14},{7,15},{8,0},{9,1},... | collective-permute-start | bytes 147464 | tf_op jit(solution)/shard_map/ppermute | solution.py:44
  19.2 11.3 %collective-permute-start.4 = (bf16[2,2,4,24,256]{4,3,2,1,0:T(8,128)(2,1)S(1)}, bf16[2,2,4,24,256]{4,3,2,1,0:T(8,128)(2,1)S(1)}, u32[]{:S(2)}, u32[]{:S(2)}) collective-permute-start(bf16[2,2,4,24,256]{4,3,2,1,0:T(8,128)(2,1)S(1)} %get-tuple-element.18.own), channel_id=1, source_target_pairs={{0,8},{1,9},{2,10},{3,11},{4,12},{5,13},{6,14},{7,15},{8,0},{9,1},... | collective-permute-start | bytes 589832 | tf_op jit(solution)/shard_map/ppermute | solution.py:44
  20.4 6.5 %collective-permute-start.6 = (bf16[2,2,2,24,256]{4,3,2,1,0:T(8,128)(2,1)S(1)}, bf16[2,2,2,24,256]{4,3,2,1,0:T(8,128)(2,1)S(1)}, u32[]{:S(2)}, u32[]{:S(2)}) collective-permute-start(bf16[2,2,2,24,256]{4,3,2,1,0:T(8,128)(2,1)S(1)} %join_core.1.own), channel_id=1, source_target_pairs={{0,4},{1,5},{2,6},{3,7},{4,0},{5,1},{6,2},{7,3},{8,12},{9,13},{10,... | collective-permute-start | bytes 294920 | tf_op jit(solution)/shard_map/ppermute | solution.py:44
  26.8 5.8 %collective-permute-start.8 = (bf16[2,2,2,24,256]{4,3,2,1,0:T(8,128)(2,1)S(1)}, bf16[2,2,2,24,256]{4,3,2,1,0:T(8,128)(2,1)S(1)}, u32[]{:S(2)}, u32[]{:S(2)}) collective-permute-start(bf16[2,2,2,24,256]{4,3,2,1,0:T(8,128)(2,1)S(1)} %choose.1.refs_1_), channel_id=1, source_target_pairs={{0,1},{1,0},{2,3},{3,2},{4,5},{5,4},{6,7},{7,6},{8,9},{9,8},{10,11... | collective-permute-start | bytes 294920 | tf_op jit(solution)/shard_map/ppermute | solution.py:44
  27.3 5.9 %collective-permute-start.9 = (bf16[2,2,2,24,256]{4,3,2,1,0:T(8,128)(2,1)S(1)}, bf16[2,2,2,24,256]{4,3,2,1,0:T(8,128)(2,1)S(1)}, u32[]{:S(2)}, u32[]{:S(2)}) collective-permute-start(bf16[2,2,2,24,256]{4,3,2,1,0:T(8,128)(2,1)S(1)} %choose.1.refs_1_), channel_id=1, source_target_pairs={{0,2},{1,3},{2,0},{3,1},{4,6},{5,7},{6,4},{7,5},{8,10},{9,11},{10,... | collective-permute-start | bytes 294920 | tf_op jit(solution)/shard_map/ppermute | solution.py:44
  28.5 5.7 %collective-permute-start.7 = (bf16[2,2,2,24,256]{4,3,2,1,0:T(8,128)(2,1)S(1)}, bf16[2,2,2,24,256]{4,3,2,1,0:T(8,128)(2,1)S(1)}, u32[]{:S(2)}, u32[]{:S(2)}) collective-permute-start(bf16[2,2,2,24,256]{4,3,2,1,0:T(8,128)(2,1)S(1)} %choose.1.refs_1_), channel_id=1, source_target_pairs={{0,3},{1,2},{2,1},{3,0},{4,7},{5,6},{6,5},{7,4},{8,11},{9,10},{10,... | collective-permute-start | bytes 294920 | tf_op jit(solution)/shard_map/ppermute | solution.py:44
  34.9 8.1 %collective-permute-start.10 = (bf16[144,128]{1,0:T(8,128)(2,1)S(1)}, bf16[144,128]{1,0:T(8,128)(2,1)S(1)}, u32[]{:S(2)}, u32[]{:S(2)}) collective-permute-start(bf16[144,128]{1,0:T(8,128)(2,1)S(1)} %get-tuple-element.27), channel_id=1, source_target_pairs={{0,64},{1,65},{2,66},{3,67},{4,68},{5,69},{6,70},{7,71},{8,72},{9,... | collective-permute-start | bytes 110600 | tf_op jit(solution)/shard_map/ppermute | solution.py:44
  38.0 6.1 %collective-permute-start.11 = (bf16[144,128]{1,0:T(8,128)(2,1)S(1)}, bf16[144,128]{1,0:T(8,128)(2,1)S(1)}, u32[]{:S(2)}, u32[]{:S(2)}) collective-permute-start(bf16[144,128]{1,0:T(8,128)(2,1)S(1)} %get-tuple-element.28), channel_id=1, source_target_pairs={{0,96},{1,97},{2,98},{3,99},{4,100},{5,101},{6,102},{7,103},{8,104... | collective-permute-start | bytes 110600 | tf_op jit(solution)/shard_map/ppermute | solution.py:44
  38.9 5.1 %collective-permute-start.12 = (bf16[144,128]{1,0:T(8,128)(2,1)S(1)}, bf16[144,128]{1,0:T(8,128)(2,1)S(1)}, u32[]{:S(2)}, u32[]{:S(2)}) collective-permute-start(bf16[144,128]{1,0:T(8,128)(2,1)S(1)} %get-tuple-element.29), channel_id=1, source_target_pairs={{0,32},{1,33},{2,34},{3,35},{4,36},{5,37},{6,38},{7,39},{8,40},{9,... | collective-permute-start | bytes 110600 | tf_op jit(solution)/shard_map/ppermute | solution.py:44

commit v13 on v12

--- a/solution.py
+++ b/solution.py
@@ -92,10 +92,13 @@
     pairs = fire.shape[0] // 2
     late = LATE // 2
     start = record.shape[1] - samples.shape[1]
+    columns = [slice(PAIR * v, PAIR * (v + 1)) for v in range(late)]
     copies = [
         pltpu.make_async_copy(fire_hbm, fire, sems.at[0]),
         pltpu.make_async_copy(table_hbm, table, sems.at[1]),
-        pltpu.make_async_copy(record.at[:, start:], samples, sems.at[2]),
+    ] + [
+        pltpu.make_async_copy(record.at[:, start + c.start : start + c.stop], samples.at[:, c], sems.at[2 + v])
+        for v, c in enumerate(columns)
     ]
     for copy in copies:
         copy.start()
@@ -112,9 +115,9 @@
         shot = 2 * (pairs - late + p)
         length = PAIR * (late - p)
         tables[p, :, :length] = pair_tables(master, delay(fire, shot), delay(fire, shot + 1), 0, length)
-    copies[2].wait()
-    blocks = [(pairs - late + v, samples[:, PAIR * v : PAIR * (v + 1)]) for v in range(late)]
-    add_products(message, tables, pairs - late, blocks)
+    for v, c in enumerate(columns):
+        copies[2 + v].wait()
+        add_products(message, tables, pairs - late, [(pairs - late + v, samples[:, c])])
 
 
 def own_kernel(fire, table, record, total, tables):
@@ -281,7 +284,7 @@
             pltpu.VMEM(table.shape, f32),
             pltpu.VMEM((late, 2 * ROWS, SPAN), bf16),
             pltpu.VMEM((receivers, WIN), bf16),
-            pltpu.SemaphoreType.DMA((3,)),
+            pltpu.SemaphoreType.DMA((2 + late,)),
         ],
     )(*(pltpu.with_memory_space_constraint(a, pltpu.HBM) for a in (shot_fire_samples, table, record)))
 

time: 45.5 us -> 45.8 us (level)
  no operation moved by 1% of the time
where the time goes in v13:
time: 45.8 us; the launch traced here: 45.1 us
  waiting for transfers between devices  21.7 us (47%)
  starting transfers between devices  16.5 us (36%)
  Pallas kernels  6.81 us (15%)
    ppermute x13, waiting for transfers between devices, send(): return lax.ppermute(block, ('shot', 'rcv'), route)  21.7 us
    ppermute x13, starting transfers between devices, send(): return lax.ppermute(block, ('shot', 'rcv'), route)  16.5 us
    pallas_call x3, Pallas kernels, per_device(): local(lambda *refs: gram_kernel(scale, *refs), 'gram', (share, wire), vme...  1.82 us
    pallas_call x1, Pallas kernels, per_device(): local(tail_kernel, 'tail_spectra', shape((late_rows + LATE, receivers), f...  1.74 us
    pallas_call x1, Pallas kernels, per_device(): local(own_kernel, 'own_spectra', shape((lanes - late_rows, receivers), f3...  1.25 us
  transfers between devices with their start and end apart: 13, of which 9 were waited for; matrix products, arithmetic and copies ran while one was open for 0% of the time, Pallas kernels for 7%

profile of v13, /device:TPU:4, one launch (start us, length us, event | category | flops | bytes accessed | tf_op | source)
XLA Modules:
  0.0 45.1 jit_solution(1415896429729055609)
XLA Ops:
  0.0 0.0 copy-start.1
  0.0 0.0 copy-start
  0.0 0.0 copy-start.2
  0.0 1.7 %tail_spectra.1 = f32[72,96]{1,0:T(8,128)S(1)} custom-call(s32[32]{0:T(128)} %fire_hbm.1, f32[8,2048]{1,0:T(8,128)} %constant.2.clone.table.table_hbm, bf16[96,8192]{1,0:T(8,128)(2,1)} %head.1), custom_call_target="tpu_custom_call" | custom-call | tf_op jit(solution)/shard_map/tail_spectra/pallas_call | solution.py:277
  1.8 0.1 collective-permute-start
  1.9 0.0 copy-done.1
  1.9 0.0 copy-done
  1.9 0.0 copy-done.2
  1.9 1.2 %own_spectra.1.total = f32[192,96]{1,0:T(8,128)S(1)} custom-call(s32[32]{0:T(128)S(1)} %copy-done.2, f32[8,2048]{1,0:T(8,128)S(1)} %copy-done.1, bf16[96,8192]{1,0:T(8,128)(2,1)S(1)} %copy-done), custom_call_target="tpu_custom_call" | custom-call | tf_op jit(solution)/shard_map/own_spectra/pallas_call | solution.py:296
  3.1 8.5 %collective-permute-done.message = f32[72,96]{1,0:T(8,128)S(1)} collective-permute-done((f32[72,96]{1,0:T(8,128)S(1)}, f32[72,96]{1,0:T(8,128)S(1)}, u32[]{:S(2)}, u32[]{:S(2)}) %collective-permute-start) | collective-permute-done | bytes 27680 | tf_op jit(solution)/shard_map/ppermute | solution.py:44
  11.7 0.5 %finish_spectra.1.y0 = bf16[4,24,256]{2,1,0:T(8,128)(2,1)S(1)} custom-call(f32[192,96]{1,0:T(8,128)S(1)} %own_spectra.1.total, bf16[96,8192]{1,0:T(8,128)(2,1)S(1)} %copy-done, f32[8,2048]{1,0:T(8,128)S(1)} %copy-done.1, f32[72,96]{1,0:T(8,128)S(1)} %collective-permute-done.message), custom_call_target="tpu_custom_call" | custom-call | tf_op jit(solution)/shard_map/finish_spectra/pallas_call | solution.py:303
  12.2 0.1 collective-permute-start.1
  12.3 0.4 collective-permute-start.2
  12.7 4.5 %collective-permute-start.3 = (bf16[4,24,256]{2,1,0:T(8,128)(2,1)S(1)}, bf16[4,24,256]{2,1,0:T(8,128)(2,1)S(1)}, u32[]{:S(2)}, u32[]{:S(2)}) collective-permute-start(bf16[4,24,256]{2,1,0:T(8,128)(2,1)S(1)} %finish_spectra.1.y0), channel_id=1, source_target_pairs={{0,16},{1,17},{2,18},{3,19},{4,20},{5,21},{6,22},{7,23},{8,24},{9,... | collective-permute-start | bytes 147464 | tf_op jit(solution)/shard_map/ppermute | solution.py:44
  17.3 1.5 %collective-permute-done.1.y3 = bf16[4,24,256]{2,1,0:T(8,128)(2,1)S(1)} collective-permute-done((bf16[4,24,256]{2,1,0:T(8,128)(2,1)S(1)}, bf16[4,24,256]{2,1,0:T(8,128)(2,1)S(1)}, u32[]{:S(2)}, u32[]{:S(2)}) %collective-permute-start.1) | collective-permute-done | bytes 49184 | tf_op jit(solution)/shard_map/ppermute | solution.py:44
  18.8 0.0 collective-permute-done.2.y2
  18.8 0.6 %collective-permute-done.3.y1 = bf16[4,24,256]{2,1,0:T(8,128)(2,1)S(1)} collective-permute-done((bf16[4,24,256]{2,1,0:T(8,128)(2,1)S(1)}, bf16[4,24,256]{2,1,0:T(8,128)(2,1)S(1)}, u32[]{:S(2)}, u32[]{:S(2)}) %collective-permute-start.3) | collective-permute-done | bytes 49184 | tf_op jit(solution)/shard_map/ppermute | solution.py:44
  19.4 0.1 collective-permute-start.5
  19.5 0.5 %collective-permute-start.4 = (bf16[2,2,4,24,256]{4,3,2,1,0:T(8,128)(2,1)S(1)}, bf16[2,2,4,24,256]{4,3,2,1,0:T(8,128)(2,1)S(1)}, u32[]{:S(2)}, u32[]{:S(2)}) collective-permute-start(bf16[2,2,4,24,256]{4,3,2,1,0:T(8,128)(2,1)S(1)} %get-tuple-element.18.own), channel_id=1, source_target_pairs={{0,8},{1,9},{2,10},{3,11},{4,12},{5,13},{6,14},{7,15},{8,0},{9,1},... | collective-permute-start | bytes 589832 | tf_op jit(solution)/shard_map/ppermute | solution.py:44
  20.0 0.7 %collective-permute-done.5.other = bf16[2,2,24,256]{3,2,1,0:T(8,128)(2,1)S(1)} collective-permute-done((bf16[2,2,24,256]{3,2,1,0:T(8,128)(2,1)S(1)}, bf16[2,2,24,256]{3,2,1,0:T(8,128)(2,1)S(1)}, u32[]{:S(2)}, u32[]{:S(2)}) %collective-permute-start.5) | collective-permute-done | bytes 49184 | tf_op jit(solution)/shard_map/ppermute | solution.py:44
  20.7 0.6 %collective-permute-start.6 = (bf16[2,2,2,24,256]{4,3,2,1,0:T(8,128)(2,1)S(1)}, bf16[2,2,2,24,256]{4,3,2,1,0:T(8,128)(2,1)S(1)}, u32[]{:S(2)}, u32[]{:S(2)}) collective-permute-start(bf16[2,2,2,24,256]{4,3,2,1,0:T(8,128)(2,1)S(1)} %join_core.1.own), channel_id=1, source_target_pairs={{0,4},{1,5},{2,6},{3,7},{4,0},{5,1},{6,2},{7,3},{8,12},{9,13},{10,... | collective-permute-start | bytes 294920 | tf_op jit(solution)/shard_map/ppermute | solution.py:44
  21.3 5.9 %collective-permute-done.6.cross = bf16[2,2,2,24,256]{4,3,2,1,0:T(8,128)(2,1)S(1)} collective-permute-done((bf16[2,2,2,24,256]{4,3,2,1,0:T(8,128)(2,1)S(1)}, bf16[2,2,2,24,256]{4,3,2,1,0:T(8,128)(2,1)S(1)}, u32[]{:S(2)}, u32[]{:S(2)}) %collective-permute-start.6) | collective-permute-done | bytes 98336 | tf_op jit(solution)/shard_map/ppermute | solution.py:44
  27.2 0.5 %collective-permute-start.8 = (bf16[2,2,2,24,256]{4,3,2,1,0:T(8,128)(2,1)S(1)}, bf16[2,2,2,24,256]{4,3,2,1,0:T(8,128)(2,1)S(1)}, u32[]{:S(2)}, u32[]{:S(2)}) collective-permute-start(bf16[2,2,2,24,256]{4,3,2,1,0:T(8,128)(2,1)S(1)} %choose.1.refs_1_), channel_id=1, source_target_pairs={{0,1},{1,0},{2,3},{3,2},{4,5},{5,4},{6,7},{7,6},{8,9},{9,8},{10,11... | collective-permute-start | bytes 294920 | tf_op jit(solution)/shard_map/ppermute | solution.py:44
  27.7 1.2 %collective-permute-start.9 = (bf16[2,2,2,24,256]{4,3,2,1,0:T(8,128)(2,1)S(1)}, bf16[2,2,2,24,256]{4,3,2,1,0:T(8,128)(2,1)S(1)}, u32[]{:S(2)}, u32[]{:S(2)}) collective-permute-start(bf16[2,2,2,24,256]{4,3,2,1,0:T(8,128)(2,1)S(1)} %choose.1.refs_1_), channel_id=1, source_target_pairs={{0,2},{1,3},{2,0},{3,1},{4,6},{5,7},{6,4},{7,5},{8,10},{9,11},{10,... | collective-permute-start | bytes 294920 | tf_op jit(solution)/shard_map/ppermute | solution.py:44
  28.9 1.9 %collective-permute-start.7 = (bf16[2,2,2,24,256]{4,3,2,1,0:T(8,128)(2,1)S(1)}, bf16[2,2,2,24,256]{4,3,2,1,0:T(8,128)(2,1)S(1)}, u32[]{:S(2)}, u32[]{:S(2)}) collective-permute-start(bf16[2,2,2,24,256]{4,3,2,1,0:T(8,128)(2,1)S(1)} %choose.1.refs_1_), channel_id=1, source_target_pairs={{0,3},{1,2},{2,1},{3,0},{4,7},{5,6},{6,5},{7,4},{8,11},{9,10},{10,... | collective-permute-start | bytes 294920 | tf_op jit(solution)/shard_map/ppermute | solution.py:44
  30.7 0.0 collective-permute-done.4.other
  30.8 0.1 right_side.1.refs_0_.refs_2_
  30.8 0.6 %gram.3 = (f32[192,96]{1,0:T(8,128)S(1)}, bf16[144,128]{1,0:T(8,128)(2,1)S(1)}) custom-call(bf16[8,192,256]{2,1,0:T(8,128)(2,1)S(1)} %right_side.1.refs_0_.refs_2_, bf16[2,2,2,24,256]{4,3,2,1,0:T(8,128)(2,1)S(1)} %choose.1.refs_1_, bf16[8,192,256]{2,1,0:T(8,128)(2,1)S(1)} %right_side.1.refs_0_.refs_2_), custom_call_target="tpu_custom_call" | custom-call | tf_op jit(solution)/shard_map/gram/pallas_call | solution.py:344
  31.4 1.5 %collective-permute-done.8.refs_1_ = bf16[2,2,2,24,256]{4,3,2,1,0:T(8,128)(2,1)S(1)} collective-permute-done((bf16[2,2,2,24,256]{4,3,2,1,0:T(8,128)(2,1)S(1)}, bf16[2,2,2,24,256]{4,3,2,1,0:T(8,128)(2,1)S(1)}, u32[]{:S(2)}, u32[]{:S(2)}) %collective-permute-start.8) | collective-permute-done | bytes 98336 | tf_op jit(solution)/shard_map/ppermute | solution.py:44
  32.9 0.6 %gram.4 = (f32[192,96]{1,0:T(8,128)S(1)}, bf16[144,128]{1,0:T(8,128)(2,1)S(1)}) custom-call(bf16[8,192,256]{2,1,0:T(8,128)(2,1)S(1)} %right_side.1.refs_0_.refs_2_, bf16[2,2,2,24,256]{4,3,2,1,0:T(8,128)(2,1)S(1)} %collective-permute-done.8.refs_1_, f32[192,96]{1,0:T(8,128)S(1)} %get-tuple-element.21.refs_2_), custom_call_target="tpu_custom_call" | custom-call | tf_op jit(solution)/shard_map/gram/pallas_call | solution.py:344
  33.5 0.0 collective-permute-done.9.refs_1_
  33.5 0.6 %gram.5 = (f32[192,96]{1,0:T(8,128)S(1)}, bf16[144,128]{1,0:T(8,128)(2,1)S(1)}) custom-call(bf16[8,192,256]{2,1,0:T(8,128)(2,1)S(1)} %right_side.1.refs_0_.refs_2_, bf16[2,2,2,24,256]{4,3,2,1,0:T(8,128)(2,1)S(1)} %collective-permute-done.9.refs_1_, f32[192,96]{1,0:T(8,128)S(1)} %get-tuple-element.23.refs_2_.refs_4_), custom_call_target="tpu_custom_call" | custom-call | tf_op jit(solution)/shard_map/gram/pallas_call | solution.py:344
  34.1 0.4 collective-permute-done.7.refs_1_
  34.6 0.6 %last_gram.1 = (f32[192,96]{1,0:T(8,128)S(1)}, bf16[144,128]{1,0:T(8,128)(2,1)S(1)}, bf16[144,128]{1,0:T(8,128)(2,1)S(1)}, bf16[144,128]{1,0:T(8,128)(2,1)S(1)}) custom-call(bf16[8,192,256]{2,1,0:T(8,128)(2,1)S(1)} %right_side.1.refs_0_.refs_2_, bf16[2,2,2,24,256]{4,3,2,1,0:T(8,128)(2,1)S(1)} %collective-permute-done.7.refs_1_, ...), custom_call_target="tpu_custom_call" | custom-call | tf_op jit(solution)/shard_map/last_gram/pallas_call | solution.py:350
  35.2 3.1 %collective-permute-start.10 = (bf16[144,128]{1,0:T(8,128)(2,1)S(1)}, bf16[144,128]{1,0:T(8,128)(2,1)S(1)}, u32[]{:S(2)}, u32[]{:S(2)}) collective-permute-start(bf16[144,128]{1,0:T(8,128)(2,1)S(1)} %get-tuple-element.27), channel_id=1, source_target_pairs={{0,64},{1,65},{2,66},{3,67},{4,68},{5,69},{6,70},{7,71},{8,72},{9,... | collective-permute-start | bytes 110600 | tf_op jit(solution)/shard_map/ppermute | solution.py:44
  38.3 0.9 %collective-permute-start.11 = (bf16[144,128]{1,0:T(8,128)(2,1)S(1)}, bf16[144,128]{1,0:T(8,128)(2,1)S(1)}, u32[]{:S(2)}, u32[]{:S(2)}) collective-permute-start(bf16[144,128]{1,0:T(8,128)(2,1)S(1)} %get-tuple-element.28), channel_id=1, source_target_pairs={{0,96},{1,97},{2,98},{3,99},{4,100},{5,101},{6,102},{7,103},{8,104... | collective-permute-start | bytes 110600 | tf_op jit(solution)/shard_map/ppermute | solution.py:44
  39.2 2.6 %collective-permute-start.12 = (bf16[144,128]{1,0:T(8,128)(2,1)S(1)}, bf16[144,128]{1,0:T(8,128)(2,1)S(1)}, u32[]{:S(2)}, u32[]{:S(2)}) collective-permute-start(bf16[144,128]{1,0:T(8,128)(2,1)S(1)} %get-tuple-element.29), channel_id=1, source_target_pairs={{0,32},{1,33},{2,34},{3,35},{4,36},{5,37},{6,38},{7,39},{8,40},{9,... | collective-permute-start | bytes 110600 | tf_op jit(solution)/shard_map/ppermute | solution.py:44
  41.8 1.6 %collective-permute-done.10.r2 = bf16[144,128]{1,0:T(8,128)(2,1)S(1)} collective-permute-done((bf16[144,128]{1,0:T(8,128)(2,1)S(1)}, bf16[144,128]{1,0:T(8,128)(2,1)S(1)}, u32[]{:S(2)}, u32[]{:S(2)}) %collective-permute-start.10) | collective-permute-done | bytes 36896 | tf_op jit(solution)/shard_map/ppermute | solution.py:44
  43.4 1.0 %collective-permute-done.11.r3 = bf16[144,128]{1,0:T(8,128)(2,1)S(1)} collective-permute-done((bf16[144,128]{1,0:T(8,128)(2,1)S(1)}, bf16[144,128]{1,0:T(8,128)(2,1)S(1)}, u32[]{:S(2)}, u32[]{:S(2)}) %collective-permute-start.11) | collective-permute-done | bytes 36896 | tf_op jit(solution)/shard_map/ppermute | solution.py:44
  44.4 0.0 collective-permute-done.12.r1
  44.4 0.7 %sum.1 = f32[192,96]{1,0:T(8,128)} custom-call(bf16[144,128]{1,0:T(8,128)(2,1)S(1)} %collective-permute-done.10.r2, bf16[144,128]{1,0:T(8,128)(2,1)S(1)} %collective-permute-done.11.r3, bf16[144,128]{1,0:T(8,128)(2,1)S(1)} %collective-permute-done.12.r1, f32[192,96]{1,0:T(8,128)S(1)} %get-tuple-element.30.p0), custom_call_target="tpu_custom_call" | custom-call | tf_op jit(solution)/shard_map/sum/pallas_call | solution.py:358
  (3 shorter events, 0.0 us)
Async XLA Ops:
  0.0 1.9 %copy-start.1 = (f32[8,2048]{1,0:T(8,128)S(1)}, f32[8,2048]{1,0:T(8,128)}, u32[]{:S(2)}) copy-start(f32[8,2048]{1,0:T(8,128)} %constant.2.clone.table.table_hbm) | copy-start | bytes 196612
  0.0 1.9 %copy-start = (bf16[96,8192]{1,0:T(8,128)(2,1)S(1)}, bf16[96,8192]{1,0:T(8,128)(2,1)}, u32[]{:S(2)}) copy-start(bf16[96,8192]{1,0:T(8,128)(2,1)} %head.1) | copy-start | bytes 4718596
  0.0 1.9 %copy-start.2 = (s32[32]{0:T(128)S(1)}, s32[32]{0:T(128)}, u32[]{:S(2)}) copy-start(s32[32]{0:T(128)} %fire_hbm.1) | copy-start | bytes 388
  1.8 9.9 %collective-permute-start = (f32[72,96]{1,0:T(8,128)S(1)}, f32[72,96]{1,0:T(8,128)S(1)}, u32[]{:S(2)}, u32[]{:S(2)}) collective-permute-start(f32[72,96]{1,0:T(8,128)S(1)} %tail_spectra.1), channel_id=1, source_target_pairs={{0,8},{1,9},{2,10},{3,11},{4,12},{5,13},{6,14},{7,15},{8,16},{9,17... | collective-permute-start | bytes 82952 | tf_op jit(solution)/shard_map/ppermute | solution.py:44
  12.2 6.6 %collective-permute-start.1 = (bf16[4,24,256]{2,1,0:T(8,128)(2,1)S(1)}, bf16[4,24,256]{2,1,0:T(8,128)(2,1)S(1)}, u32[]{:S(2)}, u32[]{:S(2)}) collective-permute-start(bf16[4,24,256]{2,1,0:T(8,128)(2,1)S(1)} %finish_spectra.1.y0), channel_id=1, source_target_pairs={{0,144},{1,145},{2,146},{3,147},{4,148},{5,149},{6,150},{7,151},{8... | collective-permute-start | bytes 147464 | tf_op jit(solution)/shard_map/ppermute | solution.py:44
  12.3 6.5 %collective-permute-start.2 = (bf16[4,24,256]{2,1,0:T(8,128)(2,1)S(1)}, bf16[4,24,256]{2,1,0:T(8,128)(2,1)S(1)}, u32[]{:S(2)}, u32[]{:S(2)}) collective-permute-start(bf16[4,24,256]{2,1,0:T(8,128)(2,1)S(1)} %finish_spectra.1.y0), channel_id=1, source_target_pairs={{0,128},{1,129},{2,130},{3,131},{4,132},{5,133},{6,134},{7,135},{8... | collective-permute-start | bytes 147464 | tf_op jit(solution)/shard_map/ppermute | solution.py:44
  12.7 6.6 %collective-permute-start.3 = (bf16[4,24,256]{2,1,0:T(8,128)(2,1)S(1)}, bf16[4,24,256]{2,1,0:T(8,128)(2,1)S(1)}, u32[]{:S(2)}, u32[]{:S(2)}) collective-permute-start(bf16[4,24,256]{2,1,0:T(8,128)(2,1)S(1)} %finish_spectra.1.y0), channel_id=1, source_target_pairs={{0,16},{1,17},{2,18},{3,19},{4,20},{5,21},{6,22},{7,23},{8,24},{9,... | collective-permute-start | bytes 147464 | tf_op jit(solution)/shard_map/ppermute | solution.py:44
  19.4 1.3 %collective-permute-start.5 = (bf16[2,2,24,256]{3,2,1,0:T(8,128)(2,1)S(1)}, bf16[2,2,24,256]{3,2,1,0:T(8,128)(2,1)S(1)}, u32[]{:S(2)}, u32[]{:S(2)}) collective-permute-start(bf16[2,2,24,256]{3,2,1,0:T(8,128)(2,1)S(1)} %get-tuple-element.20), channel_id=1, source_target_pairs={{0,8},{1,9},{2,10},{3,11},{4,12},{5,13},{6,14},{7,15},{8,0},{9,1},... | collective-permute-start | bytes 147464 | tf_op jit(solution)/shard_map/ppermute | solution.py:44
  19.5 11.3 %collective-permute-start.4 = (bf16[2,2,4,24,256]{4,3,2,1,0:T(8,128)(2,1)S(1)}, bf16[2,2,4,24,256]{4,3,2,1,0:T(8,128)(2,1)S(1)}, u32[]{:S(2)}, u32[]{:S(2)}) collective-permute-start(bf16[2,2,4,24,256]{4,3,2,1,0:T(8,128)(2,1)S(1)} %get-tuple-element.18.own), channel_id=1, source_target_pairs={{0,8},{1,9},{2,10},{3,11},{4,12},{5,13},{6,14},{7,15},{8,0},{9,1},... | collective-permute-start | bytes 589832 | tf_op jit(solution)/shard_map/ppermute | solution.py:44
  20.7 6.5 %collective-permute-start.6 = (bf16[2,2,2,24,256]{4,3,2,1,0:T(8,128)(2,1)S(1)}, bf16[2,2,2,24,256]{4,3,2,1,0:T(8,128)(2,1)S(1)}, u32[]{:S(2)}, u32[]{:S(2)}) collective-permute-start(bf16[2,2,2,24,256]{4,3,2,1,0:T(8,128)(2,1)S(1)} %join_core.1.own), channel_id=1, source_target_pairs={{0,4},{1,5},{2,6},{3,7},{4,0},{5,1},{6,2},{7,3},{8,12},{9,13},{10,... | collective-permute-start | bytes 294920 | tf_op jit(solution)/shard_map/ppermute | solution.py:44
  27.2 5.8 %collective-permute-start.8 = (bf16[2,2,2,24,256]{4,3,2,1,0:T(8,128)(2,1)S(1)}, bf16[2,2,2,24,256]{4,3,2,1,0:T(8,128)(2,1)S(1)}, u32[]{:S(2)}, u32[]{:S(2)}) collective-permute-start(bf16[2,2,2,24,256]{4,3,2,1,0:T(8,128)(2,1)S(1)} %choose.1.refs_1_), channel_id=1, source_target_pairs={{0,1},{1,0},{2,3},{3,2},{4,5},{5,4},{6,7},{7,6},{8,9},{9,8},{10,11... | collective-permute-start | bytes 294920 | tf_op jit(solution)/shard_map/ppermute | solution.py:44
  27.7 5.9 %collective-permute-start.9 = (bf16[2,2,2,24,256]{4,3,2,1,0:T(8,128)(2,1)S(1)}, bf16[2,2,2,24,256]{4,3,2,1,0:T(8,128)(2,1)S(1)}, u32[]{:S(2)}, u32[]{:S(2)}) collective-permute-start(bf16[2,2,2,24,256]{4,3,2,1,0:T(8,128)(2,1)S(1)} %choose.1.refs_1_), channel_id=1, source_target_pairs={{0,2},{1,3},{2,0},{3,1},{4,6},{5,7},{6,4},{7,5},{8,10},{9,11},{10,... | collective-permute-start | bytes 294920 | tf_op jit(solution)/shard_map/ppermute | solution.py:44
  28.9 5.7 %collective-permute-start.7 = (bf16[2,2,2,24,256]{4,3,2,1,0:T(8,128)(2,1)S(1)}, bf16[2,2,2,24,256]{4,3,2,1,0:T(8,128)(2,1)S(1)}, u32[]{:S(2)}, u32[]{:S(2)}) collective-permute-start(bf16[2,2,2,24,256]{4,3,2,1,0:T(8,128)(2,1)S(1)} %choose.1.refs_1_), channel_id=1, source_target_pairs={{0,3},{1,2},{2,1},{3,0},{4,7},{5,6},{6,5},{7,4},{8,11},{9,10},{10,... | collective-permute-start | bytes 294920 | tf_op jit(solution)/shard_map/ppermute | solution.py:44
  35.2 8.1 %collective-permute-start.10 = (bf16[144,128]{1,0:T(8,128)(2,1)S(1)}, bf16[144,128]{1,0:T(8,128)(2,1)S(1)}, u32[]{:S(2)}, u32[]{:S(2)}) collective-permute-start(bf16[144,128]{1,0:T(8,128)(2,1)S(1)} %get-tuple-element.27), channel_id=1, source_target_pairs={{0,64},{1,65},{2,66},{3,67},{4,68},{5,69},{6,70},{7,71},{8,72},{9,... | collective-permute-start | bytes 110600 | tf_op jit(solution)/shard_map/ppermute | solution.py:44
  38.3 6.1 %collective-permute-start.11 = (bf16[144,128]{1,0:T(8,128)(2,1)S(1)}, bf16[144,128]{1,0:T(8,128)(2,1)S(1)}, u32[]{:S(2)}, u32[]{:S(2)}) collective-permute-start(bf16[144,128]{1,0:T(8,128)(2,1)S(1)} %get-tuple-element.28), channel_id=1, source_target_pairs={{0,96},{1,97},{2,98},{3,99},{4,100},{5,101},{6,102},{7,103},{8,104... | collective-permute-start | bytes 110600 | tf_op jit(solution)/shard_map/ppermute | solution.py:44
  39.2 5.1 %collective-permute-start.12 = (bf16[144,128]{1,0:T(8,128)(2,1)S(1)}, bf16[144,128]{1,0:T(8,128)(2,1)S(1)}, u32[]{:S(2)}, u32[]{:S(2)}) collective-permute-start(bf16[144,128]{1,0:T(8,128)(2,1)S(1)} %get-tuple-element.29), channel_id=1, source_target_pairs={{0,32},{1,33},{2,34},{3,35},{4,36},{5,37},{6,38},{7,39},{8,40},{9,... | collective-permute-start | bytes 110600 | tf_op jit(solution)/shard_map/ppermute | solution.py:44

commit v14 on v12

--- a/solution.py
+++ b/solution.py
@@ -97,7 +97,7 @@
         pltpu.make_async_copy(table_hbm, table, sems.at[1]),
         pltpu.make_async_copy(record.at[:, start:], samples, sems.at[2]),
     ]
-    for copy in copies:
+    for copy in reversed(copies):
         copy.start()
     message[...] = jnp.zeros_like(message)
     copies[0].wait()

time: 45.5 us -> 45.5 us (level)
  no operation moved by 1% of the time
where the time goes in v14:
time: 45.5 us; the launch traced here: 44.8 us
  waiting for transfers between devices  21.6 us (47%)
  starting transfers between devices  16.5 us (36%)
  Pallas kernels  6.53 us (14%)
    ppermute x13, waiting for transfers between devices, send(): return lax.ppermute(block, ('shot', 'rcv'), route)  21.6 us
    ppermute x13, starting transfers between devices, send(): return lax.ppermute(block, ('shot', 'rcv'), route)  16.5 us
    pallas_call x3, Pallas kernels, per_device(): local(lambda *refs: gram_kernel(scale, *refs), 'gram', (share, wire), vme...  1.82 us
    pallas_call x1, Pallas kernels, per_device(): local(tail_kernel, 'tail_spectra', shape((late_rows + LATE, receivers), f...  1.46 us
    pallas_call x1, Pallas kernels, per_device(): local(own_kernel, 'own_spectra', shape((lanes - late_rows, receivers), f3...  1.25 us
  transfers between devices with their start and end apart: 13, of which 9 were waited for; matrix products, arithmetic and copies ran while one was open for 0% of the time, Pallas kernels for 7%

profile of v14, /device:TPU:4, one launch (start us, length us, event | category | flops | bytes accessed | tf_op | source)
XLA Modules:
  0.0 44.8 jit_solution(384516519320805012)
XLA Ops:
  0.0 0.0 copy-start.1
  0.0 0.0 copy-start
  0.0 0.0 copy-start.2
  0.0 1.5 %tail_spectra.1 = f32[72,96]{1,0:T(8,128)S(1)} custom-call(s32[32]{0:T(128)} %fire_hbm.1, f32[8,2048]{1,0:T(8,128)} %constant.2.clone.table.table_hbm, bf16[96,8192]{1,0:T(8,128)(2,1)} %head.1), custom_call_target="tpu_custom_call" | custom-call | tf_op jit(solution)/shard_map/tail_spectra/pallas_call | solution.py:274
  1.5 0.1 collective-permute-start
  1.6 0.0 copy-done.1
  1.6 0.0 copy-done
  1.6 0.0 copy-done.2
  1.6 1.2 %own_spectra.1.total = f32[192,96]{1,0:T(8,128)S(1)} custom-call(s32[32]{0:T(128)S(1)} %copy-done.2, f32[8,2048]{1,0:T(8,128)S(1)} %copy-done.1, bf16[96,8192]{1,0:T(8,128)(2,1)S(1)} %copy-done), custom_call_target="tpu_custom_call" | custom-call | tf_op jit(solution)/shard_map/own_spectra/pallas_call | solution.py:293
  2.8 8.5 %collective-permute-done.message = f32[72,96]{1,0:T(8,128)S(1)} collective-permute-done((f32[72,96]{1,0:T(8,128)S(1)}, f32[72,96]{1,0:T(8,128)S(1)}, u32[]{:S(2)}, u32[]{:S(2)}) %collective-permute-start) | collective-permute-done | bytes 27680 | tf_op jit(solution)/shard_map/ppermute | solution.py:44
  11.4 0.5 %finish_spectra.1.y0 = bf16[4,24,256]{2,1,0:T(8,128)(2,1)S(1)} custom-call(f32[192,96]{1,0:T(8,128)S(1)} %own_spectra.1.total, bf16[96,8192]{1,0:T(8,128)(2,1)S(1)} %copy-done, f32[8,2048]{1,0:T(8,128)S(1)} %copy-done.1, f32[72,96]{1,0:T(8,128)S(1)} %collective-permute-done.message), custom_call_target="tpu_custom_call" | custom-call | tf_op jit(solution)/shard_map/finish_spectra/pallas_call | solution.py:300
  11.9 0.1 collective-permute-start.1
  12.0 0.5 %collective-permute-start.2 = (bf16[4,24,256]{2,1,0:T(8,128)(2,1)S(1)}, bf16[4,24,256]{2,1,0:T(8,128)(2,1)S(1)}, u32[]{:S(2)}, u32[]{:S(2)}) collective-permute-start(bf16[4,24,256]{2,1,0:T(8,128)(2,1)S(1)} %finish_spectra.1.y0), channel_id=1, source_target_pairs={{0,128},{1,129},{2,130},{3,131},{4,132},{5,133},{6,134},{7,135},{8... | collective-permute-start | bytes 147464 | tf_op jit(solution)/shard_map/ppermute | solution.py:44
  12.5 4.5 %collective-permute-start.3 = (bf16[4,24,256]{2,1,0:T(8,128)(2,1)S(1)}, bf16[4,24,256]{2,1,0:T(8,128)(2,1)S(1)}, u32[]{:S(2)}, u32[]{:S(2)}) collective-permute-start(bf16[4,24,256]{2,1,0:T(8,128)(2,1)S(1)} %finish_spectra.1.y0), channel_id=1, source_target_pairs={{0,16},{1,17},{2,18},{3,19},{4,20},{5,21},{6,22},{7,23},{8,24},{9,... | collective-permute-start | bytes 147464 | tf_op jit(solution)/shard_map/ppermute | solution.py:44
  17.0 1.5 %collective-permute-done.1.y3 = bf16[4,24,256]{2,1,0:T(8,128)(2,1)S(1)} collective-permute-done((bf16[4,24,256]{2,1,0:T(8,128)(2,1)S(1)}, bf16[4,24,256]{2,1,0:T(8,128)(2,1)S(1)}, u32[]{:S(2)}, u32[]{:S(2)}) %collective-permute-start.1) | collective-permute-done | bytes 49184 | tf_op jit(solution)/shard_map/ppermute | solution.py:44
  18.5 0.0 collective-permute-done.2.y2
  18.5 0.6 %collective-permute-done.3.y1 = bf16[4,24,256]{2,1,0:T(8,128)(2,1)S(1)} collective-permute-done((bf16[4,24,256]{2,1,0:T(8,128)(2,1)S(1)}, bf16[4,24,256]{2,1,0:T(8,128)(2,1)S(1)}, u32[]{:S(2)}, u32[]{:S(2)}) %collective-permute-start.3) | collective-permute-done | bytes 49184 | tf_op jit(solution)/shard_map/ppermute | solution.py:44
  19.1 0.1 collective-permute-start.5
  19.2 0.5 %collective-permute-start.4 = (bf16[2,2,4,24,256]{4,3,2,1,0:T(8,128)(2,1)S(1)}, bf16[2,2,4,24,256]{4,3,2,1,0:T(8,128)(2,1)S(1)}, u32[]{:S(2)}, u32[]{:S(2)}) collective-permute-start(bf16[2,2,4,24,256]{4,3,2,1,0:T(8,128)(2,1)S(1)} %get-tuple-element.18.own), channel_id=1, source_target_pairs={{0,8},{1,9},{2,10},{3,11},{4,12},{5,13},{6,14},{7,15},{8,0},{9,1},... | collective-permute-start | bytes 589832 | tf_op jit(solution)/shard_map/ppermute | solution.py:44
  19.7 0.7 %collective-permute-done.5.other = bf16[2,2,24,256]{3,2,1,0:T(8,128)(2,1)S(1)} collective-permute-done((bf16[2,2,24,256]{3,2,1,0:T(8,128)(2,1)S(1)}, bf16[2,2,24,256]{3,2,1,0:T(8,128)(2,1)S(1)}, u32[]{:S(2)}, u32[]{:S(2)}) %collective-permute-start.5) | collective-permute-done | bytes 49184 | tf_op jit(solution)/shard_map/ppermute | solution.py:44
  20.4 0.6 %collective-permute-start.6 = (bf16[2,2,2,24,256]{4,3,2,1,0:T(8,128)(2,1)S(1)}, bf16[2,2,2,24,256]{4,3,2,1,0:T(8,128)(2,1)S(1)}, u32[]{:S(2)}, u32[]{:S(2)}) collective-permute-start(bf16[2,2,2,24,256]{4,3,2,1,0:T(8,128)(2,1)S(1)} %join_core.1.own), channel_id=1, source_target_pairs={{0,4},{1,5},{2,6},{3,7},{4,0},{5,1},{6,2},{7,3},{8,12},{9,13},{10,... | collective-permute-start | bytes 294920 | tf_op jit(solution)/shard_map/ppermute | solution.py:44
  21.0 5.8 %collective-permute-done.6.cross = bf16[2,2,2,24,256]{4,3,2,1,0:T(8,128)(2,1)S(1)} collective-permute-done((bf16[2,2,2,24,256]{4,3,2,1,0:T(8,128)(2,1)S(1)}, bf16[2,2,2,24,256]{4,3,2,1,0:T(8,128)(2,1)S(1)}, u32[]{:S(2)}, u32[]{:S(2)}) %collective-permute-start.6) | collective-permute-done | bytes 98336 | tf_op jit(solution)/shard_map/ppermute | solution.py:44
  26.9 0.5 %collective-permute-start.8 = (bf16[2,2,2,24,256]{4,3,2,1,0:T(8,128)(2,1)S(1)}, bf16[2,2,2,24,256]{4,3,2,1,0:T(8,128)(2,1)S(1)}, u32[]{:S(2)}, u32[]{:S(2)}) collective-permute-start(bf16[2,2,2,24,256]{4,3,2,1,0:T(8,128)(2,1)S(1)} %choose.1.refs_1_), channel_id=1, source_target_pairs={{0,1},{1,0},{2,3},{3,2},{4,5},{5,4},{6,7},{7,6},{8,9},{9,8},{10,11... | collective-permute-start | bytes 294920 | tf_op jit(solution)/shard_map/ppermute | solution.py:44
  27.4 1.2 %collective-permute-start.9 = (bf16[2,2,2,24,256]{4,3,2,1,0:T(8,128)(2,1)S(1)}, bf16[2,2,2,24,256]{4,3,2,1,0:T(8,128)(2,1)S(1)}, u32[]{:S(2)}, u32[]{:S(2)}) collective-permute-start(bf16[2,2,2,24,256]{4,3,2,1,0:T(8,128)(2,1)S(1)} %choose.1.refs_1_), channel_id=1, source_target_pairs={{0,2},{1,3},{2,0},{3,1},{4,6},{5,7},{6,4},{7,5},{8,10},{9,11},{10,... | collective-permute-start | bytes 294920 | tf_op jit(solution)/shard_map/ppermute | solution.py:44
  28.6 1.9 %collective-permute-start.7 = (bf16[2,2,2,24,256]{4,3,2,1,0:T(8,128)(2,1)S(1)}, bf16[2,2,2,24,256]{4,3,2,1,0:T(8,128)(2,1)S(1)}, u32[]{:S(2)}, u32[]{:S(2)}) collective-permute-start(bf16[2,2,2,24,256]{4,3,2,1,0:T(8,128)(2,1)S(1)} %choose.1.refs_1_), channel_id=1, source_target_pairs={{0,3},{1,2},{2,1},{3,0},{4,7},{5,6},{6,5},{7,4},{8,11},{9,10},{10,... | collective-permute-start | bytes 294920 | tf_op jit(solution)/shard_map/ppermute | solution.py:44
  30.4 0.0 collective-permute-done.4.other
  30.4 0.1 right_side.1.refs_0_.refs_2_
  30.5 0.6 %gram.3 = (f32[192,96]{1,0:T(8,128)S(1)}, bf16[144,128]{1,0:T(8,128)(2,1)S(1)}) custom-call(bf16[8,192,256]{2,1,0:T(8,128)(2,1)S(1)} %right_side.1.refs_0_.refs_2_, bf16[2,2,2,24,256]{4,3,2,1,0:T(8,128)(2,1)S(1)} %choose.1.refs_1_, bf16[8,192,256]{2,1,0:T(8,128)(2,1)S(1)} %right_side.1.refs_0_.refs_2_), custom_call_target="tpu_custom_call" | custom-call | tf_op jit(solution)/shard_map/gram/pallas_call | solution.py:341
  31.1 1.5 %collective-permute-done.8.refs_1_ = bf16[2,2,2,24,256]{4,3,2,1,0:T(8,128)(2,1)S(1)} collective-permute-done((bf16[2,2,2,24,256]{4,3,2,1,0:T(8,128)(2,1)S(1)}, bf16[2,2,2,24,256]{4,3,2,1,0:T(8,128)(2,1)S(1)}, u32[]{:S(2)}, u32[]{:S(2)}) %collective-permute-start.8) | collective-permute-done | bytes 98336 | tf_op jit(solution)/shard_map/ppermute | solution.py:44
  32.6 0.6 %gram.4 = (f32[192,96]{1,0:T(8,128)S(1)}, bf16[144,128]{1,0:T(8,128)(2,1)S(1)}) custom-call(bf16[8,192,256]{2,1,0:T(8,128)(2,1)S(1)} %right_side.1.refs_0_.refs_2_, bf16[2,2,2,24,256]{4,3,2,1,0:T(8,128)(2,1)S(1)} %collective-permute-done.8.refs_1_, f32[192,96]{1,0:T(8,128)S(1)} %get-tuple-element.21.refs_2_), custom_call_target="tpu_custom_call" | custom-call | tf_op jit(solution)/shard_map/gram/pallas_call | solution.py:341
  33.2 0.0 collective-permute-done.9.refs_1_
  33.2 0.6 %gram.5 = (f32[192,96]{1,0:T(8,128)S(1)}, bf16[144,128]{1,0:T(8,128)(2,1)S(1)}) custom-call(bf16[8,192,256]{2,1,0:T(8,128)(2,1)S(1)} %right_side.1.refs_0_.refs_2_, bf16[2,2,2,24,256]{4,3,2,1,0:T(8,128)(2,1)S(1)} %collective-permute-done.9.refs_1_, f32[192,96]{1,0:T(8,128)S(1)} %get-tuple-element.23.refs_2_.refs_4_), custom_call_target="tpu_custom_call" | custom-call | tf_op jit(solution)/shard_map/gram/pallas_call | solution.py:341
  33.8 0.4 collective-permute-done.7.refs_1_
  34.3 0.6 %last_gram.1 = (f32[192,96]{1,0:T(8,128)S(1)}, bf16[144,128]{1,0:T(8,128)(2,1)S(1)}, bf16[144,128]{1,0:T(8,128)(2,1)S(1)}, bf16[144,128]{1,0:T(8,128)(2,1)S(1)}) custom-call(bf16[8,192,256]{2,1,0:T(8,128)(2,1)S(1)} %right_side.1.refs_0_.refs_2_, bf16[2,2,2,24,256]{4,3,2,1,0:T(8,128)(2,1)S(1)} %collective-permute-done.7.refs_1_, ...), custom_call_target="tpu_custom_call" | custom-call | tf_op jit(solution)/shard_map/last_gram/pallas_call | solution.py:347
  34.9 3.1 %collective-permute-start.10 = (bf16[144,128]{1,0:T(8,128)(2,1)S(1)}, bf16[144,128]{1,0:T(8,128)(2,1)S(1)}, u32[]{:S(2)}, u32[]{:S(2)}) collective-permute-start(bf16[144,128]{1,0:T(8,128)(2,1)S(1)} %get-tuple-element.27), channel_id=1, source_target_pairs={{0,64},{1,65},{2,66},{3,67},{4,68},{5,69},{6,70},{7,71},{8,72},{9,... | collective-permute-start | bytes 110600 | tf_op jit(solution)/shard_map/ppermute | solution.py:44
  38.0 1.0 %collective-permute-start.11 = (bf16[144,128]{1,0:T(8,128)(2,1)S(1)}, bf16[144,128]{1,0:T(8,128)(2,1)S(1)}, u32[]{:S(2)}, u32[]{:S(2)}) collective-permute-start(bf16[144,128]{1,0:T(8,128)(2,1)S(1)} %get-tuple-element.28), channel_id=1, source_target_pairs={{0,96},{1,97},{2,98},{3,99},{4,100},{5,101},{6,102},{7,103},{8,104... | collective-permute-start | bytes 110600 | tf_op jit(solution)/shard_map/ppermute | solution.py:44
  39.0 2.5 %collective-permute-start.12 = (bf16[144,128]{1,0:T(8,128)(2,1)S(1)}, bf16[144,128]{1,0:T(8,128)(2,1)S(1)}, u32[]{:S(2)}, u32[]{:S(2)}) collective-permute-start(bf16[144,128]{1,0:T(8,128)(2,1)S(1)} %get-tuple-element.29), channel_id=1, source_target_pairs={{0,32},{1,33},{2,34},{3,35},{4,36},{5,37},{6,38},{7,39},{8,40},{9,... | collective-permute-start | bytes 110600 | tf_op jit(solution)/shard_map/ppermute | solution.py:44
  41.5 1.6 %collective-permute-done.10.r2 = bf16[144,128]{1,0:T(8,128)(2,1)S(1)} collective-permute-done((bf16[144,128]{1,0:T(8,128)(2,1)S(1)}, bf16[144,128]{1,0:T(8,128)(2,1)S(1)}, u32[]{:S(2)}, u32[]{:S(2)}) %collective-permute-start.10) | collective-permute-done | bytes 36896 | tf_op jit(solution)/shard_map/ppermute | solution.py:44
  43.1 1.0 %collective-permute-done.11.r3 = bf16[144,128]{1,0:T(8,128)(2,1)S(1)} collective-permute-done((bf16[144,128]{1,0:T(8,128)(2,1)S(1)}, bf16[144,128]{1,0:T(8,128)(2,1)S(1)}, u32[]{:S(2)}, u32[]{:S(2)}) %collective-permute-start.11) | collective-permute-done | bytes 36896 | tf_op jit(solution)/shard_map/ppermute | solution.py:44
  44.1 0.0 collective-permute-done.12.r1
  44.1 0.7 %sum.1 = f32[192,96]{1,0:T(8,128)} custom-call(bf16[144,128]{1,0:T(8,128)(2,1)S(1)} %collective-permute-done.10.r2, bf16[144,128]{1,0:T(8,128)(2,1)S(1)} %collective-permute-done.11.r3, bf16[144,128]{1,0:T(8,128)(2,1)S(1)} %collective-permute-done.12.r1, f32[192,96]{1,0:T(8,128)S(1)} %get-tuple-element.30.p0), custom_call_target="tpu_custom_call" | custom-call | tf_op jit(solution)/shard_map/sum/pallas_call | solution.py:355
  (3 shorter events, 0.0 us)
Async XLA Ops:
  0.0 1.6 %copy-start.1 = (f32[8,2048]{1,0:T(8,128)S(1)}, f32[8,2048]{1,0:T(8,128)}, u32[]{:S(2)}) copy-start(f32[8,2048]{1,0:T(8,128)} %constant.2.clone.table.table_hbm) | copy-start | bytes 196612
  0.0 1.6 %copy-start = (bf16[96,8192]{1,0:T(8,128)(2,1)S(1)}, bf16[96,8192]{1,0:T(8,128)(2,1)}, u32[]{:S(2)}) copy-start(bf16[96,8192]{1,0:T(8,128)(2,1)} %head.1) | copy-start | bytes 4718596
  0.0 1.6 %copy-start.2 = (s32[32]{0:T(128)S(1)}, s32[32]{0:T(128)}, u32[]{:S(2)}) copy-start(s32[32]{0:T(128)} %fire_hbm.1) | copy-start | bytes 388
  1.5 9.9 %collective-permute-start = (f32[72,96]{1,0:T(8,128)S(1)}, f32[72,96]{1,0:T(8,128)S(1)}, u32[]{:S(2)}, u32[]{:S(2)}) collective-permute-start(f32[72,96]{1,0:T(8,128)S(1)} %tail_spectra.1), channel_id=1, source_target_pairs={{0,8},{1,9},{2,10},{3,11},{4,12},{5,13},{6,14},{7,15},{8,16},{9,17... | collective-permute-start | bytes 82952 | tf_op jit(solution)/shard_map/ppermute | solution.py:44
  11.9 6.6 %collective-permute-start.1 = (bf16[4,24,256]{2,1,0:T(8,128)(2,1)S(1)}, bf16[4,24,256]{2,1,0:T(8,128)(2,1)S(1)}, u32[]{:S(2)}, u32[]{:S(2)}) collective-permute-start(bf16[4,24,256]{2,1,0:T(8,128)(2,1)S(1)} %finish_spectra.1.y0), channel_id=1, source_target_pairs={{0,144},{1,145},{2,146},{3,147},{4,148},{5,149},{6,150},{7,151},{8... | collective-permute-start | bytes 147464 | tf_op jit(solution)/shard_map/ppermute | solution.py:44
  12.0 6.5 %collective-permute-start.2 = (bf16[4,24,256]{2,1,0:T(8,128)(2,1)S(1)}, bf16[4,24,256]{2,1,0:T(8,128)(2,1)S(1)}, u32[]{:S(2)}, u32[]{:S(2)}) collective-permute-start(bf16[4,24,256]{2,1,0:T(8,128)(2,1)S(1)} %finish_spectra.1.y0), channel_id=1, source_target_pairs={{0,128},{1,129},{2,130},{3,131},{4,132},{5,133},{6,134},{7,135},{8... | collective-permute-start | bytes 147464 | tf_op jit(solution)/shard_map/ppermute | solution.py:44
  12.5 6.6 %collective-permute-start.3 = (bf16[4,24,256]{2,1,0:T(8,128)(2,1)S(1)}, bf16[4,24,256]{2,1,0:T(8,128)(2,1)S(1)}, u32[]{:S(2)}, u32[]{:S(2)}) collective-permute-start(bf16[4,24,256]{2,1,0:T(8,128)(2,1)S(1)} %finish_spectra.1.y0), channel_id=1, source_target_pairs={{0,16},{1,17},{2,18},{3,19},{4,20},{5,21},{6,22},{7,23},{8,24},{9,... | collective-permute-start | bytes 147464 | tf_op jit(solution)/shard_map/ppermute | solution.py:44
  19.1 1.3 %collective-permute-start.5 = (bf16[2,2,24,256]{3,2,1,0:T(8,128)(2,1)S(1)}, bf16[2,2,24,256]{3,2,1,0:T(8,128)(2,1)S(1)}, u32[]{:S(2)}, u32[]{:S(2)}) collective-permute-start(bf16[2,2,24,256]{3,2,1,0:T(8,128)(2,1)S(1)} %get-tuple-element.20), channel_id=1, source_target_pairs={{0,8},{1,9},{2,10},{3,11},{4,12},{5,13},{6,14},{7,15},{8,0},{9,1},... | collective-permute-start | bytes 147464 | tf_op jit(solution)/shard_map/ppermute | solution.py:44
  19.2 11.3 %collective-permute-start.4 = (bf16[2,2,4,24,256]{4,3,2,1,0:T(8,128)(2,1)S(1)}, bf16[2,2,4,24,256]{4,3,2,1,0:T(8,128)(2,1)S(1)}, u32[]{:S(2)}, u32[]{:S(2)}) collective-permute-start(bf16[2,2,4,24,256]{4,3,2,1,0:T(8,128)(2,1)S(1)} %get-tuple-element.18.own), channel_id=1, source_target_pairs={{0,8},{1,9},{2,10},{3,11},{4,12},{5,13},{6,14},{7,15},{8,0},{9,1},... | collective-permute-start | bytes 589832 | tf_op jit(solution)/shard_map/ppermute | solution.py:44
  20.4 6.5 %collective-permute-start.6 = (bf16[2,2,2,24,256]{4,3,2,1,0:T(8,128)(2,1)S(1)}, bf16[2,2,2,24,256]{4,3,2,1,0:T(8,128)(2,1)S(1)}, u32[]{:S(2)}, u32[]{:S(2)}) collective-permute-start(bf16[2,2,2,24,256]{4,3,2,1,0:T(8,128)(2,1)S(1)} %join_core.1.own), channel_id=1, source_target_pairs={{0,4},{1,5},{2,6},{3,7},{4,0},{5,1},{6,2},{7,3},{8,12},{9,13},{10,... | collective-permute-start | bytes 294920 | tf_op jit(solution)/shard_map/ppermute | solution.py:44
  26.9 5.8 %collective-permute-start.8 = (bf16[2,2,2,24,256]{4,3,2,1,0:T(8,128)(2,1)S(1)}, bf16[2,2,2,24,256]{4,3,2,1,0:T(8,128)(2,1)S(1)}, u32[]{:S(2)}, u32[]{:S(2)}) collective-permute-start(bf16[2,2,2,24,256]{4,3,2,1,0:T(8,128)(2,1)S(1)} %choose.1.refs_1_), channel_id=1, source_target_pairs={{0,1},{1,0},{2,3},{3,2},{4,5},{5,4},{6,7},{7,6},{8,9},{9,8},{10,11... | collective-permute-start | bytes 294920 | tf_op jit(solution)/shard_map/ppermute | solution.py:44
  27.4 5.8 %collective-permute-start.9 = (bf16[2,2,2,24,256]{4,3,2,1,0:T(8,128)(2,1)S(1)}, bf16[2,2,2,24,256]{4,3,2,1,0:T(8,128)(2,1)S(1)}, u32[]{:S(2)}, u32[]{:S(2)}) collective-permute-start(bf16[2,2,2,24,256]{4,3,2,1,0:T(8,128)(2,1)S(1)} %choose.1.refs_1_), channel_id=1, source_target_pairs={{0,2},{1,3},{2,0},{3,1},{4,6},{5,7},{6,4},{7,5},{8,10},{9,11},{10,... | collective-permute-start | bytes 294920 | tf_op jit(solution)/shard_map/ppermute | solution.py:44
  28.6 5.7 %collective-permute-start.7 = (bf16[2,2,2,24,256]{4,3,2,1,0:T(8,128)(2,1)S(1)}, bf16[2,2,2,24,256]{4,3,2,1,0:T(8,128)(2,1)S(1)}, u32[]{:S(2)}, u32[]{:S(2)}) collective-permute-start(bf16[2,2,2,24,256]{4,3,2,1,0:T(8,128)(2,1)S(1)} %choose.1.refs_1_), channel_id=1, source_target_pairs={{0,3},{1,2},{2,1},{3,0},{4,7},{5,6},{6,5},{7,4},{8,11},{9,10},{10,... | collective-permute-start | bytes 294920 | tf_op jit(solution)/shard_map/ppermute | solution.py:44
  34.9 8.2 %collective-permute-start.10 = (bf16[144,128]{1,0:T(8,128)(2,1)S(1)}, bf16[144,128]{1,0:T(8,128)(2,1)S(1)}, u32[]{:S(2)}, u32[]{:S(2)}) collective-permute-start(bf16[144,128]{1,0:T(8,128)(2,1)S(1)} %get-tuple-element.27), channel_id=1, source_target_pairs={{0,64},{1,65},{2,66},{3,67},{4,68},{5,69},{6,70},{7,71},{8,72},{9,... | collective-permute-start | bytes 110600 | tf_op jit(solution)/shard_map/ppermute | solution.py:44
  38.0 6.1 %collective-permute-start.11 = (bf16[144,128]{1,0:T(8,128)(2,1)S(1)}, bf16[144,128]{1,0:T(8,128)(2,1)S(1)}, u32[]{:S(2)}, u32[]{:S(2)}) collective-permute-start(bf16[144,128]{1,0:T(8,128)(2,1)S(1)} %get-tuple-element.28), channel_id=1, source_target_pairs={{0,96},{1,97},{2,98},{3,99},{4,100},{5,101},{6,102},{7,103},{8,104... | collective-permute-start | bytes 110600 | tf_op jit(solution)/shard_map/ppermute | solution.py:44
  39.0 5.1 %collective-permute-start.12 = (bf16[144,128]{1,0:T(8,128)(2,1)S(1)}, bf16[144,128]{1,0:T(8,128)(2,1)S(1)}, u32[]{:S(2)}, u32[]{:S(2)}) collective-permute-start(bf16[144,128]{1,0:T(8,128)(2,1)S(1)} %get-tuple-element.29), channel_id=1, source_target_pairs={{0,32},{1,33},{2,34},{3,35},{4,36},{5,37},{6,38},{7,39},{8,40},{9,... | collective-permute-start | bytes 110600 | tf_op jit(solution)/shard_map/ppermute | solution.py:44

commit v15 on v12

--- a/solution.py
+++ b/solution.py
@@ -88,7 +88,7 @@
         total[2 * ROWS * (low - first_pair) : 2 * ROWS * (high + 1 - first_pair), :] += part
 
 
-def tail_kernel(fire_hbm, table_hbm, record, message, fire, table, tables, samples, sems):
+def tail_kernel(fire_hbm, table_hbm, record, out, fire, table, tables, samples, message, sems):
     pairs = fire.shape[0] // 2
     late = LATE // 2
     start = record.shape[1] - samples.shape[1]
@@ -115,6 +115,7 @@
     copies[2].wait()
     blocks = [(pairs - late + v, samples[:, PAIR * v : PAIR * (v + 1)]) for v in range(late)]
     add_products(message, tables, pairs - late, blocks)
+    out[...] = message[...].astype(out.dtype)
 
 
 def own_kernel(fire, table, record, total, tables):
@@ -132,6 +133,7 @@
     late = LATE // 2
     follows = (shot_index() > 0).astype(jnp.float32)
     master = table[...]
+    message = message[...].astype(jnp.float32)
     for p in range(late):
         rows = [message[ROWS * LATE + 2 * p + i : ROWS * LATE + 2 * p + i + 1, :] for i in range(2)]
         first, second = [jnp.max(r).astype(jnp.int32) for r in rows]
@@ -274,13 +276,14 @@
     message = local(
         tail_kernel,
         "tail_spectra",
-        shape((late_rows + LATE, receivers), f32),
+        shape((late_rows + LATE, receivers), bf16),
         [hbm] * 3,
         [
             pltpu.SMEM((shots,), jnp.int32),
             pltpu.VMEM(table.shape, f32),
             pltpu.VMEM((late, 2 * ROWS, SPAN), bf16),
             pltpu.VMEM((receivers, WIN), bf16),
+            pltpu.VMEM((late_rows + LATE, receivers), f32),
             pltpu.SemaphoreType.DMA((3,)),
         ],
     )(*(pltpu.with_memory_space_constraint(a, pltpu.HBM) for a in (shot_fire_samples, table, record)))

time: 45.5 us -> 45.3 us (level)
  no operation moved by 1% of the time
where the time goes in v15:
time: 45.3 us; the launch traced here: 44.8 us
  waiting for transfers between devices  21.6 us (48%)
  starting transfers between devices  16.5 us (36%)
  Pallas kernels  6.49 us (14%)
    ppermute x13, waiting for transfers between devices, send(): return lax.ppermute(block, ('shot', 'rcv'), route)  21.6 us
    ppermute x13, starting transfers between devices, send(): return lax.ppermute(block, ('shot', 'rcv'), route)  16.5 us
    pallas_call x3, Pallas kernels, per_device(): local(lambda *refs: gram_kernel(scale, *refs), 'gram', (share, wire), vme...  1.81 us
    pallas_call x1, Pallas kernels, per_device(): local(tail_kernel, 'tail_spectra', shape((late_rows + LATE, receivers), b...  1.43 us
    pallas_call x1, Pallas kernels, per_device(): local(own_kernel, 'own_spectra', shape((lanes - late_rows, receivers), f3...  1.24 us
  transfers between devices with their start and end apart: 13, of which 9 were waited for; matrix products, arithmetic and copies ran while one was open for 0% of the time, Pallas kernels for 7%

profile of v15, /device:TPU:4, one launch (start us, length us, event | category | flops | bytes accessed | tf_op | source)
XLA Modules:
  0.0 44.8 jit_solution(935767445096063000)
XLA Ops:
  0.0 0.0 copy-start.1
  0.0 0.0 copy-start
  0.0 0.0 copy-start.2
  0.0 1.4 %tail_spectra.1 = bf16[72,96]{1,0:T(8,128)(2,1)S(1)} custom-call(s32[32]{0:T(128)} %fire_hbm.1, f32[8,2048]{1,0:T(8,128)} %constant.2.clone.table.table_hbm, bf16[96,8192]{1,0:T(8,128)(2,1)} %head.1), custom_call_target="tpu_custom_call" | custom-call | tf_op jit(solution)/shard_map/tail_spectra/pallas_call | solution.py:276
  1.5 0.1 collective-permute-start
  1.5 0.0 copy-done.1
  1.6 0.0 copy-done
  1.6 0.0 copy-done.2
  1.6 1.2 %own_spectra.1.total = f32[192,96]{1,0:T(8,128)S(1)} custom-call(s32[32]{0:T(128)S(1)} %copy-done.2, f32[8,2048]{1,0:T(8,128)S(1)} %copy-done.1, bf16[96,8192]{1,0:T(8,128)(2,1)S(1)} %copy-done), custom_call_target="tpu_custom_call" | custom-call | tf_op jit(solution)/shard_map/own_spectra/pallas_call | solution.py:296
  2.8 8.1 %collective-permute-done.message = bf16[72,96]{1,0:T(8,128)(2,1)S(1)} collective-permute-done((bf16[72,96]{1,0:T(8,128)(2,1)S(1)}, bf16[72,96]{1,0:T(8,128)(2,1)S(1)}, u32[]{:S(2)}, u32[]{:S(2)}) %collective-permute-start) | collective-permute-done | bytes 13856 | tf_op jit(solution)/shard_map/ppermute | solution.py:44
  11.0 0.5 %finish_spectra.1.y0 = bf16[4,24,256]{2,1,0:T(8,128)(2,1)S(1)} custom-call(f32[192,96]{1,0:T(8,128)S(1)} %own_spectra.1.total, bf16[96,8192]{1,0:T(8,128)(2,1)S(1)} %copy-done, f32[8,2048]{1,0:T(8,128)S(1)} %copy-done.1, bf16[72,96]{1,0:T(8,128)(2,1)S(1)} %collective-permute-done.message), custom_call_target="tpu_custom_call" | custom-call | tf_op jit(solution)/shard_map/finish_spectra/pallas_call | solution.py:303
  11.5 0.1 collective-permute-start.1
  11.6 0.7 %collective-permute-start.2 = (bf16[4,24,256]{2,1,0:T(8,128)(2,1)S(1)}, bf16[4,24,256]{2,1,0:T(8,128)(2,1)S(1)}, u32[]{:S(2)}, u32[]{:S(2)}) collective-permute-start(bf16[4,24,256]{2,1,0:T(8,128)(2,1)S(1)} %finish_spectra.1.y0), channel_id=1, source_target_pairs={{0,128},{1,129},{2,130},{3,131},{4,132},{5,133},{6,134},{7,135},{8... | collective-permute-start | bytes 147464 | tf_op jit(solution)/shard_map/ppermute | solution.py:44
  12.2 4.3 %collective-permute-start.3 = (bf16[4,24,256]{2,1,0:T(8,128)(2,1)S(1)}, bf16[4,24,256]{2,1,0:T(8,128)(2,1)S(1)}, u32[]{:S(2)}, u32[]{:S(2)}) collective-permute-start(bf16[4,24,256]{2,1,0:T(8,128)(2,1)S(1)} %finish_spectra.1.y0), channel_id=1, source_target_pairs={{0,16},{1,17},{2,18},{3,19},{4,20},{5,21},{6,22},{7,23},{8,24},{9,... | collective-permute-start | bytes 147464 | tf_op jit(solution)/shard_map/ppermute | solution.py:44
  16.6 1.5 %collective-permute-done.1.y3 = bf16[4,24,256]{2,1,0:T(8,128)(2,1)S(1)} collective-permute-done((bf16[4,24,256]{2,1,0:T(8,128)(2,1)S(1)}, bf16[4,24,256]{2,1,0:T(8,128)(2,1)S(1)}, u32[]{:S(2)}, u32[]{:S(2)}) %collective-permute-start.1) | collective-permute-done | bytes 49184 | tf_op jit(solution)/shard_map/ppermute | solution.py:44
  18.1 0.0 collective-permute-done.2.y2
  18.1 0.6 %collective-permute-done.3.y1 = bf16[4,24,256]{2,1,0:T(8,128)(2,1)S(1)} collective-permute-done((bf16[4,24,256]{2,1,0:T(8,128)(2,1)S(1)}, bf16[4,24,256]{2,1,0:T(8,128)(2,1)S(1)}, u32[]{:S(2)}, u32[]{:S(2)}) %collective-permute-start.3) | collective-permute-done | bytes 49184 | tf_op jit(solution)/shard_map/ppermute | solution.py:44
  18.7 0.1 collective-permute-start.5
  18.8 0.5 %collective-permute-start.4 = (bf16[2,2,4,24,256]{4,3,2,1,0:T(8,128)(2,1)S(1)}, bf16[2,2,4,24,256]{4,3,2,1,0:T(8,128)(2,1)S(1)}, u32[]{:S(2)}, u32[]{:S(2)}) collective-permute-start(bf16[2,2,4,24,256]{4,3,2,1,0:T(8,128)(2,1)S(1)} %get-tuple-element.18.own), channel_id=1, source_target_pairs={{0,8},{1,9},{2,10},{3,11},{4,12},{5,13},{6,14},{7,15},{8,0},{9,1},... | collective-permute-start | bytes 589832 | tf_op jit(solution)/shard_map/ppermute | solution.py:44
  19.3 0.7 %collective-permute-done.5.other = bf16[2,2,24,256]{3,2,1,0:T(8,128)(2,1)S(1)} collective-permute-done((bf16[2,2,24,256]{3,2,1,0:T(8,128)(2,1)S(1)}, bf16[2,2,24,256]{3,2,1,0:T(8,128)(2,1)S(1)}, u32[]{:S(2)}, u32[]{:S(2)}) %collective-permute-start.5) | collective-permute-done | bytes 49184 | tf_op jit(solution)/shard_map/ppermute | solution.py:44
  20.0 0.6 %collective-permute-start.6 = (bf16[2,2,2,24,256]{4,3,2,1,0:T(8,128)(2,1)S(1)}, bf16[2,2,2,24,256]{4,3,2,1,0:T(8,128)(2,1)S(1)}, u32[]{:S(2)}, u32[]{:S(2)}) collective-permute-start(bf16[2,2,2,24,256]{4,3,2,1,0:T(8,128)(2,1)S(1)} %join_core.1.own), channel_id=1, source_target_pairs={{0,4},{1,5},{2,6},{3,7},{4,0},{5,1},{6,2},{7,3},{8,12},{9,13},{10,... | collective-permute-start | bytes 294920 | tf_op jit(solution)/shard_map/ppermute | solution.py:44
  20.6 5.9 %collective-permute-done.6.cross = bf16[2,2,2,24,256]{4,3,2,1,0:T(8,128)(2,1)S(1)} collective-permute-done((bf16[2,2,2,24,256]{4,3,2,1,0:T(8,128)(2,1)S(1)}, bf16[2,2,2,24,256]{4,3,2,1,0:T(8,128)(2,1)S(1)}, u32[]{:S(2)}, u32[]{:S(2)}) %collective-permute-start.6) | collective-permute-done | bytes 98336 | tf_op jit(solution)/shard_map/ppermute | solution.py:44
  26.5 0.7 %collective-permute-start.8 = (bf16[2,2,2,24,256]{4,3,2,1,0:T(8,128)(2,1)S(1)}, bf16[2,2,2,24,256]{4,3,2,1,0:T(8,128)(2,1)S(1)}, u32[]{:S(2)}, u32[]{:S(2)}) collective-permute-start(bf16[2,2,2,24,256]{4,3,2,1,0:T(8,128)(2,1)S(1)} %choose.1.refs_1_), channel_id=1, source_target_pairs={{0,1},{1,0},{2,3},{3,2},{4,5},{5,4},{6,7},{7,6},{8,9},{9,8},{10,11... | collective-permute-start | bytes 294920 | tf_op jit(solution)/shard_map/ppermute | solution.py:44
  27.2 1.2 %collective-permute-start.9 = (bf16[2,2,2,24,256]{4,3,2,1,0:T(8,128)(2,1)S(1)}, bf16[2,2,2,24,256]{4,3,2,1,0:T(8,128)(2,1)S(1)}, u32[]{:S(2)}, u32[]{:S(2)}) collective-permute-start(bf16[2,2,2,24,256]{4,3,2,1,0:T(8,128)(2,1)S(1)} %choose.1.refs_1_), channel_id=1, source_target_pairs={{0,2},{1,3},{2,0},{3,1},{4,6},{5,7},{6,4},{7,5},{8,10},{9,11},{10,... | collective-permute-start | bytes 294920 | tf_op jit(solution)/shard_map/ppermute | solution.py:44
  28.4 1.7 %collective-permute-start.7 = (bf16[2,2,2,24,256]{4,3,2,1,0:T(8,128)(2,1)S(1)}, bf16[2,2,2,24,256]{4,3,2,1,0:T(8,128)(2,1)S(1)}, u32[]{:S(2)}, u32[]{:S(2)}) collective-permute-start(bf16[2,2,2,24,256]{4,3,2,1,0:T(8,128)(2,1)S(1)} %choose.1.refs_1_), channel_id=1, source_target_pairs={{0,3},{1,2},{2,1},{3,0},{4,7},{5,6},{6,5},{7,4},{8,11},{9,10},{10,... | collective-permute-start | bytes 294920 | tf_op jit(solution)/shard_map/ppermute | solution.py:44
  30.0 0.0 collective-permute-done.4.other
  30.0 0.1 right_side.1.refs_0_.refs_2_
  30.1 0.6 %gram.3 = (f32[192,96]{1,0:T(8,128)S(1)}, bf16[144,128]{1,0:T(8,128)(2,1)S(1)}) custom-call(bf16[8,192,256]{2,1,0:T(8,128)(2,1)S(1)} %right_side.1.refs_0_.refs_2_, bf16[2,2,2,24,256]{4,3,2,1,0:T(8,128)(2,1)S(1)} %choose.1.refs_1_, bf16[8,192,256]{2,1,0:T(8,128)(2,1)S(1)} %right_side.1.refs_0_.refs_2_), custom_call_target="tpu_custom_call" | custom-call | tf_op jit(solution)/shard_map/gram/pallas_call | solution.py:344
  30.7 1.5 %collective-permute-done.8.refs_1_ = bf16[2,2,2,24,256]{4,3,2,1,0:T(8,128)(2,1)S(1)} collective-permute-done((bf16[2,2,2,24,256]{4,3,2,1,0:T(8,128)(2,1)S(1)}, bf16[2,2,2,24,256]{4,3,2,1,0:T(8,128)(2,1)S(1)}, u32[]{:S(2)}, u32[]{:S(2)}) %collective-permute-start.8) | collective-permute-done | bytes 98336 | tf_op jit(solution)/shard_map/ppermute | solution.py:44
  32.2 0.6 %gram.4 = (f32[192,96]{1,0:T(8,128)S(1)}, bf16[144,128]{1,0:T(8,128)(2,1)S(1)}) custom-call(bf16[8,192,256]{2,1,0:T(8,128)(2,1)S(1)} %right_side.1.refs_0_.refs_2_, bf16[2,2,2,24,256]{4,3,2,1,0:T(8,128)(2,1)S(1)} %collective-permute-done.8.refs_1_, f32[192,96]{1,0:T(8,128)S(1)} %get-tuple-element.21.refs_2_), custom_call_target="tpu_custom_call" | custom-call | tf_op jit(solution)/shard_map/gram/pallas_call | solution.py:344
  32.8 0.0 collective-permute-done.9.refs_1_
  32.8 0.6 %gram.5 = (f32[192,96]{1,0:T(8,128)S(1)}, bf16[144,128]{1,0:T(8,128)(2,1)S(1)}) custom-call(bf16[8,192,256]{2,1,0:T(8,128)(2,1)S(1)} %right_side.1.refs_0_.refs_2_, bf16[2,2,2,24,256]{4,3,2,1,0:T(8,128)(2,1)S(1)} %collective-permute-done.9.refs_1_, f32[192,96]{1,0:T(8,128)S(1)} %get-tuple-element.23.refs_2_.refs_4_), custom_call_target="tpu_custom_call" | custom-call | tf_op jit(solution)/shard_map/gram/pallas_call | solution.py:344
  33.4 0.4 collective-permute-done.7.refs_1_
  33.9 0.6 %last_gram.1 = (f32[192,96]{1,0:T(8,128)S(1)}, bf16[144,128]{1,0:T(8,128)(2,1)S(1)}, bf16[144,128]{1,0:T(8,128)(2,1)S(1)}, bf16[144,128]{1,0:T(8,128)(2,1)S(1)}) custom-call(bf16[8,192,256]{2,1,0:T(8,128)(2,1)S(1)} %right_side.1.refs_0_.refs_2_, bf16[2,2,2,24,256]{4,3,2,1,0:T(8,128)(2,1)S(1)} %collective-permute-done.7.refs_1_, ...), custom_call_target="tpu_custom_call" | custom-call | tf_op jit(solution)/shard_map/last_gram/pallas_call | solution.py:350
  34.5 3.5 %collective-permute-start.10 = (bf16[144,128]{1,0:T(8,128)(2,1)S(1)}, bf16[144,128]{1,0:T(8,128)(2,1)S(1)}, u32[]{:S(2)}, u32[]{:S(2)}) collective-permute-start(bf16[144,128]{1,0:T(8,128)(2,1)S(1)} %get-tuple-element.27), channel_id=1, source_target_pairs={{0,64},{1,65},{2,66},{3,67},{4,68},{5,69},{6,70},{7,71},{8,72},{9,... | collective-permute-start | bytes 110600 | tf_op jit(solution)/shard_map/ppermute | solution.py:44
  38.0 0.8 %collective-permute-start.11 = (bf16[144,128]{1,0:T(8,128)(2,1)S(1)}, bf16[144,128]{1,0:T(8,128)(2,1)S(1)}, u32[]{:S(2)}, u32[]{:S(2)}) collective-permute-start(bf16[144,128]{1,0:T(8,128)(2,1)S(1)} %get-tuple-element.28), channel_id=1, source_target_pairs={{0,96},{1,97},{2,98},{3,99},{4,100},{5,101},{6,102},{7,103},{8,104... | collective-permute-start | bytes 110600 | tf_op jit(solution)/shard_map/ppermute | solution.py:44
  38.8 2.3 %collective-permute-start.12 = (bf16[144,128]{1,0:T(8,128)(2,1)S(1)}, bf16[144,128]{1,0:T(8,128)(2,1)S(1)}, u32[]{:S(2)}, u32[]{:S(2)}) collective-permute-start(bf16[144,128]{1,0:T(8,128)(2,1)S(1)} %get-tuple-element.29), channel_id=1, source_target_pairs={{0,32},{1,33},{2,34},{3,35},{4,36},{5,37},{6,38},{7,39},{8,40},{9,... | collective-permute-start | bytes 110600 | tf_op jit(solution)/shard_map/ppermute | solution.py:44
  41.1 1.4 %collective-permute-done.10.r2 = bf16[144,128]{1,0:T(8,128)(2,1)S(1)} collective-permute-done((bf16[144,128]{1,0:T(8,128)(2,1)S(1)}, bf16[144,128]{1,0:T(8,128)(2,1)S(1)}, u32[]{:S(2)}, u32[]{:S(2)}) %collective-permute-start.10) | collective-permute-done | bytes 36896 | tf_op jit(solution)/shard_map/ppermute | solution.py:44
  42.5 1.6 %collective-permute-done.11.r3 = bf16[144,128]{1,0:T(8,128)(2,1)S(1)} collective-permute-done((bf16[144,128]{1,0:T(8,128)(2,1)S(1)}, bf16[144,128]{1,0:T(8,128)(2,1)S(1)}, u32[]{:S(2)}, u32[]{:S(2)}) %collective-permute-start.11) | collective-permute-done | bytes 36896 | tf_op jit(solution)/shard_map/ppermute | solution.py:44
  44.0 0.0 collective-permute-done.12.r1
  44.1 0.7 %sum.1 = f32[192,96]{1,0:T(8,128)} custom-call(bf16[144,128]{1,0:T(8,128)(2,1)S(1)} %collective-permute-done.10.r2, bf16[144,128]{1,0:T(8,128)(2,1)S(1)} %collective-permute-done.11.r3, bf16[144,128]{1,0:T(8,128)(2,1)S(1)} %collective-permute-done.12.r1, f32[192,96]{1,0:T(8,128)S(1)} %get-tuple-element.30.p0), custom_call_target="tpu_custom_call" | custom-call | tf_op jit(solution)/shard_map/sum/pallas_call | solution.py:358
  (3 shorter events, 0.0 us)
Async XLA Ops:
  0.0 1.5 %copy-start.1 = (f32[8,2048]{1,0:T(8,128)S(1)}, f32[8,2048]{1,0:T(8,128)}, u32[]{:S(2)}) copy-start(f32[8,2048]{1,0:T(8,128)} %constant.2.clone.table.table_hbm) | copy-start | bytes 196612
  0.0 1.6 %copy-start = (bf16[96,8192]{1,0:T(8,128)(2,1)S(1)}, bf16[96,8192]{1,0:T(8,128)(2,1)}, u32[]{:S(2)}) copy-start(bf16[96,8192]{1,0:T(8,128)(2,1)} %head.1) | copy-start | bytes 4718596
  0.0 1.6 %copy-start.2 = (s32[32]{0:T(128)S(1)}, s32[32]{0:T(128)}, u32[]{:S(2)}) copy-start(s32[32]{0:T(128)} %fire_hbm.1) | copy-start | bytes 388
  1.5 9.5 %collective-permute-start = (bf16[72,96]{1,0:T(8,128)(2,1)S(1)}, bf16[72,96]{1,0:T(8,128)(2,1)S(1)}, u32[]{:S(2)}, u32[]{:S(2)}) collective-permute-start(bf16[72,96]{1,0:T(8,128)(2,1)S(1)} %tail_spectra.1), channel_id=1, source_target_pairs={{0,8},{1,9},{2,10},{3,11},{4,12},{5,13},{6,14},{7,15},{8,16},{9,17... | collective-permute-start | bytes 41480 | tf_op jit(solution)/shard_map/ppermute | solution.py:44
  11.5 6.6 %collective-permute-start.1 = (bf16[4,24,256]{2,1,0:T(8,128)(2,1)S(1)}, bf16[4,24,256]{2,1,0:T(8,128)(2,1)S(1)}, u32[]{:S(2)}, u32[]{:S(2)}) collective-permute-start(bf16[4,24,256]{2,1,0:T(8,128)(2,1)S(1)} %finish_spectra.1.y0), channel_id=1, source_target_pairs={{0,144},{1,145},{2,146},{3,147},{4,148},{5,149},{6,150},{7,151},{8... | collective-permute-start | bytes 147464 | tf_op jit(solution)/shard_map/ppermute | solution.py:44
  11.6 6.5 %collective-permute-start.2 = (bf16[4,24,256]{2,1,0:T(8,128)(2,1)S(1)}, bf16[4,24,256]{2,1,0:T(8,128)(2,1)S(1)}, u32[]{:S(2)}, u32[]{:S(2)}) collective-permute-start(bf16[4,24,256]{2,1,0:T(8,128)(2,1)S(1)} %finish_spectra.1.y0), channel_id=1, source_target_pairs={{0,128},{1,129},{2,130},{3,131},{4,132},{5,133},{6,134},{7,135},{8... | collective-permute-start | bytes 147464 | tf_op jit(solution)/shard_map/ppermute | solution.py:44
  12.2 6.4 %collective-permute-start.3 = (bf16[4,24,256]{2,1,0:T(8,128)(2,1)S(1)}, bf16[4,24,256]{2,1,0:T(8,128)(2,1)S(1)}, u32[]{:S(2)}, u32[]{:S(2)}) collective-permute-start(bf16[4,24,256]{2,1,0:T(8,128)(2,1)S(1)} %finish_spectra.1.y0), channel_id=1, source_target_pairs={{0,16},{1,17},{2,18},{3,19},{4,20},{5,21},{6,22},{7,23},{8,24},{9,... | collective-permute-start | bytes 147464 | tf_op jit(solution)/shard_map/ppermute | solution.py:44
  18.7 1.3 %collective-permute-start.5 = (bf16[2,2,24,256]{3,2,1,0:T(8,128)(2,1)S(1)}, bf16[2,2,24,256]{3,2,1,0:T(8,128)(2,1)S(1)}, u32[]{:S(2)}, u32[]{:S(2)}) collective-permute-start(bf16[2,2,24,256]{3,2,1,0:T(8,128)(2,1)S(1)} %get-tuple-element.20), channel_id=1, source_target_pairs={{0,8},{1,9},{2,10},{3,11},{4,12},{5,13},{6,14},{7,15},{8,0},{9,1},... | collective-permute-start | bytes 147464 | tf_op jit(solution)/shard_map/ppermute | solution.py:44
  18.8 11.3 %collective-permute-start.4 = (bf16[2,2,4,24,256]{4,3,2,1,0:T(8,128)(2,1)S(1)}, bf16[2,2,4,24,256]{4,3,2,1,0:T(8,128)(2,1)S(1)}, u32[]{:S(2)}, u32[]{:S(2)}) collective-permute-start(bf16[2,2,4,24,256]{4,3,2,1,0:T(8,128)(2,1)S(1)} %get-tuple-element.18.own), channel_id=1, source_target_pairs={{0,8},{1,9},{2,10},{3,11},{4,12},{5,13},{6,14},{7,15},{8,0},{9,1},... | collective-permute-start | bytes 589832 | tf_op jit(solution)/shard_map/ppermute | solution.py:44
  20.0 6.5 %collective-permute-start.6 = (bf16[2,2,2,24,256]{4,3,2,1,0:T(8,128)(2,1)S(1)}, bf16[2,2,2,24,256]{4,3,2,1,0:T(8,128)(2,1)S(1)}, u32[]{:S(2)}, u32[]{:S(2)}) collective-permute-start(bf16[2,2,2,24,256]{4,3,2,1,0:T(8,128)(2,1)S(1)} %join_core.1.own), channel_id=1, source_target_pairs={{0,4},{1,5},{2,6},{3,7},{4,0},{5,1},{6,2},{7,3},{8,12},{9,13},{10,... | collective-permute-start | bytes 294920 | tf_op jit(solution)/shard_map/ppermute | solution.py:44
  26.5 5.8 %collective-permute-start.8 = (bf16[2,2,2,24,256]{4,3,2,1,0:T(8,128)(2,1)S(1)}, bf16[2,2,2,24,256]{4,3,2,1,0:T(8,128)(2,1)S(1)}, u32[]{:S(2)}, u32[]{:S(2)}) collective-permute-start(bf16[2,2,2,24,256]{4,3,2,1,0:T(8,128)(2,1)S(1)} %choose.1.refs_1_), channel_id=1, source_target_pairs={{0,1},{1,0},{2,3},{3,2},{4,5},{5,4},{6,7},{7,6},{8,9},{9,8},{10,11... | collective-permute-start | bytes 294920 | tf_op jit(solution)/shard_map/ppermute | solution.py:44
  27.2 5.7 %collective-permute-start.9 = (bf16[2,2,2,24,256]{4,3,2,1,0:T(8,128)(2,1)S(1)}, bf16[2,2,2,24,256]{4,3,2,1,0:T(8,128)(2,1)S(1)}, u32[]{:S(2)}, u32[]{:S(2)}) collective-permute-start(bf16[2,2,2,24,256]{4,3,2,1,0:T(8,128)(2,1)S(1)} %choose.1.refs_1_), channel_id=1, source_target_pairs={{0,2},{1,3},{2,0},{3,1},{4,6},{5,7},{6,4},{7,5},{8,10},{9,11},{10,... | collective-permute-start | bytes 294920 | tf_op jit(solution)/shard_map/ppermute | solution.py:44
  28.4 5.5 %collective-permute-start.7 = (bf16[2,2,2,24,256]{4,3,2,1,0:T(8,128)(2,1)S(1)}, bf16[2,2,2,24,256]{4,3,2,1,0:T(8,128)(2,1)S(1)}, u32[]{:S(2)}, u32[]{:S(2)}) collective-permute-start(bf16[2,2,2,24,256]{4,3,2,1,0:T(8,128)(2,1)S(1)} %choose.1.refs_1_), channel_id=1, source_target_pairs={{0,3},{1,2},{2,1},{3,0},{4,7},{5,6},{6,5},{7,4},{8,11},{9,10},{10,... | collective-permute-start | bytes 294920 | tf_op jit(solution)/shard_map/ppermute | solution.py:44
  34.5 8.0 %collective-permute-start.10 = (bf16[144,128]{1,0:T(8,128)(2,1)S(1)}, bf16[144,128]{1,0:T(8,128)(2,1)S(1)}, u32[]{:S(2)}, u32[]{:S(2)}) collective-permute-start(bf16[144,128]{1,0:T(8,128)(2,1)S(1)} %get-tuple-element.27), channel_id=1, source_target_pairs={{0,64},{1,65},{2,66},{3,67},{4,68},{5,69},{6,70},{7,71},{8,72},{9,... | collective-permute-start | bytes 110600 | tf_op jit(solution)/shard_map/ppermute | solution.py:44
  38.0 6.1 %collective-permute-start.11 = (bf16[144,128]{1,0:T(8,128)(2,1)S(1)}, bf16[144,128]{1,0:T(8,128)(2,1)S(1)}, u32[]{:S(2)}, u32[]{:S(2)}) collective-permute-start(bf16[144,128]{1,0:T(8,128)(2,1)S(1)} %get-tuple-element.28), channel_id=1, source_target_pairs={{0,96},{1,97},{2,98},{3,99},{4,100},{5,101},{6,102},{7,103},{8,104... | collective-permute-start | bytes 110600 | tf_op jit(solution)/shard_map/ppermute | solution.py:44
  38.8 5.3 %collective-permute-start.12 = (bf16[144,128]{1,0:T(8,128)(2,1)S(1)}, bf16[144,128]{1,0:T(8,128)(2,1)S(1)}, u32[]{:S(2)}, u32[]{:S(2)}) collective-permute-start(bf16[144,128]{1,0:T(8,128)(2,1)S(1)} %get-tuple-element.29), channel_id=1, source_target_pairs={{0,32},{1,33},{2,34},{3,35},{4,36},{5,37},{6,38},{7,39},{8,40},{9,... | collective-permute-start | bytes 110600 | tf_op jit(solution)/shard_map/ppermute | solution.py:44

commit v16 on v15

--- a/solution.py
+++ b/solution.py
@@ -239,7 +239,7 @@
     out[:, lanes:] = jnp.concatenate(pieces, axis=0).astype(out.dtype)
 
 
-def sum_kernel(r2, r3, r1, p0, out):
+def sum_kernel(r2, r1, r3, p0, out):
     shares = r1[...].astype(jnp.float32) + r2[...].astype(jnp.float32) + r3[...].astype(jnp.float32)
     rows = shares.shape[0]
     lanes = out.shape[1]
@@ -355,7 +355,7 @@
         [pltpu.VMEM((QUARTERS,) + share.shape, f32), pltpu.VMEM((QUARTERS,) + wire.shape, bf16)],
     )(right, qs[3], *early)
     r1, r2, r3 = [send(p, lambda yh, u, k, xh, v, n=n: (yh, u ^ n, k, xh, v)) for n, p in ((1, p1), (2, p2), (3, p3))]
-    sums = local(sum_kernel, "sum", share, vmem(4))(r2, r3, r1, p0)
+    sums = local(sum_kernel, "sum", share, vmem(4))(r2, r1, r3, p0)
     return sums.reshape(2, NF, count, receivers).transpose(0, 1, 3, 2)
 
 

time: 45.3 us -> 46.2 us (1.020)
  waiting for transfers between devices: 21.6 us -> 22.9 us
    ppermute x13, waiting for transfers between devices: 21.6 us -> 22.9 us  [send(): return lax.ppermute(block, ('shot', 'rcv'), route)]
  transfers between devices with their start and end apart: 13 -> 13, of which waited for: 9 -> 10; matrix products, arithmetic and copies ran while one was open for 0% -> 0% of each run, Pallas kernels for 7% -> 7%
where the time goes in v16:
time: 46.2 us; the launch traced here: 46.1 us
  waiting for transfers between devices  22.9 us (50%)
  starting transfers between devices  16.5 us (36%)
  Pallas kernels  6.49 us (14%)
    ppermute x13, waiting for transfers between devices, send(): return lax.ppermute(block, ('shot', 'rcv'), route)  22.9 us
    ppermute x13, starting transfers between devices, send(): return lax.ppermute(block, ('shot', 'rcv'), route)  16.5 us
    pallas_call x3, Pallas kernels, per_device(): local(lambda *refs: gram_kernel(scale, *refs), 'gram', (share, wire), vme...  1.81 us
    pallas_call x1, Pallas kernels, per_device(): local(tail_kernel, 'tail_spectra', shape((late_rows + LATE, receivers), b...  1.43 us
    pallas_call x1, Pallas kernels, per_device(): local(own_kernel, 'own_spectra', shape((lanes - late_rows, receivers), f3...  1.24 us
  transfers between devices with their start and end apart: 13, of which 10 were waited for; matrix products, arithmetic and copies ran while one was open for 0% of the time, Pallas kernels for 7%

profile of v16, /device:TPU:4, one launch (start us, length us, event | category | flops | bytes accessed | tf_op | source)
XLA Modules:
  0.0 46.1 jit_solution(11052672630991727004)
XLA Ops:
  0.0 0.0 copy-start.1
  0.0 0.0 copy-start
  0.0 0.0 copy-start.2
  0.0 1.4 %tail_spectra.1 = bf16[72,96]{1,0:T(8,128)(2,1)S(1)} custom-call(s32[32]{0:T(128)} %fire_hbm.1, f32[8,2048]{1,0:T(8,128)} %constant.2.clone.table.table_hbm, bf16[96,8192]{1,0:T(8,128)(2,1)} %head.1), custom_call_target="tpu_custom_call" | custom-call | tf_op jit(solution)/shard_map/tail_spectra/pallas_call | solution.py:276
  1.5 0.1 collective-permute-start
  1.5 0.0 copy-done.1
  1.6 0.0 copy-done
  1.6 0.0 copy-done.2
  1.6 1.2 %own_spectra.1.total = f32[192,96]{1,0:T(8,128)S(1)} custom-call(s32[32]{0:T(128)S(1)} %copy-done.2, f32[8,2048]{1,0:T(8,128)S(1)} %copy-done.1, bf16[96,8192]{1,0:T(8,128)(2,1)S(1)} %copy-done), custom_call_target="tpu_custom_call" | custom-call | tf_op jit(solution)/shard_map/own_spectra/pallas_call | solution.py:296
  2.8 8.1 %collective-permute-done.message = bf16[72,96]{1,0:T(8,128)(2,1)S(1)} collective-permute-done((bf16[72,96]{1,0:T(8,128)(2,1)S(1)}, bf16[72,96]{1,0:T(8,128)(2,1)S(1)}, u32[]{:S(2)}, u32[]{:S(2)}) %collective-permute-start) | collective-permute-done | bytes 13856 | tf_op jit(solution)/shard_map/ppermute | solution.py:44
  11.0 0.5 %finish_spectra.1.y0 = bf16[4,24,256]{2,1,0:T(8,128)(2,1)S(1)} custom-call(f32[192,96]{1,0:T(8,128)S(1)} %own_spectra.1.total, bf16[96,8192]{1,0:T(8,128)(2,1)S(1)} %copy-done, f32[8,2048]{1,0:T(8,128)S(1)} %copy-done.1, bf16[72,96]{1,0:T(8,128)(2,1)S(1)} %collective-permute-done.message), custom_call_target="tpu_custom_call" | custom-call | tf_op jit(solution)/shard_map/finish_spectra/pallas_call | solution.py:303
  11.5 0.1 collective-permute-start.1
  11.6 0.7 %collective-permute-start.2 = (bf16[4,24,256]{2,1,0:T(8,128)(2,1)S(1)}, bf16[4,24,256]{2,1,0:T(8,128)(2,1)S(1)}, u32[]{:S(2)}, u32[]{:S(2)}) collective-permute-start(bf16[4,24,256]{2,1,0:T(8,128)(2,1)S(1)} %finish_spectra.1.y0), channel_id=1, source_target_pairs={{0,128},{1,129},{2,130},{3,131},{4,132},{5,133},{6,134},{7,135},{8... | collective-permute-start | bytes 147464 | tf_op jit(solution)/shard_map/ppermute | solution.py:44
  12.2 4.3 %collective-permute-start.3 = (bf16[4,24,256]{2,1,0:T(8,128)(2,1)S(1)}, bf16[4,24,256]{2,1,0:T(8,128)(2,1)S(1)}, u32[]{:S(2)}, u32[]{:S(2)}) collective-permute-start(bf16[4,24,256]{2,1,0:T(8,128)(2,1)S(1)} %finish_spectra.1.y0), channel_id=1, source_target_pairs={{0,16},{1,17},{2,18},{3,19},{4,20},{5,21},{6,22},{7,23},{8,24},{9,... | collective-permute-start | bytes 147464 | tf_op jit(solution)/shard_map/ppermute | solution.py:44
  16.6 1.5 %collective-permute-done.1.y3 = bf16[4,24,256]{2,1,0:T(8,128)(2,1)S(1)} collective-permute-done((bf16[4,24,256]{2,1,0:T(8,128)(2,1)S(1)}, bf16[4,24,256]{2,1,0:T(8,128)(2,1)S(1)}, u32[]{:S(2)}, u32[]{:S(2)}) %collective-permute-start.1) | collective-permute-done | bytes 49184 | tf_op jit(solution)/shard_map/ppermute | solution.py:44
  18.1 0.0 collective-permute-done.2.y2
  18.1 0.6 %collective-permute-done.3.y1 = bf16[4,24,256]{2,1,0:T(8,128)(2,1)S(1)} collective-permute-done((bf16[4,24,256]{2,1,0:T(8,128)(2,1)S(1)}, bf16[4,24,256]{2,1,0:T(8,128)(2,1)S(1)}, u32[]{:S(2)}, u32[]{:S(2)}) %collective-permute-start.3) | collective-permute-done | bytes 49184 | tf_op jit(solution)/shard_map/ppermute | solution.py:44
  18.7 0.1 collective-permute-start.5
  18.8 0.5 %collective-permute-start.4 = (bf16[2,2,4,24,256]{4,3,2,1,0:T(8,128)(2,1)S(1)}, bf16[2,2,4,24,256]{4,3,2,1,0:T(8,128)(2,1)S(1)}, u32[]{:S(2)}, u32[]{:S(2)}) collective-permute-start(bf16[2,2,4,24,256]{4,3,2,1,0:T(8,128)(2,1)S(1)} %get-tuple-element.18.own), channel_id=1, source_target_pairs={{0,8},{1,9},{2,10},{3,11},{4,12},{5,13},{6,14},{7,15},{8,0},{9,1},... | collective-permute-start | bytes 589832 | tf_op jit(solution)/shard_map/ppermute | solution.py:44
  19.3 0.7 %collective-permute-done.5.other = bf16[2,2,24,256]{3,2,1,0:T(8,128)(2,1)S(1)} collective-permute-done((bf16[2,2,24,256]{3,2,1,0:T(8,128)(2,1)S(1)}, bf16[2,2,24,256]{3,2,1,0:T(8,128)(2,1)S(1)}, u32[]{:S(2)}, u32[]{:S(2)}) %collective-permute-start.5) | collective-permute-done | bytes 49184 | tf_op jit(solution)/shard_map/ppermute | solution.py:44
  20.0 0.6 %collective-permute-start.6 = (bf16[2,2,2,24,256]{4,3,2,1,0:T(8,128)(2,1)S(1)}, bf16[2,2,2,24,256]{4,3,2,1,0:T(8,128)(2,1)S(1)}, u32[]{:S(2)}, u32[]{:S(2)}) collective-permute-start(bf16[2,2,2,24,256]{4,3,2,1,0:T(8,128)(2,1)S(1)} %join_core.1.own), channel_id=1, source_target_pairs={{0,4},{1,5},{2,6},{3,7},{4,0},{5,1},{6,2},{7,3},{8,12},{9,13},{10,... | collective-permute-start | bytes 294920 | tf_op jit(solution)/shard_map/ppermute | solution.py:44
  20.6 5.9 %collective-permute-done.6.cross = bf16[2,2,2,24,256]{4,3,2,1,0:T(8,128)(2,1)S(1)} collective-permute-done((bf16[2,2,2,24,256]{4,3,2,1,0:T(8,128)(2,1)S(1)}, bf16[2,2,2,24,256]{4,3,2,1,0:T(8,128)(2,1)S(1)}, u32[]{:S(2)}, u32[]{:S(2)}) %collective-permute-start.6) | collective-permute-done | bytes 98336 | tf_op jit(solution)/shard_map/ppermute | solution.py:44
  26.5 0.7 %collective-permute-start.8 = (bf16[2,2,2,24,256]{4,3,2,1,0:T(8,128)(2,1)S(1)}, bf16[2,2,2,24,256]{4,3,2,1,0:T(8,128)(2,1)S(1)}, u32[]{:S(2)}, u32[]{:S(2)}) collective-permute-start(bf16[2,2,2,24,256]{4,3,2,1,0:T(8,128)(2,1)S(1)} %choose.1.refs_1_), channel_id=1, source_target_pairs={{0,1},{1,0},{2,3},{3,2},{4,5},{5,4},{6,7},{7,6},{8,9},{9,8},{10,11... | collective-permute-start | bytes 294920 | tf_op jit(solution)/shard_map/ppermute | solution.py:44
  27.2 1.2 %collective-permute-start.9 = (bf16[2,2,2,24,256]{4,3,2,1,0:T(8,128)(2,1)S(1)}, bf16[2,2,2,24,256]{4,3,2,1,0:T(8,128)(2,1)S(1)}, u32[]{:S(2)}, u32[]{:S(2)}) collective-permute-start(bf16[2,2,2,24,256]{4,3,2,1,0:T(8,128)(2,1)S(1)} %choose.1.refs_1_), channel_id=1, source_target_pairs={{0,2},{1,3},{2,0},{3,1},{4,6},{5,7},{6,4},{7,5},{8,10},{9,11},{10,... | collective-permute-start | bytes 294920 | tf_op jit(solution)/shard_map/ppermute | solution.py:44
  28.4 1.7 %collective-permute-start.7 = (bf16[2,2,2,24,256]{4,3,2,1,0:T(8,128)(2,1)S(1)}, bf16[2,2,2,24,256]{4,3,2,1,0:T(8,128)(2,1)S(1)}, u32[]{:S(2)}, u32[]{:S(2)}) collective-permute-start(bf16[2,2,2,24,256]{4,3,2,1,0:T(8,128)(2,1)S(1)} %choose.1.refs_1_), channel_id=1, source_target_pairs={{0,3},{1,2},{2,1},{3,0},{4,7},{5,6},{6,5},{7,4},{8,11},{9,10},{10,... | collective-permute-start | bytes 294920 | tf_op jit(solution)/shard_map/ppermute | solution.py:44
  30.0 0.0 collective-permute-done.4.other
  30.0 0.1 right_side.1.refs_0_.refs_2_
  30.1 0.6 %gram.3 = (f32[192,96]{1,0:T(8,128)S(1)}, bf16[144,128]{1,0:T(8,128)(2,1)S(1)}) custom-call(bf16[8,192,256]{2,1,0:T(8,128)(2,1)S(1)} %right_side.1.refs_0_.refs_2_, bf16[2,2,2,24,256]{4,3,2,1,0:T(8,128)(2,1)S(1)} %choose.1.refs_1_, bf16[8,192,256]{2,1,0:T(8,128)(2,1)S(1)} %right_side.1.refs_0_.refs_2_), custom_call_target="tpu_custom_call" | custom-call | tf_op jit(solution)/shard_map/gram/pallas_call | solution.py:344
  30.7 1.5 %collective-permute-done.8.refs_1_ = bf16[2,2,2,24,256]{4,3,2,1,0:T(8,128)(2,1)S(1)} collective-permute-done((bf16[2,2,2,24,256]{4,3,2,1,0:T(8,128)(2,1)S(1)}, bf16[2,2,2,24,256]{4,3,2,1,0:T(8,128)(2,1)S(1)}, u32[]{:S(2)}, u32[]{:S(2)}) %collective-permute-start.8) | collective-permute-done | bytes 98336 | tf_op jit(solution)/shard_map/ppermute | solution.py:44
  32.2 0.6 %gram.4 = (f32[192,96]{1,0:T(8,128)S(1)}, bf16[144,128]{1,0:T(8,128)(2,1)S(1)}) custom-call(bf16[8,192,256]{2,1,0:T(8,128)(2,1)S(1)} %right_side.1.refs_0_.refs_2_, bf16[2,2,2,24,256]{4,3,2,1,0:T(8,128)(2,1)S(1)} %collective-permute-done.8.refs_1_, f32[192,96]{1,0:T(8,128)S(1)} %get-tuple-element.21.refs_2_), custom_call_target="tpu_custom_call" | custom-call | tf_op jit(solution)/shard_map/gram/pallas_call | solution.py:344
  32.8 0.0 collective-permute-done.9.refs_1_
  32.8 0.6 %gram.5 = (f32[192,96]{1,0:T(8,128)S(1)}, bf16[144,128]{1,0:T(8,128)(2,1)S(1)}) custom-call(bf16[8,192,256]{2,1,0:T(8,128)(2,1)S(1)} %right_side.1.refs_0_.refs_2_, bf16[2,2,2,24,256]{4,3,2,1,0:T(8,128)(2,1)S(1)} %collective-permute-done.9.refs_1_, f32[192,96]{1,0:T(8,128)S(1)} %get-tuple-element.23.refs_2_.refs_4_), custom_call_target="tpu_custom_call" | custom-call | tf_op jit(solution)/shard_map/gram/pallas_call | solution.py:344
  33.4 0.4 collective-permute-done.7.refs_1_
  33.9 0.6 %last_gram.1 = (f32[192,96]{1,0:T(8,128)S(1)}, bf16[144,128]{1,0:T(8,128)(2,1)S(1)}, bf16[144,128]{1,0:T(8,128)(2,1)S(1)}, bf16[144,128]{1,0:T(8,128)(2,1)S(1)}) custom-call(bf16[8,192,256]{2,1,0:T(8,128)(2,1)S(1)} %right_side.1.refs_0_.refs_2_, bf16[2,2,2,24,256]{4,3,2,1,0:T(8,128)(2,1)S(1)} %collective-permute-done.7.refs_1_, ...), custom_call_target="tpu_custom_call" | custom-call | tf_op jit(solution)/shard_map/last_gram/pallas_call | solution.py:350
  34.5 3.5 %collective-permute-start.10 = (bf16[144,128]{1,0:T(8,128)(2,1)S(1)}, bf16[144,128]{1,0:T(8,128)(2,1)S(1)}, u32[]{:S(2)}, u32[]{:S(2)}) collective-permute-start(bf16[144,128]{1,0:T(8,128)(2,1)S(1)} %get-tuple-element.27), channel_id=1, source_target_pairs={{0,64},{1,65},{2,66},{3,67},{4,68},{5,69},{6,70},{7,71},{8,72},{9,... | collective-permute-start | bytes 110600 | tf_op jit(solution)/shard_map/ppermute | solution.py:44
  38.0 1.3 %collective-permute-start.11 = (bf16[144,128]{1,0:T(8,128)(2,1)S(1)}, bf16[144,128]{1,0:T(8,128)(2,1)S(1)}, u32[]{:S(2)}, u32[]{:S(2)}) collective-permute-start(bf16[144,128]{1,0:T(8,128)(2,1)S(1)} %get-tuple-element.28), channel_id=1, source_target_pairs={{0,32},{1,33},{2,34},{3,35},{4,36},{5,37},{6,38},{7,39},{8,40},{9,... | collective-permute-start | bytes 110600 | tf_op jit(solution)/shard_map/ppermute | solution.py:44
  39.2 1.8 %collective-permute-start.12 = (bf16[144,128]{1,0:T(8,128)(2,1)S(1)}, bf16[144,128]{1,0:T(8,128)(2,1)S(1)}, u32[]{:S(2)}, u32[]{:S(2)}) collective-permute-start(bf16[144,128]{1,0:T(8,128)(2,1)S(1)} %get-tuple-element.29), channel_id=1, source_target_pairs={{0,96},{1,97},{2,98},{3,99},{4,100},{5,101},{6,102},{7,103},{8,104... | collective-permute-start | bytes 110600 | tf_op jit(solution)/shard_map/ppermute | solution.py:44
  41.1 1.4 %collective-permute-done.10.r2 = bf16[144,128]{1,0:T(8,128)(2,1)S(1)} collective-permute-done((bf16[144,128]{1,0:T(8,128)(2,1)S(1)}, bf16[144,128]{1,0:T(8,128)(2,1)S(1)}, u32[]{:S(2)}, u32[]{:S(2)}) %collective-permute-start.10) | collective-permute-done | bytes 36896 | tf_op jit(solution)/shard_map/ppermute | solution.py:44
  42.5 0.4 collective-permute-done.11.r1
  42.8 2.5 %collective-permute-done.12.r3 = bf16[144,128]{1,0:T(8,128)(2,1)S(1)} collective-permute-done((bf16[144,128]{1,0:T(8,128)(2,1)S(1)}, bf16[144,128]{1,0:T(8,128)(2,1)S(1)}, u32[]{:S(2)}, u32[]{:S(2)}) %collective-permute-start.12) | collective-permute-done | bytes 36896 | tf_op jit(solution)/shard_map/ppermute | solution.py:44
  45.3 0.7 %sum.1 = f32[192,96]{1,0:T(8,128)} custom-call(bf16[144,128]{1,0:T(8,128)(2,1)S(1)} %collective-permute-done.10.r2, bf16[144,128]{1,0:T(8,128)(2,1)S(1)} %collective-permute-done.11.r1, bf16[144,128]{1,0:T(8,128)(2,1)S(1)} %collective-permute-done.12.r3, f32[192,96]{1,0:T(8,128)S(1)} %get-tuple-element.30.p0), custom_call_target="tpu_custom_call" | custom-call | tf_op jit(solution)/shard_map/sum/pallas_call | solution.py:358
  (3 shorter events, 0.0 us)
Async XLA Ops:
  0.0 1.5 %copy-start.1 = (f32[8,2048]{1,0:T(8,128)S(1)}, f32[8,2048]{1,0:T(8,128)}, u32[]{:S(2)}) copy-start(f32[8,2048]{1,0:T(8,128)} %constant.2.clone.table.table_hbm) | copy-start | bytes 196612
  0.0 1.6 %copy-start = (bf16[96,8192]{1,0:T(8,128)(2,1)S(1)}, bf16[96,8192]{1,0:T(8,128)(2,1)}, u32[]{:S(2)}) copy-start(bf16[96,8192]{1,0:T(8,128)(2,1)} %head.1) | copy-start | bytes 4718596
  0.0 1.6 %copy-start.2 = (s32[32]{0:T(128)S(1)}, s32[32]{0:T(128)}, u32[]{:S(2)}) copy-start(s32[32]{0:T(128)} %fire_hbm.1) | copy-start | bytes 388
  1.5 9.5 %collective-permute-start = (bf16[72,96]{1,0:T(8,128)(2,1)S(1)}, bf16[72,96]{1,0:T(8,128)(2,1)S(1)}, u32[]{:S(2)}, u32[]{:S(2)}) collective-permute-start(bf16[72,96]{1,0:T(8,128)(2,1)S(1)} %tail_spectra.1), channel_id=1, source_target_pairs={{0,8},{1,9},{2,10},{3,11},{4,12},{5,13},{6,14},{7,15},{8,16},{9,17... | collective-permute-start | bytes 41480 | tf_op jit(solution)/shard_map/ppermute | solution.py:44
  11.5 6.6 %collective-permute-start.1 = (bf16[4,24,256]{2,1,0:T(8,128)(2,1)S(1)}, bf16[4,24,256]{2,1,0:T(8,128)(2,1)S(1)}, u32[]{:S(2)}, u32[]{:S(2)}) collective-permute-start(bf16[4,24,256]{2,1,0:T(8,128)(2,1)S(1)} %finish_spectra.1.y0), channel_id=1, source_target_pairs={{0,144},{1,145},{2,146},{3,147},{4,148},{5,149},{6,150},{7,151},{8... | collective-permute-start | bytes 147464 | tf_op jit(solution)/shard_map/ppermute | solution.py:44
  11.6 6.5 %collective-permute-start.2 = (bf16[4,24,256]{2,1,0:T(8,128)(2,1)S(1)}, bf16[4,24,256]{2,1,0:T(8,128)(2,1)S(1)}, u32[]{:S(2)}, u32[]{:S(2)}) collective-permute-start(bf16[4,24,256]{2,1,0:T(8,128)(2,1)S(1)} %finish_spectra.1.y0), channel_id=1, source_target_pairs={{0,128},{1,129},{2,130},{3,131},{4,132},{5,133},{6,134},{7,135},{8... | collective-permute-start | bytes 147464 | tf_op jit(solution)/shard_map/ppermute | solution.py:44
  12.2 6.4 %collective-permute-start.3 = (bf16[4,24,256]{2,1,0:T(8,128)(2,1)S(1)}, bf16[4,24,256]{2,1,0:T(8,128)(2,1)S(1)}, u32[]{:S(2)}, u32[]{:S(2)}) collective-permute-start(bf16[4,24,256]{2,1,0:T(8,128)(2,1)S(1)} %finish_spectra.1.y0), channel_id=1, source_target_pairs={{0,16},{1,17},{2,18},{3,19},{4,20},{5,21},{6,22},{7,23},{8,24},{9,... | collective-permute-start | bytes 147464 | tf_op jit(solution)/shard_map/ppermute | solution.py:44
  18.7 1.3 %collective-permute-start.5 = (bf16[2,2,24,256]{3,2,1,0:T(8,128)(2,1)S(1)}, bf16[2,2,24,256]{3,2,1,0:T(8,128)(2,1)S(1)}, u32[]{:S(2)}, u32[]{:S(2)}) collective-permute-start(bf16[2,2,24,256]{3,2,1,0:T(8,128)(2,1)S(1)} %get-tuple-element.20), channel_id=1, source_target_pairs={{0,8},{1,9},{2,10},{3,11},{4,12},{5,13},{6,14},{7,15},{8,0},{9,1},... | collective-permute-start | bytes 147464 | tf_op jit(solution)/shard_map/ppermute | solution.py:44
  18.8 11.3 %collective-permute-start.4 = (bf16[2,2,4,24,256]{4,3,2,1,0:T(8,128)(2,1)S(1)}, bf16[2,2,4,24,256]{4,3,2,1,0:T(8,128)(2,1)S(1)}, u32[]{:S(2)}, u32[]{:S(2)}) collective-permute-start(bf16[2,2,4,24,256]{4,3,2,1,0:T(8,128)(2,1)S(1)} %get-tuple-element.18.own), channel_id=1, source_target_pairs={{0,8},{1,9},{2,10},{3,11},{4,12},{5,13},{6,14},{7,15},{8,0},{9,1},... | collective-permute-start | bytes 589832 | tf_op jit(solution)/shard_map/ppermute | solution.py:44
  20.0 6.5 %collective-permute-start.6 = (bf16[2,2,2,24,256]{4,3,2,1,0:T(8,128)(2,1)S(1)}, bf16[2,2,2,24,256]{4,3,2,1,0:T(8,128)(2,1)S(1)}, u32[]{:S(2)}, u32[]{:S(2)}) collective-permute-start(bf16[2,2,2,24,256]{4,3,2,1,0:T(8,128)(2,1)S(1)} %join_core.1.own), channel_id=1, source_target_pairs={{0,4},{1,5},{2,6},{3,7},{4,0},{5,1},{6,2},{7,3},{8,12},{9,13},{10,... | collective-permute-start | bytes 294920 | tf_op jit(solution)/shard_map/ppermute | solution.py:44
  26.5 5.8 %collective-permute-start.8 = (bf16[2,2,2,24,256]{4,3,2,1,0:T(8,128)(2,1)S(1)}, bf16[2,2,2,24,256]{4,3,2,1,0:T(8,128)(2,1)S(1)}, u32[]{:S(2)}, u32[]{:S(2)}) collective-permute-start(bf16[2,2,2,24,256]{4,3,2,1,0:T(8,128)(2,1)S(1)} %choose.1.refs_1_), channel_id=1, source_target_pairs={{0,1},{1,0},{2,3},{3,2},{4,5},{5,4},{6,7},{7,6},{8,9},{9,8},{10,11... | collective-permute-start | bytes 294920 | tf_op jit(solution)/shard_map/ppermute | solution.py:44
  27.2 5.7 %collective-permute-start.9 = (bf16[2,2,2,24,256]{4,3,2,1,0:T(8,128)(2,1)S(1)}, bf16[2,2,2,24,256]{4,3,2,1,0:T(8,128)(2,1)S(1)}, u32[]{:S(2)}, u32[]{:S(2)}) collective-permute-start(bf16[2,2,2,24,256]{4,3,2,1,0:T(8,128)(2,1)S(1)} %choose.1.refs_1_), channel_id=1, source_target_pairs={{0,2},{1,3},{2,0},{3,1},{4,6},{5,7},{6,4},{7,5},{8,10},{9,11},{10,... | collective-permute-start | bytes 294920 | tf_op jit(solution)/shard_map/ppermute | solution.py:44
  28.4 5.5 %collective-permute-start.7 = (bf16[2,2,2,24,256]{4,3,2,1,0:T(8,128)(2,1)S(1)}, bf16[2,2,2,24,256]{4,3,2,1,0:T(8,128)(2,1)S(1)}, u32[]{:S(2)}, u32[]{:S(2)}) collective-permute-start(bf16[2,2,2,24,256]{4,3,2,1,0:T(8,128)(2,1)S(1)} %choose.1.refs_1_), channel_id=1, source_target_pairs={{0,3},{1,2},{2,1},{3,0},{4,7},{5,6},{6,5},{7,4},{8,11},{9,10},{10,... | collective-permute-start | bytes 294920 | tf_op jit(solution)/shard_map/ppermute | solution.py:44
  34.5 8.0 %collective-permute-start.10 = (bf16[144,128]{1,0:T(8,128)(2,1)S(1)}, bf16[144,128]{1,0:T(8,128)(2,1)S(1)}, u32[]{:S(2)}, u32[]{:S(2)}) collective-permute-start(bf16[144,128]{1,0:T(8,128)(2,1)S(1)} %get-tuple-element.27), channel_id=1, source_target_pairs={{0,64},{1,65},{2,66},{3,67},{4,68},{5,69},{6,70},{7,71},{8,72},{9,... | collective-permute-start | bytes 110600 | tf_op jit(solution)/shard_map/ppermute | solution.py:44
  38.0 4.9 %collective-permute-start.11 = (bf16[144,128]{1,0:T(8,128)(2,1)S(1)}, bf16[144,128]{1,0:T(8,128)(2,1)S(1)}, u32[]{:S(2)}, u32[]{:S(2)}) collective-permute-start(bf16[144,128]{1,0:T(8,128)(2,1)S(1)} %get-tuple-element.28), channel_id=1, source_target_pairs={{0,32},{1,33},{2,34},{3,35},{4,36},{5,37},{6,38},{7,39},{8,40},{9,... | collective-permute-start | bytes 110600 | tf_op jit(solution)/shard_map/ppermute | solution.py:44
  39.2 6.1 %collective-permute-start.12 = (bf16[144,128]{1,0:T(8,128)(2,1)S(1)}, bf16[144,128]{1,0:T(8,128)(2,1)S(1)}, u32[]{:S(2)}, u32[]{:S(2)}) collective-permute-start(bf16[144,128]{1,0:T(8,128)(2,1)S(1)} %get-tuple-element.29), channel_id=1, source_target_pairs={{0,96},{1,97},{2,98},{3,99},{4,100},{5,101},{6,102},{7,103},{8,104... | collective-permute-start | bytes 110600 | tf_op jit(solution)/shard_map/ppermute | solution.py:44

commit v17 on v16

--- a/solution.py
+++ b/solution.py
@@ -239,7 +239,7 @@
     out[:, lanes:] = jnp.concatenate(pieces, axis=0).astype(out.dtype)
 
 
-def sum_kernel(r2, r1, r3, p0, out):
+def sum_kernel(r3, r2, r1, p0, out):
     shares = r1[...].astype(jnp.float32) + r2[...].astype(jnp.float32) + r3[...].astype(jnp.float32)
     rows = shares.shape[0]
     lanes = out.shape[1]
@@ -355,7 +355,7 @@
         [pltpu.VMEM((QUARTERS,) + share.shape, f32), pltpu.VMEM((QUARTERS,) + wire.shape, bf16)],
     )(right, qs[3], *early)
     r1, r2, r3 = [send(p, lambda yh, u, k, xh, v, n=n: (yh, u ^ n, k, xh, v)) for n, p in ((1, p1), (2, p2), (3, p3))]
-    sums = local(sum_kernel, "sum", share, vmem(4))(r2, r1, r3, p0)
+    sums = local(sum_kernel, "sum", share, vmem(4))(r3, r2, r1, p0)
     return sums.reshape(2, NF, count, receivers).transpose(0, 1, 3, 2)
 
 

time: 46.2 us -> 45.8 us (level)
  waiting for transfers between devices: 22.9 us -> 22.4 us
    ppermute x13, waiting for transfers between devices: 22.9 us -> 22.4 us  [send(): return lax.ppermute(block, ('shot', 'rcv'), route)]
  transfers between devices with their start and end apart: 13 -> 13, of which waited for: 10 -> 8; matrix products, arithmetic and copies ran while one was open for 0% -> 0% of each run, Pallas kernels for 7% -> 7%
where the time goes in v17:
time: 45.8 us; the launch traced here: 45.5 us
  waiting for transfers between devices  22.4 us (49%)
  starting transfers between devices  16.5 us (36%)
  Pallas kernels  6.49 us (14%)
    ppermute x13, waiting for transfers between devices, send(): return lax.ppermute(block, ('shot', 'rcv'), route)  22.4 us
    ppermute x13, starting transfers between devices, send(): return lax.ppermute(block, ('shot', 'rcv'), route)  16.5 us
    pallas_call x3, Pallas kernels, per_device(): local(lambda *refs: gram_kernel(scale, *refs), 'gram', (share, wire), vme...  1.81 us
    pallas_call x1, Pallas kernels, per_device(): local(tail_kernel, 'tail_spectra', shape((late_rows + LATE, receivers), b...  1.43 us
    pallas_call x1, Pallas kernels, per_device(): local(own_kernel, 'own_spectra', shape((lanes - late_rows, receivers), f3...  1.24 us
  transfers between devices with their start and end apart: 13, of which 8 were waited for; matrix products, arithmetic and copies ran while one was open for 0% of the time, Pallas kernels for 7%

profile of v17, /device:TPU:4, one launch (start us, length us, event | category | flops | bytes accessed | tf_op | source)
XLA Modules:
  0.0 45.5 jit_solution(15812005202863177102)
XLA Ops:
  0.0 0.0 copy-start.1
  0.0 0.0 copy-start
  0.0 0.0 copy-start.2
  0.0 1.4 %tail_spectra.1 = bf16[72,96]{1,0:T(8,128)(2,1)S(1)} custom-call(s32[32]{0:T(128)} %fire_hbm.1, f32[8,2048]{1,0:T(8,128)} %constant.2.clone.table.table_hbm, bf16[96,8192]{1,0:T(8,128)(2,1)} %head.1), custom_call_target="tpu_custom_call" | custom-call | tf_op jit(solution)/shard_map/tail_spectra/pallas_call | solution.py:276
  1.5 0.1 collective-permute-start
  1.5 0.0 copy-done.1
  1.6 0.0 copy-done
  1.6 0.0 copy-done.2
  1.6 1.2 %own_spectra.1.total = f32[192,96]{1,0:T(8,128)S(1)} custom-call(s32[32]{0:T(128)S(1)} %copy-done.2, f32[8,2048]{1,0:T(8,128)S(1)} %copy-done.1, bf16[96,8192]{1,0:T(8,128)(2,1)S(1)} %copy-done), custom_call_target="tpu_custom_call" | custom-call | tf_op jit(solution)/shard_map/own_spectra/pallas_call | solution.py:296
  2.8 8.1 %collective-permute-done.message = bf16[72,96]{1,0:T(8,128)(2,1)S(1)} collective-permute-done((bf16[72,96]{1,0:T(8,128)(2,1)S(1)}, bf16[72,96]{1,0:T(8,128)(2,1)S(1)}, u32[]{:S(2)}, u32[]{:S(2)}) %collective-permute-start) | collective-permute-done | bytes 13856 | tf_op jit(solution)/shard_map/ppermute | solution.py:44
  11.0 0.5 %finish_spectra.1.y0 = bf16[4,24,256]{2,1,0:T(8,128)(2,1)S(1)} custom-call(f32[192,96]{1,0:T(8,128)S(1)} %own_spectra.1.total, bf16[96,8192]{1,0:T(8,128)(2,1)S(1)} %copy-done, f32[8,2048]{1,0:T(8,128)S(1)} %copy-done.1, bf16[72,96]{1,0:T(8,128)(2,1)S(1)} %collective-permute-done.message), custom_call_target="tpu_custom_call" | custom-call | tf_op jit(solution)/shard_map/finish_spectra/pallas_call | solution.py:303
  11.5 0.1 collective-permute-start.1
  11.6 0.7 %collective-permute-start.2 = (bf16[4,24,256]{2,1,0:T(8,128)(2,1)S(1)}, bf16[4,24,256]{2,1,0:T(8,128)(2,1)S(1)}, u32[]{:S(2)}, u32[]{:S(2)}) collective-permute-start(bf16[4,24,256]{2,1,0:T(8,128)(2,1)S(1)} %finish_spectra.1.y0), channel_id=1, source_target_pairs={{0,128},{1,129},{2,130},{3,131},{4,132},{5,133},{6,134},{7,135},{8... | collective-permute-start | bytes 147464 | tf_op jit(solution)/shard_map/ppermute | solution.py:44
  12.2 4.3 %collective-permute-start.3 = (bf16[4,24,256]{2,1,0:T(8,128)(2,1)S(1)}, bf16[4,24,256]{2,1,0:T(8,128)(2,1)S(1)}, u32[]{:S(2)}, u32[]{:S(2)}) collective-permute-start(bf16[4,24,256]{2,1,0:T(8,128)(2,1)S(1)} %finish_spectra.1.y0), channel_id=1, source_target_pairs={{0,16},{1,17},{2,18},{3,19},{4,20},{5,21},{6,22},{7,23},{8,24},{9,... | collective-permute-start | bytes 147464 | tf_op jit(solution)/shard_map/ppermute | solution.py:44
  16.6 1.5 %collective-permute-done.1.y3 = bf16[4,24,256]{2,1,0:T(8,128)(2,1)S(1)} collective-permute-done((bf16[4,24,256]{2,1,0:T(8,128)(2,1)S(1)}, bf16[4,24,256]{2,1,0:T(8,128)(2,1)S(1)}, u32[]{:S(2)}, u32[]{:S(2)}) %collective-permute-start.1) | collective-permute-done | bytes 49184 | tf_op jit(solution)/shard_map/ppermute | solution.py:44
  18.1 0.0 collective-permute-done.2.y2
  18.1 0.6 %collective-permute-done.3.y1 = bf16[4,24,256]{2,1,0:T(8,128)(2,1)S(1)} collective-permute-done((bf16[4,24,256]{2,1,0:T(8,128)(2,1)S(1)}, bf16[4,24,256]{2,1,0:T(8,128)(2,1)S(1)}, u32[]{:S(2)}, u32[]{:S(2)}) %collective-permute-start.3) | collective-permute-done | bytes 49184 | tf_op jit(solution)/shard_map/ppermute | solution.py:44
  18.7 0.1 collective-permute-start.5
  18.8 0.5 %collective-permute-start.4 = (bf16[2,2,4,24,256]{4,3,2,1,0:T(8,128)(2,1)S(1)}, bf16[2,2,4,24,256]{4,3,2,1,0:T(8,128)(2,1)S(1)}, u32[]{:S(2)}, u32[]{:S(2)}) collective-permute-start(bf16[2,2,4,24,256]{4,3,2,1,0:T(8,128)(2,1)S(1)} %get-tuple-element.18.own), channel_id=1, source_target_pairs={{0,8},{1,9},{2,10},{3,11},{4,12},{5,13},{6,14},{7,15},{8,0},{9,1},... | collective-permute-start | bytes 589832 | tf_op jit(solution)/shard_map/ppermute | solution.py:44
  19.3 0.7 %collective-permute-done.5.other = bf16[2,2,24,256]{3,2,1,0:T(8,128)(2,1)S(1)} collective-permute-done((bf16[2,2,24,256]{3,2,1,0:T(8,128)(2,1)S(1)}, bf16[2,2,24,256]{3,2,1,0:T(8,128)(2,1)S(1)}, u32[]{:S(2)}, u32[]{:S(2)}) %collective-permute-start.5) | collective-permute-done | bytes 49184 | tf_op jit(solution)/shard_map/ppermute | solution.py:44
  20.0 0.6 %collective-permute-start.6 = (bf16[2,2,2,24,256]{4,3,2,1,0:T(8,128)(2,1)S(1)}, bf16[2,2,2,24,256]{4,3,2,1,0:T(8,128)(2,1)S(1)}, u32[]{:S(2)}, u32[]{:S(2)}) collective-permute-start(bf16[2,2,2,24,256]{4,3,2,1,0:T(8,128)(2,1)S(1)} %join_core.1.own), channel_id=1, source_target_pairs={{0,4},{1,5},{2,6},{3,7},{4,0},{5,1},{6,2},{7,3},{8,12},{9,13},{10,... | collective-permute-start | bytes 294920 | tf_op jit(solution)/shard_map/ppermute | solution.py:44
  20.6 5.9 %collective-permute-done.6.cross = bf16[2,2,2,24,256]{4,3,2,1,0:T(8,128)(2,1)S(1)} collective-permute-done((bf16[2,2,2,24,256]{4,3,2,1,0:T(8,128)(2,1)S(1)}, bf16[2,2,2,24,256]{4,3,2,1,0:T(8,128)(2,1)S(1)}, u32[]{:S(2)}, u32[]{:S(2)}) %collective-permute-start.6) | collective-permute-done | bytes 98336 | tf_op jit(solution)/shard_map/ppermute | solution.py:44
  26.5 0.7 %collective-permute-start.8 = (bf16[2,2,2,24,256]{4,3,2,1,0:T(8,128)(2,1)S(1)}, bf16[2,2,2,24,256]{4,3,2,1,0:T(8,128)(2,1)S(1)}, u32[]{:S(2)}, u32[]{:S(2)}) collective-permute-start(bf16[2,2,2,24,256]{4,3,2,1,0:T(8,128)(2,1)S(1)} %choose.1.refs_1_), channel_id=1, source_target_pairs={{0,1},{1,0},{2,3},{3,2},{4,5},{5,4},{6,7},{7,6},{8,9},{9,8},{10,11... | collective-permute-start | bytes 294920 | tf_op jit(solution)/shard_map/ppermute | solution.py:44
  27.2 1.2 %collective-permute-start.9 = (bf16[2,2,2,24,256]{4,3,2,1,0:T(8,128)(2,1)S(1)}, bf16[2,2,2,24,256]{4,3,2,1,0:T(8,128)(2,1)S(1)}, u32[]{:S(2)}, u32[]{:S(2)}) collective-permute-start(bf16[2,2,2,24,256]{4,3,2,1,0:T(8,128)(2,1)S(1)} %choose.1.refs_1_), channel_id=1, source_target_pairs={{0,2},{1,3},{2,0},{3,1},{4,6},{5,7},{6,4},{7,5},{8,10},{9,11},{10,... | collective-permute-start | bytes 294920 | tf_op jit(solution)/shard_map/ppermute | solution.py:44
  28.4 1.7 %collective-permute-start.7 = (bf16[2,2,2,24,256]{4,3,2,1,0:T(8,128)(2,1)S(1)}, bf16[2,2,2,24,256]{4,3,2,1,0:T(8,128)(2,1)S(1)}, u32[]{:S(2)}, u32[]{:S(2)}) collective-permute-start(bf16[2,2,2,24,256]{4,3,2,1,0:T(8,128)(2,1)S(1)} %choose.1.refs_1_), channel_id=1, source_target_pairs={{0,3},{1,2},{2,1},{3,0},{4,7},{5,6},{6,5},{7,4},{8,11},{9,10},{10,... | collective-permute-start | bytes 294920 | tf_op jit(solution)/shard_map/ppermute | solution.py:44
  30.0 0.0 collective-permute-done.4.other
  30.0 0.1 right_side.1.refs_0_.refs_2_
  30.1 0.6 %gram.3 = (f32[192,96]{1,0:T(8,128)S(1)}, bf16[144,128]{1,0:T(8,128)(2,1)S(1)}) custom-call(bf16[8,192,256]{2,1,0:T(8,128)(2,1)S(1)} %right_side.1.refs_0_.refs_2_, bf16[2,2,2,24,256]{4,3,2,1,0:T(8,128)(2,1)S(1)} %choose.1.refs_1_, bf16[8,192,256]{2,1,0:T(8,128)(2,1)S(1)} %right_side.1.refs_0_.refs_2_), custom_call_target="tpu_custom_call" | custom-call | tf_op jit(solution)/shard_map/gram/pallas_call | solution.py:344
  30.7 1.5 %collective-permute-done.8.refs_1_ = bf16[2,2,2,24,256]{4,3,2,1,0:T(8,128)(2,1)S(1)} collective-permute-done((bf16[2,2,2,24,256]{4,3,2,1,0:T(8,128)(2,1)S(1)}, bf16[2,2,2,24,256]{4,3,2,1,0:T(8,128)(2,1)S(1)}, u32[]{:S(2)}, u32[]{:S(2)}) %collective-permute-start.8) | collective-permute-done | bytes 98336 | tf_op jit(solution)/shard_map/ppermute | solution.py:44
  32.2 0.6 %gram.4 = (f32[192,96]{1,0:T(8,128)S(1)}, bf16[144,128]{1,0:T(8,128)(2,1)S(1)}) custom-call(bf16[8,192,256]{2,1,0:T(8,128)(2,1)S(1)} %right_side.1.refs_0_.refs_2_, bf16[2,2,2,24,256]{4,3,2,1,0:T(8,128)(2,1)S(1)} %collective-permute-done.8.refs_1_, f32[192,96]{1,0:T(8,128)S(1)} %get-tuple-element.21.refs_2_), custom_call_target="tpu_custom_call" | custom-call | tf_op jit(solution)/shard_map/gram/pallas_call | solution.py:344
  32.8 0.0 collective-permute-done.9.refs_1_
  32.8 0.6 %gram.5 = (f32[192,96]{1,0:T(8,128)S(1)}, bf16[144,128]{1,0:T(8,128)(2,1)S(1)}) custom-call(bf16[8,192,256]{2,1,0:T(8,128)(2,1)S(1)} %right_side.1.refs_0_.refs_2_, bf16[2,2,2,24,256]{4,3,2,1,0:T(8,128)(2,1)S(1)} %collective-permute-done.9.refs_1_, f32[192,96]{1,0:T(8,128)S(1)} %get-tuple-element.23.refs_2_.refs_4_), custom_call_target="tpu_custom_call" | custom-call | tf_op jit(solution)/shard_map/gram/pallas_call | solution.py:344
  33.4 0.4 collective-permute-done.7.refs_1_
  33.9 0.6 %last_gram.1 = (f32[192,96]{1,0:T(8,128)S(1)}, bf16[144,128]{1,0:T(8,128)(2,1)S(1)}, bf16[144,128]{1,0:T(8,128)(2,1)S(1)}, bf16[144,128]{1,0:T(8,128)(2,1)S(1)}) custom-call(bf16[8,192,256]{2,1,0:T(8,128)(2,1)S(1)} %right_side.1.refs_0_.refs_2_, bf16[2,2,2,24,256]{4,3,2,1,0:T(8,128)(2,1)S(1)} %collective-permute-done.7.refs_1_, ...), custom_call_target="tpu_custom_call" | custom-call | tf_op jit(solution)/shard_map/last_gram/pallas_call | solution.py:350
  34.5 2.4 %collective-permute-start.10 = (bf16[144,128]{1,0:T(8,128)(2,1)S(1)}, bf16[144,128]{1,0:T(8,128)(2,1)S(1)}, u32[]{:S(2)}, u32[]{:S(2)}) collective-permute-start(bf16[144,128]{1,0:T(8,128)(2,1)S(1)} %get-tuple-element.27), channel_id=1, source_target_pairs={{0,96},{1,97},{2,98},{3,99},{4,100},{5,101},{6,102},{7,103},{8,104... | collective-permute-start | bytes 110600 | tf_op jit(solution)/shard_map/ppermute | solution.py:44
  36.9 1.9 %collective-permute-start.11 = (bf16[144,128]{1,0:T(8,128)(2,1)S(1)}, bf16[144,128]{1,0:T(8,128)(2,1)S(1)}, u32[]{:S(2)}, u32[]{:S(2)}) collective-permute-start(bf16[144,128]{1,0:T(8,128)(2,1)S(1)} %get-tuple-element.28), channel_id=1, source_target_pairs={{0,64},{1,65},{2,66},{3,67},{4,68},{5,69},{6,70},{7,71},{8,72},{9,... | collective-permute-start | bytes 110600 | tf_op jit(solution)/shard_map/ppermute | solution.py:44
  38.8 2.3 %collective-permute-start.12 = (bf16[144,128]{1,0:T(8,128)(2,1)S(1)}, bf16[144,128]{1,0:T(8,128)(2,1)S(1)}, u32[]{:S(2)}, u32[]{:S(2)}) collective-permute-start(bf16[144,128]{1,0:T(8,128)(2,1)S(1)} %get-tuple-element.29), channel_id=1, source_target_pairs={{0,32},{1,33},{2,34},{3,35},{4,36},{5,37},{6,38},{7,39},{8,40},{9,... | collective-permute-start | bytes 110600 | tf_op jit(solution)/shard_map/ppermute | solution.py:44
  41.1 0.0 collective-permute-done.10.r3
  41.1 3.7 %collective-permute-done.11.r2 = bf16[144,128]{1,0:T(8,128)(2,1)S(1)} collective-permute-done((bf16[144,128]{1,0:T(8,128)(2,1)S(1)}, bf16[144,128]{1,0:T(8,128)(2,1)S(1)}, u32[]{:S(2)}, u32[]{:S(2)}) %collective-permute-start.11) | collective-permute-done | bytes 36896 | tf_op jit(solution)/shard_map/ppermute | solution.py:44
  44.8 0.0 collective-permute-done.12.r1
  44.8 0.7 %sum.1 = f32[192,96]{1,0:T(8,128)} custom-call(bf16[144,128]{1,0:T(8,128)(2,1)S(1)} %collective-permute-done.10.r3, bf16[144,128]{1,0:T(8,128)(2,1)S(1)} %collective-permute-done.11.r2, bf16[144,128]{1,0:T(8,128)(2,1)S(1)} %collective-permute-done.12.r1, f32[192,96]{1,0:T(8,128)S(1)} %get-tuple-element.30.p0), custom_call_target="tpu_custom_call" | custom-call | tf_op jit(solution)/shard_map/sum/pallas_call | solution.py:358
  (3 shorter events, 0.0 us)
Async XLA Ops:
  0.0 1.5 %copy-start.1 = (f32[8,2048]{1,0:T(8,128)S(1)}, f32[8,2048]{1,0:T(8,128)}, u32[]{:S(2)}) copy-start(f32[8,2048]{1,0:T(8,128)} %constant.2.clone.table.table_hbm) | copy-start | bytes 196612
  0.0 1.6 %copy-start = (bf16[96,8192]{1,0:T(8,128)(2,1)S(1)}, bf16[96,8192]{1,0:T(8,128)(2,1)}, u32[]{:S(2)}) copy-start(bf16[96,8192]{1,0:T(8,128)(2,1)} %head.1) | copy-start | bytes 4718596
  0.0 1.6 %copy-start.2 = (s32[32]{0:T(128)S(1)}, s32[32]{0:T(128)}, u32[]{:S(2)}) copy-start(s32[32]{0:T(128)} %fire_hbm.1) | copy-start | bytes 388
  1.5 9.5 %collective-permute-start = (bf16[72,96]{1,0:T(8,128)(2,1)S(1)}, bf16[72,96]{1,0:T(8,128)(2,1)S(1)}, u32[]{:S(2)}, u32[]{:S(2)}) collective-permute-start(bf16[72,96]{1,0:T(8,128)(2,1)S(1)} %tail_spectra.1), channel_id=1, source_target_pairs={{0,8},{1,9},{2,10},{3,11},{4,12},{5,13},{6,14},{7,15},{8,16},{9,17... | collective-permute-start | bytes 41480 | tf_op jit(solution)/shard_map/ppermute | solution.py:44
  11.5 6.6 %collective-permute-start.1 = (bf16[4,24,256]{2,1,0:T(8,128)(2,1)S(1)}, bf16[4,24,256]{2,1,0:T(8,128)(2,1)S(1)}, u32[]{:S(2)}, u32[]{:S(2)}) collective-permute-start(bf16[4,24,256]{2,1,0:T(8,128)(2,1)S(1)} %finish_spectra.1.y0), channel_id=1, source_target_pairs={{0,144},{1,145},{2,146},{3,147},{4,148},{5,149},{6,150},{7,151},{8... | collective-permute-start | bytes 147464 | tf_op jit(solution)/shard_map/ppermute | solution.py:44
  11.6 6.5 %collective-permute-start.2 = (bf16[4,24,256]{2,1,0:T(8,128)(2,1)S(1)}, bf16[4,24,256]{2,1,0:T(8,128)(2,1)S(1)}, u32[]{:S(2)}, u32[]{:S(2)}) collective-permute-start(bf16[4,24,256]{2,1,0:T(8,128)(2,1)S(1)} %finish_spectra.1.y0), channel_id=1, source_target_pairs={{0,128},{1,129},{2,130},{3,131},{4,132},{5,133},{6,134},{7,135},{8... | collective-permute-start | bytes 147464 | tf_op jit(solution)/shard_map/ppermute | solution.py:44
  12.2 6.4 %collective-permute-start.3 = (bf16[4,24,256]{2,1,0:T(8,128)(2,1)S(1)}, bf16[4,24,256]{2,1,0:T(8,128)(2,1)S(1)}, u32[]{:S(2)}, u32[]{:S(2)}) collective-permute-start(bf16[4,24,256]{2,1,0:T(8,128)(2,1)S(1)} %finish_spectra.1.y0), channel_id=1, source_target_pairs={{0,16},{1,17},{2,18},{3,19},{4,20},{5,21},{6,22},{7,23},{8,24},{9,... | collective-permute-start | bytes 147464 | tf_op jit(solution)/shard_map/ppermute | solution.py:44
  18.7 1.3 %collective-permute-start.5 = (bf16[2,2,24,256]{3,2,1,0:T(8,128)(2,1)S(1)}, bf16[2,2,24,256]{3,2,1,0:T(8,128)(2,1)S(1)}, u32[]{:S(2)}, u32[]{:S(2)}) collective-permute-start(bf16[2,2,24,256]{3,2,1,0:T(8,128)(2,1)S(1)} %get-tuple-element.20), channel_id=1, source_target_pairs={{0,8},{1,9},{2,10},{3,11},{4,12},{5,13},{6,14},{7,15},{8,0},{9,1},... | collective-permute-start | bytes 147464 | tf_op jit(solution)/shard_map/ppermute | solution.py:44
  18.8 11.3 %collective-permute-start.4 = (bf16[2,2,4,24,256]{4,3,2,1,0:T(8,128)(2,1)S(1)}, bf16[2,2,4,24,256]{4,3,2,1,0:T(8,128)(2,1)S(1)}, u32[]{:S(2)}, u32[]{:S(2)}) collective-permute-start(bf16[2,2,4,24,256]{4,3,2,1,0:T(8,128)(2,1)S(1)} %get-tuple-element.18.own), channel_id=1, source_target_pairs={{0,8},{1,9},{2,10},{3,11},{4,12},{5,13},{6,14},{7,15},{8,0},{9,1},... | collective-permute-start | bytes 589832 | tf_op jit(solution)/shard_map/ppermute | solution.py:44
  20.0 6.5 %collective-permute-start.6 = (bf16[2,2,2,24,256]{4,3,2,1,0:T(8,128)(2,1)S(1)}, bf16[2,2,2,24,256]{4,3,2,1,0:T(8,128)(2,1)S(1)}, u32[]{:S(2)}, u32[]{:S(2)}) collective-permute-start(bf16[2,2,2,24,256]{4,3,2,1,0:T(8,128)(2,1)S(1)} %join_core.1.own), channel_id=1, source_target_pairs={{0,4},{1,5},{2,6},{3,7},{4,0},{5,1},{6,2},{7,3},{8,12},{9,13},{10,... | collective-permute-start | bytes 294920 | tf_op jit(solution)/shard_map/ppermute | solution.py:44
  26.5 5.8 %collective-permute-start.8 = (bf16[2,2,2,24,256]{4,3,2,1,0:T(8,128)(2,1)S(1)}, bf16[2,2,2,24,256]{4,3,2,1,0:T(8,128)(2,1)S(1)}, u32[]{:S(2)}, u32[]{:S(2)}) collective-permute-start(bf16[2,2,2,24,256]{4,3,2,1,0:T(8,128)(2,1)S(1)} %choose.1.refs_1_), channel_id=1, source_target_pairs={{0,1},{1,0},{2,3},{3,2},{4,5},{5,4},{6,7},{7,6},{8,9},{9,8},{10,11... | collective-permute-start | bytes 294920 | tf_op jit(solution)/shard_map/ppermute | solution.py:44
  27.2 5.7 %collective-permute-start.9 = (bf16[2,2,2,24,256]{4,3,2,1,0:T(8,128)(2,1)S(1)}, bf16[2,2,2,24,256]{4,3,2,1,0:T(8,128)(2,1)S(1)}, u32[]{:S(2)}, u32[]{:S(2)}) collective-permute-start(bf16[2,2,2,24,256]{4,3,2,1,0:T(8,128)(2,1)S(1)} %choose.1.refs_1_), channel_id=1, source_target_pairs={{0,2},{1,3},{2,0},{3,1},{4,6},{5,7},{6,4},{7,5},{8,10},{9,11},{10,... | collective-permute-start | bytes 294920 | tf_op jit(solution)/shard_map/ppermute | solution.py:44
  28.4 5.5 %collective-permute-start.7 = (bf16[2,2,2,24,256]{4,3,2,1,0:T(8,128)(2,1)S(1)}, bf16[2,2,2,24,256]{4,3,2,1,0:T(8,128)(2,1)S(1)}, u32[]{:S(2)}, u32[]{:S(2)}) collective-permute-start(bf16[2,2,2,24,256]{4,3,2,1,0:T(8,128)(2,1)S(1)} %choose.1.refs_1_), channel_id=1, source_target_pairs={{0,3},{1,2},{2,1},{3,0},{4,7},{5,6},{6,5},{7,4},{8,11},{9,10},{10,... | collective-permute-start | bytes 294920 | tf_op jit(solution)/shard_map/ppermute | solution.py:44
  34.5 6.6 %collective-permute-start.10 = (bf16[144,128]{1,0:T(8,128)(2,1)S(1)}, bf16[144,128]{1,0:T(8,128)(2,1)S(1)}, u32[]{:S(2)}, u32[]{:S(2)}) collective-permute-start(bf16[144,128]{1,0:T(8,128)(2,1)S(1)} %get-tuple-element.27), channel_id=1, source_target_pairs={{0,96},{1,97},{2,98},{3,99},{4,100},{5,101},{6,102},{7,103},{8,104... | collective-permute-start | bytes 110600 | tf_op jit(solution)/shard_map/ppermute | solution.py:44
  36.9 7.9 %collective-permute-start.11 = (bf16[144,128]{1,0:T(8,128)(2,1)S(1)}, bf16[144,128]{1,0:T(8,128)(2,1)S(1)}, u32[]{:S(2)}, u32[]{:S(2)}) collective-permute-start(bf16[144,128]{1,0:T(8,128)(2,1)S(1)} %get-tuple-element.28), channel_id=1, source_target_pairs={{0,64},{1,65},{2,66},{3,67},{4,68},{5,69},{6,70},{7,71},{8,72},{9,... | collective-permute-start | bytes 110600 | tf_op jit(solution)/shard_map/ppermute | solution.py:44
  38.8 6.0 %collective-permute-start.12 = (bf16[144,128]{1,0:T(8,128)(2,1)S(1)}, bf16[144,128]{1,0:T(8,128)(2,1)S(1)}, u32[]{:S(2)}, u32[]{:S(2)}) collective-permute-start(bf16[144,128]{1,0:T(8,128)(2,1)S(1)} %get-tuple-element.29), channel_id=1, source_target_pairs={{0,32},{1,33},{2,34},{3,35},{4,36},{5,37},{6,38},{7,39},{8,40},{9,... | collective-permute-start | bytes 110600 | tf_op jit(solution)/shard_map/ppermute | solution.py:44
